TPU v7x, 32 devices: a whole 2x2x4 slice. The times are simulated.
32 devices in a mesh: row: 4 (over y, x), col: 8 (over z, core).
Axes of the slice: x: 2, y: 2, z: 4, core: 2. Of those that a mesh axis runs over, the one named last changes fastest.
Arguments:
- tokens: bfloat16 [8192, 2048], P('row', 'col'), may hold values from -6 to 6
- gain_attn: float32 [2048], P('col'), may hold values from 0.5 to 1.5
- gain_ffn: float32 [2048], P('col'), may hold values from 0.5 to 1.5
- gain_query: float32 [128], replicated, may hold values from 0.5 to 1.5
- gain_key: float32 [128], replicated, may hold values from 0.5 to 1.5
- w_query: bfloat16 [2048, 1024], P('col', 'row'), may hold values from -0.125 to 0.125
- w_key: bfloat16 [2048, 1024], P('col', 'row'), may hold values from -0.125 to 0.125
- w_value: bfloat16 [2048, 1024], P('col', 'row'), may hold values from -0.125 to 0.125
- w_out: bfloat16 [1024, 2048], P('col', 'row'), may hold values from -3 to 3
- w_router: bfloat16 [2048, 32], P('col', 'row'), may hold values from -0.0625 to 0.0625
- w_gate: bfloat16 [32, 2048, 1024], P('col', 'row'), may hold values from -0.125 to 0.125
- w_up: bfloat16 [32, 2048, 1024], P('col', 'row'), may hold values from -0.125 to 0.125
- w_down: bfloat16 [32, 1024, 2048], P('col', None, 'row'), may hold values from -0.75 to 0.75
- routes: int32 [8192, 8], P('row'), may hold values from 0 to 31, all different within a row; in each aligned block of 1024 rows (0 to 1023, 1024 to 2047, ...) at most 512 rows name the same one
- lengths: int32 [8, 4], P('row'), may hold values from 1 to 512, 1024 in all within a row
- cotangent: bfloat16 [8192, 2048], P('row', 'col'), may hold values from -6 to 6
Outputs:
- mixed: bfloat16 [8192, 2048], P('row', 'col')
- input_grad: float32 [8192, 2048], P('row', 'col')
- grad_gain_attn: float32 [2048], P('col')
- grad_gain_ffn: float32 [2048], P('col')
- grad_gain_query: float32 [128], replicated
- grad_gain_key: float32 [128], replicated
- grad_query: float32 [2048, 1024], P('col', 'row')
- grad_key: float32 [2048, 1024], P('col', 'row')
- grad_value: float32 [2048, 1024], P('col', 'row')
- grad_out: float32 [1024, 2048], P('col', 'row')
- grad_router: float32 [2048, 32], P('col', 'row')
- grad_gate: float32 [32, 2048, 1024], P('col', 'row')
- grad_up: float32 [32, 2048, 1024], P('col', 'row')
- grad_down: float32 [32, 1024, 2048], P('col', None, 'row')
Inputs may be any that keep to these rules, and one draw needn't show every extreme that they name: `routes`: in each aligned block of 1024 rows (one group), each row names 8 different experts and no expert is named more than 512 times; in every draw some expert is named exactly 512 times in a block. `lengths`: each row sums to 1024; the last entry counts padded rows; the largest entry of each row is exactly 512.
All inputs are finite; a program needn't handle non-finite values.
Results may differ from a plain program's by a relative error of at most 0.02.
Values may be sent and summed in bfloat16 or wider, within the bound.
A program may use at most 384 MiB of HBM per device.

v0:
```python
import math

import jax
import jax.numpy as jnp
from jax import lax
from jax.sharding import PartitionSpec as P

EPSILON = 1e-06
ROPE_BASE = 10000.0
MASKED = -1e30


def inverse_rms(values):
    return lax.rsqrt(jnp.mean(values * values, -1, keepdims=True) + EPSILON)


def rotary(values, position):
    half = values.shape[-1] // 2
    inverse = jnp.exp(
        -math.log(ROPE_BASE) * 2.0 / values.shape[-1] * jnp.arange(half, dtype=jnp.float32)
    )
    angles = position[:, None] * inverse[None, :]
    cosine = jnp.cos(angles)[:, None, :]
    sine = jnp.sin(angles)[:, None, :]
    first = values[..., :half]
    second = values[..., half:]
    return jnp.concatenate([first * cosine - second * sine, second * cosine + first * sine], -1)


def layout(lengths_row, group):
    ends = jnp.cumsum(lengths_row)
    starts = ends - lengths_row
    row_index = jnp.arange(group, dtype=jnp.int32)
    segment = jnp.sum((row_index[:, None] >= ends[None, :]).astype(jnp.int32), 1)
    member = segment[:, None] == jnp.arange(lengths_row.shape[0], dtype=jnp.int32)[None, :]
    position = (row_index - jnp.sum(jnp.where(member, starts[None, :], 0), 1)).astype(jnp.float32)
    live = (segment < lengths_row.shape[0] - 1).astype(jnp.float32)
    return (segment, position, live)


def slot_table(route_rows, experts, capacity):
    flat_experts = route_rows.reshape(-1)
    hits = (flat_experts[:, None] == jnp.arange(experts, dtype=jnp.int32)[None, :]).astype(
        jnp.int32
    )
    before = jnp.cumsum(hits, 0) - hits
    place = jnp.sum(before * hits, 1)
    flat = flat_experts * capacity + place
    pairs = flat_experts.shape[0]
    slot_token = (
        jnp.zeros((experts * capacity,), jnp.int32)
        .at[flat]
        .set(jnp.arange(pairs, dtype=jnp.int32) // route_rows.shape[1])
    )
    slot_live = jnp.zeros((experts * capacity,), jnp.float32).at[flat].set(1.0)
    return (flat, slot_token, slot_live)


def col_total(parts):
    return lax.psum(parts, "col")


def reduce_rows(parts, n_row):
    stacked = (
        tuple((jnp.broadcast_to(item[None], (n_row,) + item.shape) for item in parts[:4]))
        + parts[4:]
    )
    summed = (
        lax.psum_scatter(
            stacked[0].astype(jnp.bfloat16), "row", scatter_dimension=0, tiled=True
        ).astype(jnp.float32),
        lax.psum_scatter(
            stacked[1].astype(jnp.bfloat16), "row", scatter_dimension=0, tiled=True
        ).astype(jnp.float32),
        lax.psum_scatter(
            stacked[2].astype(jnp.bfloat16), "row", scatter_dimension=0, tiled=True
        ).astype(jnp.float32),
        lax.psum_scatter(
            stacked[3].astype(jnp.bfloat16), "row", scatter_dimension=0, tiled=True
        ).astype(jnp.float32),
        lax.psum_scatter(
            stacked[4].astype(jnp.bfloat16), "row", scatter_dimension=1, tiled=True
        ).astype(jnp.float32),
        lax.psum_scatter(
            stacked[5].astype(jnp.bfloat16), "row", scatter_dimension=1, tiled=True
        ).astype(jnp.float32),
        lax.psum_scatter(
            stacked[6].astype(jnp.bfloat16), "row", scatter_dimension=1, tiled=True
        ).astype(jnp.float32),
        lax.psum_scatter(
            stacked[7].astype(jnp.bfloat16), "row", scatter_dimension=1, tiled=True
        ).astype(jnp.float32),
        lax.psum_scatter(
            stacked[8].astype(jnp.bfloat16), "row", scatter_dimension=1, tiled=True
        ).astype(jnp.float32),
        lax.psum_scatter(
            stacked[9].astype(jnp.bfloat16), "row", scatter_dimension=1, tiled=True
        ).astype(jnp.float32),
        lax.psum_scatter(
            stacked[10].astype(jnp.bfloat16), "row", scatter_dimension=1, tiled=True
        ).astype(jnp.float32),
        lax.psum_scatter(
            stacked[11].astype(jnp.bfloat16), "row", scatter_dimension=2, tiled=True
        ).astype(jnp.float32),
    )
    return tuple((item[0] for item in summed[:4])) + summed[4:]


def micro_step(tokens_part, upstream_part, route_rows, lengths_row, gains, weights, width, n_col):
    gain_attn, gain_ffn, gain_query, gain_key = gains
    full_q, full_k, full_v, full_o, full_r, full_g, full_u, full_d = weights
    group = tokens_part.shape[0]
    head = gain_query.shape[0]
    local_heads = full_o.shape[0] // head
    experts = full_r.shape[1]
    exp_dev = full_g.shape[0]
    topk = route_rows.shape[1]
    capacity = 2 * group * topk // experts
    scale = head ** (-0.5)
    segment, position, live = layout(lengths_row, group)
    inputs = tokens_part.astype(jnp.float32)
    scale_one = lax.rsqrt(col_total(jnp.sum(inputs * inputs, -1)) / width + EPSILON)[:, None]
    normed = (inputs * scale_one * gain_attn).astype(jnp.bfloat16)
    query_pre, key_pre, value_pre = (
        lax.psum_scatter(
            jnp.dot(normed, full_q, preferred_element_type=jnp.float32),
            "col",
            scatter_dimension=1,
            tiled=True,
        ),
        lax.psum_scatter(
            jnp.dot(normed, full_k, preferred_element_type=jnp.float32),
            "col",
            scatter_dimension=1,
            tiled=True,
        ),
        lax.psum_scatter(
            jnp.dot(normed, full_v, preferred_element_type=jnp.float32),
            "col",
            scatter_dimension=1,
            tiled=True,
        ),
    )
    query_heads = query_pre.reshape(group, local_heads, head)
    key_heads = key_pre.reshape(group, local_heads, head)

    def head_norm(values, gain):
        return rotary(values * inverse_rms(values) * gain, position)

    query_rot, query_pull = jax.vjp(head_norm, query_heads, gain_query)
    key_rot, key_pull = jax.vjp(head_norm, key_heads, gain_key)
    queries = query_rot.astype(jnp.bfloat16)
    keys_low = key_rot.astype(jnp.bfloat16)
    values_low = value_pre.reshape(group, local_heads, head).astype(jnp.bfloat16)
    same = (segment[:, None] == segment[None, :])[None]

    def scores_of():
        raw = (
            jnp.einsum("qhd,khd->hqk", queries, keys_low, preferred_element_type=jnp.float32)
            * scale
        )
        return jnp.where(same, raw, MASKED)

    scores = scores_of()
    highest = jnp.max(scores, -1, keepdims=True)
    log_total = highest + jnp.log(jnp.sum(jnp.exp(scores - highest), -1, keepdims=True))
    probs_low = jnp.exp(scores - log_total).astype(jnp.bfloat16)
    attended = (
        jnp.einsum("hqk,khd->qhd", probs_low, values_low, preferred_element_type=jnp.float32)
        .astype(jnp.bfloat16)
        .reshape(group, local_heads * head)
    )
    branch = lax.psum_scatter(
        jnp.dot(attended, full_o, preferred_element_type=jnp.float32),
        "col",
        scatter_dimension=1,
        tiled=True,
    )
    hidden = inputs + branch
    scale_two = lax.rsqrt(col_total(jnp.sum(hidden * hidden, -1)) / width + EPSILON)[:, None]
    scaled_two = hidden * scale_two
    normed_ffn = (scaled_two * gain_ffn).astype(jnp.bfloat16)
    logits = col_total(jnp.dot(normed_ffn, full_r, preferred_element_type=jnp.float32))
    gates = jax.nn.softmax(jnp.take_along_axis(logits, route_rows, 1), -1)
    flat, slot_token, slot_live = slot_table(route_rows, experts, capacity)
    outgoing = (normed_ffn[slot_token] * slot_live[:, None].astype(jnp.bfloat16)).reshape(
        n_col, exp_dev, capacity, -1
    )
    expert_in = lax.all_to_all(outgoing, "col", split_axis=0, concat_axis=3, tiled=True)[0]
    gate_pre = jnp.einsum("ecd,edf->ecf", expert_in, full_g, preferred_element_type=jnp.float32)
    up_pre = jnp.einsum("ecd,edf->ecf", expert_in, full_u, preferred_element_type=jnp.float32)
    sigmoid_gate = jax.nn.sigmoid(gate_pre)
    silu_gate = gate_pre * sigmoid_gate
    inner = (silu_gate * up_pre).astype(jnp.bfloat16)
    expert_out = jnp.einsum(
        "ecf,efd->ecd", inner, full_d, preferred_element_type=jnp.float32
    ).astype(jnp.bfloat16)
    returned = lax.all_to_all(
        expert_out[None], "col", split_axis=3, concat_axis=0, tiled=True
    ).reshape(experts * capacity, -1)
    picked = returned[flat].reshape(group, topk, -1).astype(jnp.float32)
    mixed = (hidden + jnp.sum(gates[:, :, None] * picked, 1)).astype(jnp.bfloat16)
    upstream = upstream_part.astype(jnp.float32) * live[:, None]
    slot_grad = (
        jnp.zeros((experts * capacity, upstream.shape[1]), jnp.float32)
        .at[flat]
        .set((gates[:, :, None] * upstream[:, None, :]).reshape(group * topk, -1))
    )
    gate_dots = col_total(jnp.sum(picked * upstream[:, None, :], -1))
    expert_grad = lax.all_to_all(
        slot_grad.astype(jnp.bfloat16).reshape(n_col, exp_dev, capacity, -1),
        "col",
        split_axis=0,
        concat_axis=3,
        tiled=True,
    )[0]
    inner_grad = jnp.einsum("ecd,efd->ecf", expert_grad, full_d, preferred_element_type=jnp.float32)
    grad_down = jnp.einsum("ecf,ecd->efd", inner, expert_grad, preferred_element_type=jnp.float32)
    gate_grad = (
        inner_grad * up_pre * sigmoid_gate * (1.0 + gate_pre * (1.0 - sigmoid_gate))
    ).astype(jnp.bfloat16)
    up_grad = (inner_grad * silu_gate).astype(jnp.bfloat16)
    grad_gate = jnp.einsum("ecd,ecf->edf", expert_in, gate_grad, preferred_element_type=jnp.float32)
    grad_up = jnp.einsum("ecd,ecf->edf", expert_in, up_grad, preferred_element_type=jnp.float32)
    input_slots = (
        jnp.einsum("ecf,edf->ecd", gate_grad, full_g, preferred_element_type=jnp.float32)
        + jnp.einsum("ecf,edf->ecd", up_grad, full_u, preferred_element_type=jnp.float32)
    ).astype(jnp.bfloat16)
    back_slots = lax.all_to_all(
        input_slots[None], "col", split_axis=3, concat_axis=0, tiled=True
    ).reshape(experts * capacity, -1)
    selected_grad = gates * (gate_dots - jnp.sum(gates * gate_dots, -1, keepdims=True))
    chosen = (route_rows[:, :, None] == jnp.arange(experts, dtype=jnp.int32)[None, None, :]).astype(
        jnp.float32
    )
    logit_grad = jnp.sum(chosen * selected_grad[:, :, None], 1).astype(jnp.bfloat16)
    normed_grad = jnp.sum(
        back_slots[flat].reshape(group, topk, -1).astype(jnp.float32), 1
    ) + jnp.einsum("te,de->td", logit_grad, full_r, preferred_element_type=jnp.float32)
    grad_router = jnp.einsum(
        "td,te->de", normed_ffn, logit_grad, preferred_element_type=jnp.float32
    )
    grad_gain_ffn = jnp.sum(normed_grad * scaled_two, 0)
    weighted_two = normed_grad * gain_ffn
    dot_two = col_total(jnp.sum(weighted_two * hidden, -1))[:, None]
    hidden_grad = upstream + scale_two * weighted_two - hidden * scale_two**3 * dot_two / width
    branch_grad = lax.all_gather(hidden_grad.astype(jnp.bfloat16), "col", axis=1, tiled=True)
    attended_grad = (
        jnp.einsum("td,kd->tk", branch_grad, full_o, preferred_element_type=jnp.float32)
        .astype(jnp.bfloat16)
        .reshape(group, local_heads, head)
    )
    grad_out = jnp.einsum("tk,td->kd", attended, branch_grad, preferred_element_type=jnp.float32)
    scores_again = scores_of()
    probs = jnp.exp(scores_again - log_total)
    probs_again = probs.astype(jnp.bfloat16)
    probs_grad = jnp.einsum(
        "qhd,khd->hqk", attended_grad, values_low, preferred_element_type=jnp.float32
    )
    values_grad = jnp.einsum(
        "hqk,qhd->khd", probs_again, attended_grad, preferred_element_type=jnp.float32
    )
    score_grad = (probs * (probs_grad - jnp.sum(probs_grad * probs, -1, keepdims=True))).astype(
        jnp.bfloat16
    )
    query_grad_rot = (
        jnp.einsum("hqk,khd->qhd", score_grad, keys_low, preferred_element_type=jnp.float32) * scale
    )
    key_grad_rot = (
        jnp.einsum("hqk,qhd->khd", score_grad, queries, preferred_element_type=jnp.float32) * scale
    )
    query_grad, gain_query_part = query_pull(query_grad_rot)
    key_grad, gain_key_part = key_pull(key_grad_rot)
    full_dq, full_dk, full_dv = (
        lax.all_gather(
            query_grad.reshape(group, -1).astype(jnp.bfloat16), "col", axis=1, tiled=True
        ),
        lax.all_gather(key_grad.reshape(group, -1).astype(jnp.bfloat16), "col", axis=1, tiled=True),
        lax.all_gather(
            values_grad.reshape(group, -1).astype(jnp.bfloat16), "col", axis=1, tiled=True
        ),
    )
    normed_back = (
        jnp.einsum("tf,df->td", full_dq, full_q, preferred_element_type=jnp.float32)
        + jnp.einsum("tf,df->td", full_dk, full_k, preferred_element_type=jnp.float32)
        + jnp.einsum("tf,df->td", full_dv, full_v, preferred_element_type=jnp.float32)
    )
    grad_query = jnp.einsum("td,tf->df", normed, full_dq, preferred_element_type=jnp.float32)
    grad_key = jnp.einsum("td,tf->df", normed, full_dk, preferred_element_type=jnp.float32)
    grad_value = jnp.einsum("td,tf->df", normed, full_dv, preferred_element_type=jnp.float32)
    grad_gain_attn = jnp.sum(normed_back * inputs * scale_one, 0)
    weighted_one = normed_back * gain_attn
    dot_one, grad_gain_query, grad_gain_key = col_total(
        (jnp.sum(weighted_one * inputs, -1), gain_query_part, gain_key_part)
    )
    input_grad = (
        hidden_grad + scale_one * weighted_one - inputs * scale_one**3 * dot_one[:, None] / width
    )
    grads = (
        grad_gain_attn,
        grad_gain_ffn,
        grad_gain_query,
        grad_gain_key,
        grad_query,
        grad_key,
        grad_value,
        grad_out,
        grad_router,
        grad_gate,
        grad_up,
        grad_down,
    )
    return (mixed, input_grad, grads)


def shards(
    tokens,
    gain_attn,
    gain_ffn,
    gain_query,
    gain_key,
    w_query,
    w_key,
    w_value,
    w_out,
    w_router,
    w_gate,
    w_up,
    w_down,
    routes,
    lengths,
    cotangent,
):
    n_col = lax.axis_size("col")
    n_row = lax.axis_size("row")
    micro = lengths.shape[0]
    group = tokens.shape[0] // micro
    width = tokens.shape[1] * n_col
    weights = (
        lax.all_gather(w_query, "row", axis=1, tiled=True),
        lax.all_gather(w_key, "row", axis=1, tiled=True),
        lax.all_gather(w_value, "row", axis=1, tiled=True),
        lax.all_gather(w_out, "row", axis=1, tiled=True),
        lax.all_gather(w_router, "row", axis=1, tiled=True),
        lax.all_gather(w_gate, "row", axis=1, tiled=True),
        lax.all_gather(w_up, "row", axis=1, tiled=True),
        lax.all_gather(w_down, "row", axis=2, tiled=True),
    )
    gains = (gain_attn, gain_ffn, gain_query, gain_key)
    outputs = []
    input_grads = []
    totals = None
    for index in range(micro):
        rows = slice(index * group, (index + 1) * group)
        mixed, input_grad, grads = micro_step(
            tokens[rows],
            cotangent[rows],
            routes[rows],
            lengths[index],
            gains,
            weights,
            width,
            n_col,
        )
        outputs.append(mixed)
        input_grads.append(input_grad)
        totals = (
            grads
            if totals is None
            else tuple((first + second for first, second in zip(totals, grads)))
        )
    reduced = reduce_rows(totals, n_row)
    return (jnp.concatenate(outputs, 0), jnp.concatenate(input_grads, 0)) + tuple(reduced)


def solution(mesh):
    placed = (
        P("row", "col"),
        P("col"),
        P("col"),
        P(),
        P(),
        P("col", "row"),
        P("col", "row"),
        P("col", "row"),
        P("col", "row"),
        P("col", "row"),
        P("col", "row", None),
        P("col", "row", None),
        P("col", None, "row"),
        P("row", None),
        P("row", None),
        P("row", "col"),
    )
    return jax.shard_map(
        shards,
        mesh=mesh,
        in_specs=placed,
        out_specs=(
            P("row", "col"),
            P("row", "col"),
            P("col"),
            P("col"),
            P(),
            P(),
            P("col", "row"),
            P("col", "row"),
            P("col", "row"),
            P("col", "row"),
            P("col", "row"),
            P("col", "row", None),
            P("col", "row", None),
            P("col", None, "row"),
        ),
        check_vma=False,
    )
```

profile of v0, /device:TPU:0, one launch (start us, length us, event | category | flops | bytes accessed | tf_op | source)
XLA Modules:
  0.0 3152.2 jit_solution(3800082917945694567)
XLA Ops:
  9.6 18.3 all-reduce.17
  95.1 48.7 %reduce-scatter.20.cloned.1.call-done = f32[1024,128]{1,0:T(8,128)} async-done(((f32[1024,1024]{1,0:T(8,128)}), f32[1024,128]{1,0:T(8,128)}) %reduce-scatter.20.cloned.1.call-update) | async-done | bytes 524304 | tf_op jit(solution)/shard_map/reduce_scatter | solution.py:131
  145.1 49.8 %reduce-scatter.26.cloned.1.call-done = f32[1024,128]{1,0:T(8,128)} async-done(((f32[1024,1024]{1,0:T(8,128)}), f32[1024,128]{1,0:T(8,128)}) %reduce-scatter.26.cloned.1.call-update) | async-done | bytes 524304 | tf_op jit(solution)/shard_map/reduce_scatter | solution.py:125
  196.2 49.7 %reduce-scatter.18.cloned.1.call-done = f32[1024,128]{1,0:T(8,128)} async-done(((f32[1024,1024]{1,0:T(8,128)}), f32[1024,128]{1,0:T(8,128)}) %reduce-scatter.18.cloned.1.call-update) | async-done | bytes 524304 | tf_op jit(solution)/shard_map/reduce_scatter | solution.py:125
  260.2 36.0 %reduce-scatter.24.cloned.1.call-done = f32[1024,128]{1,0:T(8,128)} async-done(((f32[1024,1024]{1,0:T(8,128)}), f32[1024,128]{1,0:T(8,128)}) %reduce-scatter.24.cloned.1.call-update) | async-done | bytes 524304 | tf_op jit(solution)/shard_map/reduce_scatter | solution.py:137
  308.6 37.9 %reduce-scatter.16.cloned.1.call-done = f32[1024,128]{1,0:T(8,128)} async-done(((f32[1024,1024]{1,0:T(8,128)}), f32[1024,128]{1,0:T(8,128)}) %reduce-scatter.16.cloned.1.call-update) | async-done | bytes 524304 | tf_op jit(solution)/shard_map/reduce_scatter | solution.py:137
  364.1 73.1 %reduce-scatter.30.cloned.1.call-done = f32[1024,256]{1,0:T(8,128)} async-done(((f32[1024,2048]{1,0:T(8,128)}), f32[1024,256]{1,0:T(8,128)}) %reduce-scatter.30.cloned.1.call-update) | async-done | bytes 1048592 | tf_op jit(solution)/shard_map/reduce_scatter | solution.py:173
  437.2 90.9 %reduce-scatter.22.cloned.1.call-done = f32[1024,256]{1,0:T(8,128)} async-done(((f32[1024,2048]{1,0:T(8,128)}), f32[1024,256]{1,0:T(8,128)}) %reduce-scatter.22.cloned.1.call-update) | async-done | bytes 1048592 | tf_op jit(solution)/shard_map/reduce_scatter | solution.py:173
  550.2 17.2 reduce-window.21
  569.8 30.5 scatter_custom_fusion.1
  600.4 30.5 scatter_custom_fusion
  630.9 65.3 %gather_fusion = bf16[16384,256]{1,0:T(8,128)(2,1)} fusion(bf16[1024,256]{1,0:T(8,128)(2,1)S(1)} %get-tuple-element.118, s32[16384]{0:T(1024)S(1)} %fusion.198), kind=kCustom, calls=%fused_computation.2 | custom fusion | bytes 16842752 | tf_op jit(solution)/shard_map/gather | solution.py:186
  711.9 17.2 reduce-window.26
  731.4 30.5 scatter_custom_fusion.3
  761.9 30.5 scatter_custom_fusion.2
  792.5 65.3 %gather_fusion.2 = bf16[16384,256]{1,0:T(8,128)(2,1)} fusion(bf16[1024,256]{1,0:T(8,128)(2,1)S(1)} %get-tuple-element.119, s32[16384]{0:T(1024)S(1)} %fusion.199), kind=kCustom, calls=%fused_computation.4 | custom fusion | bytes 16842752 | tf_op jit(solution)/shard_map/gather | solution.py:186
  865.7 27.3 all-to-all-done
  901.8 56.6 %gather_fusion.6 = f32[8192]{0:T(1024)S(1)} fusion(f32[1024,32]{0,1:T(8,128)} %get-tuple-element.52, s32[8192]{0:T(1024)S(1)} %reshape.1015), kind=kCustom, calls=%fused_computation.clone | custom fusion | bytes 131072 | tf_op jit(solution)/shard_map/jit(take_along_axis)/gather | solution.py:184
  959.5 65.5 %gather_fusion.7 = f32[8192]{0:T(1024)S(1)} fusion(f32[1024,32]{0,1:T(8,128)S(1)} %copy-done, s32[8192]{0:T(1024)S(1)} %copy-done.5), kind=kCustom, calls=%fused_computation.1.clone | custom fusion | bytes 131072 | tf_op jit(solution)/shard_map/jit(take_along_axis)/gather | solution.py:184
  1027.8 45.2 %scatter_custom_fusion.4 = f32[16384,256]{1,0:T(8,128)} fusion(s32[8192]{0:T(1024)} %bitcast.399, f32[]{:T(128)} %constant.77.clone.1, f32[1024,256]{1,0:T(8,128)S(1)} %copy-done.32, f32[8192]{0:T(1024)S(1)} %mul.1018), kind=kCustom, calls=%fused_computation.34 | custom fusion | flops 2097152 | bytes 17859072 | tf_op jit(solution)/shard_map/scatter | solution.py:207
  1088.3 45.2 %scatter_custom_fusion.5 = f32[16384,256]{1,0:T(8,128)} fusion(s32[8192]{0:T(1024)} %bitcast.403, f32[]{:T(128)} %constant.77.clone.1, f32[1024,256]{1,0:T(8,128)S(1)} %copy-done.30, f32[8192]{0:T(1024)S(1)} %mul.1083), kind=kCustom, calls=%fused_computation.32 | custom fusion | flops 2097152 | bytes 17859072 | tf_op jit(solution)/shard_map/scatter | solution.py:207
  1142.3 128.8 %all-to-all-done.4 = bf16[8,4,512,256]{3,2,1,0:T(8,128)(2,1)} async-done(((bf16[8,4,512,256]{3,2,1,0:T(8,128)(2,1)}), bf16[8,4,512,256]{3,2,1,0:T(8,128)(2,1)}, u32[]{:S(2)}, u32[]{:S(2)}) %all-to-all-start.4) | async-done | bytes 8388640 | tf_op jit(solution)/shard_map/all_to_all | solution.py:210
  1301.6 16.8 fusion.262
  1318.5 17.0 fusion.261
  1360.6 22.9 multiply_convert_fusion.2
  1383.4 17.5 convert_bitcast_fusion.1
  1400.9 14.5 copy.100
  1415.4 45.0 %all-to-all-done.6 = bf16[8,4,512,256]{3,2,1,0:T(8,128)(2,1)} async-done(((bf16[8,4,512,256]{3,2,1,0:T(8,128)(2,1)}), bf16[8,4,512,256]{3,2,1,0:T(8,128)(2,1)}, u32[]{:S(2)}, u32[]{:S(2)}) %all-to-all-start.6) | async-done | bytes 8388640 | tf_op jit(solution)/shard_map/all_to_all | solution.py:210
  1490.7 16.9 fusion.266
  1507.6 14.9 fusion.265
  1547.6 22.7 multiply_convert_fusion
  1570.3 17.6 convert_bitcast_fusion
  1588.0 14.5 copy.104
  1602.5 47.1 %all-to-all-done.1 = bf16[1,4,512,2048]{2,1,0,3:T(4,128)(2,1)} async-done(((bf16[1,4,512,2048]{2,1,0,3:T(4,128)(2,1)}), bf16[1,4,512,2048]{2,1,0,3:T(4,128)(2,1)}, u32[]{:S(2)}, u32[]{:S(2)}) %all-to-all-start.1) | async-done | bytes 8388640 | tf_op jit(solution)/shard_map/all_to_all | solution.py:198
  1654.5 17.0 fusion.267
  1671.5 18.2 fusion.4
  1689.6 14.6 copy.107
  1704.2 134.2 %all-to-all-done.3 = bf16[1,4,512,2048]{2,1,0,3:T(4,128)(2,1)} async-done(((bf16[1,4,512,2048]{2,1,0,3:T(4,128)(2,1)}), bf16[1,4,512,2048]{2,1,0,3:T(4,128)(2,1)}, u32[]{:S(2)}, u32[]{:S(2)}) %all-to-all-start.3) | async-done | bytes 8388640 | tf_op jit(solution)/shard_map/all_to_all | solution.py:198
  1843.6 17.0 fusion.268
  1860.5 18.2 fusion.5
  1878.7 14.5 copy.114
  1893.2 134.2 %all-to-all-done.5 = bf16[1,4,512,2048]{2,1,0,3:T(4,128)(2,1)} async-done(((bf16[1,4,512,2048]{2,1,0,3:T(4,128)(2,1)}), bf16[1,4,512,2048]{2,1,0,3:T(4,128)(2,1)}, u32[]{:S(2)}, u32[]{:S(2)}) %all-to-all-start.5) | async-done | bytes 8388640 | tf_op jit(solution)/shard_map/all_to_all | solution.py:229
  2074.0 35.4 %gather_fusion.1 = bf16[8192,256]{1,0:T(8,128)(2,1)} fusion(bf16[16384,256]{1,0:T(8,128)(2,1)} %bitcast.386, s32[8192]{0:T(1024)S(1)} %broadcast_clamp_fusion.1), kind=kCustom, calls=%fused_computation.3 | custom fusion | bytes 8421376 | tf_op jit(solution)/shard_map/gather | solution.py:201
  2109.4 35.4 %gather_fusion.4 = bf16[8192,256]{1,0:T(8,128)(2,1)} fusion(bf16[16384,256]{1,0:T(8,128)(2,1)} %bitcast.387, s32[8192]{0:T(1024)S(1)} %broadcast_clamp_fusion.1), kind=kCustom, calls=%fused_computation.6 | custom fusion | bytes 8421376 | tf_op jit(solution)/shard_map/gather | solution.py:238
  2144.8 35.5 %gather_fusion.3 = bf16[8192,256]{1,0:T(8,128)(2,1)} fusion(bf16[16384,256]{1,0:T(8,128)(2,1)} %bitcast.385, s32[8192]{0:T(1024)S(1)} %broadcast_clamp_fusion), kind=kCustom, calls=%fused_computation.5 | custom fusion | bytes 8421376 | tf_op jit(solution)/shard_map/gather | solution.py:201
  2202.0 14.3 all-to-all-done.7
  2230.1 35.6 %gather_fusion.5 = bf16[8192,256]{1,0:T(8,128)(2,1)} fusion(bf16[16384,256]{1,0:T(8,128)(2,1)} %bitcast.388, s32[8192]{0:T(1024)S(1)} %broadcast_clamp_fusion), kind=kCustom, calls=%fused_computation.7 | custom fusion | bytes 8421376 | tf_op jit(solution)/shard_map/gather | solution.py:238
  2271.7 52.1 %all-reduce.23.cloned.1.call-done = (f32[1024,8]{1,0:T(8,128)}, f32[1024,8]{1,0:T(8,128)}) async-done(((f32[1024,8]{1,0:T(8,128)}, f32[1024,8]{1,0:T(8,128)}), (f32[1024,8]{1,0:T(8,128)}, f32[1024,8]{1,0:T(8,128)})) %all-reduce.23.cloned.1.call-update) | async-done | bytes 65552 | tf_op jit(solution)/shard_map/psum | solution.py:60
  2356.6 45.5 %all-gather.26.cloned.1.call-done = bf16[1024,2048]{1,0:T(8,128)(2,1)} async-done(((bf16[1024,256]{1,0:T(8,128)(2,1)}), bf16[1024,2048]{1,0:T(8,128)(2,1)}) %all-gather.26.cloned.1.call-update) | async-done | bytes 4194320 | tf_op jit(solution)/shard_map/all_gather | solution.py:247
  2407.4 42.8 %all-gather.24.cloned.1.call-done = bf16[1024,2048]{1,0:T(8,128)(2,1)} async-done(((bf16[1024,256]{1,0:T(8,128)(2,1)}), bf16[1024,2048]{1,0:T(8,128)(2,1)}) %all-gather.24.cloned.1.call-update) | async-done | bytes 4194320 | tf_op jit(solution)/shard_map/all_gather | solution.py:247
  2486.7 23.2 all-gather.32.cloned.1.call-done
  2513.5 29.0 all-gather.34.cloned.1.call-done
  2544.9 29.6 all-gather.28.cloned.1.call-done
  2577.8 19.7 fusion.272
  2609.0 29.6 all-gather.30.cloned.1.call-done
  2642.1 22.6 add_convert_fusion
  2664.7 19.7 fusion.271
  2684.4 23.3 add_convert_fusion.1
  2708.0 20.0 fusion.270
  2728.0 23.1 add_convert_fusion.2
  2767.9 27.0 all-reduce.13
  2794.9 17.1 all-reduce.19
  2832.8 147.8 %reduce-scatter.42.cloned.1.call-done = bf16[4,512,1024]{2,1,0:T(8,128)(2,1)} async-done(((bf16[4,2048,1024]{2,1,0:T(8,128)(2,1)}), bf16[4,512,1024]{2,1,0:T(8,128)(2,1)}) %reduce-scatter.42.cloned.1.call-update) | async-done | bytes 4194320 | tf_op jit(solution)/shard_map/reduce_scatter | solution.py:99
  2987.2 150.4 %reduce-scatter.40.cloned.1.call-done = bf16[4,512,1024]{2,1,0:T(8,128)(2,1)} async-done(((bf16[4,2048,1024]{2,1,0:T(8,128)(2,1)}), bf16[4,512,1024]{2,1,0:T(8,128)(2,1)}) %reduce-scatter.40.cloned.1.call-update) | async-done | bytes 4194320 | tf_op jit(solution)/shard_map/reduce_scatter | solution.py:96
  (565 shorter events, 558.9 us)
Async XLA Ops:
  8.0 85.8 %reduce-scatter.28.cloned.1.call-start = ((), (), s32[]{:S(2)}) async-start(), calls=%async_computation.32 | async-start | bytes 4718592 | tf_op jit(solution)/shard_map/reduce_scatter | solution.py:131
  45.1 98.7 %reduce-scatter.20.cloned.1.call-start = ((), (), s32[]{:S(2)}) async-start(), calls=%async_computation.25 | async-start | bytes 4718592 | tf_op jit(solution)/shard_map/reduce_scatter | solution.py:131
  48.6 146.3 %reduce-scatter.26.cloned.1.call-start = ((), (), s32[]{:S(2)}) async-start(), calls=%async_computation.31 | async-start | bytes 4718592 | tf_op jit(solution)/shard_map/reduce_scatter | solution.py:125
  63.2 182.6 %reduce-scatter.18.cloned.1.call-start = ((), (), s32[]{:S(2)}) async-start(), calls=%async_computation.24 | async-start | bytes 4718592 | tf_op jit(solution)/shard_map/reduce_scatter | solution.py:125
  66.1 230.1 %reduce-scatter.24.cloned.1.call-start = ((), (), s32[]{:S(2)}) async-start(), calls=%async_computation.30 | async-start | bytes 4718592 | tf_op jit(solution)/shard_map/reduce_scatter | solution.py:137
  80.5 266.0 %reduce-scatter.16.cloned.1.call-start = ((), (), s32[]{:S(2)}) async-start(), calls=%async_computation.23 | async-start | bytes 4718592 | tf_op jit(solution)/shard_map/reduce_scatter | solution.py:137
  83.3 164.4 %copy-start.140 = (f32[128]{0:T(128)S(1)}, f32[128]{0:T(128)}, u32[]{:S(2)}) copy-start(f32[128]{0:T(128)} %param.22) | copy-start | bytes 1540
  83.3 166.0 %copy-start.138 = (f32[128]{0:T(128)S(1)}, f32[128]{0:T(128)}, u32[]{:S(2)}) copy-start(f32[128]{0:T(128)} %param.21) | copy-start | bytes 1540
  83.3 353.9 %reduce-scatter.30.cloned.1.call-start = ((), (), s32[]{:S(2)}) async-start(), calls=%async_computation.33 | async-start | bytes 9437184 | tf_op jit(solution)/shard_map/reduce_scatter | solution.py:173
  93.4 256.3 %copy-start.45 = (bf16[128,2048]{1,0:T(8,128)(2,1)}, bf16[128,2048]{1,0:T(8,128)(2,1)S(1)}, u32[]{:S(2)}) copy-start(bf16[128,2048]{1,0:T(8,128)(2,1)S(1)} %all_gather.51) | copy-start | bytes 1572868
  93.4 162.5 %copy-start.144 = (f32[64]{0:T(128)}, f32[64]{0:T(128)S(1)}, u32[]{:S(2)}) copy-start(f32[64]{0:T(128)S(1)} %multiply_exponential_fusion) | copy-start | bytes 772
  93.8 162.1 %copy-start.116 = (f32[1024]{0:T(1024)}, f32[1024]{0:T(1024)S(1)}, u32[]{:S(2)}) copy-start(f32[1024]{0:T(1024)S(1)} %subtract_convert_fusion) | copy-start | bytes 12292
  93.8 162.1 %copy-start.118 = (f32[1024]{0:T(1024)}, f32[1024]{0:T(1024)S(1)}, u32[]{:S(2)}) copy-start(f32[1024]{0:T(1024)S(1)} %subtract_convert_fusion.1) | copy-start | bytes 12292
  95.1 155.7 %copy-start.124 = (f32[1024]{0:T(1024)}, f32[1024]{0:T(1024)S(1)}, u32[]{:S(2)}) copy-start(f32[1024]{0:T(1024)S(1)} %multiply_reduce_fusion.10) | copy-start | bytes 12292
  145.1 105.7 %copy-start.126 = (f32[1024]{0:T(1024)}, f32[1024]{0:T(1024)S(1)}, u32[]{:S(2)}) copy-start(f32[1024]{0:T(1024)S(1)} %multiply_reduce_fusion.12) | copy-start | bytes 12292
  196.1 54.7 %copy-start.128 = (f32[1024]{0:T(1024)}, f32[1024]{0:T(1024)S(1)}, u32[]{:S(2)}) copy-start(f32[1024]{0:T(1024)S(1)} %multiply_reduce_fusion.11) | copy-start | bytes 12292
  304.7 223.3 %reduce-scatter.22.cloned.1.call-start = ((), (), s32[]{:S(2)}) async-start(), calls=%async_computation.26 | async-start | bytes 9437184 | tf_op jit(solution)/shard_map/reduce_scatter | solution.py:173
  355.3 189.8 %copy-start.136 = (f32[256]{0:T(256)S(1)}, f32[256]{0:T(256)}, u32[]{:S(2)}) copy-start(f32[256]{0:T(256)} %param.20) | copy-start | bytes 3076
  355.3 546.5 %all-reduce.25.cloned.1.call-start = ((), (), s32[]{:S(2)}) async-start(), calls=%async_computation.50 | async-start | bytes 524288 | tf_op jit(solution)/shard_map/psum | solution.py:60
  364.1 182.4 %copy-start.80 = (bf16[256,32]{0,1:T(8,128)(2,1)}, bf16[256,32]{0,1:T(8,128)(2,1)S(1)}, u32[]{:S(2)}) copy-start(bf16[256,32]{0,1:T(8,128)(2,1)S(1)} %all_gather.52) | copy-start | bytes 49156
  545.5 85.4 %copy-start.3 = (bf16[1024,256]{1,0:T(8,128)(2,1)}, bf16[1024,256]{1,0:T(8,128)(2,1)S(1)}, u32[]{:S(2)}) copy-start(bf16[1024,256]{1,0:T(8,128)(2,1)S(1)} %get-tuple-element.118) | copy-start | bytes 1572868
  545.5 247.0 %copy-start.1 = (bf16[1024,256]{1,0:T(8,128)(2,1)}, bf16[1024,256]{1,0:T(8,128)(2,1)S(1)}, u32[]{:S(2)}) copy-start(bf16[1024,256]{1,0:T(8,128)(2,1)S(1)} %get-tuple-element.119) | copy-start | bytes 1572868
  547.4 754.2 %all-gather.20.cloned.1.call-start = ((), (), s32[]{:S(2)}) async-start(), calls=%async_computation.28 | async-start | bytes 20971520 | tf_op jit(solution)/shard_map/all_gather | solution.py:346
  548.1 161.6 %copy-start.88 = (s32[1024,8]{0,1:T(8,128)}, s32[1024,8]{0,1:T(8,128)S(1)}, u32[]{:S(2)}) copy-start(s32[1024,8]{0,1:T(8,128)S(1)} %get-tuple-element.99) | copy-start | bytes 98308
  548.3 351.3 %copy-start.14 = (s32[1024,8]{1,0:T(8,128)}, s32[1024,8]{1,0:T(8,128)S(1)}, u32[]{:S(2)}) copy-start(s32[1024,8]{1,0:T(8,128)S(1)} %copy.136) | copy-start | bytes 98308
  569.8 126.4 %copy-start.95 = (s32[8192,1]{0,1:T(1,128)}, s32[8192,1]{0,1:T(1,128)S(1)}, u32[]{:S(2)}) copy-start(s32[8192,1]{0,1:T(1,128)S(1)} %compare_select_fusion.3) | copy-start | bytes 98308
  704.1 188.9 %all-to-all-start = ((bf16[8,4,512,256]{3,2,1,0:T(8,128)(2,1)}), bf16[8,4,512,256]{3,2,1,0:T(8,128)(2,1)}, u32[]{:S(2)}, u32[]{:S(2)}) async-start(bf16[8,4,512,256]{3,2,1,0:T(8,128)(2,1)} %broadcast_multiply_fusion.1), calls=%async_computation.4 | async-start | bytes 16777216 | tf_op jit(solution)/shard_map/all_to_all | solution.py:189
  709.1 609.4 %all-gather.18.cloned.1.call-start = ((), (), s32[]{:S(2)}) async-start(), calls=%async_computation.27 | async-start | bytes 20971520 | tf_op jit(solution)/shard_map/all_gather | solution.py:345
  709.9 188.6 %copy-start.16 = (s32[1024,8]{1,0:T(8,128)}, s32[1024,8]{1,0:T(8,128)S(1)}, u32[]{:S(2)}) copy-start(s32[1024,8]{1,0:T(8,128)S(1)} %copy.137) | copy-start | bytes 98308
  731.4 61.0 %copy-start.97 = (s32[8192,1]{0,1:T(1,128)}, s32[8192,1]{0,1:T(1,128)S(1)}, u32[]{:S(2)}) copy-start(s32[8192,1]{0,1:T(1,128)S(1)} %compare_select_fusion.2) | copy-start | bytes 98308
  893.0 188.9 %all-to-all-start.2 = ((bf16[8,4,512,256]{3,2,1,0:T(8,128)(2,1)}), bf16[8,4,512,256]{3,2,1,0:T(8,128)(2,1)}, u32[]{:S(2)}, u32[]{:S(2)}) async-start(bf16[8,4,512,256]{3,2,1,0:T(8,128)(2,1)} %broadcast_multiply_fusion), calls=%async_computation.10 | async-start | bytes 16777216 | tf_op jit(solution)/shard_map/all_to_all | solution.py:189
  898.0 462.6 %all-gather.22.cloned.1.call-start = ((), (), s32[]{:S(2)}) async-start(), calls=%async_computation.29 | async-start | bytes 20971520 | tf_op jit(solution)/shard_map/all_gather | solution.py:347
  901.8 57.7 %copy-start.5 = (s32[8192]{0:T(1024)S(1)}, s32[8192]{0:T(1024)}, u32[]{:S(2)}) copy-start(s32[8192]{0:T(1024)} %reshape.1020) | copy-start | bytes 98308
  959.5 65.9 %copy-start.15 = (s32[1024,8]{1,0:T(8,128)S(1)}, s32[1024,8]{1,0:T(8,128)}, u32[]{:S(2)}) copy-start(s32[1024,8]{1,0:T(8,128)} %copy-done.14) | copy-start | bytes 98308
  959.5 65.9 %copy-start.17 = (s32[1024,8]{1,0:T(8,128)S(1)}, s32[1024,8]{1,0:T(8,128)}, u32[]{:S(2)}) copy-start(s32[1024,8]{1,0:T(8,128)} %copy-done.16) | copy-start | bytes 98308
  959.5 65.9 %copy-start.41 = (f32[1024,8]{1,0:T(8,128)S(1)}, f32[1024,8]{1,0:T(8,128)}, u32[]{:S(2)}) copy-start(f32[1024,8]{1,0:T(8,128)} %reshape.1018) | copy-start | bytes 98308
  1081.9 189.3 %all-to-all-start.4 = ((bf16[8,4,512,256]{3,2,1,0:T(8,128)(2,1)}), bf16[8,4,512,256]{3,2,1,0:T(8,128)(2,1)}, u32[]{:S(2)}, u32[]{:S(2)}) async-start(bf16[8,4,512,256]{3,2,1,0:T(8,128)(2,1)} %bitcast.390), calls=%async_computation.12 | async-start | bytes 16777216 | tf_op jit(solution)/shard_map/all_to_all | solution.py:210
  1271.2 189.2 %all-to-all-start.6 = ((bf16[8,4,512,256]{3,2,1,0:T(8,128)(2,1)}), bf16[8,4,512,256]{3,2,1,0:T(8,128)(2,1)}, u32[]{:S(2)}, u32[]{:S(2)}) async-start(bf16[8,4,512,256]{3,2,1,0:T(8,128)(2,1)} %bitcast.389), calls=%async_computation.14 | async-start | bytes 16777216 | tf_op jit(solution)/shard_map/all_to_all | solution.py:210
  1460.4 189.1 %all-to-all-start.1 = ((bf16[1,4,512,2048]{2,1,0,3:T(4,128)(2,1)}), bf16[1,4,512,2048]{2,1,0,3:T(4,128)(2,1)}, u32[]{:S(2)}, u32[]{:S(2)}) async-start(bf16[1,4,512,2048]{2,1,0,3:T(4,128)(2,1)} %copy.100), calls=%async_computation.5 | async-start | bytes 16777216 | tf_op jit(solution)/shard_map/all_to_all | solution.py:198
  1649.5 188.8 %all-to-all-start.3 = ((bf16[1,4,512,2048]{2,1,0,3:T(4,128)(2,1)}), bf16[1,4,512,2048]{2,1,0,3:T(4,128)(2,1)}, u32[]{:S(2)}, u32[]{:S(2)}) async-start(bf16[1,4,512,2048]{2,1,0,3:T(4,128)(2,1)} %copy.104), calls=%async_computation.11 | async-start | bytes 16777216 | tf_op jit(solution)/shard_map/all_to_all | solution.py:198
  1838.4 189.1 %all-to-all-start.5 = ((bf16[1,4,512,2048]{2,1,0,3:T(4,128)(2,1)}), bf16[1,4,512,2048]{2,1,0,3:T(4,128)(2,1)}, u32[]{:S(2)}, u32[]{:S(2)}) async-start(bf16[1,4,512,2048]{2,1,0,3:T(4,128)(2,1)} %copy.107), calls=%async_computation.13 | async-start | bytes 16777216 | tf_op jit(solution)/shard_map/all_to_all | solution.py:229
  1893.2 139.2 %copy-start.98 = (s32[8192,1]{0,1:T(1,128)S(1)}, s32[8192,1]{0,1:T(1,128)}, u32[]{:S(2)}) copy-start(s32[8192,1]{0,1:T(1,128)} %copy-done.97) | copy-start | bytes 98308
  1893.2 139.3 %copy-start.96 = (s32[8192,1]{0,1:T(1,128)S(1)}, s32[8192,1]{0,1:T(1,128)}, u32[]{:S(2)}) copy-start(s32[8192,1]{0,1:T(1,128)} %copy-done.95) | copy-start | bytes 98308
  2027.4 188.8 %all-to-all-start.7 = ((bf16[1,4,512,2048]{2,1,0,3:T(4,128)(2,1)}), bf16[1,4,512,2048]{2,1,0,3:T(4,128)(2,1)}, u32[]{:S(2)}, u32[]{:S(2)}) async-start(bf16[1,4,512,2048]{2,1,0,3:T(4,128)(2,1)} %copy.114), calls=%async_computation.15 | async-start | bytes 16777216 | tf_op jit(solution)/shard_map/all_to_all | solution.py:229
  2032.4 291.5 %all-reduce.23.cloned.1.call-start = ((), (), s32[]{:S(2)}) async-start(), calls=%async_computation.49 | async-start | bytes 2097152 | tf_op jit(solution)/shard_map/psum | solution.py:60
  2265.8 62.8 %copy-start.89 = (s32[1024,8]{0,1:T(8,128)S(1)}, s32[1024,8]{0,1:T(8,128)}, u32[]{:S(2)}) copy-start(s32[1024,8]{0,1:T(8,128)} %copy-done.88) | copy-start | bytes 98308
  2265.8 136.2 %all-gather.26.cloned.1.call-start = ((), (), s32[]{:S(2)}) async-start(), calls=%async_computation.35 | async-start | bytes 4718592 | tf_op jit(solution)/shard_map/all_gather | solution.py:247
  2271.7 59.6 %copy-start.87 = (s32[1024,8]{0,1:T(8,128)S(1)}, s32[1024,8]{0,1:T(8,128)}, u32[]{:S(2)}) copy-start(s32[1024,8]{0,1:T(8,128)} %copy-done.86) | copy-start | bytes 98308
  2271.7 59.8 %copy-start.81 = (bf16[256,32]{0,1:T(8,128)(2,1)S(1)}, bf16[256,32]{0,1:T(8,128)(2,1)}, u32[]{:S(2)}) copy-start(bf16[256,32]{0,1:T(8,128)(2,1)} %copy-done.80) | copy-start | bytes 49156
  2355.9 94.3 %all-gather.24.cloned.1.call-start = ((), (), s32[]{:S(2)}) async-start(), calls=%async_computation.34 | async-start | bytes 4718592 | tf_op jit(solution)/shard_map/all_gather | solution.py:247
  2356.5 93.7 %copy-start.46 = (bf16[128,2048]{1,0:T(8,128)(2,1)S(1)}, bf16[128,2048]{1,0:T(8,128)(2,1)}, u32[]{:S(2)}) copy-start(bf16[128,2048]{1,0:T(8,128)(2,1)} %copy-done.45) | copy-start | bytes 1572868
  2356.5 127.6 %all-gather.38.cloned.1.call-start = ((), (), s32[]{:S(2)}) async-start(), calls=%async_computation.48 | async-start | bytes 2359296 | tf_op jit(solution)/shard_map/all_gather | solution.py:279
  2407.4 102.6 %all-gather.32.cloned.1.call-start = ((), (), s32[]{:S(2)}) async-start(), calls=%async_computation.45 | async-start | bytes 2359296 | tf_op jit(solution)/shard_map/all_gather | solution.py:279
  2455.4 87.1 %all-gather.34.cloned.1.call-start = ((), (), s32[]{:S(2)}) async-start(), calls=%async_computation.46 | async-start | bytes 2359296 | tf_op jit(solution)/shard_map/all_gather | solution.py:275
  2474.5 100.0 %all-gather.28.cloned.1.call-start = ((), (), s32[]{:S(2)}) async-start(), calls=%async_computation.43 | async-start | bytes 2359296 | tf_op jit(solution)/shard_map/all_gather | solution.py:275
  2475.1 131.5 %all-gather.36.cloned.1.call-start = ((), (), s32[]{:S(2)}) async-start(), calls=%async_computation.47 | async-start | bytes 2359296 | tf_op jit(solution)/shard_map/all_gather | solution.py:278
  2478.3 160.3 %all-gather.30.cloned.1.call-start = ((), (), s32[]{:S(2)}) async-start(), calls=%async_computation.44 | async-start | bytes 2359296 | tf_op jit(solution)/shard_map/all_gather | solution.py:278
  2478.9 276.7 %reduce-scatter.38.cloned.1.call-start = ((), (), s32[]{:S(2)}) async-start(), calls=%async_computation.39 | async-start | bytes 655360 | tf_op jit(solution)/shard_map/reduce_scatter | solution.py:90
  2484.0 337.1 %reduce-scatter.36.cloned.1.call-start = ((), (), s32[]{:S(2)}) async-start(), calls=%async_computation.38 | async-start | bytes 655360 | tf_op jit(solution)/shard_map/reduce_scatter | solution.py:87
  2513.4 309.3 %reduce-scatter.32.cloned.1.call-start = ((), (), s32[]{:S(2)}) async-start(), calls=%async_computation.36 | async-start | bytes 655360 | tf_op jit(solution)/shard_map/reduce_scatter | solution.py:81
  2577.7 246.7 %reduce-scatter.34.cloned.1.call-start = ((), (), s32[]{:S(2)}) async-start(), calls=%async_computation.37 | async-start | bytes 655360 | tf_op jit(solution)/shard_map/reduce_scatter | solution.py:84
  2641.9 184.2 %reduce-scatter.44.cloned.1.call-start = ((), (), s32[]{:S(2)}) async-start(), calls=%async_computation.42 | async-start | bytes 20971520 | tf_op jit(solution)/shard_map/reduce_scatter | solution.py:102
  2664.7 315.9 %reduce-scatter.42.cloned.1.call-start = ((), (), s32[]{:S(2)}) async-start(), calls=%async_computation.41 | async-start | bytes 20971520 | tf_op jit(solution)/shard_map/reduce_scatter | solution.py:99
  2707.7 429.9 %reduce-scatter.40.cloned.1.call-start = ((), (), s32[]{:S(2)}) async-start(), calls=%async_computation.40 | async-start | bytes 20971520 | tf_op jit(solution)/shard_map/reduce_scatter | solution.py:96
  (119 other events, 1349.3 us)
Sparse Core Ops, SparseCore 0:
  45.2 47.4 reduce-scatter.27
  95.6 48.1 reduce-scatter.19
  146.7 48.1 reduce-scatter.25
  197.6 48.1 reduce-scatter.17
  247.9 48.1 reduce-scatter.23
  298.3 48.1 reduce-scatter.15
  349.4 87.7 reduce-scatter.29
  440.0 87.9 reduce-scatter.21
  547.5 53.3 all-reduce.24
  2265.9 57.9 all-reduce.22
  2356.0 45.9 all-gather.25
  2404.1 46.0 all-gather.23
  2452.4 27.3 all-gather.37
  2481.3 28.5 all-gather.31
  2512.1 30.3 all-gather.33
  2544.6 29.8 all-gather.27
  2576.6 29.9 all-gather.35
  2608.7 29.8 all-gather.29
Sparse Core Ops, SparseCore 1:
  549.7 155.5 all-gather.19
  711.4 158.6 all-gather.17
  900.4 158.5 all-gather.21
  2484.1 22.9 reduce-scatter.37
  2513.5 24.3 reduce-scatter.35
  2577.8 23.8 reduce-scatter.31
  2641.9 23.8 reduce-scatter.33
  2669.0 154.5 reduce-scatter.43
  2826.9 153.7 reduce-scatter.41
  2984.0 153.6 reduce-scatter.39
where the time goes:
time: 3170 us; the launch traced here: 3150 us
  waiting for transfers between devices  1480 us (47%)
  local copies, waits for them, and re-layouts  751 us (24%)
  matrix products  436 us (14%)
  other arithmetic  280 us (9%)
  blocking collectives  144 us (5%)
  starting transfers between devices  43.9 us (1%)
    all_to_all x2, waiting for transfers between devices, micro_step(): lax.all_to_all(expert_out[None], 'col', split_axis=3, concat_axis=0, tile...  181 us
    all_to_all x2, waiting for transfers between devices, micro_step(): lax.all_to_all(slot_grad.astype(jnp.bfloat16).reshape(n_col, exp_dev, cap...  174 us
    reduce_scatter x2, waiting for transfers between devices, micro_step(): lax.psum_scatter(jnp.dot(attended, full_o, preferred_element_type=jnp.flo...  164 us
    reduce_scatter x1, waiting for transfers between devices, reduce_rows(): lax.psum_scatter(stacked[9].astype(jnp.bfloat16), 'row', scatter_dimensio...  150 us
    all_to_all x2, waiting for transfers between devices, micro_step(): lax.all_to_all(input_slots[None], 'col', split_axis=3, concat_axis=0, til...  149 us
    reduce_scatter x1, waiting for transfers between devices, reduce_rows(): lax.psum_scatter(stacked[10].astype(jnp.bfloat16), 'row', scatter_dimensi...  148 us
    gather x2, local copies, waits for them, and re-layouts, micro_step(): normed_ffn[slot_token] * slot_live[:, None].astype(jnp.bfloat16)  131 us
    gather x6, local copies, waits for them, and re-layouts, micro_step(): gates = jax.nn.softmax(jnp.take_along_axis(logits, route_rows, 1), -1)  125 us
  transfers between devices with their start and end apart: 36, of which 24 were waited for; matrix products, arithmetic and copies ran while one was open for 43% of the time, Pallas kernels for 0%

commit v1 on v0

v1 whole, which is shorter than its diff:
```python
import functools
import math

import jax
import jax.numpy as jnp
from jax import lax
from jax.experimental import pallas as pl
from jax.experimental.pallas import tpu as pltpu
from jax.sharding import PartitionSpec as P

EPSILON = 1e-06
ROPE_BASE = 10000.0
MASKED = -1e30
F32 = jnp.float32
BF16 = jnp.bfloat16
VMEM_LIMIT = 60 * 1024 * 1024


def inverse_rms(values):
    return lax.rsqrt(jnp.mean(values * values, -1, keepdims=True) + EPSILON)


def rope_tables(position, head):
    half = head // 2
    inverse = jnp.exp(-math.log(ROPE_BASE) * 2.0 / head * jnp.arange(half, dtype=F32))
    angles = position[:, None] * inverse[None, :]
    return jnp.cos(angles)[:, None, :], jnp.sin(angles)[:, None, :]


def rotary(values, cosine, sine):
    half = values.shape[-1] // 2
    first = values[..., :half]
    second = values[..., half:]
    return jnp.concatenate([first * cosine - second * sine, second * cosine + first * sine], -1)


def layout(lengths_row, group):
    ends = jnp.cumsum(lengths_row)
    starts = ends - lengths_row
    row_index = jnp.arange(group, dtype=jnp.int32)
    segment = jnp.sum((row_index[:, None] >= ends[None, :]).astype(jnp.int32), 1)
    member = segment[:, None] == jnp.arange(lengths_row.shape[0], dtype=jnp.int32)[None, :]
    position = (row_index - jnp.sum(jnp.where(member, starts[None, :], 0), 1)).astype(F32)
    live = (segment < lengths_row.shape[0] - 1).astype(F32)
    return (segment, position, live)


def nn(a, b):
    return lax.dot_general(a, b, (((1,), (0,)), ((), ())), preferred_element_type=F32)


def nt(a, b):
    return lax.dot_general(a, b, (((1,), (1,)), ((), ())), preferred_element_type=F32)


def tn(a, b):
    return lax.dot_general(a, b, (((0,), (0,)), ((), ())), preferred_element_type=F32)


def expert_body(
    counts, place, gate, hn, dy, wg, wu, wd, xe_o, dyr_o, hg_o, dgp_o, dup_o, ye_o, dxe_o, tok_o
):
    e, g, i = pl.program_id(0), pl.program_id(1), pl.program_id(2)
    rows = xe_o.shape[2]
    base = i * rows

    @pl.when(i == 0)
    def _():
        tok_o[...] = jnp.zeros_like(tok_o)

    @pl.when(counts[e, g] <= base)
    def _():
        for ref in (xe_o, dyr_o, hg_o, dgp_o, dup_o, ye_o, dxe_o):
            ref[...] = jnp.zeros_like(ref)

    @pl.when(counts[e, g] > base)
    def _():
        slot = lax.broadcasted_iota(jnp.int32, (rows, place.shape[3]), 0) + base
        hit = slot == place[0, 0]
        pick = jnp.where(hit, 1.0, 0.0).astype(BF16)
        weight = jnp.sum(jnp.where(hit, gate[0, 0], 0.0), 1, keepdims=True)
        xe = nn(pick, hn[0]).astype(BF16)
        xe_o[0, 0] = xe
        gp = nn(xe, wg[0])
        up = nn(xe, wu[0])
        sig = jax.nn.sigmoid(gp)
        silu = gp * sig
        hid = silu * up
        hg = (hid * weight).astype(BF16)
        hg_o[0, 0] = hg
        ye_o[0, 0] = nn(hg, wd[0]).astype(BF16)
        dyr = nn(pick, dy[0]).astype(BF16)
        dyr_o[0, 0] = dyr
        back = nt(dyr, wd[0])
        dgate = jnp.sum(back * hid, 1, keepdims=True)
        dhid = back * weight
        dgp = (dhid * up * sig * (1.0 + gp * (1.0 - sig))).astype(BF16)
        dup = (dhid * silu).astype(BF16)
        dgp_o[0, 0] = dgp
        dup_o[0, 0] = dup
        dots = jnp.sum(dgp.astype(F32) * gp + dup.astype(F32) * up, 1, keepdims=True)
        dxe_o[0, 0] = (nt(dgp, wg[0]) + nt(dup, wu[0])).astype(BF16)
        tok_o[0, 0, 0:1, :] += jnp.sum(jnp.where(hit, dgate, 0.0), 0, keepdims=True)
        tok_o[0, 0, 1:2, :] += jnp.sum(jnp.where(hit, dots, 0.0), 0, keepdims=True)


def expert_pass(counts, place, gate, hn, dy, wg, wu, wd, capacity):
    experts, width, ff = wg.shape
    micro, group, _ = hn.shape
    rows = min(256, capacity)
    blocks = capacity // rows
    tall = lambda e, g, i, c: (e, g, i, 0)
    line = lambda e, g, i, c: (e, g, 0, 0)
    whole = lambda e, g, i, c: (g, 0, 0)
    matrix = lambda e, g, i, c: (e, 0, 0)
    slots = lambda n: jax.ShapeDtypeStruct((experts, micro, capacity, n), BF16)
    sizes = (width, width, ff, ff, ff, width, width)
    flops = 2 * experts * micro * capacity * width * (6 * ff + 2 * group)
    return pl.pallas_call(
        expert_body,
        grid_spec=pltpu.PrefetchScalarGridSpec(
            num_scalar_prefetch=1,
            grid=(experts, micro, blocks),
            in_specs=[
                pl.BlockSpec((1, 1, 1, group), line),
                pl.BlockSpec((1, 1, 1, group), line),
                pl.BlockSpec((1, group, width), whole, pipeline_mode=pl.Buffered(1)),
                pl.BlockSpec((1, group, width), whole, pipeline_mode=pl.Buffered(1)),
                pl.BlockSpec((1, width, ff), matrix),
                pl.BlockSpec((1, width, ff), matrix),
                pl.BlockSpec((1, ff, width), matrix),
            ],
            out_specs=[pl.BlockSpec((1, 1, rows, n), tall) for n in sizes]
            + [pl.BlockSpec((1, 1, 2, group), line)],
        ),
        out_shape=[slots(n) for n in sizes]
        + [jax.ShapeDtypeStruct((experts, micro, 2, group), F32)],
        compiler_params=pltpu.CompilerParams(vmem_limit_bytes=VMEM_LIMIT),
        cost_estimate=pl.CostEstimate(
            flops=flops, bytes_accessed=100 << 20, transcendentals=experts * micro * capacity * ff
        ),
        name="expert_pass",
    )(counts, place, gate, hn, dy, wg, wu, wd)


def grads_body(xe, dgp, dup, hg, dyr, gg_o, gu_o, gd_o):
    part = xe[0]
    gg_o[0] = tn(part, dgp[0]).astype(BF16)
    gu_o[0] = tn(part, dup[0]).astype(BF16)
    gd_o[0] = tn(hg[0], dyr[0]).astype(BF16)


def expert_grads(xe, dgp, dup, hg, dyr):
    experts, micro, capacity, width = xe.shape
    ff = dgp.shape[3]
    rows = micro * capacity
    xe, dyr = (a.reshape(experts, rows, width) for a in (xe, dyr))
    dgp, dup, hg = (a.reshape(experts, rows, ff) for a in (dgp, dup, hg))
    part = min(512, width)
    return pl.pallas_call(
        grads_body,
        grid=(experts, width // part),
        in_specs=[
            pl.BlockSpec((1, rows, part), lambda e, r: (e, 0, r)),
            pl.BlockSpec((1, rows, ff), lambda e, r: (e, 0, 0)),
            pl.BlockSpec((1, rows, ff), lambda e, r: (e, 0, 0)),
            pl.BlockSpec((1, rows, ff), lambda e, r: (e, 0, 0)),
            pl.BlockSpec((1, rows, part), lambda e, r: (e, 0, r)),
        ],
        out_specs=[
            pl.BlockSpec((1, part, ff), lambda e, r: (e, r, 0)),
            pl.BlockSpec((1, part, ff), lambda e, r: (e, r, 0)),
            pl.BlockSpec((1, ff, part), lambda e, r: (e, 0, r)),
        ],
        out_shape=[
            jax.ShapeDtypeStruct((experts, width, ff), BF16),
            jax.ShapeDtypeStruct((experts, width, ff), BF16),
            jax.ShapeDtypeStruct((experts, ff, width), BF16),
        ],
        compiler_params=pltpu.CompilerParams(vmem_limit_bytes=VMEM_LIMIT),
        cost_estimate=pl.CostEstimate(
            flops=6 * experts * rows * width * ff, bytes_accessed=experts * 26 << 20, transcendentals=0
        ),
        name="expert_grads",
    )(xe, dgp, dup, hg, dyr)


def combine_body(place, *refs):
    out = refs[-1]
    slots = refs[:-1]
    total = jnp.zeros((out.shape[1], out.shape[2]), F32)
    at = 0
    for ref in slots:
        capacity = ref.shape[2]
        for e in range(ref.shape[0]):
            slot = lax.broadcasted_iota(jnp.int32, (out.shape[1], capacity), 1)
            pick = jnp.where(slot == place[0, :, at : at + 1], 1.0, 0.0).astype(BF16)
            total = total + nn(pick, ref[e, 0])
            at += 1
    out[0] = total.astype(BF16)


def combine(place, slots):
    micro, group, local = place.shape
    capacity, width = slots[0].shape[2:]
    tile = min(256, group)
    return pl.pallas_call(
        combine_body,
        grid=(micro, group // tile),
        in_specs=[pl.BlockSpec((1, tile, local), lambda g, i: (g, i, 0))]
        + [
            pl.BlockSpec((s.shape[0], 1, capacity, width), lambda g, i: (0, g, 0, 0))
            for s in slots
        ],
        out_specs=pl.BlockSpec((1, tile, width), lambda g, i: (g, i, 0)),
        out_shape=jax.ShapeDtypeStruct((micro, group, width), BF16),
        compiler_params=pltpu.CompilerParams(vmem_limit_bytes=VMEM_LIMIT),
        cost_estimate=pl.CostEstimate(
            flops=2 * micro * group * local * capacity * width,
            bytes_accessed=micro * (local * capacity + group) * width * 2,
            transcendentals=0,
        ),
        name="combine",
    )(place, *slots).reshape(micro * group, width)


def shards(
    tokens,
    gain_attn,
    gain_ffn,
    gain_query,
    gain_key,
    w_query,
    w_key,
    w_value,
    w_out,
    w_router,
    w_gate,
    w_up,
    w_down,
    routes,
    lengths,
    cotangent,
):
    n_col = lax.axis_size("col")
    n_row = lax.axis_size("row")
    col = lax.axis_index("col")
    micro, spans = lengths.shape
    rows, part = tokens.shape
    group = rows // micro
    width = part * n_col
    head = gain_query.shape[0]
    local_exp = w_gate.shape[0]
    experts = local_exp * n_col
    topk = routes.shape[1]
    capacity = 2 * group * topk // experts
    local_heads = w_out.shape[0] // head
    hd = w_out.shape[0] * n_col
    scale = head ** (-0.5)

    def gather(value, axis_name, axis):
        return lax.all_gather(value, axis_name, axis=axis, tiled=True)

    def mine(value, axis):
        size = value.shape[axis] // n_col
        return lax.dynamic_slice_in_dim(value, col * size, size, axis)

    step = max(1, local_exp // 2)
    chunks = [slice(at, at + step) for at in range(0, local_exp, step)]
    big = [
        (
            gather(w_gate[c], "row", 1),
            gather(w_up[c], "row", 1),
            gather(w_down[c], "row", 2),
        )
        for c in chunks
    ]

    inputs_low = gather(tokens, "col", 1)
    packed = jnp.concatenate([w_query, w_key, w_value], 0)
    packed = gather(packed, "row", 1).reshape(3, part, n_col, local_heads * head)
    w_heads = lax.all_to_all(
        packed.transpose(2, 0, 1, 3), "col", split_axis=0, concat_axis=0, tiled=True
    )
    w_heads = w_heads.transpose(1, 0, 2, 3).reshape(3, width, local_heads * head)
    full_o = gather(gather(w_out, "row", 1), "col", 0)
    full_r = gather(gather(w_router, "row", 1), "col", 0)
    gains = gather(jnp.stack([gain_attn, gain_ffn]), "col", 1)
    upstream_low = gather(cotangent, "col", 1)

    segment, position, live = jax.vmap(lambda l: layout(l, group))(lengths)
    position = position.reshape(rows)
    live = live.reshape(rows)
    member = jnp.any(
        routes[:, None, :] == jnp.arange(experts, dtype=jnp.int32)[None, :, None], -1
    )
    member_f = member.astype(F32)
    member_loc = mine(member_f, 1).reshape(micro, group, local_exp)
    lower = (
        jnp.arange(group, dtype=jnp.int32)[:, None] > jnp.arange(group, dtype=jnp.int32)[None, :]
    ).astype(BF16)
    before = jnp.einsum("st,gte->gse", lower, member_loc.astype(BF16), preferred_element_type=F32)
    place = jnp.where(member_loc > 0, before, -1.0).astype(jnp.int32)
    counts = jnp.sum(member_loc, 1).astype(jnp.int32).T
    place_t = place.transpose(2, 0, 1)[:, :, None, :]

    inputs = inputs_low.astype(F32)
    scale_one = inverse_rms(inputs)
    normed = (inputs * scale_one * gains[0]).astype(BF16)
    query_pre, key_pre, value_pre = (nn(normed, w_heads[j]) for j in range(3))
    shape = (rows, local_heads, head)
    cosine, sine = rope_tables(position, head)

    def head_norm(values, gain):
        return rotary(values * inverse_rms(values) * gain, cosine, sine)

    query_rot, query_pull = jax.vjp(head_norm, query_pre.reshape(shape), gain_query)
    key_rot, key_pull = jax.vjp(head_norm, key_pre.reshape(shape), gain_key)
    batch = (micro, group, local_heads, head)
    queries = query_rot.astype(BF16).reshape(batch)
    keys_low = key_rot.astype(BF16).reshape(batch)
    values_low = value_pre.astype(BF16).reshape(batch)
    same = (segment[:, :, None] == segment[:, None, :])[:, None]

    def scores_of():
        raw = jnp.einsum("gqhd,gkhd->ghqk", queries, keys_low, preferred_element_type=F32) * scale
        return jnp.where(same, raw, MASKED)

    scores = scores_of()
    highest = jnp.max(scores, -1, keepdims=True)
    log_total = highest + jnp.log(jnp.sum(jnp.exp(scores - highest), -1, keepdims=True))
    probs_low = jnp.exp(scores - log_total).astype(BF16)
    attended = jnp.einsum(
        "ghqk,gkhd->gqhd", probs_low, values_low, preferred_element_type=F32
    ).astype(BF16)
    attended_full = gather(attended.reshape(rows, local_heads * head), "col", 1)

    hidden = inputs + nn(attended_full, full_o)
    scale_two = inverse_rms(hidden)
    normed_ffn = (hidden * scale_two * gains[1]).astype(BF16)
    logits = nn(normed_ffn, full_r)
    peak = jnp.max(jnp.where(member, logits, -jnp.inf), -1, keepdims=True)
    raised = jnp.where(member, jnp.exp(jnp.where(member, logits - peak, 0.0)), 0.0)
    gates = raised / jnp.sum(raised, -1, keepdims=True)
    gate_t = mine(gates, 1).reshape(micro, group, local_exp).transpose(2, 0, 1)[:, :, None, :]
    upstream_full = (upstream_low * live[:, None].astype(BF16)).reshape(micro, group, width)
    hn = normed_ffn.reshape(micro, group, width)

    outs, weight_grads = [], []
    for c, (wg, wu, wd) in zip(chunks, big):
        xe, dyr, hg, dgp, dup, ye, dxe, tok = expert_pass(
            counts[c], place_t[c], gate_t[c], hn, upstream_full, wg, wu, wd, capacity
        )
        outs.append((ye, dxe, tok))
        gg, gu, gd = expert_grads(xe, dgp, dup, hg, dyr)
        weight_grads.append(
            (
                lax.psum_scatter(gg, "row", scatter_dimension=1, tiled=True),
                lax.psum_scatter(gu, "row", scatter_dimension=1, tiled=True),
                lax.psum_scatter(gd, "row", scatter_dimension=2, tiled=True),
            )
        )
    grad_gate, grad_up, grad_down = (
        jnp.concatenate([w[j] for w in weight_grads], 0).astype(F32) for j in range(3)
    )
    back_sum = lax.psum_scatter(
        combine(place, [o[1] for o in outs]), "col", scatter_dimension=1, tiled=True
    )
    mixed_sum = lax.psum_scatter(
        combine(place, [o[0] for o in outs]), "col", scatter_dimension=1, tiled=True
    )
    tok = jnp.concatenate([o[2] for o in outs], 0)
    tok = gather(tok, "col", 0)
    gate_dots = tok[:, :, 0].reshape(experts, rows).T
    hidden_part = mine(hidden, 1)
    mixed = (hidden_part + mixed_sum.astype(F32)).astype(BF16)

    selected = gates * (gate_dots - jnp.sum(gates * gate_dots, -1, keepdims=True))
    logit_grad = selected.astype(BF16)
    router_part = mine(full_r, 0)
    normed_grad = back_sum.astype(F32) + nt(logit_grad, router_part)
    grad_router = tn(mine(normed_ffn, 1), logit_grad)
    scaled_two = hidden_part * scale_two
    grad_gain_ffn = jnp.sum(normed_grad * scaled_two, 0)
    dot_two = jnp.sum(tok[:, :, 1].reshape(experts, rows), 0) + jnp.sum(
        logit_grad.astype(F32) * logits, 1
    )
    upstream_part = cotangent.astype(F32) * live[:, None]
    hidden_grad = (
        upstream_part
        + scale_two * (normed_grad * gain_ffn)
        - hidden_part * scale_two**2 * dot_two[:, None] / width
    )

    branch_grad = hidden_grad.astype(BF16)
    attended_grad = lax.psum_scatter(
        nt(branch_grad, mine(full_o, 1)).astype(BF16), "col", scatter_dimension=1, tiled=True
    ).reshape(batch)
    grad_out = tn(attended_full, branch_grad)
    scores_again = scores_of()
    probs = jnp.exp(scores_again - log_total)
    probs_again = probs.astype(BF16)
    probs_grad = jnp.einsum(
        "gqhd,gkhd->ghqk", attended_grad, values_low, preferred_element_type=F32
    )
    values_grad = jnp.einsum(
        "ghqk,gqhd->gkhd", probs_again, attended_grad, preferred_element_type=F32
    )
    score_grad = (probs * (probs_grad - jnp.sum(probs_grad * probs, -1, keepdims=True))).astype(
        BF16
    )
    query_grad_rot = (
        jnp.einsum("ghqk,gkhd->gqhd", score_grad, keys_low, preferred_element_type=F32) * scale
    )
    key_grad_rot = (
        jnp.einsum("ghqk,gqhd->gkhd", score_grad, queries, preferred_element_type=F32) * scale
    )
    query_grad, gain_query_part = query_pull(query_grad_rot.reshape(shape))
    key_grad, gain_key_part = key_pull(key_grad_rot.reshape(shape))
    flat = (rows, local_heads * head)
    heads_grad = [
        v.reshape(flat).astype(BF16) for v in (query_grad, key_grad, values_grad)
    ]
    back_heads = sum(nt(g, w_heads[j]) for j, g in enumerate(heads_grad))
    normed_back = lax.psum_scatter(
        back_heads.astype(BF16), "col", scatter_dimension=1, tiled=True
    ).astype(F32)
    pre = (query_pre, key_pre, value_pre)
    dot_part = sum(jnp.sum(g.astype(F32) * p, -1) for g, p in zip(heads_grad, pre))
    dot_one, gain_query_sum, gain_key_sum = lax.psum(
        (dot_part, gain_query_part, gain_key_part), "col"
    )
    scale_one_part = scale_one
    inputs_part = tokens.astype(F32)
    grad_gain_attn = jnp.sum(normed_back * inputs_part * scale_one_part, 0)
    input_grad = (
        hidden_grad
        + scale_one_part * (normed_back * gain_attn)
        - inputs_part * scale_one_part**2 * dot_one[:, None] / width
    )

    heads_weights = jnp.stack([tn(normed, g) for g in heads_grad]).astype(BF16)
    heads_weights = heads_weights.reshape(3, n_col, part, local_heads * head).transpose(1, 0, 2, 3)
    heads_weights = lax.all_to_all(heads_weights, "col", split_axis=0, concat_axis=0, tiled=True)
    heads_weights = heads_weights.transpose(1, 2, 0, 3).reshape(3 * part, hd)
    heads_weights = lax.psum_scatter(heads_weights, "row", scatter_dimension=1, tiled=True)
    grad_query, grad_key, grad_value = (
        heads_weights[j * part : (j + 1) * part].astype(F32) for j in range(3)
    )
    out_weights = lax.all_to_all(
        grad_out.astype(BF16).reshape(n_col, local_heads * head, part),
        "col",
        split_axis=0,
        concat_axis=0,
        tiled=True,
    )
    out_weights = out_weights.transpose(1, 0, 2).reshape(local_heads * head, width)
    grad_out = lax.psum_scatter(out_weights, "row", scatter_dimension=1, tiled=True).astype(F32)
    grad_router = lax.psum_scatter(
        grad_router.astype(BF16), "row", scatter_dimension=1, tiled=True
    ).astype(F32)
    grad_gain_attn, grad_gain_ffn, grad_gain_query, grad_gain_key = lax.psum(
        (grad_gain_attn, grad_gain_ffn, gain_query_sum, gain_key_sum), "row"
    )
    return (
        mixed,
        input_grad,
        grad_gain_attn,
        grad_gain_ffn,
        grad_gain_query,
        grad_gain_key,
        grad_query,
        grad_key,
        grad_value,
        grad_out,
        grad_router,
        grad_gate,
        grad_up,
        grad_down,
    )


def solution(mesh):
    placed = (
        P("row", "col"),
        P("col"),
        P("col"),
        P(),
        P(),
        P("col", "row"),
        P("col", "row"),
        P("col", "row"),
        P("col", "row"),
        P("col", "row"),
        P("col", "row", None),
        P("col", "row", None),
        P("col", None, "row"),
        P("row", None),
        P("row", None),
        P("row", "col"),
    )
    return jax.shard_map(
        shards,
        mesh=mesh,
        in_specs=placed,
        out_specs=(
            P("row", "col"),
            P("row", "col"),
            P("col"),
            P("col"),
            P(),
            P(),
            P("col", "row"),
            P("col", "row"),
            P("col", "row"),
            P("col", "row"),
            P("col", "row"),
            P("col", "row", None),
            P("col", "row", None),
            P("col", None, "row"),
        ),
        check_vma=False,
    )
```

time: 3170 us -> 1970 us (0.62)
  local copies, waits for them, and re-layouts: 751 us -> 64 us
  matrix products: 436 us -> 108 us
  Pallas kernels: 0 us -> 292 us
  waiting for transfers between devices: 1480 us -> 1190 us
  other arithmetic: 280 us -> 79.7 us
  blocking collectives: 144 us -> 198 us
    all_to_all x8 -> x3, waiting for transfers between devices: 531 us -> 35.9 us  [the longest x1 35.9 us: shards(): lax.all_to_all(heads_weights, 'col', split_axis=0, concat_axis=0, tiled=T...]
    gather x12 -> x0, local copies, waits for them, and re-layouts: 397 us -> none  [the longest x2 131 us: micro_step(): normed_ffn[slot_token] * slot_live[:, None].astype(jnp.bfloat16)]
    all_gather x11, waiting for transfers between devices: 209 us -> 551 us  [gather(): return lax.all_gather(value, axis_name, axis=axis, tiled=True)]
    dot_general x60 -> x22, matrix products: 436 us -> 108 us  [the longest x5 42.8 us: nt(): lax.dot_general(a, b, (((1,), (1,)), ((), ())), preferred_element_type=F32)]
    pallas_call x0 -> x6, Pallas kernels: none -> 292 us  [the longest x2 173 us: expert_pass(): pl.pallas_call(expert_body, grid_spec=pltpu.PrefetchScalarGridSpec(num_sc...]
    scatter x4 -> x0, local copies, waits for them, and re-layouts: 122 us -> none  [the longest x2 61 us: slot_table(): slot_live = jnp.zeros((experts * capacity,), jnp.float32).at[flat].set(1.0)]
    all_to_all x8 -> x1, local copies, waits for them, and re-layouts: 102 us -> 0.15 us  [shards(): lax.all_to_all(packed.transpose(2, 0, 1, 3), 'col', split_axis=0, concat_...]
    all_gather x5, blocking collectives: 53.6 us -> 155 us  [gather(): return lax.all_gather(value, axis_name, axis=axis, tiled=True)]
  transfers between devices with their start and end apart: 36 -> 26, of which waited for: 24 -> 19; matrix products, arithmetic and copies ran while one was open for 43% -> 11% of each run, Pallas kernels for 0% -> 10%
where the time goes in v1:
time: 1970 us
  waiting for transfers between devices  1190 us (60%)
  Pallas kernels  292 us (15%)
  blocking collectives  198 us (10%)
  matrix products  108 us (5%)
  other arithmetic  79.7 us (4%)
  local copies, waits for them, and re-layouts  64 us (3%)
    all_gather x11, waiting for transfers between devices, gather(): return lax.all_gather(value, axis_name, axis=axis, tiled=True)  551 us
    pallas_call x2, Pallas kernels, expert_pass(): pl.pallas_call(expert_body, grid_spec=pltpu.PrefetchScalarGridSpec(num_sc...  173 us
    reduce_scatter x2, waiting for transfers between devices, shards(): lax.psum_scatter(gg, 'row', scatter_dimension=1, tiled=True)  173 us
    reduce_scatter x2, waiting for transfers between devices, shards(): lax.psum_scatter(gu, 'row', scatter_dimension=1, tiled=True)  161 us
    all_gather x5, blocking collectives, gather(): return lax.all_gather(value, axis_name, axis=axis, tiled=True)  155 us
    reduce_scatter x1, waiting for transfers between devices, shards(): lax.psum_scatter(combine(place, [o[0] for o in outs]), 'col', scatter_dim...  90.9 us
    reduce_scatter x1, waiting for transfers between devices, shards(): lax.psum_scatter(back_heads.astype(BF16), 'col', scatter_dimension=1, til...  90.1 us
    pallas_call x2, Pallas kernels, expert_grads(): pl.pallas_call(grads_body, grid=(experts, width // part), in_specs=[pl.Bl...  67.1 us
  transfers between devices with their start and end apart: 26, of which 19 were waited for; matrix products, arithmetic and copies ran while one was open for 11% of the time, Pallas kernels for 10%

profile of v1, /device:TPU:0, one launch (start us, length us, event | category | flops | bytes accessed | tf_op | source)
XLA Modules:
  0.0 1965.6 jit_solution(4094896627876194087)
XLA Ops:
  10.5 33.4 %all-gather.14.cloned.1.call-done = bf16[768,1024]{1,0:T(8,128)(2,1)} async-done(((bf16[768,256]{1,0:T(8,128)(2,1)}), bf16[768,1024]{1,0:T(8,128)(2,1)}) %all-gather.14.cloned.1.call-update) | async-done | bytes 1572880 | tf_op jit(solution)/shard_map/all_gather | solution.py:262
  47.5 4.6 all-to-all-start
  52.1 11.2 all_gather.52
  63.6 73.1 %all_gather.49 = f32[2,2048]{1,0:T(2,128)S(1)} all-gather(f32[2,256]{1,0:T(2,128)S(1)} %pad_maximum_fusion.8), channel_id=1, replica_groups=mesh['row'=4,'col'=8] {'col'}, dimensions={1}, use_global_device_ids=true | all-gather | bytes 18432 | tf_op jit(solution)/shard_map/all_gather | solution.py:262
  137.4 22.3 %all-gather.12.cloned.1.call-done = bf16[2048,2048]{1,0:T(8,128)(2,1)} async-done(((bf16[2048,256]{1,0:T(8,128)(2,1)}), bf16[2048,2048]{1,0:T(8,128)(2,1)}) %all-gather.12.cloned.1.call-update) | async-done | bytes 8388624 | tf_op jit(solution)/shard_map/all_gather | solution.py:262
  159.6 5.1 fusion
  165.3 9.1 fusion.2
  174.4 6.5 multiply_reduce_fusion.7
  181.0 2.9 multiply_reduce_fusion.6
  184.9 2.6 fusion.57
  191.9 8.5 fusion.106
  203.8 4.7 fusion.101
  208.6 4.7 fusion.100
  213.3 4.6 fusion.99
  220.9 8.1 all_gather.54
  229.0 16.4 all_gather.55
  250.5 8.0 broadcast_multiply_fusion
  258.5 33.0 %all-gather.18.cloned.1.call-done = bf16[1024,2048]{1,0:T(8,128)(2,1)} async-done(((bf16[128,2048]{1,0:T(8,128)(2,1)}), bf16[1024,2048]{1,0:T(8,128)(2,1)}) %all-gather.18.cloned.1.call-update) | async-done | bytes 4194320 | tf_op jit(solution)/shard_map/all_gather | solution.py:262
  291.5 48.6 %all-gather.16.cloned.1.call-done = bf16[2048,1024]{1,0:T(8,128)(2,1)} async-done(((bf16[2048,128]{1,0:T(8,128)(2,1)}), bf16[2048,1024]{1,0:T(8,128)(2,1)}) %all-gather.16.cloned.1.call-update) | async-done | bytes 4194320 | tf_op jit(solution)/shard_map/all_gather | solution.py:262
  340.1 13.5 multiply_reduce_fusion
  365.6 62.6 %all-gather.22.cloned.1.call-done.wg = bf16[2,2048,1024]{2,1,0:T(8,128)(2,1)} async-done(((bf16[2,512,1024]{2,1,0:T(8,128)(2,1)}), bf16[2,2048,1024]{2,1,0:T(8,128)(2,1)}) %all-gather.22.cloned.1.call-update) | async-done | bytes 8388624 | tf_op jit(solution)/shard_map/all_gather | solution.py:262
  428.2 89.5 %all-gather.24.cloned.1.call-done.wu = bf16[2,2048,1024]{2,1,0:T(8,128)(2,1)} async-done(((bf16[2,512,1024]{2,1,0:T(8,128)(2,1)}), bf16[2,2048,1024]{2,1,0:T(8,128)(2,1)}) %all-gather.24.cloned.1.call-update) | async-done | bytes 8388624 | tf_op jit(solution)/shard_map/all_gather | solution.py:262
  517.7 89.3 %all-gather.26.cloned.1.call-done.wd = bf16[2,1024,2048]{2,1,0:T(8,128)(2,1)} async-done(((bf16[2,1024,512]{2,1,0:T(8,128)(2,1)}), bf16[2,1024,2048]{2,1,0:T(8,128)(2,1)}) %all-gather.26.cloned.1.call-update) | async-done | bytes 8388624 | tf_op jit(solution)/shard_map/all_gather | solution.py:262
  607.1 96.8 %expert_pass.2 = (bf16[2,2,512,2048]{3,2,1,0:T(8,128)(2,1)}, bf16[2,2,512,2048]{3,2,1,0:T(8,128)(2,1)}, bf16[2,2,512,1024]{3,2,1,0:T(8,128)(2,1)}, bf16[2,2,512,...) custom-call(s32[2,2]{1,0:T(2,128)} %get-tuple-element.117.counts, ...), custom_call_target="tpu_custom_call" | custom-call | flops 68719476736 | bytes 104857600 | tf_op jit(solution)/shard_map/expert_pass/pallas_call | solution.py:119
  703.9 82.6 %all-gather.30.cloned.1.call-done.wu = bf16[2,2048,1024]{2,1,0:T(8,128)(2,1)} async-done(((bf16[2,512,1024]{2,1,0:T(8,128)(2,1)}), bf16[2,2048,1024]{2,1,0:T(8,128)(2,1)}) %all-gather.30.cloned.1.call-update) | async-done | bytes 8388624 | tf_op jit(solution)/shard_map/all_gather | solution.py:262
  786.5 89.3 %all-gather.32.cloned.1.call-done.wd = bf16[2,1024,2048]{2,1,0:T(8,128)(2,1)} async-done(((bf16[2,1024,512]{2,1,0:T(8,128)(2,1)}), bf16[2,1024,2048]{2,1,0:T(8,128)(2,1)}) %all-gather.32.cloned.1.call-update) | async-done | bytes 8388624 | tf_op jit(solution)/shard_map/all_gather | solution.py:262
  875.8 76.4 %expert_pass.3 = (bf16[2,2,512,2048]{3,2,1,0:T(8,128)(2,1)}, bf16[2,2,512,2048]{3,2,1,0:T(8,128)(2,1)}, bf16[2,2,512,1024]{3,2,1,0:T(8,128)(2,1)}, bf16[2,2,512,...) custom-call(s32[2,2]{1,0:T(2,128)} %get-tuple-element.116.counts, ...), custom_call_target="tpu_custom_call" | custom-call | flops 68719476736 | bytes 104857600 | tf_op jit(solution)/shard_map/expert_pass/pallas_call | solution.py:119
  952.3 25.6 %combine.3 = bf16[2,1024,2048]{2,1,0:T(8,128)(2,1)} custom-call(s32[2,1024,4]{2,1,0:T(8,128)} %copy-done.21, bf16[2,2,512,2048]{3,2,1,0:T(8,128)(2,1)} %get-tuple-element.38.refs_0_, bf16[2,2,512,2048]{3,2,1,0:T(8,128)(2,1)} %get-tuple-element.39.refs_1_), custom_call_target="tpu_custom_call" | custom-call | flops 17179869184 | bytes 25165824 | tf_op jit(solution)/shard_map/combine/pallas_call | solution.py:207
  977.9 26.0 %combine.2 = bf16[2,1024,2048]{2,1,0:T(8,128)(2,1)} custom-call(s32[2,1024,4]{2,1,0:T(8,128)} %copy-done.21, bf16[2,2,512,2048]{3,2,1,0:T(8,128)(2,1)} %get-tuple-element.36.refs_0_, bf16[2,2,512,2048]{3,2,1,0:T(8,128)(2,1)} %get-tuple-element.37.refs_1_), custom_call_target="tpu_custom_call" | custom-call | flops 17179869184 | bytes 25165824 | tf_op jit(solution)/shard_map/combine/pallas_call | solution.py:207
  1004.8 46.1 %all_gather.63 = f32[32,2,2,1024]{3,2,1,0:T(2,128)S(1)} all-gather(f32[4,2,2,1024]{3,2,1,0:T(2,128)S(1)} %pad_maximum_fusion.7), channel_id=1, replica_groups=mesh['row'=4,'col'=8] {'col'}, dimensions={0}, use_global_device_ids=true | all-gather | bytes 589824 | tf_op jit(solution)/shard_map/all_gather | solution.py:262
  1052.1 48.3 %reduce-scatter.17.cloned.1.call-done = bf16[2048,256]{1,0:T(8,128)(2,1)} async-done(((bf16[2048,2048]{1,0:T(8,128)(2,1)}), bf16[2048,256]{1,0:T(8,128)(2,1)}) %reduce-scatter.17.cloned.1.call-update) | async-done | bytes 1048592 | tf_op jit(solution)/shard_map/reduce_scatter | solution.py:366
  1100.4 90.9 %reduce-scatter.15.cloned.1.call-done = bf16[2048,256]{1,0:T(8,128)(2,1)} async-done(((bf16[2048,2048]{1,0:T(8,128)(2,1)}), bf16[2048,256]{1,0:T(8,128)(2,1)}) %reduce-scatter.15.cloned.1.call-update) | async-done | bytes 1048592 | tf_op jit(solution)/shard_map/reduce_scatter | solution.py:369
  1191.3 4.4 multiply_reduce_fusion.2
  1195.8 4.3 convolution_convert_fusion
  1200.1 6.5 copy.206
  1206.7 33.7 %expert_grads.2 = (bf16[2,2048,1024]{2,1,0:T(8,128)(2,1)}, bf16[2,2048,1024]{2,1,0:T(8,128)(2,1)}, bf16[2,1024,2048]{2,1,0:T(8,128)(2,1)}) custom-call(bf16[2,1024,2048]{2,1,0:T(8,128)(2,1)} %bitcast.270, bf16[2,1024,1024]{2,1,0:T(8,128)(2,1)} %bitcast.275, bf16[2,1024,1024]{2,1,0:T(8,128)(2,1)} %bitcast.276, bf16[2,1024,1024]{2,1,0:T(8,128)(2,1)} %bitcast.274, ...), custom_call_target="tpu_custom_call" | custom-call | flops 25769803776 | bytes 54525952 | tf_op jit(solution)/shard_map/expert_grads/pallas_call | solution.py:160
  1240.4 33.4 %expert_grads.3 = (bf16[2,2048,1024]{2,1,0:T(8,128)(2,1)}, bf16[2,2048,1024]{2,1,0:T(8,128)(2,1)}, bf16[2,1024,2048]{2,1,0:T(8,128)(2,1)}) custom-call(bf16[2,1024,2048]{2,1,0:T(8,128)(2,1)} %bitcast.272, bf16[2,1024,1024]{2,1,0:T(8,128)(2,1)} %bitcast.278, bf16[2,1024,1024]{2,1,0:T(8,128)(2,1)} %bitcast.279, bf16[2,1024,1024]{2,1,0:T(8,128)(2,1)} %bitcast.277, ...), custom_call_target="tpu_custom_call" | custom-call | flops 25769803776 | bytes 54525952 | tf_op jit(solution)/shard_map/expert_grads/pallas_call | solution.py:160
  1276.7 9.0 fusion.135
  1285.7 12.4 copy.208
  1298.1 4.4 convolution_convert_fusion.3
  1302.5 4.1 all-to-all-start.2
  1308.8 5.9 fusion.30
  1316.0 5.7 multiply_reduce_fusion.1
  1321.7 5.0 multiply_convert_fusion.1
  1329.7 2.6 fusion.66
  1342.5 5.0 all-to-all-start.1
  1349.5 35.9 %all-to-all-done.1 = bf16[8,3,256,128]{3,2,1,0:T(8,128)(2,1)} async-done(((bf16[8,3,256,128]{3,2,1,0:T(8,128)(2,1)}), bf16[8,3,256,128]{3,2,1,0:T(8,128)(2,1)}, u32[]{:S(2)}, u32[]{:S(2)}) %all-to-all-start.1) | async-done | bytes 1572896 | tf_op jit(solution)/shard_map/all_to_all | solution.py:444
  1389.8 9.3 fusion.70
  1399.1 8.6 fusion.72
  1407.8 16.1 add_convert_fusion
  1427.3 16.3 all-reduce.4
  1444.3 6.2 maximum_convert_fusion.2
  1450.4 71.2 %reduce-scatter.29.cloned.1.call-done = bf16[2,512,1024]{2,1,0:T(8,128)(2,1)} async-done(((bf16[2,2048,1024]{2,1,0:T(8,128)(2,1)}), bf16[2,512,1024]{2,1,0:T(8,128)(2,1)}) %reduce-scatter.29.cloned.1.call-update) | async-done | bytes 2097168 | tf_op jit(solution)/shard_map/reduce_scatter | solution.py:359
  1521.7 89.6 %reduce-scatter.31.cloned.1.call-done = bf16[2,512,1024]{2,1,0:T(8,128)(2,1)} async-done(((bf16[2,2048,1024]{2,1,0:T(8,128)(2,1)}), bf16[2,512,1024]{2,1,0:T(8,128)(2,1)}) %reduce-scatter.31.cloned.1.call-update) | async-done | bytes 2097168 | tf_op jit(solution)/shard_map/reduce_scatter | solution.py:359
  1611.3 6.2 maximum_convert_fusion.1
  1617.5 83.3 %reduce-scatter.25.cloned.1.call-done = bf16[2,512,1024]{2,1,0:T(8,128)(2,1)} async-done(((bf16[2,2048,1024]{2,1,0:T(8,128)(2,1)}), bf16[2,512,1024]{2,1,0:T(8,128)(2,1)}) %reduce-scatter.25.cloned.1.call-update) | async-done | bytes 2097168 | tf_op jit(solution)/shard_map/reduce_scatter | solution.py:358
  1700.8 89.6 %reduce-scatter.27.cloned.1.call-done = bf16[2,512,1024]{2,1,0:T(8,128)(2,1)} async-done(((bf16[2,2048,1024]{2,1,0:T(8,128)(2,1)}), bf16[2,512,1024]{2,1,0:T(8,128)(2,1)}) %reduce-scatter.27.cloned.1.call-update) | async-done | bytes 2097168 | tf_op jit(solution)/shard_map/reduce_scatter | solution.py:358
  1790.4 6.2 maximum_convert_fusion
  1796.6 21.5 %reduce-scatter.23.cloned.1.call-done = bf16[128,512]{1,0:T(8,128)(2,1)} async-done(((bf16[128,2048]{1,0:T(8,128)(2,1)}), bf16[128,512]{1,0:T(8,128)(2,1)}) %reduce-scatter.23.cloned.1.call-update) | async-done | bytes 131088 | tf_op jit(solution)/shard_map/reduce_scatter | solution.py:458
  1821.2 16.8 all-reduce.5
  1838.0 14.9 reduce-scatter.21.cloned.1.call-done
  1854.8 90.1 %reduce-scatter.19.cloned.1.call-done = bf16[2048,256]{1,0:T(8,128)(2,1)} async-done(((bf16[2048,2048]{1,0:T(8,128)(2,1)}), bf16[2048,256]{1,0:T(8,128)(2,1)}) %reduce-scatter.19.cloned.1.call-update) | async-done | bytes 1048592 | tf_op jit(solution)/shard_map/reduce_scatter | solution.py:425
  1944.9 3.4 fusion.13
  1948.3 10.4 all-reduce.6
  (301 shorter events, 72.7 us)
Async XLA Ops:
  7.2 36.8 %all-gather.14.cloned.1.call-start = ((), (), s32[]{:S(2)}) async-start(), calls=%async_computation.16 | async-start | bytes 1966080 | tf_op jit(solution)/shard_map/all_gather | solution.py:262
  9.1 150.6 %all-gather.12.cloned.1.call-start = ((), (), s32[]{:S(2)}) async-start(), calls=%async_computation.15 | async-start | bytes 9437184 | tf_op jit(solution)/shard_map/all_gather | solution.py:262
  9.8 240.7 %all-gather.20.cloned.1.call-start = ((), (), s32[]{:S(2)}) async-start(), calls=%async_computation.19 | async-start | bytes 9437184 | tf_op jit(solution)/shard_map/all_gather | solution.py:262
  45.8 6.3 copy-start.47
  45.9 17.5 copy-start.72
  46.0 17.7 copy-start.69
  46.0 17.7 copy-start.76
  47.5 89.5 %all-to-all-start = ((bf16[8,3,256,128]{3,2,1,0:T(8,128)(2,1)}), bf16[8,3,256,128]{3,2,1,0:T(8,128)(2,1)S(1)}, u32[]{:S(2)}, u32[]{:S(2)}) async-start(bf16[8,3,256,128]{3,2,1,0:T(8,128)(2,1)} %copy.155), calls=%async_computation | async-start | bytes 3145728 | tf_op jit(solution)/shard_map/all_to_all | solution.py:282
  52.1 239.4 %all-gather.18.cloned.1.call-start = ((), (), s32[]{:S(2)}) async-start(), calls=%async_computation.18 | async-start | bytes 4718592 | tf_op jit(solution)/shard_map/all_gather | solution.py:262
  63.4 276.7 %all-gather.16.cloned.1.call-start = ((), (), s32[]{:S(2)}) async-start(), calls=%async_computation.17 | async-start | bytes 4718592 | tf_op jit(solution)/shard_map/all_gather | solution.py:262
  137.0 28.4 %copy-start.48 = (f32[1,2048]{1,0:T(1,128)}, f32[1,2048]{1,0:T(1,128)S(1)}, u32[]{:S(2)}) copy-start(f32[1,2048]{1,0:T(1,128)S(1)} %get-tuple-element.107) | copy-start | bytes 24580
  137.0 47.9 %copy-start.73 = (f32[64]{0:T(128)}, f32[64]{0:T(128)S(1)}, u32[]{:S(2)}) copy-start(f32[64]{0:T(128)S(1)} %multiply_exponential_fusion) | copy-start | bytes 772
  137.0 47.9 %copy-start.50 = (f32[1,8,2,128]{3,1,2,0:T(8,128)}, f32[1,8,2,128]{3,1,2,0:T(8,128)S(1)}, u32[]{:S(2)}) copy-start(f32[1,8,2,128]{3,1,2,0:T(8,128)S(1)} %copy.228) | copy-start | bytes 24580
  137.3 37.1 %copy-start.16 = (bf16[1,8,256,128]{3,2,1,0:T(8,128)(2,1)}, bf16[1,8,256,128]{3,2,1,0:T(8,128)(2,1)S(1)}, u32[]{:S(2)}) copy-start(bf16[1,8,256,128]{3,2,1,0:T(8,128)(2,1)S(1)} %get-tuple-element.88) | copy-start | bytes 1572868
  137.4 43.6 %copy-start.18 = (bf16[1,8,256,128]{3,2,1,0:T(8,128)(2,1)}, bf16[1,8,256,128]{3,2,1,0:T(8,128)(2,1)S(1)}, u32[]{:S(2)}) copy-start(bf16[1,8,256,128]{3,2,1,0:T(8,128)(2,1)S(1)} %get-tuple-element.89) | copy-start | bytes 1572868
  137.4 54.5 %copy-start.14 = (bf16[1,8,256,128]{3,2,1,0:T(8,128)(2,1)}, bf16[1,8,256,128]{3,2,1,0:T(8,128)(2,1)S(1)}, u32[]{:S(2)}) copy-start(bf16[1,8,256,128]{3,2,1,0:T(8,128)(2,1)S(1)} %get-tuple-element.90) | copy-start | bytes 1572868
  165.3 9.1 copy-start.41
  174.4 6.5 copy-start
  190.7 9.7 copy-start.1
  191.9 8.5 copy-start.39
  203.8 224.5 %all-gather.22.cloned.1.call-start = ((), (), s32[]{:S(2)}) async-start(), calls=%async_computation.20 | async-start | bytes 10485760 | tf_op jit(solution)/shard_map/all_gather | solution.py:262
  208.5 309.2 %all-gather.24.cloned.1.call-start = ((), (), s32[]{:S(2)}) async-start(), calls=%async_computation.21 | async-start | bytes 10485760 | tf_op jit(solution)/shard_map/all_gather | solution.py:262
  213.3 393.8 %all-gather.26.cloned.1.call-start = ((), (), s32[]{:S(2)}) async-start(), calls=%async_computation.22 | async-start | bytes 10485760 | tf_op jit(solution)/shard_map/all_gather | solution.py:262
  217.9 486.0 %all-gather.28.cloned.1.call-start = ((), (), s32[]{:S(2)}) async-start(), calls=%async_computation.23 | async-start | bytes 10485760 | tf_op jit(solution)/shard_map/all_gather | solution.py:262
  218.7 567.8 %all-gather.30.cloned.1.call-start = ((), (), s32[]{:S(2)}) async-start(), calls=%async_computation.24 | async-start | bytes 10485760 | tf_op jit(solution)/shard_map/all_gather | solution.py:262
  219.3 656.6 %all-gather.32.cloned.1.call-start = ((), (), s32[]{:S(2)}) async-start(), calls=%async_computation.25 | async-start | bytes 10485760 | tf_op jit(solution)/shard_map/all_gather | solution.py:262
  220.0 880.4 %reduce-scatter.17.cloned.1.call-start = ((), (), s32[]{:S(2)}) async-start(), calls=%async_computation.27 | async-start | bytes 9437184 | tf_op jit(solution)/shard_map/reduce_scatter | solution.py:366
  220.1 29.5 %copy-start.56 = (f32[1,8,2,128]{3,2,1,0:T(2,128)}, f32[1,8,2,128]{3,2,1,0:T(2,128)S(1)}, u32[]{:S(2)}) copy-start(f32[1,8,2,128]{3,2,1,0:T(2,128)S(1)} %fusion.84) | copy-start | bytes 24580
  245.4 112.1 %copy-start.36 = (bf16[2048,32]{0,1:T(8,128)(2,1)}, bf16[2048,32]{0,1:T(8,128)(2,1)S(1)}, u32[]{:S(2)}) copy-start(bf16[2048,32]{0,1:T(8,128)(2,1)S(1)} %all_gather.55) | copy-start | bytes 393220
  353.6 5.8 copy-start.7
  977.9 213.4 %reduce-scatter.15.cloned.1.call-start = ((), (), s32[]{:S(2)}) async-start(), calls=%async_computation.26 | async-start | bytes 9437184 | tf_op jit(solution)/shard_map/reduce_scatter | solution.py:369
  1003.9 48.0 %copy-start.23 = (f32[2048,32]{0,1:T(8,128)S(1)}, f32[2048,32]{0,1:T(8,128)}, u32[]{:S(2)}) copy-start(f32[2048,32]{0,1:T(8,128)} %copy-done.22) | copy-start | bytes 786436
  1003.9 48.0 %copy-start.12 = (f32[2048,32]{0,1:T(8,128)S(1)}, f32[2048,32]{0,1:T(8,128)}, u32[]{:S(2)}) copy-start(f32[2048,32]{0,1:T(8,128)} %copy-done.11) | copy-start | bytes 786436
  1004.0 187.4 %copy-start.35 = (bf16[2048,256]{1,0:T(8,128)(2,1)S(1)}, bf16[2048,256]{1,0:T(8,128)(2,1)}, u32[]{:S(2)}) copy-start(bf16[2048,256]{1,0:T(8,128)(2,1)} %param.31) | copy-start | bytes 3145732
  1004.0 187.3 %copy-start.61 = (f32[2048]{0:T(1024)S(1)}, f32[2048]{0:T(1024)}, u32[]{:S(2)}) copy-start(f32[2048]{0:T(1024)} %copy-done.60) | copy-start | bytes 24580
  1004.0 187.3 %copy-start.64 = (f32[2048]{0:T(1024)S(1)}, f32[2048]{0:T(1024)}, u32[]{:S(2)}) copy-start(f32[2048]{0:T(1024)} %get-tuple-element.114) | copy-start | bytes 24580
  1004.0 187.3 %copy-start.77 = (f32[256]{0:T(256)S(1)}, f32[256]{0:T(256)}, u32[]{:S(2)}) copy-start(f32[256]{0:T(256)} %param.18) | copy-start | bytes 3076
  1004.0 302.6 %reduce-scatter.37.cloned.1.call-start = ((), (), s32[]{:S(2)}) async-start(), calls=%async_computation.37 | async-start | bytes 4718592
  1052.1 143.7 %copy-start.37 = (bf16[2048,32]{0,1:T(8,128)(2,1)}, bf16[2048,32]{0,1:T(8,128)(2,1)S(1)}, u32[]{:S(2)}) copy-start(bf16[2048,32]{0,1:T(8,128)(2,1)S(1)} %get-tuple-element.76) | copy-start | bytes 393220
  1206.6 237.7 %reduce-scatter.33.cloned.1.call-start = ((), (), s32[]{:S(2)}) async-start(), calls=%async_computation.35 | async-start | bytes 10485760 | tf_op jit(solution)/shard_map/reduce_scatter | solution.py:360
  1240.4 203.9 %reduce-scatter.35.cloned.1.call-start = ((), (), s32[]{:S(2)}) async-start(), calls=%async_computation.36 | async-start | bytes 10485760 | tf_op jit(solution)/shard_map/reduce_scatter | solution.py:360
  1273.9 247.8 %reduce-scatter.29.cloned.1.call-start = ((), (), s32[]{:S(2)}) async-start(), calls=%async_computation.33 | async-start | bytes 10485760 | tf_op jit(solution)/shard_map/reduce_scatter | solution.py:359
  1274.5 336.9 %reduce-scatter.31.cloned.1.call-start = ((), (), s32[]{:S(2)}) async-start(), calls=%async_computation.34 | async-start | bytes 10485760 | tf_op jit(solution)/shard_map/reduce_scatter | solution.py:359
  1275.0 425.8 %reduce-scatter.25.cloned.1.call-start = ((), (), s32[]{:S(2)}) async-start(), calls=%async_computation.31 | async-start | bytes 10485760 | tf_op jit(solution)/shard_map/reduce_scatter | solution.py:358
  1275.8 514.7 %reduce-scatter.27.cloned.1.call-start = ((), (), s32[]{:S(2)}) async-start(), calls=%async_computation.32 | async-start | bytes 10485760 | tf_op jit(solution)/shard_map/reduce_scatter | solution.py:358
  1298.1 10.7 copy-start.40
  1302.5 40.0 %all-to-all-start.2 = ((bf16[8,128,256]{2,1,0:T(8,128)(2,1)}), bf16[8,128,256]{2,1,0:T(8,128)(2,1)}, u32[]{:S(2)}, u32[]{:S(2)}) async-start(bf16[8,128,256]{2,1,0:T(8,128)(2,1)} %bitcast.58), calls=%async_computation.6 | async-start | bytes 1048576 | tf_op jit(solution)/shard_map/all_to_all | solution.py:450
  1308.8 7.2 copy-start.9
  1316.0 91.8 %copy-start.13 = (bf16[2,1024,1,128]{3,1,0,2:T(8,128)(2,1)}, bf16[2,1024,1,128]{3,1,0,2:T(8,128)(2,1)S(1)}, u32[]{:S(2)}) copy-start(bf16[2,1024,1,128]{3,1,0,2:T(8,128)(2,1)S(1)} %copy.179) | copy-start | bytes 1572868
  1321.7 5.0 copy-start.32
  1321.7 5.0 copy-start.34
  1327.9 5.5 slice-start
  1342.5 42.9 %all-to-all-start.1 = ((bf16[8,3,256,128]{3,2,1,0:T(8,128)(2,1)}), bf16[8,3,256,128]{3,2,1,0:T(8,128)(2,1)}, u32[]{:S(2)}, u32[]{:S(2)}) async-start(bf16[8,3,256,128]{3,2,1,0:T(8,128)(2,1)} %copy.185), calls=%async_computation.4 | async-start | bytes 3145728 | tf_op jit(solution)/shard_map/all_to_all | solution.py:444
  1347.5 470.6 %reduce-scatter.23.cloned.1.call-start = ((), (), s32[]{:S(2)}) async-start(), calls=%async_computation.30 | async-start | bytes 655360 | tf_op jit(solution)/shard_map/reduce_scatter | solution.py:458
  1349.4 40.4 %copy-start.19 = (bf16[1,8,256,128]{3,2,1,0:T(8,128)(2,1)S(1)}, bf16[1,8,256,128]{3,2,1,0:T(8,128)(2,1)}, u32[]{:S(2)}) copy-start(bf16[1,8,256,128]{3,2,1,0:T(8,128)(2,1)} %copy-done.18) | copy-start | bytes 1572868
  1349.5 503.4 %reduce-scatter.21.cloned.1.call-start = ((), (), s32[]{:S(2)}) async-start(), calls=%async_computation.29 | async-start | bytes 1966080 | tf_op jit(solution)/shard_map/reduce_scatter | solution.py:446
  1389.5 555.4 %reduce-scatter.19.cloned.1.call-start = ((), (), s32[]{:S(2)}) async-start(), calls=%async_computation.28 | async-start | bytes 9437184 | tf_op jit(solution)/shard_map/reduce_scatter | solution.py:425
  1389.8 9.3 copy-start.17
  1389.8 9.3 copy-start.26
  1399.1 8.6 copy-start.15
  1617.5 202.3 %copy-start.10 = (f32[2048,128]{1,0:T(8,128)S(1)}, f32[2048,128]{1,0:T(8,128)}, u32[]{:S(2)}) copy-start(f32[2048,128]{1,0:T(8,128)} %get-tuple-element.119) | copy-start | bytes 3145732
  1617.5 327.4 %copy-start.59 = (f32[2048]{0:T(1024)S(1)}, f32[2048]{0:T(1024)}, u32[]{:S(2)}) copy-start(f32[2048]{0:T(1024)} %get-tuple-element.112) | copy-start | bytes 24580
  1617.5 327.4 %copy-start.70 = (f32[256]{0:T(256)S(1)}, f32[256]{0:T(256)}, u32[]{:S(2)}) copy-start(f32[256]{0:T(256)} %param.17) | copy-start | bytes 3076
  1819.7 128.5 %copy-start.75 = (f32[256]{0:T(256)S(1)}, f32[256]{0:T(256)}, u32[]{:S(2)}) copy-start(f32[256]{0:T(256)} %get-tuple-element.77) | copy-start | bytes 3076
  (43 other events, 87.0 us)
Sparse Core Ops, SparseCore 0:
  10.4 33.5 all-gather.13
  45.6 114.0 all-gather.11
  161.2 83.2 all-gather.19
  246.0 45.4 all-gather.17
  293.5 46.5 all-gather.15
  342.4 85.8 all-gather.21
  430.1 87.5 all-gather.23
  519.6 87.4 all-gather.25
  609.5 87.6 all-gather.27
  698.8 87.6 all-gather.29
  788.3 87.4 all-gather.31
  978.0 122.3 reduce-scatter.16
  1103.3 87.9 reduce-scatter.14
  1206.8 48.3 reduce-scatter.36
  1258.1 84.5 reduce-scatter.32
  1345.8 86.3 reduce-scatter.34
  1435.1 86.4 reduce-scatter.28
  1524.9 86.3 reduce-scatter.30
  1614.4 86.3 reduce-scatter.24
  1704.0 86.3 reduce-scatter.26
  1793.3 24.7 reduce-scatter.22
  1821.9 30.9 reduce-scatter.20
  1855.3 89.5 reduce-scatter.18

commit v2 on v1

--- a/solution.py
+++ b/solution.py
@@ -14,6 +14,7 @@
 F32 = jnp.float32
 BF16 = jnp.bfloat16
 VMEM_LIMIT = 60 * 1024 * 1024
+MESH = pl.DeviceIdType.MESH
 
 
 def inverse_rms(values):
@@ -224,6 +225,327 @@
     )(place, *slots).reshape(micro * group, width)
 
 
+def places():
+    col = lax.axis_index("col")
+    row = lax.axis_index("row")
+    n_col = lax.axis_size("col")
+    pair, core = col // 2, col % 2
+
+    def at(pair_index, core_index):
+        return (row, pair_index * 2 + core_index)
+
+    return col, n_col // 2, pair, core, at
+
+
+def greet(pairs, pair, core, at):
+    barrier = pltpu.get_barrier_semaphore()
+    pl.semaphore_signal(barrier, inc=1, device_id=at(pair, 1 - core), device_id_type=MESH)
+
+    @pl.when(pair > 0)
+    def _():
+        pl.semaphore_signal(barrier, inc=1, device_id=at(pair - 1, core), device_id_type=MESH)
+
+    @pl.when(pair < pairs - 1)
+    def _():
+        pl.semaphore_signal(barrier, inc=1, device_id=at(pair + 1, core), device_id_type=MESH)
+
+    peers = 1 + jnp.where(pair > 0, 1, 0) + jnp.where(pair < pairs - 1, 1, 0)
+    pl.semaphore_wait(barrier, peers)
+
+
+def gather_body(axes, *refs):
+    n = len(axes)
+    ins, outs = refs[:n], refs[n : 2 * n]
+    own_sem, right_s, right_r, left_s, left_r, side_s, side_r = refs[2 * n :]
+    col, pairs, pair, core, at = places()
+
+    def block(j, source):
+        ref = outs[j]
+        size = ins[j].shape[axes[j]]
+        start = pl.multiple_of(source * size, size)
+        if axes[j] == 0:
+            return ref.at[pl.ds(start, size)]
+        return ref.at[:, pl.ds(start, size)]
+
+    def send(j, src, source, sems, recvs, slot, where):
+        return pltpu.make_async_remote_copy(
+            src_ref=src,
+            dst_ref=block(j, source),
+            send_sem=sems.at[j, slot],
+            recv_sem=recvs.at[j, slot],
+            device_id=where,
+            device_id_type=MESH,
+        )
+
+    greet(pairs, pair, core, at)
+
+    def right(j, s):
+        source = (pair - s) * 2 + core
+        src = ins[j] if s == 0 else block(j, source)
+        return send(j, src, source, right_s, right_r, s, at(pair + 1, core))
+
+    def left(j, s):
+        source = (pair + s) * 2 + core
+        src = ins[j] if s == 0 else block(j, source)
+        return send(j, src, source, left_s, left_r, s, at(pair - 1, core))
+
+    def side(j, source_pair, first=False):
+        source = source_pair * 2 + core
+        src = ins[j] if first else block(j, source)
+        return pltpu.make_async_remote_copy(
+            src_ref=src,
+            dst_ref=block(j, source),
+            send_sem=side_s.at[j, source_pair],
+            recv_sem=side_r.at[j, source_pair],
+            device_id=at(pair, 1 - core),
+            device_id_type=MESH,
+        )
+
+    def arrived(j, recvs, slot, source):
+        pltpu.make_async_remote_copy(
+            src_ref=ins[j],
+            dst_ref=block(j, source),
+            send_sem=recvs.at[j, slot],
+            recv_sem=recvs.at[j, slot],
+            device_id=at(pair, 1 - core),
+            device_id_type=MESH,
+        ).wait_recv()
+
+    for j in range(n):
+
+        @pl.when(pair < pairs - 1)
+        def _():
+            right(j, 0).start()
+
+        @pl.when(pair > 0)
+        def _():
+            left(j, 0).start()
+
+    for j in range(n):
+        side(j, pair, True).start()
+        pltpu.make_async_copy(ins[j], block(j, col), own_sem.at[j]).start()
+    for s in range(1, pairs):
+        for j in range(n):
+
+            @pl.when(pair >= s)
+            def _():
+                arrived(j, right_r, s - 1, (pair - s) * 2 + core)
+
+                @pl.when(pair < pairs - 1)
+                def _():
+                    right(j, s).start()
+
+                side(j, pair - s).start()
+
+            @pl.when(pair + s < pairs)
+            def _():
+                arrived(j, left_r, s - 1, (pair + s) * 2 + core)
+
+                @pl.when(pair > 0)
+                def _():
+                    left(j, s).start()
+
+                side(j, pair + s).start()
+
+    for j in range(n):
+        pltpu.make_async_copy(ins[j], block(j, col), own_sem.at[j]).wait()
+        for p in range(pairs):
+            side(j, p).wait_send()
+            arrived(j, side_r, p, p * 2 + 1 - core)
+        for s in range(pairs):
+
+            @pl.when((pair >= s) & (pair < pairs - 1))
+            def _():
+                right(j, s).wait_send()
+
+            @pl.when((pair + s < pairs) & (pair > 0))
+            def _():
+                left(j, s).wait_send()
+
+
+def gather_col(arrays, axes, ident):
+    n_col = lax.axis_size("col")
+    pairs, n = n_col // 2, len(arrays)
+    shapes = [
+        tuple(d * n_col if at == axis else d for at, d in enumerate(a.shape))
+        for a, axis in zip(arrays, axes)
+    ]
+    dma = pltpu.SemaphoreType.DMA
+    return pl.pallas_call(
+        functools.partial(gather_body, axes),
+        in_specs=[pl.BlockSpec(memory_space=pl.ANY)] * n,
+        out_specs=[pl.BlockSpec(memory_space=pl.ANY)] * n,
+        out_shape=[jax.ShapeDtypeStruct(s, a.dtype) for s, a in zip(shapes, arrays)],
+        scratch_shapes=[dma((n,))] + [dma((n, pairs))] * 6,
+        compiler_params=pltpu.CompilerParams(collective_id=ident, has_side_effects=True),
+        cost_estimate=pl.CostEstimate(
+            flops=0,
+            bytes_accessed=sum(math.prod(s) for s in shapes) * 16,
+            transcendentals=0,
+        ),
+        name="gather_col",
+    )(*arrays)
+
+
+def scatter_body(
+    part, x, out, acc, side, from_left, from_right, load, side_s, side_r, right_s, right_r, left_s, left_r
+):
+    col, pairs, pair, core, at = places()
+    rows = out.shape[0]
+    tile = min(256, rows)
+
+    def block(owner):
+        return x.at[:, pl.ds(pl.multiple_of(owner * part, part), part)]
+
+    def fetch(d):
+        return pltpu.make_async_copy(block(d * 2 + core), acc.at[d], load.at[d])
+
+    def across(d):
+        return pltpu.make_async_remote_copy(
+            src_ref=block(d * 2 + 1 - core),
+            dst_ref=side.at[d],
+            send_sem=side_s.at[d],
+            recv_sem=side_r.at[d],
+            device_id=at(pair, 1 - core),
+            device_id_type=MESH,
+        )
+
+    def right(d):
+        return pltpu.make_async_remote_copy(
+            src_ref=acc.at[d],
+            dst_ref=from_left.at[d],
+            send_sem=right_s.at[d],
+            recv_sem=right_r.at[d],
+            device_id=at(pair + 1, core),
+            device_id_type=MESH,
+        )
+
+    def left(d):
+        return pltpu.make_async_remote_copy(
+            src_ref=acc.at[d],
+            dst_ref=from_right.at[d],
+            send_sem=left_s.at[d],
+            recv_sem=left_r.at[d],
+            device_id=at(pair - 1, core),
+            device_id_type=MESH,
+        )
+
+    greet(pairs, pair, core, at)
+    order = []
+    for t in range(pairs):
+        for d in (pairs - 1 - t, t):
+            if d not in order:
+                order.append(d)
+    for d in order:
+        across(d).start()
+        fetch(d).start()
+
+    def add(into, *refs):
+        def step(i, _):
+            at_rows = pl.ds(pl.multiple_of(i * tile, tile), tile)
+            total = refs[0][at_rows, :].astype(F32)
+            for ref in refs[1:]:
+                total = total + ref[at_rows, :].astype(F32)
+            into[at_rows, :] = total.astype(into.dtype)
+            return 0
+
+        lax.fori_loop(0, rows // tile, step, 0)
+
+    def ready(d):
+        fetch(d).wait()
+        across(d).wait_recv()
+
+    def go_right(d):
+        ready(d)
+
+        @pl.when(pair > 0)
+        def _():
+            right(d).wait_recv()
+            add(acc.at[d], acc.at[d], side.at[d], from_left.at[d])
+
+        @pl.when(pair == 0)
+        def _():
+            add(acc.at[d], acc.at[d], side.at[d])
+
+        right(d).start()
+
+    def go_left(d):
+        ready(d)
+
+        @pl.when(pair < pairs - 1)
+        def _():
+            left(d).wait_recv()
+            add(acc.at[d], acc.at[d], side.at[d], from_right.at[d])
+
+        @pl.when(pair == pairs - 1)
+        def _():
+            add(acc.at[d], acc.at[d], side.at[d])
+
+        left(d).start()
+
+    for t in range(pairs - 1):
+        far, near = pairs - 1 - t, t
+
+        @pl.when(far > pair)
+        def _():
+            go_right(far)
+
+        @pl.when(near < pair)
+        def _():
+            go_left(near)
+
+    ready(pair)
+
+    @pl.when(pair == 0)
+    def _():
+        left(pair).wait_recv()
+        add(out, acc.at[pair], side.at[pair], from_right.at[pair])
+
+    @pl.when(pair == pairs - 1)
+    def _():
+        right(pair).wait_recv()
+        add(out, acc.at[pair], side.at[pair], from_left.at[pair])
+
+    @pl.when((pair > 0) & (pair < pairs - 1))
+    def _():
+        left(pair).wait_recv()
+        right(pair).wait_recv()
+        add(out, acc.at[pair], side.at[pair], from_left.at[pair], from_right.at[pair])
+
+    for d in range(pairs):
+        across(d).wait_send()
+
+        @pl.when(pair < d)
+        def _():
+            right(d).wait_send()
+
+        @pl.when(pair > d)
+        def _():
+            left(d).wait_send()
+
+
+def scatter_col(x, ident):
+    n_col = lax.axis_size("col")
+    pairs = n_col // 2
+    rows, part = x.shape[0], x.shape[1] // n_col
+    dma = pltpu.SemaphoreType.DMA
+    buffer = pltpu.VMEM((pairs, rows, part), BF16)
+    return pl.pallas_call(
+        functools.partial(scatter_body, part),
+        in_specs=[pl.BlockSpec(memory_space=pl.ANY)],
+        out_specs=pl.BlockSpec(memory_space=pltpu.VMEM),
+        out_shape=jax.ShapeDtypeStruct((rows, part), F32),
+        scratch_shapes=[buffer] * 4 + [dma((pairs,))] * 7,
+        compiler_params=pltpu.CompilerParams(
+            vmem_limit_bytes=VMEM_LIMIT, collective_id=ident, has_side_effects=True
+        ),
+        cost_estimate=pl.CostEstimate(
+            flops=0, bytes_accessed=rows * part * n_col * 24, transcendentals=0
+        ),
+        name="scatter_col",
+    )(x)
+
+
 def shards(
     tokens,
     gain_attn,
@@ -276,17 +598,18 @@
         for c in chunks
     ]
 
-    inputs_low = gather(tokens, "col", 1)
     packed = jnp.concatenate([w_query, w_key, w_value], 0)
     packed = gather(packed, "row", 1).reshape(3, part, n_col, local_heads * head)
     w_heads = lax.all_to_all(
         packed.transpose(2, 0, 1, 3), "col", split_axis=0, concat_axis=0, tiled=True
     )
     w_heads = w_heads.transpose(1, 0, 2, 3).reshape(3, width, local_heads * head)
-    full_o = gather(gather(w_out, "row", 1), "col", 0)
-    full_r = gather(gather(w_router, "row", 1), "col", 0)
-    gains = gather(jnp.stack([gain_attn, gain_ffn]), "col", 1)
-    upstream_low = gather(cotangent, "col", 1)
+    router_t = gather(w_router, "row", 1).T
+    inputs_low, gains, full_rt = gather_col(
+        [tokens, jnp.stack([gain_attn, gain_ffn]), router_t], (1, 1, 1), 0
+    )
+    full_r = full_rt.T
+    upstream_low, full_o = gather_col([cotangent, gather(w_out, "row", 1)], (1, 0), 1)
 
     segment, position, live = jax.vmap(lambda l: layout(l, group))(lengths)
     position = position.reshape(rows)
@@ -333,7 +656,7 @@
     attended = jnp.einsum(
         "ghqk,gkhd->gqhd", probs_low, values_low, preferred_element_type=F32
     ).astype(BF16)
-    attended_full = gather(attended.reshape(rows, local_heads * head), "col", 1)
+    (attended_full,) = gather_col([attended.reshape(rows, local_heads * head)], (1,), 2)
 
     hidden = inputs + nn(attended_full, full_o)
     scale_two = inverse_rms(hidden)
@@ -351,34 +674,35 @@
         xe, dyr, hg, dgp, dup, ye, dxe, tok = expert_pass(
             counts[c], place_t[c], gate_t[c], hn, upstream_full, wg, wu, wd, capacity
         )
+        gg, gu, gd = expert_grads(xe, dgp, dup, hg, dyr)
+        hn, upstream_full, ye, dxe, tok, gg, gu, gd = lax.optimization_barrier(
+            (hn, upstream_full, ye, dxe, tok, gg, gu, gd)
+        )
         outs.append((ye, dxe, tok))
-        gg, gu, gd = expert_grads(xe, dgp, dup, hg, dyr)
         weight_grads.append(
-            (
+            [
                 lax.psum_scatter(gg, "row", scatter_dimension=1, tiled=True),
                 lax.psum_scatter(gu, "row", scatter_dimension=1, tiled=True),
                 lax.psum_scatter(gd, "row", scatter_dimension=2, tiled=True),
-            )
+            ]
         )
-    grad_gate, grad_up, grad_down = (
-        jnp.concatenate([w[j] for w in weight_grads], 0).astype(F32) for j in range(3)
-    )
-    back_sum = lax.psum_scatter(
-        combine(place, [o[1] for o in outs]), "col", scatter_dimension=1, tiled=True
-    )
-    mixed_sum = lax.psum_scatter(
-        combine(place, [o[0] for o in outs]), "col", scatter_dimension=1, tiled=True
-    )
+    def tie(value, c, j):
+        value, done = lax.optimization_barrier((value, weight_grads[c][j]))
+        weight_grads[c][j] = done
+        return value
+
+    back_sum = scatter_col(combine(place, [tie(o[1], 0, 2) for o in outs]), 3)
+    mixed_sum = scatter_col(combine(place, [o[0] for o in outs]), 4)
     tok = jnp.concatenate([o[2] for o in outs], 0)
     tok = gather(tok, "col", 0)
     gate_dots = tok[:, :, 0].reshape(experts, rows).T
     hidden_part = mine(hidden, 1)
-    mixed = (hidden_part + mixed_sum.astype(F32)).astype(BF16)
+    mixed = (hidden_part + mixed_sum).astype(BF16)
 
     selected = gates * (gate_dots - jnp.sum(gates * gate_dots, -1, keepdims=True))
     logit_grad = selected.astype(BF16)
     router_part = mine(full_r, 0)
-    normed_grad = back_sum.astype(F32) + nt(logit_grad, router_part)
+    normed_grad = back_sum + nt(logit_grad, router_part)
     grad_router = tn(mine(normed_ffn, 1), logit_grad)
     scaled_two = hidden_part * scale_two
     grad_gain_ffn = jnp.sum(normed_grad * scaled_two, 0)
@@ -392,10 +716,9 @@
         - hidden_part * scale_two**2 * dot_two[:, None] / width
     )
 
-    branch_grad = hidden_grad.astype(BF16)
-    attended_grad = lax.psum_scatter(
-        nt(branch_grad, mine(full_o, 1)).astype(BF16), "col", scatter_dimension=1, tiled=True
-    ).reshape(batch)
+    branch_grad = tie(hidden_grad.astype(BF16), 0, 0)
+    attended_grad = scatter_col(nt(branch_grad, mine(full_o, 1)).astype(BF16), 5)
+    attended_grad = tie(attended_grad.astype(BF16).reshape(batch), 0, 1)
     grad_out = tn(attended_full, branch_grad)
     scores_again = scores_of()
     probs = jnp.exp(scores_again - log_total)
@@ -422,9 +745,7 @@
         v.reshape(flat).astype(BF16) for v in (query_grad, key_grad, values_grad)
     ]
     back_heads = sum(nt(g, w_heads[j]) for j, g in enumerate(heads_grad))
-    normed_back = lax.psum_scatter(
-        back_heads.astype(BF16), "col", scatter_dimension=1, tiled=True
-    ).astype(F32)
+    normed_back = scatter_col(tie(back_heads.astype(BF16), -1, 2), 6)
     pre = (query_pre, key_pre, value_pre)
     dot_part = sum(jnp.sum(g.astype(F32) * p, -1) for g, p in zip(heads_grad, pre))
     dot_one, gain_query_sum, gain_key_sum = lax.psum(
@@ -437,6 +758,10 @@
         hidden_grad
         + scale_one_part * (normed_back * gain_attn)
         - inputs_part * scale_one_part**2 * dot_one[:, None] / width
+    )
+
+    grad_gate, grad_up, grad_down = (
+        jnp.concatenate([w[j] for w in weight_grads], 0).astype(F32) for j in range(3)
     )
 
     heads_weights = jnp.stack([tn(normed, g) for g in heads_grad]).astype(BF16)

time: 1970 us -> 1360 us (0.69)
  waiting for transfers between devices: 1190 us -> 108 us
  Pallas kernels: 292 us -> 879 us
  blocking collectives: 198 us -> 85.4 us
    pallas_call x0 -> x7, Pallas kernels: none -> 584 us  [the longest x4 359 us: scatter_col(): pl.pallas_call(functools.partial(scatter_body, part), in_specs=[pl.BlockS...]
    all_gather x11 -> x7, waiting for transfers between devices: 551 us -> 83.1 us  [gather(): return lax.all_gather(value, axis_name, axis=axis, tiled=True)]
    reduce_scatter x3 -> x0, waiting for transfers between devices: 229 us -> none  [the longest x1 90.9 us: shards(): lax.psum_scatter(combine(place, [o[0] for o in outs]), 'col', scatter_dim...]
    reduce_scatter x2, waiting for transfers between devices: 173 us -> 0.01 us  [shards(): lax.psum_scatter(gg, 'row', scatter_dimension=1, tiled=True)]
    reduce_scatter x2, waiting for transfers between devices: 161 us -> 0.01 us  [shards(): lax.psum_scatter(gu, 'row', scatter_dimension=1, tiled=True)]
    all_gather x5 -> x3, blocking collectives: 155 us -> 37.7 us  [gather(): return lax.all_gather(value, axis_name, axis=axis, tiled=True)]
    all_to_all x1, waiting for transfers between devices: 35.9 us -> 0.01 us  [shards(): lax.all_to_all(heads_weights, 'col', split_axis=0, concat_axis=0, tiled=T...]
    reduce_scatter x1, waiting for transfers between devices: 21.5 us -> 0.01 us  [shards(): lax.psum_scatter(out_weights, 'row', scatter_dimension=1, tiled=True)]
  transfers between devices with their start and end apart: 26 -> 18, of which waited for: 19 -> 2; matrix products, arithmetic and copies ran while one was open for 11% -> 17% of each run, Pallas kernels for 10% -> 65%
where the time goes in v2:
time: 1360 us; the launch traced here: 1350 us
  Pallas kernels  879 us (65%)
  waiting for transfers between devices  108 us (8%)
  matrix products  103 us (8%)
  blocking collectives  85.4 us (6%)
  other arithmetic  80.1 us (6%)
  local copies, waits for them, and re-layouts  59.5 us (4%)
  between operations  16.6 us (1%)
  starting transfers between devices  14.3 us (1%)
    pallas_call x4, Pallas kernels, scatter_col(): pl.pallas_call(functools.partial(scatter_body, part), in_specs=[pl.BlockS...  359 us
    pallas_call x3, Pallas kernels, gather_col(): pl.pallas_call(functools.partial(gather_body, axes), in_specs=[pl.BlockSp...  225 us
    pallas_call x2, Pallas kernels, expert_pass(): pl.pallas_call(expert_body, grid_spec=pltpu.PrefetchScalarGridSpec(num_sc...  175 us
    all_gather x7, waiting for transfers between devices, gather(): return lax.all_gather(value, axis_name, axis=axis, tiled=True)  83.1 us
    pallas_call x2, Pallas kernels, expert_grads(): pl.pallas_call(grads_body, grid=(experts, width // part), in_specs=[pl.Bl...  68 us
    pallas_call x2, Pallas kernels, combine(): pl.pallas_call(combine_body, grid=(micro, group // tile), in_specs=[pl.Bl...  51.9 us
    dot_general x5, matrix products, nt(): lax.dot_general(a, b, (((1,), (1,)), ((), ())), preferred_element_type=F32)  42 us
    all_gather x3, blocking collectives, gather(): return lax.all_gather(value, axis_name, axis=axis, tiled=True)  37.7 us
  transfers between devices with their start and end apart: 18, of which 2 were waited for; matrix products, arithmetic and copies ran while one was open for 17% of the time, Pallas kernels for 65%

profile of v2, /device:TPU:0, one launch (start us, length us, event | category | flops | bytes accessed | tf_op | source)
XLA Modules:
  0.0 1346.6 jit_solution(5151219149395301579)
XLA Ops:
  9.1 4.7 fusion.101
  13.9 4.6 fusion.100
  18.6 4.8 fusion.99
  25.9 10.2 all_gather.30
  36.9 12.5 all_gather.32.refs_1_
  55.2 77.9 %gather_col.3 = (bf16[2048,2048]{1,0:T(8,128)(2,1)}, f32[2,2048]{1,0:T(2,128)}, bf16[32,2048]{1,0:T(8,128)(2,1)}) custom-call(bf16[2048,256]{1,0:T(8,128)(2,1)} %refs_0_.2, f32[2,256]{1,0:T(2,128)} %pad_maximum_fusion.8.refs_1_, bf16[32,256]{1,0:T(8,128)(2,1)} %bitcast.273), custom_call_target="tpu_custom_call" | custom-call | bytes 68222976 | tf_op jit(solution)/shard_map/gather_col/pallas_call | solution.py:374
  133.9 5.1 fusion
  139.6 106.8 %gather_col.5 = (bf16[2048,2048]{1,0:T(8,128)(2,1)}, bf16[1024,2048]{1,0:T(8,128)(2,1)}) custom-call(bf16[2048,256]{1,0:T(8,128)(2,1)} %refs_0_.3, bf16[128,2048]{1,0:T(8,128)(2,1)} %all_gather.32.refs_1_), custom_call_target="tpu_custom_call" | custom-call | bytes 100663296 | tf_op jit(solution)/shard_map/gather_col/pallas_call | solution.py:374
  249.9 3.6 all-to-all-start
  253.8 7.4 broadcast_multiply_fusion
  261.1 8.8 fusion.2
  269.9 21.3 %all-to-all-done = bf16[8,3,256,128]{3,2,1,0:T(8,128)(2,1)S(1)} async-done(((bf16[8,3,256,128]{3,2,1,0:T(8,128)(2,1)}), bf16[8,3,256,128]{3,2,1,0:T(8,128)(2,1)S(1)}, u32[]{:S(2)}, u32[]{:S(2)}) %all-to-all-start) | async-done | bytes 1572896 | tf_op jit(solution)/shard_map/all_to_all | solution.py:603
  291.5 6.9 multiply_reduce_fusion.6
  299.1 2.9 multiply_reduce_fusion.7
  302.1 3.4 fusion.106
  305.8 2.8 fusion.55
  309.8 1.9 fusion.107
  313.0 2.0 copy-done
  317.5 40.8 %gather_col.4 = bf16[2048,1024]{1,0:T(8,128)(2,1)} custom-call(bf16[2048,128]{1,0:T(8,128)(2,1)} %bitcast.263), custom_call_target="tpu_custom_call" | custom-call | bytes 33554432 | tf_op jit(solution)/shard_map/gather_col/pallas_call | solution.py:374
  358.3 14.2 %multiply_reduce_fusion = (f32[2048]{0:T(1024)S(1)}, f32[2048,2048]{1,0:T(8,128)S(1)}) fusion(bf16[2048,1024]{1,0:T(8,128)(2,1)} %gather_col.4, bf16[1024,2048]{1,0:T(8,128)(2,1)} %get-tuple-element.67, bf16[2048,2048]{1,0:T(8,128)(2,1)} %get-tuple-element.65), kind=kOutput, calls=%fused_computation.8 | convolution fusion | flops 8606709760 | bytes 33562624 | tf_op jit(solution)/shard_map/dot_general | solution.py:50
  373.2 2.2 multiply_convert_fusion
  375.4 2.9 copy-done.6
  378.3 3.4 copy-done.1
  381.7 2.6 select_reduce_fusion
  386.5 77.8 %expert_pass.2 = (bf16[2,2,512,2048]{3,2,1,0:T(8,128)(2,1)}, bf16[2,2,512,2048]{3,2,1,0:T(8,128)(2,1)}, bf16[2,2,512,1024]{3,2,1,0:T(8,128)(2,1)}, bf16[2,2,512,...) custom-call(s32[2,2]{1,0:T(2,128)} %get-tuple-element.176.counts, ...), custom_call_target="tpu_custom_call" | custom-call | flops 68719476736 | bytes 104857600 | tf_op jit(solution)/shard_map/expert_pass/pallas_call | solution.py:120
  464.3 33.3 %expert_grads.2 = (bf16[2,2048,1024]{2,1,0:T(8,128)(2,1)}, bf16[2,2048,1024]{2,1,0:T(8,128)(2,1)}, bf16[2,1024,2048]{2,1,0:T(8,128)(2,1)}) custom-call(bf16[2,1024,2048]{2,1,0:T(8,128)(2,1)} %bitcast.282, bf16[2,1024,1024]{2,1,0:T(8,128)(2,1)} %bitcast.288, bf16[2,1024,1024]{2,1,0:T(8,128)(2,1)} %bitcast.289, bf16[2,1024,1024]{2,1,0:T(8,128)(2,1)} %bitcast.287, ...), custom_call_target="tpu_custom_call" | custom-call | flops 25769803776 | bytes 54525952 | tf_op jit(solution)/shard_map/expert_grads/pallas_call | solution.py:161
  500.6 83.1 %all-gather.20.cloned.1.call-done.wd = bf16[2,1024,2048]{2,1,0:T(8,128)(2,1)} async-done(((bf16[2,1024,512]{2,1,0:T(8,128)(2,1)}), bf16[2,1024,2048]{2,1,0:T(8,128)(2,1)}) %all-gather.20.cloned.1.call-update) | async-done | bytes 8388624 | tf_op jit(solution)/shard_map/all_gather | solution.py:584
  583.7 97.2 %expert_pass.3 = (bf16[2,2,512,2048]{3,2,1,0:T(8,128)(2,1)}, bf16[2,2,512,2048]{3,2,1,0:T(8,128)(2,1)}, bf16[2,2,512,1024]{3,2,1,0:T(8,128)(2,1)}, bf16[2,2,512,...) custom-call(s32[2,2]{1,0:T(2,128)} %get-tuple-element.175.counts, ...), custom_call_target="tpu_custom_call" | custom-call | flops 68719476736 | bytes 104857600 | tf_op jit(solution)/shard_map/expert_pass/pallas_call | solution.py:120
  680.9 34.8 %expert_grads.3 = (bf16[2,2048,1024]{2,1,0:T(8,128)(2,1)}, bf16[2,2048,1024]{2,1,0:T(8,128)(2,1)}, bf16[2,1024,2048]{2,1,0:T(8,128)(2,1)}) custom-call(bf16[2,1024,2048]{2,1,0:T(8,128)(2,1)} %bitcast.280, bf16[2,1024,1024]{2,1,0:T(8,128)(2,1)} %bitcast.285, bf16[2,1024,1024]{2,1,0:T(8,128)(2,1)} %bitcast.286, bf16[2,1024,1024]{2,1,0:T(8,128)(2,1)} %bitcast.284, ...), custom_call_target="tpu_custom_call" | custom-call | flops 25769803776 | bytes 54525952 | tf_op jit(solution)/shard_map/expert_grads/pallas_call | solution.py:161
  717.1 9.0 fusion.135
  726.1 12.3 copy.214
  738.4 25.8 %combine.2 = bf16[2,1024,2048]{2,1,0:T(8,128)(2,1)} custom-call(s32[2,1024,4]{2,1,0:T(8,128)} %copy-done.20, bf16[2,2,512,2048]{3,2,1,0:T(8,128)(2,1)} %get-tuple-element.81.refs_0_, bf16[2,2,512,2048]{3,2,1,0:T(8,128)(2,1)} %get-tuple-element.95.refs_1_), custom_call_target="tpu_custom_call" | custom-call | flops 17179869184 | bytes 25165824 | tf_op jit(solution)/shard_map/combine/pallas_call | solution.py:208
  764.2 100.2 %scatter_col.4 = f32[2048,256]{1,0:T(8,128)} custom-call(bf16[2048,2048]{1,0:T(8,128)(2,1)} %bitcast.227), custom_call_target="tpu_custom_call" | custom-call | bytes 100663296 | tf_op jit(solution)/shard_map/scatter_col/pallas_call | solution.py:533
  864.4 15.0 %all_gather.39 = f32[32,2,2,1024]{3,2,1,0:T(2,128)S(1)} all-gather(f32[4,2,2,1024]{3,2,1,0:T(2,128)S(1)} %pad_maximum_fusion.7), channel_id=1, replica_groups=mesh['row'=4,'col'=8] {'col'}, dimensions={0}, use_global_device_ids=true | all-gather | bytes 589824 | tf_op jit(solution)/shard_map/all_gather | solution.py:584
  880.7 26.1 %combine.3 = bf16[2,1024,2048]{2,1,0:T(8,128)(2,1)} custom-call(s32[2,1024,4]{2,1,0:T(8,128)} %copy-done.20, bf16[2,2,512,2048]{3,2,1,0:T(8,128)(2,1)} %get-tuple-element.98.refs_0_, bf16[2,2,512,2048]{3,2,1,0:T(8,128)(2,1)} %get-tuple-element.101.refs_1_), custom_call_target="tpu_custom_call" | custom-call | flops 17179869184 | bytes 25165824 | tf_op jit(solution)/shard_map/combine/pallas_call | solution.py:208
  906.8 102.2 %scatter_col.5 = f32[2048,256]{1,0:T(8,128)} custom-call(bf16[2048,2048]{1,0:T(8,128)(2,1)} %bitcast.226), custom_call_target="tpu_custom_call" | custom-call | bytes 100663296 | tf_op jit(solution)/shard_map/scatter_col/pallas_call | solution.py:533
  1009.1 4.8 fusion.97
  1013.9 4.4 convolution_convert_fusion.x
  1018.2 53.1 %scatter_col.6 = f32[2048,128]{1,0:T(8,128)} custom-call(bf16[2048,1024]{1,0:T(8,128)(2,1)} %convolution_convert_fusion.x), custom_call_target="tpu_custom_call" | custom-call | bytes 50331648 | tf_op jit(solution)/shard_map/scatter_col/pallas_call | solution.py:533
  1071.3 2.1 convert_element_type.224
  1073.4 4.3 convolution_convert_fusion.3
  1077.7 4.3 all-to-all-start.2
  1082.0 6.0 fusion.28
  1089.4 5.4 multiply_reduce_fusion.1
  1094.8 5.0 multiply_convert_fusion.1
  1102.8 2.6 fusion.64
  1106.6 2.3 fusion.26
  1109.0 2.4 fusion.24
  1111.7 2.4 fusion.25
  1115.5 5.0 all-to-all-start.1
  1123.3 24.2 %all-reduce.4 = bf16[256,32]{0,1:T(8,128)(2,1)S(1)} all-reduce(bf16[256,32]{0,1:T(8,128)(2,1)S(1)} %convolution_convert_fusion.7), channel_id=8, replica_groups=mesh['row'=4,'col'=8] {'row'}, use_global_device_ids=true, to_apply=%region_39.40.clone | all-reduce | flops 8192 | bytes 32768
  1148.1 2.0 copy.217
  1150.4 9.3 fusion.68
  1159.7 8.1 fusion.70
  1167.8 2.4 copy.192
  1171.9 15.4 %add_convert_fusion.x = bf16[2048,2048]{1,0:T(8,128)(2,1)} fusion(f32[2048,2048]{1,0:T(8,128)} %fusion.70, f32[2048,2048]{1,0:T(8,128)} %fusion.68, bf16[2048,128]{1,0:T(8,128)(2,1)S(1)} %bitcast.240, bf16[2048,128]{1,0:T(8,128)(2,1)S(1)} %bitcast.242), kind=kOutput, calls=%fused_computation.6 | convolution fusion | flops 1086324736 | bytes 42991616 | tf_op jit(solution)/shard_map/dot_general | solution.py:54
  1187.4 103.4 %scatter_col.7 = f32[2048,256]{1,0:T(8,128)} custom-call(bf16[2048,2048]{1,0:T(8,128)(2,1)} %add_convert_fusion.x), custom_call_target="tpu_custom_call" | custom-call | bytes 100663296 | tf_op jit(solution)/shard_map/scatter_col/pallas_call | solution.py:533
  1291.2 14.8 %all-reduce.5 = (f32[2048]{0:T(1024)S(1)}, f32[128]{0:T(128)S(1)}, f32[128]{0:T(128)S(1)}) all-reduce(f32[2048]{0:T(1024)S(1)} %add_add_fusion.2, f32[128]{0:T(128)S(1)} %get-tuple-element.118, f32[128]{0:T(128)S(1)} %get-tuple-element.116), channel_id=1, replica_groups=mesh['row'=4,'col'=8] {'col'}, use_global_device_ids=true, to_apply=%region_26.27 | all-reduce | flops 2304 | bytes 18432 | tf_op jit(solution)/shard_map/psum | solution.py:751
  1306.0 3.3 fusion.11
  1309.3 8.7 all-reduce.6
  1318.1 6.2 maximum_convert_fusion.2
  1324.3 6.3 maximum_convert_fusion.1
  1330.6 5.5 maximum_convert_fusion
  1337.7 1.9 slice_convert_fusion
  (280 shorter events, 44.1 us)
Async XLA Ops:
  7.2 239.2 %all-gather.8.cloned.1.call-start = ((), (), s32[]{:S(2)}) async-start(), calls=%async_computation.11 | async-start | bytes 1966080 | tf_op jit(solution)/shard_map/all_gather | solution.py:584
  9.1 377.4 %all-gather.10.cloned.1.call-start = ((), (), s32[]{:S(2)}) async-start(), calls=%async_computation.12 | async-start | bytes 10485760 | tf_op jit(solution)/shard_map/all_gather | solution.py:584
  13.8 372.7 %all-gather.12.cloned.1.call-start = ((), (), s32[]{:S(2)}) async-start(), calls=%async_computation.13 | async-start | bytes 10485760 | tf_op jit(solution)/shard_map/all_gather | solution.py:584
  18.5 6.9 copy-start.72
  18.5 7.3 copy-start.71
  18.5 17.5 %copy-start.58 = (s32[2048,8]{0,1:T(8,128)S(1)}, s32[2048,8]{0,1:T(8,128)}, u32[]{:S(2)}) copy-start(s32[2048,8]{0,1:T(8,128)} %param.29) | copy-start | bytes 196612
  18.6 18.4 %copy-start.45 = (bf16[128,512]{1,0:T(8,128)(2,1)S(1)}, bf16[128,512]{1,0:T(8,128)(2,1)}, u32[]{:S(2)}) copy-start(bf16[128,512]{1,0:T(8,128)(2,1)} %param.24) | copy-start | bytes 393220
  18.6 367.9 %all-gather.14.cloned.1.call-start = ((), (), s32[]{:S(2)}) async-start(), calls=%async_computation.14 | async-start | bytes 10485760 | tf_op jit(solution)/shard_map/all_gather | solution.py:584
  23.4 477.1 %all-gather.16.cloned.1.call-start = ((), (), s32[]{:S(2)}) async-start(), calls=%async_computation.15 | async-start | bytes 10485760 | tf_op jit(solution)/shard_map/all_gather | solution.py:584
  24.0 30.6 %copy-start.67 = (f32[256]{0:T(256)S(1)}, f32[256]{0:T(256)}, u32[]{:S(2)}) copy-start(f32[256]{0:T(256)} %param.18) | copy-start | bytes 3076
  24.0 30.6 %copy-start.69 = (f32[256]{0:T(256)S(1)}, f32[256]{0:T(256)}, u32[]{:S(2)}) copy-start(f32[256]{0:T(256)} %param.17) | copy-start | bytes 3076
  24.1 476.5 %all-gather.18.cloned.1.call-start = ((), (), s32[]{:S(2)}) async-start(), calls=%async_computation.16 | async-start | bytes 10485760 | tf_op jit(solution)/shard_map/all_gather | solution.py:584
  24.6 559.0 %all-gather.20.cloned.1.call-start = ((), (), s32[]{:S(2)}) async-start(), calls=%async_computation.17 | async-start | bytes 10485760 | tf_op jit(solution)/shard_map/all_gather | solution.py:584
  25.7 23.7 %copy-start.56 = (f32[1,8,2,128]{3,2,1,0:T(2,128)}, f32[1,8,2,128]{3,2,1,0:T(2,128)S(1)}, u32[]{:S(2)}) copy-start(f32[1,8,2,128]{3,2,1,0:T(2,128)S(1)} %fusion.83) | copy-start | bytes 24580
  25.8 280.0 %copy-start.50 = (f32[1,8,2,128]{3,1,2,0:T(8,128)}, f32[1,8,2,128]{3,1,2,0:T(8,128)S(1)}, u32[]{:S(2)}) copy-start(f32[1,8,2,128]{3,1,2,0:T(8,128)S(1)} %copy.234) | copy-start | bytes 24580
  133.9 127.3 %copy-start.46 = (f32[1,2048]{1,0:T(1,128)}, f32[1,2048]{1,0:T(1,128)S(1)}, u32[]{:S(2)}) copy-start(f32[1,2048]{1,0:T(1,128)S(1)} %get-tuple-element.166) | copy-start | bytes 24580
  139.6 121.6 %copy-start.39 = (f32[2048]{0:T(1024)}, f32[2048]{0:T(1024)S(1)}, u32[]{:S(2)}) copy-start(f32[2048]{0:T(1024)S(1)} %get-tuple-element.172) | copy-start | bytes 24580
  249.9 41.3 %all-to-all-start = ((bf16[8,3,256,128]{3,2,1,0:T(8,128)(2,1)}), bf16[8,3,256,128]{3,2,1,0:T(8,128)(2,1)S(1)}, u32[]{:S(2)}, u32[]{:S(2)}) async-start(bf16[8,3,256,128]{3,2,1,0:T(8,128)(2,1)} %copy.160), calls=%async_computation | async-start | bytes 3145728 | tf_op jit(solution)/shard_map/all_to_all | solution.py:603
  253.5 627.2 %reduce-scatter.9.cloned.1.call-start = ((), (), s32[]{:S(2)}) async-start(), calls=%async_computation.18 | async-start | bytes 10485760 | tf_op jit(solution)/shard_map/reduce_scatter | solution.py:686
  253.7 52.1 %copy-start.73 = (f32[64]{0:T(128)}, f32[64]{0:T(128)S(1)}, u32[]{:S(2)}) copy-start(f32[64]{0:T(128)S(1)} %multiply_exponential_fusion) | copy-start | bytes 772
  291.4 7.7 slice-start
  291.5 7.0 copy-start.18
  291.5 10.5 copy-start.16
  291.5 10.6 copy-start.14
  291.5 7.6 slice-start.1
  298.5 7.0 copy-start.2
  298.5 7.0 copy-start.41
  305.5 7.5 copy-start.7
  372.5 5.8 copy-start.6
  373.2 5.1 copy-start.48
  373.2 8.5 copy-start.38
  497.6 516.2 %reduce-scatter.11.cloned.1.call-start = ((), (), s32[]{:S(2)}) async-start(), calls=%async_computation.19 | async-start | bytes 10485760 | tf_op jit(solution)/shard_map/reduce_scatter | solution.py:684
  498.4 575.1 %reduce-scatter.13.cloned.1.call-start = ((), (), s32[]{:S(2)}) async-start(), calls=%async_computation.20 | async-start | bytes 10485760 | tf_op jit(solution)/shard_map/reduce_scatter | solution.py:685
  498.9 688.4 %reduce-scatter.15.cloned.1.call-start = ((), (), s32[]{:S(2)}) async-start(), calls=%async_computation.21 | async-start | bytes 10485760 | tf_op jit(solution)/shard_map/reduce_scatter | solution.py:686
  715.7 608.5 %reduce-scatter.23.cloned.1.call-start = ((), (), s32[]{:S(2)}) async-start(), calls=%async_computation.25 | async-start | bytes 10485760 | tf_op jit(solution)/shard_map/reduce_scatter | solution.py:685
  716.3 614.3 %reduce-scatter.21.cloned.1.call-start = ((), (), s32[]{:S(2)}) async-start(), calls=%async_computation.24 | async-start | bytes 10485760 | tf_op jit(solution)/shard_map/reduce_scatter | solution.py:684
  764.2 100.2 %copy-start.61 = (f32[2,2,2,1024]{3,2,1,0:T(2,128)S(1)}, f32[2,2,2,1024]{3,2,1,0:T(2,128)}, u32[]{:S(2)}) copy-start(f32[2,2,2,1024]{3,2,1,0:T(2,128)} %get-tuple-element.102) | copy-start | bytes 98308
  764.2 100.2 %copy-start.62 = (f32[2,2,2,1024]{3,2,1,0:T(2,128)S(1)}, f32[2,2,2,1024]{3,2,1,0:T(2,128)}, u32[]{:S(2)}) copy-start(f32[2,2,2,1024]{3,2,1,0:T(2,128)} %get-tuple-element.103) | copy-start | bytes 98308
  764.2 116.3 %copy-start.23 = (f32[2048,32]{0,1:T(8,128)S(1)}, f32[2048,32]{0,1:T(8,128)}, u32[]{:S(2)}) copy-start(f32[2048,32]{0,1:T(8,128)} %copy-done.22) | copy-start | bytes 786436
  764.2 116.4 %copy-start.11 = (f32[2048,32]{0,1:T(8,128)S(1)}, f32[2048,32]{0,1:T(8,128)}, u32[]{:S(2)}) copy-start(f32[2048,32]{0,1:T(8,128)} %copy-done.10) | copy-start | bytes 786436
  906.8 102.2 %copy-start.49 = (f32[2048]{0:T(1024)S(1)}, f32[2048]{0:T(1024)}, u32[]{:S(2)}) copy-start(f32[2048]{0:T(1024)} %copy-done.48) | copy-start | bytes 24580
  906.8 102.2 %copy-start.60 = (f32[2048]{0:T(1024)S(1)}, f32[2048]{0:T(1024)}, u32[]{:S(2)}) copy-start(f32[2048]{0:T(1024)} %get-tuple-element.173) | copy-start | bytes 24580
  906.8 102.3 %copy-start.68 = (f32[256]{0:T(256)S(1)}, f32[256]{0:T(256)}, u32[]{:S(2)}) copy-start(f32[256]{0:T(256)} %param.18) | copy-start | bytes 3076
  1018.2 63.8 %copy-start.37 = (f32[2,1024]{1,0:T(2,128)S(1)}, f32[2,1024]{1,0:T(2,128)}, u32[]{:S(2)}) copy-start(f32[2,1024]{1,0:T(2,128)} %copy-done.36) | copy-start | bytes 24580
  1077.7 11.6 copy-start.8
  1077.7 37.8 %all-to-all-start.2 = ((bf16[8,128,256]{2,1,0:T(8,128)(2,1)}), bf16[8,128,256]{2,1,0:T(8,128)(2,1)}, u32[]{:S(2)}, u32[]{:S(2)}) async-start(bf16[8,128,256]{2,1,0:T(8,128)(2,1)} %bitcast.267), calls=%async_computation.7 | async-start | bytes 1048576 | tf_op jit(solution)/shard_map/all_to_all | solution.py:775
  1089.3 82.6 %copy-start.12 = (bf16[2,1024,1,128]{3,1,0,2:T(8,128)(2,1)}, bf16[2,1024,1,128]{3,1,0,2:T(8,128)(2,1)S(1)}, u32[]{:S(2)}) copy-start(bf16[2,1024,1,128]{3,1,0,2:T(8,128)(2,1)S(1)} %copy.185) | copy-start | bytes 1572868
  1094.8 5.0 copy-start.32
  1101.0 5.1 copy-start.55
  1101.1 5.5 copy-start.53
  1101.1 5.5 slice-start.2
  1111.7 8.9 copy-start.75
  1114.1 36.3 %copy-start.19 = (bf16[1,8,256,128]{3,2,1,0:T(8,128)(2,1)S(1)}, bf16[1,8,256,128]{3,2,1,0:T(8,128)(2,1)}, u32[]{:S(2)}) copy-start(bf16[1,8,256,128]{3,2,1,0:T(8,128)(2,1)} %copy-done.18) | copy-start | bytes 1572868
  1115.5 52.3 %all-to-all-start.1 = ((bf16[8,3,256,128]{3,2,1,0:T(8,128)(2,1)}), bf16[8,3,256,128]{3,2,1,0:T(8,128)(2,1)}, u32[]{:S(2)}, u32[]{:S(2)}) async-start(bf16[8,3,256,128]{3,2,1,0:T(8,128)(2,1)} %copy.191), calls=%async_computation.5 | async-start | bytes 3145728 | tf_op jit(solution)/shard_map/all_to_all | solution.py:769
  1120.5 215.6 %reduce-scatter.19.cloned.1.call-start = ((), (), s32[]{:S(2)}) async-start(), calls=%async_computation.23 | async-start | bytes 655360 | tf_op jit(solution)/shard_map/reduce_scatter | solution.py:783
  1150.1 187.7 %reduce-scatter.17.cloned.1.call-start = ((), (), s32[]{:S(2)}) async-start(), calls=%async_computation.22 | async-start | bytes 1966080 | tf_op jit(solution)/shard_map/reduce_scatter | solution.py:771
  1150.4 9.3 copy-start.17
  1150.4 9.3 copy-start.25
  1159.7 12.2 copy-start.15
  1187.3 103.5 %copy-start.9 = (f32[2048,128]{1,0:T(8,128)S(1)}, f32[2048,128]{1,0:T(8,128)}, u32[]{:S(2)}) copy-start(f32[2048,128]{1,0:T(8,128)} %get-tuple-element.178) | copy-start | bytes 3145732
  1187.3 118.7 %copy-start.59 = (f32[2048]{0:T(1024)S(1)}, f32[2048]{0:T(1024)}, u32[]{:S(2)}) copy-start(f32[2048]{0:T(1024)} %get-tuple-element.171) | copy-start | bytes 24580
  1187.3 118.7 %copy-start.70 = (f32[256]{0:T(256)S(1)}, f32[256]{0:T(256)}, u32[]{:S(2)}) copy-start(f32[256]{0:T(256)} %param.17) | copy-start | bytes 3076
  1187.4 103.5 %copy-start.13 = (bf16[2,1024,1,128]{3,1,0,2:T(8,128)(2,1)S(1)}, bf16[2,1024,1,128]{3,1,0,2:T(8,128)(2,1)}, u32[]{:S(2)}) copy-start(bf16[2,1024,1,128]{3,1,0,2:T(8,128)(2,1)} %copy-done.12) | copy-start | bytes 1572868
  1324.3 6.3 copy-start.35
  (34 other events, 101.6 us)
Sparse Core Ops, SparseCore 0:
  10.4 35.7 all-gather.7
  48.7 87.6 all-gather.9
  138.2 87.5 all-gather.11
  227.6 87.4 all-gather.13
  317.3 87.6 all-gather.15
  406.7 87.6 all-gather.17
  496.2 87.4 all-gather.19
  586.7 86.3 reduce-scatter.8
  676.5 86.4 reduce-scatter.10
  765.9 86.3 reduce-scatter.12
  855.6 86.3 reduce-scatter.14
  945.0 86.3 reduce-scatter.22
  1034.7 86.4 reduce-scatter.20
  1150.2 24.9 reduce-scatter.18
  1178.3 30.9 reduce-scatter.16

commit v3 on v1

--- a/solution.py
+++ b/solution.py
@@ -14,6 +14,7 @@
 F32 = jnp.float32
 BF16 = jnp.bfloat16
 VMEM_LIMIT = 60 * 1024 * 1024
+MESH = pl.DeviceIdType.MESH
 
 
 def inverse_rms(values):
@@ -104,15 +105,16 @@
         tok_o[0, 0, 1:2, :] += jnp.sum(jnp.where(hit, dots, 0.0), 0, keepdims=True)
 
 
-def expert_pass(counts, place, gate, hn, dy, wg, wu, wd, capacity):
-    experts, width, ff = wg.shape
+def expert_pass(counts, place, gate, hn, dy, wg, wu, wd, capacity, first):
+    experts = counts.shape[0]
+    _, width, ff = wg.shape
     micro, group, _ = hn.shape
     rows = min(256, capacity)
     blocks = capacity // rows
     tall = lambda e, g, i, c: (e, g, i, 0)
     line = lambda e, g, i, c: (e, g, 0, 0)
     whole = lambda e, g, i, c: (g, 0, 0)
-    matrix = lambda e, g, i, c: (e, 0, 0)
+    matrix = lambda e, g, i, c: (e + first, 0, 0)
     slots = lambda n: jax.ShapeDtypeStruct((experts, micro, capacity, n), BF16)
     sizes = (width, width, ff, ff, ff, width, width)
     flops = 2 * experts * micro * capacity * width * (6 * ff + 2 * group)
@@ -224,6 +226,702 @@
     )(place, *slots).reshape(micro * group, width)
 
 
+def places():
+    row, col = lax.axis_index("row"), lax.axis_index("col")
+    n_row, n_col = lax.axis_size("row"), lax.axis_size("col")
+    return row, col, n_row, n_col
+
+
+def remote(src, dst, send_sem, recv_sem, where):
+    return pltpu.make_async_remote_copy(
+        src_ref=src,
+        dst_ref=dst,
+        send_sem=send_sem,
+        recv_sem=recv_sem,
+        device_id=where,
+        device_id_type=MESH,
+    )
+
+
+def shake(sources, targets):
+    barrier = pltpu.get_barrier_semaphore()
+    for ok, where in sources:
+        if ok is True:
+            pl.semaphore_signal(barrier, inc=1, device_id=where, device_id_type=MESH)
+        else:
+
+            @pl.when(ok)
+            def _():
+                pl.semaphore_signal(barrier, inc=1, device_id=where, device_id_type=MESH)
+
+    count = 0
+    for ok in targets:
+        count = count + (1 if ok is True else jnp.where(ok, 1, 0))
+    pl.semaphore_wait(barrier, count)
+
+
+def line_peers():
+    row, col, n_row, n_col = places()
+    pair, core = col // 2, col % 2
+    return [
+        (True, (row, pair * 2 + 1 - core)),
+        (pair > 0, (row, (pair - 1) * 2 + core)),
+        (pair < n_col // 2 - 1, (row, (pair + 1) * 2 + core)),
+    ]
+
+
+def row_peers():
+    row, col, n_row, n_col = places()
+    return [(True, ((row + k) % n_row, col)) for k in range(1, n_row)]
+
+
+def col_slice(ref, index, size):
+    return ref.at[..., pl.ds(pl.multiple_of(index * size, size), size)]
+
+
+def line_gather(axes, ins, outs, sems):
+    own_sem, right_s, right_r, left_s, left_r, side_s, side_r = sems
+    n = len(ins)
+    row, col, n_row, n_col = places()
+    pairs, pair, core = n_col // 2, col // 2, col % 2
+
+    def at(pair_index, core_index):
+        return (row, pair_index * 2 + core_index)
+
+    def block(j, source):
+        size = ins[j].shape[axes[j]]
+        if axes[j] == 0:
+            return outs[j].at[pl.ds(pl.multiple_of(source * size, size), size)]
+        return col_slice(outs[j], source, size)
+
+    def right(j, s):
+        source = (pair - s) * 2 + core
+        src = ins[j] if s == 0 else block(j, source)
+        return remote(src, block(j, source), right_s.at[j, s], right_r.at[j, s], at(pair + 1, core))
+
+    def left(j, s):
+        source = (pair + s) * 2 + core
+        src = ins[j] if s == 0 else block(j, source)
+        return remote(src, block(j, source), left_s.at[j, s], left_r.at[j, s], at(pair - 1, core))
+
+    def side(j, source_pair, first=False):
+        source = source_pair * 2 + core
+        src = ins[j] if first else block(j, source)
+        return remote(
+            src,
+            block(j, source),
+            side_s.at[j, source_pair],
+            side_r.at[j, source_pair],
+            at(pair, 1 - core),
+        )
+
+    def arrived(j, recvs, slot, source):
+        remote(
+            ins[j], block(j, source), recvs.at[j, slot], recvs.at[j, slot], at(pair, 1 - core)
+        ).wait_recv()
+
+    def own(j):
+        return pltpu.make_async_copy(ins[j], block(j, col), own_sem.at[j])
+
+    def begin():
+        for j in range(n):
+
+            @pl.when(pair < pairs - 1)
+            def _():
+                right(j, 0).start()
+
+            @pl.when(pair > 0)
+            def _():
+                left(j, 0).start()
+
+        for j in range(n):
+            side(j, pair, True).start()
+            own(j).start()
+
+    def middle():
+        for s in range(1, pairs):
+            for j in range(n):
+
+                @pl.when(pair >= s)
+                def _():
+                    arrived(j, right_r, s - 1, (pair - s) * 2 + core)
+
+                    @pl.when(pair < pairs - 1)
+                    def _():
+                        right(j, s).start()
+
+                    side(j, pair - s).start()
+
+                @pl.when(pair + s < pairs)
+                def _():
+                    arrived(j, left_r, s - 1, (pair + s) * 2 + core)
+
+                    @pl.when(pair > 0)
+                    def _():
+                        left(j, s).start()
+
+                    side(j, pair + s).start()
+
+    def end():
+        for j in range(n):
+            own(j).wait()
+            for p in range(pairs):
+                side(j, p).wait_send()
+                arrived(j, side_r, p, p * 2 + 1 - core)
+            for s in range(pairs):
+
+                @pl.when((pair >= s) & (pair < pairs - 1))
+                def _():
+                    right(j, s).wait_send()
+
+                @pl.when((pair + s < pairs) & (pair > 0))
+                def _():
+                    left(j, s).wait_send()
+
+    return begin, middle, end
+
+
+def line_sems(n, pairs):
+    dma = pltpu.SemaphoreType.DMA
+    return [dma((n,))] + [dma((n, pairs))] * 6
+
+
+def front_body(
+    tokens, gains, cot, wq, wk, wv, wo, wr, wd, x_o, gains_o, dy_o, wh_o, wo_o, wr_o, wd_o, *sems
+):
+    line, (heads_s, heads_r, row_s, row_r, own_s, down_s, down_r) = sems[:7], sems[7:]
+    row, col, n_row, n_col = places()
+    head = wh_o.shape[2]
+    part = wq.shape[0]
+    per = wq.shape[1] // head
+    shared = wd.shape[2]
+    small = [(wo, wo_o), (wr, wr_o)]
+    begin, middle, end = line_gather(
+        (1, 1, 1), [tokens, gains, cot], [x_o, gains_o, dy_o], line
+    )
+
+    def heads_dst(m, source):
+        return wh_o.at[m, pl.ds(pl.multiple_of(source * part, part), part), :]
+
+    def heads(m, r, j):
+        src = (wq, wk, wv)[m].at[:, pl.ds(j * head, head)]
+        return remote(
+            src,
+            heads_dst(m, col),
+            heads_s.at[m, r * per + j],
+            heads_r.at[m, col],
+            (r, row * per + j),
+        )
+
+    def heads_own(m, j):
+        src = (wq, wk, wv)[m].at[:, pl.ds(j * head, head)]
+        return pltpu.make_async_copy(src, heads_dst(m, col), own_s.at[m])
+
+    def to_self(r, j):
+        return (row == r) & (col == row * per + j)
+
+    def heads_come(m, c):
+        return remote(
+            heads_dst(m, c), heads_dst(m, c), heads_r.at[m, c], heads_r.at[m, c], (row, col)
+        )
+
+    def from_self(c):
+        return (row == col // per) & (col == c)
+
+    def small_dst(k, source):
+        if k == 0:
+            return col_slice(wo_o, source, wo.shape[1])
+        size = wr.shape[0]
+        return wr_o.at[pl.ds(pl.multiple_of(source * size, size), size), :]
+
+    def small_copy(k, step):
+        return remote(
+            small[k][0],
+            small_dst(k, row),
+            row_s.at[k, step],
+            row_r.at[k, step],
+            ((row + step) % n_row, col),
+        )
+
+    def small_come(k, step):
+        source = (row + n_row - step) % n_row
+        return remote(
+            small[k][0], small_dst(k, source), row_s.at[k, step], row_r.at[k, step], (source, col)
+        )
+
+    def small_own(k):
+        return pltpu.make_async_copy(small[k][0], small_dst(k, row), own_s.at[3 + k])
+
+    couples = n_row // 2
+    couple, side = row // 2, row % 2
+
+    def down_to(where_row, slot):
+        return remote(
+            wd, col_slice(wd_o, row, shared), down_s.at[slot], down_r.at[slot], (where_row, col)
+        )
+
+    def down_come(source_row, slot):
+        return remote(
+            wd, col_slice(wd_o, source_row, shared), down_s.at[slot], down_r.at[slot], (row, col)
+        )
+
+    def down_own():
+        return pltpu.make_async_copy(wd, col_slice(wd_o, row, shared), own_s.at[5])
+
+    inner = couple * 2 + 1 - side
+
+    def outer(k):
+        return ((couple + k) % couples) * 2 + side
+
+    sources = line_peers() + row_peers()
+    targets = [ok for ok, _ in sources]
+    for c in range(n_col):
+        sources.append((jnp.logical_not(from_self(c)), (col // per, c)))
+    for r in range(n_row):
+        for j in range(per):
+            targets.append(jnp.logical_not(to_self(r, j)))
+    shake(sources, targets)
+    begin()
+    for k in range(2):
+        small_own(k).start()
+        for step in range(1, n_row):
+            small_copy(k, step).start()
+    for r in range(n_row):
+        for j in range(per):
+
+            @pl.when(to_self(r, j))
+            def _():
+                for m in range(3):
+                    heads_own(m, j).start()
+
+            @pl.when(jnp.logical_not(to_self(r, j)))
+            def _():
+                for m in range(3):
+                    heads(m, r, j).start()
+
+    down_to(inner, 0).start()
+    for k in range(1, couples):
+        down_to(outer(k), k).start()
+    down_own().start()
+    middle()
+    end()
+    for k in range(2):
+        small_own(k).wait()
+        for step in range(1, n_row):
+            small_copy(k, step).wait_send()
+            small_come(k, step).wait_recv()
+    for r in range(n_row):
+        for j in range(per):
+
+            @pl.when(to_self(r, j))
+            def _():
+                for m in range(3):
+                    heads_own(m, j).wait()
+
+            @pl.when(jnp.logical_not(to_self(r, j)))
+            def _():
+                for m in range(3):
+                    heads(m, r, j).wait_send()
+
+    for c in range(n_col):
+
+        @pl.when(jnp.logical_not(from_self(c)))
+        def _():
+            for m in range(3):
+                heads_come(m, c).wait_recv()
+
+    down_own().wait()
+    down_to(inner, 0).wait_send()
+    down_come(inner, 0).wait_recv()
+    for k in range(1, couples):
+        down_to(outer(k), k).wait_send()
+        down_come(((couple + couples - k) % couples) * 2 + side, k).wait_recv()
+
+
+ANY = pl.BlockSpec(memory_space=pl.ANY)
+
+
+def front(tokens, gains, cot, wq, wk, wv, wo, wr, wd, head, ident):
+    n_row, n_col = lax.axis_size("row"), lax.axis_size("col")
+    rows, part = tokens.shape
+    width = part * n_col
+    per = wq.shape[1] // head
+    local_exp, ff, shared = wd.shape
+    dma = pltpu.SemaphoreType.DMA
+    shapes = [
+        ((rows, width), BF16),
+        ((gains.shape[0], width), F32),
+        ((rows, width), BF16),
+        ((3, width, head), BF16),
+        ((wo.shape[0], wo.shape[1] * n_row), BF16),
+        ((wr.shape[0] * n_row, part), BF16),
+        ((local_exp, ff, width), BF16),
+    ]
+    return pl.pallas_call(
+        front_body,
+        in_specs=[ANY] * 9,
+        out_specs=[ANY] * 7,
+        out_shape=[jax.ShapeDtypeStruct(s, t) for s, t in shapes],
+        scratch_shapes=line_sems(3, n_col // 2)
+        + [
+            dma((3, n_row * per)),
+            dma((3, n_col)),
+            dma((2, n_row)),
+            dma((2, n_row)),
+            dma((6,)),
+            dma((n_row,)),
+            dma((n_row,)),
+        ],
+        compiler_params=pltpu.CompilerParams(collective_id=ident, has_side_effects=True),
+        cost_estimate=pl.CostEstimate(
+            flops=0, bytes_accessed=rows * width * 64, transcendentals=0
+        ),
+        name="front",
+    )(tokens, gains, cot, wq, wk, wv, wo, wr, wd)
+
+
+def middle_body(o, wo, wr, wd_in, o_o, wo_o, wr_o, wd_o, *sems):
+    line, (near_s, near_r, far_s, far_r) = sems[:7], sems[7:]
+    row, col, n_row, n_col = places()
+    begin, middle, end = line_gather((1, 0, 1), [o, wo, wr], [o_o, wo_o, wr_o], line)
+    couples = n_row // 2
+    couple, side = row // 2, row % 2
+    shared = wd_o.shape[2] // n_row
+    half = wd_o.shape[0] // 2
+    inner = couple * 2 + 1 - side
+
+    def piece(second, source_row):
+        return col_slice(wd_o.at[pl.ds(half if second else 0, half)], source_row, shared)
+
+    def near(k):
+        block = ((couple + k) % couples) * 2 + side
+        return remote(
+            piece(False, block), piece(False, block), near_s.at[k], near_r.at[k], (inner, col)
+        )
+
+    def near_come(k):
+        block = ((couple + k) % couples) * 2 + 1 - side
+        return remote(
+            piece(False, block), piece(False, block), near_s.at[k], near_r.at[k], (inner, col)
+        )
+
+    def far(k):
+        where = ((couple + k) % couples) * 2 + side
+        return remote(
+            piece(True, inner), piece(True, inner), far_s.at[k], far_r.at[k], (where, col)
+        )
+
+    def far_come(k):
+        source = (couple + couples - k) % couples
+        block = source * 2 + 1 - side
+        return remote(
+            piece(True, block), piece(True, block), far_s.at[k], far_r.at[k], (source * 2 + side, col)
+        )
+
+    sources = line_peers() + row_peers()
+    shake(sources, [ok for ok, _ in sources])
+    begin()
+    for k in range(1, couples):
+        near(k).start()
+        far(k).start()
+    middle()
+    end()
+    for k in range(1, couples):
+        near(k).wait_send()
+        near_come(k).wait_recv()
+        far(k).wait_send()
+        far_come(k).wait_recv()
+
+
+def middle_gather(o, wo, wr, wd, ident):
+    n_row, n_col = lax.axis_size("row"), lax.axis_size("col")
+    dma = pltpu.SemaphoreType.DMA
+    shapes = [
+        (o.shape[0], o.shape[1] * n_col),
+        (wo.shape[0] * n_col, wo.shape[1]),
+        (wr.shape[0], wr.shape[1] * n_col),
+        wd.shape,
+    ]
+    return pl.pallas_call(
+        middle_body,
+        in_specs=[ANY] * 4,
+        out_specs=[ANY] * 4,
+        out_shape=[jax.ShapeDtypeStruct(s, BF16) for s in shapes],
+        input_output_aliases={3: 3},
+        scratch_shapes=line_sems(3, n_col // 2) + [dma((n_row,))] * 4,
+        compiler_params=pltpu.CompilerParams(collective_id=ident, has_side_effects=True),
+        cost_estimate=pl.CostEstimate(
+            flops=0, bytes_accessed=o.shape[0] * o.shape[1] * n_col * 64, transcendentals=0
+        ),
+        name="middle_gather",
+    )(o, wo, wr, wd)
+
+
+def scatter_body(part, stage, *refs):
+    n_in = (1, 4, 4)[stage]
+    n_out = (1, 4, 4)[stage]
+    x, ins = refs[0], refs[1:n_in]
+    out, outs = refs[n_in], refs[n_in + 1 : n_in + n_out]
+    rest = refs[n_in + n_out :]
+    acc, side, from_left, from_right, load, side_s, side_r = rest[:7]
+    right_s, right_r, left_s, left_r = rest[7:11]
+    row, col, n_row, n_col = places()
+    pairs, pair, core = n_col // 2, col // 2, col % 2
+    couples, couple, inside = n_row // 2, row // 2, row % 2
+    inner = couple * 2 + 1 - inside
+    rows = out.shape[0]
+    cuts = load.shape[1]
+    height = rows // cuts
+    tile = min(256, height)
+
+    def at(pair_index, core_index):
+        return (row, pair_index * 2 + core_index)
+
+    def block(owner, q):
+        return x.at[
+            pl.ds(q * height, height), pl.ds(pl.multiple_of(owner * part, part), part)
+        ]
+
+    def cut(ref, d, q):
+        return ref.at[d, pl.ds(q * height, height)]
+
+    def fetch(d, q):
+        return pltpu.make_async_copy(block(d * 2 + core, q), cut(acc, d, q), load.at[d, q])
+
+    def across(d, q):
+        return remote(
+            block(d * 2 + 1 - core, q),
+            cut(side, d, q),
+            side_s.at[d, q],
+            side_r.at[d, q],
+            at(pair, 1 - core),
+        )
+
+    def right(d, q):
+        return remote(
+            cut(acc, d, q),
+            cut(from_left, d, q),
+            right_s.at[d, q],
+            right_r.at[d, q],
+            at(pair + 1, core),
+        )
+
+    def left(d, q):
+        return remote(
+            cut(acc, d, q),
+            cut(from_right, d, q),
+            left_s.at[d, q],
+            left_r.at[d, q],
+            at(pair - 1, core),
+        )
+
+    copies, arrivals, own = [], [], []
+    if stage:
+        small_s, small_r, step_s, step_r, own_s = rest[11:]
+        extra, extra_o = ins[0], outs[0]
+        for k in range(1, n_col):
+            where, source = (col + k) % n_col, (col + n_col - k) % n_col
+            copies.append(
+                remote(extra, extra_o.at[col], small_s.at[k], small_r.at[k], (row, where))
+            )
+            arrivals.append(
+                remote(extra, extra_o.at[source], small_s.at[k], small_r.at[k], (row, where))
+            )
+        own.append(pltpu.make_async_copy(extra, extra_o.at[col], own_s))
+    if stage == 1:
+        first, second = ins[1:]
+        near_o, far_o = outs[1:]
+        shared = first.shape[2] // n_row
+        for k in range(couples):
+            dst = near_o.at[k]
+            there = remote(
+                col_slice(first, k * 2 + 1 - inside, shared),
+                dst,
+                step_s.at[k],
+                step_r.at[k],
+                (inner, col),
+            )
+            copies.append(there)
+            arrivals.append(there)
+        for k in range(1, couples):
+            there = remote(
+                col_slice(second, (couple + k) % couples, 2 * shared),
+                far_o.at[k - 1],
+                step_s.at[couples + k],
+                step_r.at[couples + k],
+                (((couple + k) % couples) * 2 + inside, col),
+            )
+            copies.append(there)
+            arrivals.append(there)
+    if stage == 2:
+        first, second = ins[1:]
+        near_o, far_o = outs[1:]
+        for k in range(1, couples):
+            there = remote(
+                first.at[k - 1],
+                far_o.at[k - 1],
+                step_s.at[k],
+                step_r.at[k],
+                (((couple + k) % couples) * 2 + inside, col),
+            )
+            copies.append(there)
+            arrivals.append(there)
+        there = remote(second, near_o, step_s.at[0], step_r.at[0], (inner, col))
+        copies.append(there)
+        arrivals.append(there)
+
+    if stage:
+        peers = [(True, (row, (col + k) % n_col)) for k in range(1, n_col)] + row_peers()
+    else:
+        peers = line_peers()
+    shake(peers, [ok for ok, _ in peers])
+    order = []
+    for t in range(pairs):
+        for d in (pairs - 1 - t, t):
+            if d not in order:
+                order.append(d)
+    for d in order:
+        for q in range(cuts):
+            across(d, q).start()
+            fetch(d, q).start()
+    for c in copies + own:
+        c.start()
+
+    def add(q, into, *sources):
+        def step(i, _):
+            lines = pl.ds(pl.multiple_of(q * height + i * tile, tile), tile)
+            total = sources[0][lines, :].astype(F32)
+            for ref in sources[1:]:
+                total = total + ref[lines, :].astype(F32)
+            into[lines, :] = total.astype(into.dtype)
+            return 0
+
+        lax.fori_loop(0, height // tile, step, 0)
+
+    def ready(d, q):
+        fetch(d, q).wait()
+        across(d, q).wait_recv()
+
+    def go_right(d, q):
+        ready(d, q)
+
+        @pl.when(pair > 0)
+        def _():
+            right(d, q).wait_recv()
+            add(q, acc.at[d], acc.at[d], side.at[d], from_left.at[d])
+
+        @pl.when(pair == 0)
+        def _():
+            add(q, acc.at[d], acc.at[d], side.at[d])
+
+        right(d, q).start()
+
+    def go_left(d, q):
+        ready(d, q)
+
+        @pl.when(pair < pairs - 1)
+        def _():
+            left(d, q).wait_recv()
+            add(q, acc.at[d], acc.at[d], side.at[d], from_right.at[d])
+
+        @pl.when(pair == pairs - 1)
+        def _():
+            add(q, acc.at[d], acc.at[d], side.at[d])
+
+        left(d, q).start()
+
+    for t in range(pairs - 1):
+        far, near = pairs - 1 - t, t
+        for q in range(cuts):
+
+            @pl.when(far > pair)
+            def _():
+                go_right(far, q)
+
+            @pl.when(near < pair)
+            def _():
+                go_left(near, q)
+
+    for q in range(cuts):
+        ready(pair, q)
+
+        @pl.when(pair == 0)
+        def _():
+            left(pair, q).wait_recv()
+            add(q, out, acc.at[pair], side.at[pair], from_right.at[pair])
+
+        @pl.when(pair == pairs - 1)
+        def _():
+            right(pair, q).wait_recv()
+            add(q, out, acc.at[pair], side.at[pair], from_left.at[pair])
+
+        @pl.when((pair > 0) & (pair < pairs - 1))
+        def _():
+            left(pair, q).wait_recv()
+            right(pair, q).wait_recv()
+            add(q, out, acc.at[pair], side.at[pair], from_left.at[pair], from_right.at[pair])
+
+    for d in range(pairs):
+        for q in range(cuts):
+            across(d, q).wait_send()
+
+            @pl.when(pair < d)
+            def _():
+                right(d, q).wait_send()
+
+            @pl.when(pair > d)
+            def _():
+                left(d, q).wait_send()
+
+    for c in copies:
+        c.wait_send()
+    for c in arrivals:
+        c.wait_recv()
+    for c in own:
+        c.wait()
+
+
+def scatter_col(x, ident, stage=0, others=()):
+    n_row, n_col = lax.axis_size("row"), lax.axis_size("col")
+    pairs, couples = n_col // 2, n_row // 2
+    rows, part = x.shape[0], x.shape[1] // n_col
+    cuts = 4 if rows % 1024 == 0 else 1
+    dma = pltpu.SemaphoreType.DMA
+    buffer = pltpu.VMEM((pairs, rows, part), BF16)
+    scratch = [buffer] * 4 + [dma((pairs, cuts))] * 7
+    out_shape = [jax.ShapeDtypeStruct((rows, part), F32)]
+    if stage:
+        extra = others[0]
+        out_shape.append(jax.ShapeDtypeStruct((n_col,) + extra.shape, extra.dtype))
+        scratch += [dma((n_col,)), dma((n_col,)), dma((n_row + 2,)), dma((n_row + 2,)), dma(())]
+    if stage == 1:
+        half, ff, width = others[1].shape
+        shared = width // n_row
+        out_shape += [
+            jax.ShapeDtypeStruct((couples, half, ff, shared), BF16),
+            jax.ShapeDtypeStruct((couples - 1, half, ff, 2 * shared), BF16),
+        ]
+    if stage == 2:
+        out_shape += [
+            jax.ShapeDtypeStruct(others[2].shape, BF16),
+            jax.ShapeDtypeStruct(others[1].shape, BF16),
+        ]
+    return pl.pallas_call(
+        functools.partial(scatter_body, part, stage),
+        in_specs=[ANY] * (1 + len(others)),
+        out_specs=[pl.BlockSpec(memory_space=pltpu.VMEM)] + [ANY] * (len(out_shape) - 1),
+        out_shape=out_shape,
+        scratch_shapes=scratch,
+        compiler_params=pltpu.CompilerParams(
+            vmem_limit_bytes=VMEM_LIMIT, collective_id=ident, has_side_effects=True
+        ),
+        cost_estimate=pl.CostEstimate(
+            flops=0, bytes_accessed=rows * part * n_col * 40, transcendentals=0
+        ),
+        name="scatter_col",
+    )(x, *others)
+
+
 def shards(
     tokens,
     gain_attn,
@@ -267,26 +965,21 @@
 
     step = max(1, local_exp // 2)
     chunks = [slice(at, at + step) for at in range(0, local_exp, step)]
-    big = [
-        (
-            gather(w_gate[c], "row", 1),
-            gather(w_up[c], "row", 1),
-            gather(w_down[c], "row", 2),
-        )
-        for c in chunks
-    ]
-
-    inputs_low = gather(tokens, "col", 1)
-    packed = jnp.concatenate([w_query, w_key, w_value], 0)
-    packed = gather(packed, "row", 1).reshape(3, part, n_col, local_heads * head)
-    w_heads = lax.all_to_all(
-        packed.transpose(2, 0, 1, 3), "col", split_axis=0, concat_axis=0, tiled=True
-    )
-    w_heads = w_heads.transpose(1, 0, 2, 3).reshape(3, width, local_heads * head)
-    full_o = gather(gather(w_out, "row", 1), "col", 0)
-    full_r = gather(gather(w_router, "row", 1), "col", 0)
-    gains = gather(jnp.stack([gain_attn, gain_ffn]), "col", 1)
-    upstream_low = gather(cotangent, "col", 1)
+    full_g = gather(w_gate, "row", 1)
+    full_u = gather(w_up, "row", 1)
+    inputs_low, gains, upstream_low, w_heads, rows_o, rows_r, half_d = front(
+        tokens,
+        jnp.stack([gain_attn, gain_ffn]),
+        cotangent,
+        w_query,
+        w_key,
+        w_value,
+        w_out,
+        w_router.T,
+        w_down,
+        head,
+        0,
+    )
 
     segment, position, live = jax.vmap(lambda l: layout(l, group))(lengths)
     position = position.reshape(rows)
@@ -333,7 +1026,10 @@
     attended = jnp.einsum(
         "ghqk,gkhd->gqhd", probs_low, values_low, preferred_element_type=F32
     ).astype(BF16)
-    attended_full = gather(attended.reshape(rows, local_heads * head), "col", 1)
+    attended_full, full_o, full_rt, full_d = middle_gather(
+        attended.reshape(rows, local_heads * head), rows_o, rows_r, half_d, 1
+    )
+    full_r = full_rt.T
 
     hidden = inputs + nn(attended_full, full_o)
     scale_two = inverse_rms(hidden)
@@ -347,38 +1043,73 @@
     hn = normed_ffn.reshape(micro, group, width)
 
     outs, weight_grads = [], []
-    for c, (wg, wu, wd) in zip(chunks, big):
+    for c in chunks:
         xe, dyr, hg, dgp, dup, ye, dxe, tok = expert_pass(
-            counts[c], place_t[c], gate_t[c], hn, upstream_full, wg, wu, wd, capacity
+            counts[c],
+            place_t[c],
+            gate_t[c],
+            hn,
+            upstream_full,
+            full_g,
+            full_u,
+            full_d,
+            capacity,
+            c.start,
+        )
+        gg, gu, gd = expert_grads(xe, dgp, dup, hg, dyr)
+        hn, upstream_full, ye, dxe, tok, gg, gu, gd = lax.optimization_barrier(
+            (hn, upstream_full, ye, dxe, tok, gg, gu, gd)
         )
         outs.append((ye, dxe, tok))
-        gg, gu, gd = expert_grads(xe, dgp, dup, hg, dyr)
         weight_grads.append(
-            (
+            [
                 lax.psum_scatter(gg, "row", scatter_dimension=1, tiled=True),
                 lax.psum_scatter(gu, "row", scatter_dimension=1, tiled=True),
-                lax.psum_scatter(gd, "row", scatter_dimension=2, tiled=True),
-            )
-        )
-    grad_gate, grad_up, grad_down = (
-        jnp.concatenate([w[j] for w in weight_grads], 0).astype(F32) for j in range(3)
-    )
-    back_sum = lax.psum_scatter(
-        combine(place, [o[1] for o in outs]), "col", scatter_dimension=1, tiled=True
-    )
-    mixed_sum = lax.psum_scatter(
-        combine(place, [o[0] for o in outs]), "col", scatter_dimension=1, tiled=True
-    )
-    tok = jnp.concatenate([o[2] for o in outs], 0)
-    tok = gather(tok, "col", 0)
+                gd,
+            ]
+        )
+    def tie(value, c, j):
+        value, done = lax.optimization_barrier((value, weight_grads[c][j]))
+        weight_grads[c][j] = done
+        return value
+
+    row = lax.axis_index("row")
+    couples, couple, inside = n_row // 2, row // 2, row % 2
+    shared = w_down.shape[2]
+    own_tok = jnp.concatenate([o[2] for o in outs], 0)
+    back_sum, tok, near, far = scatter_col(
+        combine(place, [tie(o[1], 0, 0) if n == 0 else o[1] for n, o in enumerate(outs)]),
+        2,
+        1,
+        (own_tok, weight_grads[0][2], weight_grads[1][2]),
+    )
+    back_sum = tie(back_sum, 0, 1)
+
+    def down_block(value, block, size):
+        return lax.dynamic_slice_in_dim(value, block * size, size, 2).astype(F32)
+
+    down_first = [
+        down_block(weight_grads[0][2], ((couple + k) % couples) * 2 + inside, shared)
+        + lax.dynamic_index_in_dim(near, (couple + k) % couples, 0, False).astype(F32)
+        for k in range(couples)
+    ]
+    down_second = down_block(weight_grads[1][2], couple, 2 * shared) + jnp.sum(
+        far.astype(F32), 0
+    )
+    down_first_out = jnp.stack(down_first[1:]).astype(BF16)
+    down_second_out = lax.dynamic_slice_in_dim(
+        down_second, (1 - inside) * shared, shared, 2
+    ).astype(BF16)
+    down_second = lax.dynamic_slice_in_dim(down_second, inside * shared, shared, 2)
+    tok = tok.reshape((experts,) + tok.shape[2:])
+    hidden_part = tokens.astype(F32) + nn(attended_full, mine(full_o, 1))
     gate_dots = tok[:, :, 0].reshape(experts, rows).T
     hidden_part = mine(hidden, 1)
-    mixed = (hidden_part + mixed_sum.astype(F32)).astype(BF16)
 
     selected = gates * (gate_dots - jnp.sum(gates * gate_dots, -1, keepdims=True))
     logit_grad = selected.astype(BF16)
     router_part = mine(full_r, 0)
-    normed_grad = back_sum.astype(F32) + nt(logit_grad, router_part)
+    normed_grad = back_sum + nt(logit_grad, router_part)
     grad_router = tn(mine(normed_ffn, 1), logit_grad)
     scaled_two = hidden_part * scale_two
     grad_gain_ffn = jnp.sum(normed_grad * scaled_two, 0)
@@ -393,9 +1124,13 @@
     )
 
     branch_grad = hidden_grad.astype(BF16)
-    attended_grad = lax.psum_scatter(
-        nt(branch_grad, mine(full_o, 1)).astype(BF16), "col", scatter_dimension=1, tiled=True
-    ).reshape(batch)
+    (attended_grad,) = scatter_col(nt(branch_grad, mine(full_o, 1)).astype(BF16), 3)
+    attended_grad, mixed_slots = lax.optimization_barrier(
+        (attended_grad.astype(BF16).reshape(batch), [o[0] for o in outs])
+    )
+    mixed_sum = lax.psum_scatter(
+        combine(place, mixed_slots), "col", scatter_dimension=1, tiled=True
+    )
     grad_out = tn(attended_full, branch_grad)
     scores_again = scores_of()
     probs = jnp.exp(scores_again - log_total)
@@ -422,14 +1157,18 @@
         v.reshape(flat).astype(BF16) for v in (query_grad, key_grad, values_grad)
     ]
     back_heads = sum(nt(g, w_heads[j]) for j, g in enumerate(heads_grad))
-    normed_back = lax.psum_scatter(
-        back_heads.astype(BF16), "col", scatter_dimension=1, tiled=True
-    ).astype(F32)
     pre = (query_pre, key_pre, value_pre)
     dot_part = sum(jnp.sum(g.astype(F32) * p, -1) for g, p in zip(heads_grad, pre))
-    dot_one, gain_query_sum, gain_key_sum = lax.psum(
-        (dot_part, gain_query_part, gain_key_part), "col"
-    )
+    sums = jnp.concatenate([dot_part, gain_query_part, gain_key_part])
+    sums = jnp.pad(sums, (0, -sums.shape[0] % 1024)).reshape(-1, 128)
+    normed_back, sums, down_near, down_far = scatter_col(
+        back_heads.astype(BF16), 4, 2, (sums, down_first_out, down_second_out)
+    )
+    normed_back, mixed_sum = lax.optimization_barrier((normed_back, mixed_sum))
+    mixed = (hidden_part + mixed_sum.astype(F32)).astype(BF16)
+    sums = jnp.sum(sums, 0).reshape(-1)
+    dot_one = sums[:rows]
+    gain_query_sum, gain_key_sum = sums[rows : rows + head], sums[rows + head : rows + 2 * head]
     scale_one_part = scale_one
     inputs_part = tokens.astype(F32)
     grad_gain_attn = jnp.sum(normed_back * inputs_part * scale_one_part, 0)
@@ -439,6 +1178,17 @@
         - inputs_part * scale_one_part**2 * dot_one[:, None] / width
     )
 
+    grad_gate, grad_up = (
+        jnp.concatenate([w[j] for w in weight_grads], 0).astype(F32) for j in range(2)
+    )
+    grad_down = jnp.concatenate(
+        [
+            down_first[0] + jnp.sum(down_far.astype(F32), 0),
+            down_second + down_near.astype(F32),
+        ],
+        0,
+    )
+
     heads_weights = jnp.stack([tn(normed, g) for g in heads_grad]).astype(BF16)
     heads_weights = heads_weights.reshape(3, n_col, part, local_heads * head).transpose(1, 0, 2, 3)
     heads_weights = lax.all_to_all(heads_weights, "col", split_axis=0, concat_axis=0, tiled=True)
@@ -456,12 +1206,20 @@
     )
     out_weights = out_weights.transpose(1, 0, 2).reshape(local_heads * head, width)
     grad_out = lax.psum_scatter(out_weights, "row", scatter_dimension=1, tiled=True).astype(F32)
-    grad_router = lax.psum_scatter(
-        grad_router.astype(BF16), "row", scatter_dimension=1, tiled=True
-    ).astype(F32)
-    grad_gain_attn, grad_gain_ffn, grad_gain_query, grad_gain_key = lax.psum(
-        (grad_gain_attn, grad_gain_ffn, gain_query_sum, gain_key_sum), "row"
-    )
+    smalls = [
+        grad_gain_attn,
+        grad_gain_ffn,
+        gain_query_sum,
+        gain_key_sum,
+        grad_router.T.reshape(-1),
+    ]
+    total = lax.psum(jnp.concatenate(smalls).reshape(-1, 128), "row").reshape(-1)
+    grad_gain_attn, grad_gain_ffn = total[:part], total[part : 2 * part]
+    grad_gain_query = total[2 * part : 2 * part + head]
+    grad_gain_key = total[2 * part + head : 2 * part + 2 * head]
+    grad_router = lax.dynamic_slice_in_dim(
+        total[2 * part + 2 * head :].reshape(experts, part), row * (experts // n_row), experts // n_row, 0
+    ).T
     return (
         mixed,
         input_grad,

time: 1970 us -> 1400 us (0.71)
  waiting for transfers between devices: 1190 us -> 99.3 us
  Pallas kernels: 292 us -> 995 us
  blocking collectives: 198 us -> 16.8 us
    pallas_call x0 -> x5, Pallas kernels: none -> 701 us  [the longest x3 343 us: scatter_col(): pl.pallas_call(functools.partial(scatter_body, part, stage), in_specs=[AN...]
    all_gather x11 -> x2, waiting for transfers between devices: 551 us -> 61.3 us  [gather(): return lax.all_gather(value, axis_name, axis=axis, tiled=True)]
    reduce_scatter x5 -> x1, waiting for transfers between devices: 229 us -> 0.01 us  [shards(): lax.psum_scatter(combine(place, mixed_slots), 'col', scatter_dimension=1,...]
    reduce_scatter x2, waiting for transfers between devices: 173 us -> 0.01 us  [shards(): lax.psum_scatter(gg, 'row', scatter_dimension=1, tiled=True)]
    reduce_scatter x2, waiting for transfers between devices: 161 us -> 0.04 us  [shards(): lax.psum_scatter(gu, 'row', scatter_dimension=1, tiled=True)]
    all_gather x5 -> x0, blocking collectives: 155 us -> none  [gather(): return lax.all_gather(value, axis_name, axis=axis, tiled=True)]
    reduce_scatter x1, waiting for transfers between devices: 21.5 us -> 0.01 us  [shards(): lax.psum_scatter(out_weights, 'row', scatter_dimension=1, tiled=True)]
  transfers between devices with their start and end apart: 26 -> 11, of which waited for: 19 -> 2; matrix products, arithmetic and copies ran while one was open for 11% -> 16% of each run, Pallas kernels for 10% -> 64%
where the time goes in v3:
time: 1400 us; the launch traced here: 1390 us
  Pallas kernels  995 us (71%)
  matrix products  107 us (8%)
  waiting for transfers between devices  99.3 us (7%)
  other arithmetic  96.8 us (7%)
  local copies, waits for them, and re-layouts  46.7 us (3%)
  blocking collectives  16.8 us (1%)
  between operations  15.4 us (1%)
    pallas_call x3, Pallas kernels, scatter_col(): pl.pallas_call(functools.partial(scatter_body, part, stage), in_specs=[AN...  343 us
    pallas_call x1, Pallas kernels, front(): pl.pallas_call(front_body, in_specs=[ANY] * 9, out_specs=[ANY] * 7, out_s...  264 us
    pallas_call x2, Pallas kernels, expert_pass(): pl.pallas_call(expert_body, grid_spec=pltpu.PrefetchScalarGridSpec(num_sc...  174 us
    pallas_call x1, Pallas kernels, middle_gather(): pl.pallas_call(middle_body, in_specs=[ANY] * 4, out_specs=[ANY] * 4, out_...  93.7 us
    pallas_call x2, Pallas kernels, expert_grads(): pl.pallas_call(grads_body, grid=(experts, width // part), in_specs=[pl.Bl...  67.5 us
    all_gather x2, waiting for transfers between devices, gather(): return lax.all_gather(value, axis_name, axis=axis, tiled=True)  61.3 us
    pallas_call x2, Pallas kernels, combine(): pl.pallas_call(combine_body, grid=(micro, group // tile), in_specs=[pl.Bl...  52 us
    dot_general x5, matrix products, nt(): lax.dot_general(a, b, (((1,), (1,)), ((), ())), preferred_element_type=F32)  39.8 us
  transfers between devices with their start and end apart: 11, of which 2 were waited for; matrix products, arithmetic and copies ran while one was open for 16% of the time, Pallas kernels for 64%

profile of v3, /device:TPU:0, one launch (start us, length us, event | category | flops | bytes accessed | tf_op | source)
XLA Modules:
  0.0 1390.2 jit_solution(13362332624358107740)
XLA Ops:
  9.8 264.2 %front.1 = (bf16[2048,2048]{1,0:T(8,128)(2,1)}, f32[2,2048]{1,0:T(2,128)}, bf16[2048,2048]{1,0:T(8,128)(2,1)}, bf16[3,2048,128]{2,1,0:T(8,128)(2,1)}, bf16[128,2...) custom-call(bf16[2048,256]{1,0:T(8,128)(2,1)} %tokens.1, ...), custom_call_target="tpu_custom_call" | custom-call | bytes 268435456 | tf_op jit(solution)/shard_map/front/pallas_call | solution.py:560
  274.0 5.1 fusion
  279.8 8.9 fusion.2
  288.7 6.4 multiply_reduce_fusion.6
  295.8 2.9 multiply_reduce_fusion.7
  300.0 3.4 fusion.57
  303.9 1.4 copy.170
  306.3 2.9 fusion.122
  310.4 8.4 fusion.121
  319.7 1.5 fusion.29
  326.7 93.7 %middle_gather.1 = (bf16[2048,1024]{1,0:T(8,128)(2,1)}, bf16[1024,2048]{1,0:T(8,128)(2,1)}, bf16[32,2048]{1,0:T(8,128)(2,1)}, bf16[4,1024,2048]{2,1,0:T(8,128)(2,1)}) custom-call(bf16[2048,128]{1,0:T(8,128)(2,1)} %bitcast.296, bf16[128,2048]{1,0:T(8,128)(2,1)} %get-tuple-element.81.wo, ...), custom_call_target="tpu_custom_call", output_to_operand_aliasing={{3}: (3, {})} | custom-call | bytes 134217728 | tf_op jit(solution)/shard_map/middle_gather/pallas_call | solution.py:645
  420.4 15.0 %multiply_reduce_fusion = (f32[2048]{0:T(1024)S(1)}, f32[2048,2048]{1,0:T(8,128)S(1)}) fusion(bf16[2048,1024]{1,0:T(8,128)(2,1)} %get-tuple-element.84, bf16[1024,2048]{1,0:T(8,128)(2,1)} %get-tuple-element.85, bf16[2048,2048]{1,0:T(8,128)(2,1)} %get-tuple-element.78), kind=kOutput, calls=%fused_computation.8 | convolution fusion | flops 8606709760 | bytes 33562624 | tf_op jit(solution)/shard_map/dot_general | solution.py:50
  436.1 2.2 multiply_convert_fusion
  438.3 2.9 copy-done.8
  441.2 2.6 select_reduce_fusion
  447.3 7.4 broadcast_multiply_fusion
  454.7 61.3 %all-gather.5.cloned.1.call-done.wu = bf16[4,2048,1024]{2,1,0:T(8,128)(2,1)} async-done(((bf16[4,512,1024]{2,1,0:T(8,128)(2,1)}), bf16[4,2048,1024]{2,1,0:T(8,128)(2,1)}) %all-gather.5.cloned.1.call-update) | async-done | bytes 16777232 | tf_op jit(solution)/shard_map/all_gather | solution.py:960
  516.1 76.5 %expert_pass.2 = (bf16[2,2,512,2048]{3,2,1,0:T(8,128)(2,1)}, bf16[2,2,512,2048]{3,2,1,0:T(8,128)(2,1)}, bf16[2,2,512,1024]{3,2,1,0:T(8,128)(2,1)}, bf16[2,2,512,...) custom-call(s32[2,2]{1,0:T(2,128)} %get-tuple-element.188.counts, ...), custom_call_target="tpu_custom_call" | custom-call | flops 68719476736 | bytes 104857600 | tf_op jit(solution)/shard_map/expert_pass/pallas_call | solution.py:121
  592.6 33.3 %expert_grads.2 = (bf16[2,2048,1024]{2,1,0:T(8,128)(2,1)}, bf16[2,2048,1024]{2,1,0:T(8,128)(2,1)}, bf16[2,1024,2048]{2,1,0:T(8,128)(2,1)}) custom-call(bf16[2,1024,2048]{2,1,0:T(8,128)(2,1)} %bitcast.316, bf16[2,1024,1024]{2,1,0:T(8,128)(2,1)} %bitcast.322, bf16[2,1024,1024]{2,1,0:T(8,128)(2,1)} %bitcast.323, bf16[2,1024,1024]{2,1,0:T(8,128)(2,1)} %bitcast.321, ...), custom_call_target="tpu_custom_call" | custom-call | flops 25769803776 | bytes 54525952 | tf_op jit(solution)/shard_map/expert_grads/pallas_call | solution.py:162
  628.0 97.7 %expert_pass.3 = (bf16[2,2,512,2048]{3,2,1,0:T(8,128)(2,1)}, bf16[2,2,512,2048]{3,2,1,0:T(8,128)(2,1)}, bf16[2,2,512,1024]{3,2,1,0:T(8,128)(2,1)}, bf16[2,2,512,...) custom-call(s32[2,2]{1,0:T(2,128)} %get-tuple-element.187.counts, ...), custom_call_target="tpu_custom_call" | custom-call | flops 68719476736 | bytes 104857600 | tf_op jit(solution)/shard_map/expert_pass/pallas_call | solution.py:121
  725.7 34.2 %expert_grads.3 = (bf16[2,2048,1024]{2,1,0:T(8,128)(2,1)}, bf16[2,2048,1024]{2,1,0:T(8,128)(2,1)}, bf16[2,1024,2048]{2,1,0:T(8,128)(2,1)}) custom-call(bf16[2,1024,2048]{2,1,0:T(8,128)(2,1)} %bitcast.314, bf16[2,1024,1024]{2,1,0:T(8,128)(2,1)} %bitcast.319, bf16[2,1024,1024]{2,1,0:T(8,128)(2,1)} %bitcast.320, bf16[2,1024,1024]{2,1,0:T(8,128)(2,1)} %bitcast.318, ...), custom_call_target="tpu_custom_call" | custom-call | flops 25769803776 | bytes 54525952 | tf_op jit(solution)/shard_map/expert_grads/pallas_call | solution.py:162
  760.8 9.0 fusion.142
  769.8 12.3 copy.177
  782.8 26.1 %combine.2 = bf16[2,1024,2048]{2,1,0:T(8,128)(2,1)} custom-call(s32[2,1024,4]{2,1,0:T(8,128)} %copy-done.19, bf16[2,2,512,2048]{3,2,1,0:T(8,128)(2,1)} %get-tuple-element.102.refs_0_, bf16[2,2,512,2048]{3,2,1,0:T(8,128)(2,1)} %get-tuple-element.116.refs_1_), custom_call_target="tpu_custom_call" | custom-call | flops 17179869184 | bytes 25165824 | tf_op jit(solution)/shard_map/combine/pallas_call | solution.py:209
  808.9 182.9 %scatter_col.3 = (f32[2048,256]{1,0:T(8,128)}, f32[8,4,2,2,1024]{4,3,2,1,0:T(2,128)}, bf16[2,2,1024,512]{3,2,1,0:T(8,128)(2,1)}, bf16[1,2,1024,1024]{3,2,1,0:T(8,128)(2,1)}) custom-call(bf16[2048,2048]{1,0:T(8,128)(2,1)} %bitcast.264, f32[4,2,2,1024]{3,2,1,0:T(2,128)} %pad_maximum_fusion.7.refs_1_, bf16[2,1024,2048]{2,1,0:T(8,128)(2,1)} %get-tuple-element.119.refs_2_, ...), custom_call_target="tpu_custom_call" | custom-call | bytes 167772160 | tf_op jit(solution)/shard_map/scatter_col/pallas_call | solution.py:909
  991.8 2.4 slice_reduce_fusion
  994.5 3.2 multiply_reduce_fusion.2
  997.7 4.8 convolution_convert_fusion.refs_0_
  1002.5 47.4 %scatter_col.4 = f32[2048,128]{1,0:T(8,128)} custom-call(bf16[2048,1024]{1,0:T(8,128)(2,1)} %convolution_convert_fusion.refs_0_), custom_call_target="tpu_custom_call" | custom-call | bytes 83886080 | tf_op jit(solution)/shard_map/scatter_col/pallas_call | solution.py:909
  1049.9 1.3 convert_element_type.253
  1051.2 5.5 multiply_reduce_fusion.1
  1057.6 2.5 multiply_convert_fusion.1
  1060.1 1.5 fusion.24
  1064.8 1.6 fusion.30
  1066.7 4.3 convolution_convert_fusion.3
  1071.0 7.4 all-to-all-start.1
  1078.5 4.0 fusion.66
  1083.7 5.9 fusion.28
  1089.6 2.4 fusion.27
  1092.4 2.4 fusion.26
  1096.3 5.1 all-to-all-start
  1101.4 1.9 copy.180
  1103.4 35.8 %all-to-all-done = bf16[8,3,256,128]{3,2,1,0:T(8,128)(2,1)S(1)} async-done(((bf16[8,3,256,128]{3,2,1,0:T(8,128)(2,1)}), bf16[8,3,256,128]{3,2,1,0:T(8,128)(2,1)S(1)}, u32[]{:S(2)}, u32[]{:S(2)}) %all-to-all-start) | async-done | bytes 1572896 | tf_op jit(solution)/shard_map/all_to_all | solution.py:1194
  1140.2 1.6 copy.193
  1142.3 25.9 %combine.3 = bf16[2,1024,2048]{2,1,0:T(8,128)(2,1)} custom-call(s32[2,1024,4]{2,1,0:T(8,128)} %copy-done.19, bf16[2,2,512,2048]{3,2,1,0:T(8,128)(2,1)} %get-tuple-element.131.refs_0_, bf16[2,2,512,2048]{3,2,1,0:T(8,128)(2,1)} %get-tuple-element.132.refs_1_), custom_call_target="tpu_custom_call" | custom-call | flops 17179869184 | bytes 25165824 | tf_op jit(solution)/shard_map/combine/pallas_call | solution.py:209
  1168.3 1.6 convolution_bitcast_fusion
  1171.0 5.5 convert_add_fusion.1
  1176.5 1.7 dynamic-slice_convert_fusion.refs_3_
  1178.2 3.7 copy-done.20
  1181.9 3.7 fusion.13.refs_2_
  1185.6 8.1 fusion.72
  1193.7 8.1 fusion.70
  1201.8 15.6 %add_convert_fusion.refs_0_ = bf16[2048,2048]{1,0:T(8,128)(2,1)} fusion(f32[2048,2048]{1,0:T(8,128)} %fusion.72, f32[2048,2048]{1,0:T(8,128)} %fusion.70, bf16[2048,128]{1,0:T(8,128)(2,1)S(1)} %bitcast.279, bf16[3,2048,128]{2,1,0:T(8,128)(2,1)S(1)} %copy-done.12), kind=kOutput, calls=%fused_computation.6 | convolution fusion | flops 1086324736 | bytes 42991616 | tf_op jit(solution)/shard_map/dot_general | solution.py:54
  1217.4 113.1 %scatter_col.5 = (f32[2048,256]{1,0:T(8,128)}, f32[8,24,128]{2,1,0:T(8,128)}, bf16[2,1024,512]{2,1,0:T(8,128)(2,1)}, bf16[1,2,1024,512]{3,2,1,0:T(8,128)(2,1)}) custom-call(bf16[2048,2048]{1,0:T(8,128)(2,1)} %add_convert_fusion.refs_0_, f32[24,128]{1,0:T(8,128)} %fusion.102.refs_1_, bf16[1,2,1024,512]{3,2,1,0:T(8,128)(2,1)} %fusion.13.refs_2_, ...), custom_call_target="tpu_custom_call" | custom-call | bytes 167772160 | tf_op jit(solution)/shard_map/scatter_col/pallas_call | solution.py:909
  1331.5 3.8 convert_add_fusion.5
  1336.2 2.4 convert_add_fusion.2
  1338.6 4.4 pad_maximum_fusion
  1343.1 5.5 maximum_convert_fusion
  1348.6 6.3 maximum_convert_fusion.1
  1355.0 1.6 convert_element_type.281
  1356.6 1.9 slice_convert_fusion
  1358.6 3.2 fusion.12
  1361.8 16.8 %psum.7 = f32[70,128]{1,0:T(8,128)S(1)} all-reduce(f32[70,128]{1,0:T(8,128)S(1)} %bitcast.306), channel_id=1, replica_groups=mesh['row'=4,'col'=8] {'row'}, use_global_device_ids=true, to_apply=%region_30.31 | all-reduce | flops 8960 | bytes 71680 | tf_op jit(solution)/shard_map/psum | solution.py:1216
  1379.7 3.1 add_convert_fusion.1
  (257 shorter events, 35.4 us)
Async XLA Ops:
  7.2 447.5 %all-gather.3.cloned.1.call-start = ((), (), s32[]{:S(2)}) async-start(), calls=%async_computation.9 | async-start | bytes 20971520 | tf_op jit(solution)/shard_map/all_gather | solution.py:960
  7.9 508.1 %all-gather.5.cloned.1.call-start = ((), (), s32[]{:S(2)}) async-start(), calls=%async_computation.10 | async-start | bytes 20971520 | tf_op jit(solution)/shard_map/all_gather | solution.py:960
  8.7 774.1 %reduce-scatter.8.cloned.1.call-start = ((), (), s32[]{:S(2)}) async-start(), calls=%async_computation.11 | async-start | bytes 10485760 | tf_op jit(solution)/shard_map/reduce_scatter | solution.py:1066
  9.2 290.8 %copy-start.46 = (f32[1,8,2,128]{3,1,2,0:T(8,128)}, f32[1,8,2,128]{3,1,2,0:T(8,128)S(1)}, u32[]{:S(2)}) copy-start(f32[1,8,2,128]{3,1,2,0:T(8,128)S(1)} %copy.195) | copy-start | bytes 24580
  274.0 25.9 %copy-start.69 = (f32[64]{0:T(128)}, f32[64]{0:T(128)S(1)}, u32[]{:S(2)}) copy-start(f32[64]{0:T(128)S(1)} %multiply_exponential_fusion) | copy-start | bytes 772
  274.0 5.7 copy-start.60
  279.7 8.9 copy-start.36
  279.8 8.9 copy-start.44
  279.8 8.9 copy-start.11
  288.7 7.1 copy-start
  295.2 4.1 copy-start.6
  295.8 3.9 copy-start.62
  298.7 4.6 copy-start.40
  303.6 5.6 copy-start.24
  303.9 5.3 copy-start.26
  305.3 3.9 copy-start.28
  309.2 9.7 copy-start.1
  310.4 8.5 copy-start.34
  435.4 5.8 copy-start.8
  436.1 5.1 copy-start.56
  436.1 5.1 copy-start.39
  625.9 368.4 %reduce-scatter.10.cloned.1.call-start = ((), (), s32[]{:S(2)}) async-start(), calls=%async_computation.12 | async-start | bytes 10485760 | tf_op jit(solution)/shard_map/reduce_scatter | solution.py:1067
  626.5 716.6 %reduce-scatter.18.cloned.1.call-start = ((), (), s32[]{:S(2)}) async-start(), calls=%async_computation.16 | async-start | bytes 10485760 | tf_op jit(solution)/shard_map/reduce_scatter | solution.py:1066
  760.0 588.6 %reduce-scatter.20.cloned.1.call-start = ((), (), s32[]{:S(2)}) async-start(), calls=%async_computation.17 | async-start | bytes 10485760 | tf_op jit(solution)/shard_map/reduce_scatter | solution.py:1067
  769.8 12.4 copy-start.58
  769.8 12.4 copy-start.59
  808.9 185.4 %copy-start.23 = (f32[2048,32]{0,1:T(8,128)S(1)}, f32[2048,32]{0,1:T(8,128)}, u32[]{:S(2)}) copy-start(f32[2048,32]{0,1:T(8,128)} %copy-done.22) | copy-start | bytes 786436
  808.9 185.4 %copy-start.17 = (f32[2048,32]{0,1:T(8,128)S(1)}, f32[2048,32]{0,1:T(8,128)}, u32[]{:S(2)}) copy-start(f32[2048,32]{0,1:T(8,128)} %copy-done.16) | copy-start | bytes 786436
  808.9 185.5 %copy-start.33 = (bf16[2048,256]{1,0:T(8,128)(2,1)S(1)}, bf16[2048,256]{1,0:T(8,128)(2,1)}, u32[]{:S(2)}) copy-start(bf16[2048,256]{1,0:T(8,128)(2,1)} %cot.1) | copy-start | bytes 3145732
  808.9 185.5 %copy-start.57 = (f32[2048]{0:T(1024)S(1)}, f32[2048]{0:T(1024)}, u32[]{:S(2)}) copy-start(f32[2048]{0:T(1024)} %copy-done.56) | copy-start | bytes 24580
  808.9 185.5 %copy-start.61 = (f32[2048]{0:T(1024)S(1)}, f32[2048]{0:T(1024)}, u32[]{:S(2)}) copy-start(f32[2048]{0:T(1024)} %get-tuple-element.185) | copy-start | bytes 24580
  808.9 185.5 %copy-start.72 = (f32[256]{0:T(256)S(1)}, f32[256]{0:T(256)}, u32[]{:S(2)}) copy-start(f32[256]{0:T(256)} %param.18) | copy-start | bytes 3076
  997.6 69.0 %copy-start.9 = (f32[2048,256]{1,0:T(8,128)}, f32[2048,256]{1,0:T(8,128)S(1)}, u32[]{:S(2)}) copy-start(f32[2048,256]{1,0:T(8,128)S(1)} %get-tuple-element.155) | copy-start | bytes 6291460
  1002.5 48.8 %copy-start.14 = (bf16[2048,128]{1,0:T(8,128)(2,1)S(1)}, bf16[2048,128]{1,0:T(8,128)(2,1)}, u32[]{:S(2)}) copy-start(bf16[2048,128]{1,0:T(8,128)(2,1)} %copy-done.13) | copy-start | bytes 1572868
  1002.5 48.8 %copy-start.35 = (f32[2,1024]{1,0:T(2,128)S(1)}, f32[2,1024]{1,0:T(2,128)}, u32[]{:S(2)}) copy-start(f32[2,1024]{1,0:T(2,128)} %copy-done.34) | copy-start | bytes 24580
  1051.2 5.5 slice-start
  1051.2 6.4 slice-start.1
  1066.7 11.8 copy-start.47
  1066.7 11.8 copy-start.70
  1071.0 11.5 copy-start.5
  1071.0 11.5 copy-start.41
  1071.0 11.5 copy-start.65
  1071.0 11.9 copy-start.7
  1071.0 11.9 copy-start.43
  1071.0 11.9 copy-start.63
  1071.0 25.2 %all-to-all-start.1 = ((bf16[8,128,256]{2,1,0:T(8,128)(2,1)}), bf16[8,128,256]{2,1,0:T(8,128)(2,1)}, u32[]{:S(2)}, u32[]{:S(2)}) async-start(bf16[8,128,256]{2,1,0:T(8,128)(2,1)} %bitcast.82), calls=%async_computation.5 | async-start | bytes 1048576 | tf_op jit(solution)/shard_map/all_to_all | solution.py:1200
  1078.5 4.8 copy-start.51
  1082.5 7.1 slice-start.2
  1083.7 5.9 slice-start.3
  1096.3 42.9 %all-to-all-start = ((bf16[8,3,256,128]{3,2,1,0:T(8,128)(2,1)}), bf16[8,3,256,128]{3,2,1,0:T(8,128)(2,1)S(1)}, u32[]{:S(2)}, u32[]{:S(2)}) async-start(bf16[8,3,256,128]{3,2,1,0:T(8,128)(2,1)} %copy.154), calls=%async_computation.3 | async-start | bytes 3145728 | tf_op jit(solution)/shard_map/all_to_all | solution.py:1194
  1101.4 253.6 %reduce-scatter.16.cloned.1.call-start = ((), (), s32[]{:S(2)}) async-start(), calls=%async_computation.15 | async-start | bytes 655360 | tf_op jit(solution)/shard_map/reduce_scatter | solution.py:1208
  1103.3 253.2 %reduce-scatter.14.cloned.1.call-start = ((), (), s32[]{:S(2)}) async-start(), calls=%async_computation.14 | async-start | bytes 1966080 | tf_op jit(solution)/shard_map/reduce_scatter | solution.py:1196
  1141.9 216.7 %reduce-scatter.12.cloned.1.call-start = ((), (), s32[]{:S(2)}) async-start(), calls=%async_computation.13 | async-start | bytes 9437184 | tf_op jit(solution)/shard_map/reduce_scatter | solution.py:1131
  1176.5 9.1 copy-start.3
  1176.5 5.4 copy-start.20
  1178.2 7.4 copy-start.12
  1331.5 4.0 copy-start.21
  1331.5 4.7 copy-start.32
  1338.6 4.4 copy-start.31
  1348.6 9.9 copy-start.10
  1348.6 9.9 copy-start.18
  1348.6 9.9 copy-start.38
  1348.6 9.9 copy-start.55
  1348.6 9.9 copy-start.67
  (24 other events, 40.6 us)
Sparse Core Ops, SparseCore 0:
  9.9 302.5 all-gather.2
  314.4 201.6 all-gather.4
  626.0 106.8 reduce-scatter.7
  736.1 86.4 reduce-scatter.9
  825.5 154.1 reduce-scatter.17
  983.0 86.5 reduce-scatter.19
  1105.0 26.4 reduce-scatter.15
  1142.0 30.0 reduce-scatter.13
  1174.5 129.2 reduce-scatter.11

commit v4 on v3

--- a/solution.py
+++ b/solution.py
@@ -58,162 +58,186 @@
     return lax.dot_general(a, b, (((0,), (0,)), ((), ())), preferred_element_type=F32)
 
 
-def expert_body(
-    counts, place, gate, hn, dy, wg, wu, wd, xe_o, dyr_o, hg_o, dgp_o, dup_o, ye_o, dxe_o, tok_o
-):
-    e, g, i = pl.program_id(0), pl.program_id(1), pl.program_id(2)
-    rows = xe_o.shape[2]
+def expert_body(shared, counts, place, gate, hn, dy, w, xe_o, dyr_o, hg_o, dgp_o, dup_o, ye_o, dxe_o, tok_o):
+    g, i = pl.program_id(0), pl.program_id(1)
+    rows = xe_o.shape[1]
+    width, ff = w.shape[1:]
     base = i * rows
 
     @pl.when(i == 0)
     def _():
         tok_o[...] = jnp.zeros_like(tok_o)
 
-    @pl.when(counts[e, g] <= base)
+    @pl.when(counts[g] <= base)
     def _():
         for ref in (xe_o, dyr_o, hg_o, dgp_o, dup_o, ye_o, dxe_o):
             ref[...] = jnp.zeros_like(ref)
 
-    @pl.when(counts[e, g] > base)
+    @pl.when(counts[g] > base)
     def _():
-        slot = lax.broadcasted_iota(jnp.int32, (rows, place.shape[3]), 0) + base
-        hit = slot == place[0, 0]
+        slot = lax.broadcasted_iota(jnp.int32, (rows, place.shape[2]), 0) + base
+        hit = slot == place[0]
         pick = jnp.where(hit, 1.0, 0.0).astype(BF16)
-        weight = jnp.sum(jnp.where(hit, gate[0, 0], 0.0), 1, keepdims=True)
+        weight = jnp.sum(jnp.where(hit, gate[0], 0.0), 1, keepdims=True)
         xe = nn(pick, hn[0]).astype(BF16)
-        xe_o[0, 0] = xe
-        gp = nn(xe, wg[0])
-        up = nn(xe, wu[0])
+        xe_o[0] = xe
+        gp = nn(xe, w[0])
+        up = nn(xe, w[1])
         sig = jax.nn.sigmoid(gp)
         silu = gp * sig
         hid = silu * up
         hg = (hid * weight).astype(BF16)
-        hg_o[0, 0] = hg
-        ye_o[0, 0] = nn(hg, wd[0]).astype(BF16)
+        hg_o[0] = hg
         dyr = nn(pick, dy[0]).astype(BF16)
-        dyr_o[0, 0] = dyr
-        back = nt(dyr, wd[0])
+        dyr_o[0] = dyr
+        parts = []
+        for r in range(width // shared):
+            at = r * shared
+            total = None
+            for b in range(ff // shared):
+                low = b * shared
+                term = nn(hg[:, low : low + shared], w[2, at : at + shared, low : low + shared])
+                total = term if total is None else total + term
+            ye_o[0, :, at : at + shared] = total.astype(BF16)
+        for b in range(ff // shared):
+            low = b * shared
+            total = None
+            for r in range(width // shared):
+                at = r * shared
+                term = nt(dyr[:, at : at + shared], w[2, at : at + shared, low : low + shared])
+                total = term if total is None else total + term
+            parts.append(total)
+        back = jnp.concatenate(parts, 1)
         dgate = jnp.sum(back * hid, 1, keepdims=True)
         dhid = back * weight
         dgp = (dhid * up * sig * (1.0 + gp * (1.0 - sig))).astype(BF16)
         dup = (dhid * silu).astype(BF16)
-        dgp_o[0, 0] = dgp
-        dup_o[0, 0] = dup
+        dgp_o[0] = dgp
+        dup_o[0] = dup
         dots = jnp.sum(dgp.astype(F32) * gp + dup.astype(F32) * up, 1, keepdims=True)
-        dxe_o[0, 0] = (nt(dgp, wg[0]) + nt(dup, wu[0])).astype(BF16)
-        tok_o[0, 0, 0:1, :] += jnp.sum(jnp.where(hit, dgate, 0.0), 0, keepdims=True)
-        tok_o[0, 0, 1:2, :] += jnp.sum(jnp.where(hit, dots, 0.0), 0, keepdims=True)
-
-
-def expert_pass(counts, place, gate, hn, dy, wg, wu, wd, capacity, first):
-    experts = counts.shape[0]
-    _, width, ff = wg.shape
+        dxe_o[0] = (nt(dgp, w[0]) + nt(dup, w[1])).astype(BF16)
+        tok_o[0, 0:1, :] += jnp.sum(jnp.where(hit, dgate, 0.0), 0, keepdims=True)
+        tok_o[0, 1:2, :] += jnp.sum(jnp.where(hit, dots, 0.0), 0, keepdims=True)
+
+
+def expert_pass(counts, place, gate, hn, dy, w, capacity, shared):
+    _, width, ff = w.shape
     micro, group, _ = hn.shape
     rows = min(256, capacity)
     blocks = capacity // rows
-    tall = lambda e, g, i, c: (e, g, i, 0)
-    line = lambda e, g, i, c: (e, g, 0, 0)
-    whole = lambda e, g, i, c: (g, 0, 0)
-    matrix = lambda e, g, i, c: (e + first, 0, 0)
-    slots = lambda n: jax.ShapeDtypeStruct((experts, micro, capacity, n), BF16)
+    tall = lambda g, i, c: (g, i, 0)
+    line = lambda g, i, c: (g, 0, 0)
+    slots = lambda n: jax.ShapeDtypeStruct((micro, capacity, n), BF16)
     sizes = (width, width, ff, ff, ff, width, width)
-    flops = 2 * experts * micro * capacity * width * (6 * ff + 2 * group)
+    flops = 2 * micro * capacity * width * (6 * ff + 2 * group)
     return pl.pallas_call(
-        expert_body,
+        functools.partial(expert_body, shared),
         grid_spec=pltpu.PrefetchScalarGridSpec(
             num_scalar_prefetch=1,
-            grid=(experts, micro, blocks),
+            grid=(micro, blocks),
             in_specs=[
-                pl.BlockSpec((1, 1, 1, group), line),
-                pl.BlockSpec((1, 1, 1, group), line),
-                pl.BlockSpec((1, group, width), whole, pipeline_mode=pl.Buffered(1)),
-                pl.BlockSpec((1, group, width), whole, pipeline_mode=pl.Buffered(1)),
-                pl.BlockSpec((1, width, ff), matrix),
-                pl.BlockSpec((1, width, ff), matrix),
-                pl.BlockSpec((1, ff, width), matrix),
+                pl.BlockSpec((1, 1, group), line),
+                pl.BlockSpec((1, 1, group), line),
+                pl.BlockSpec((1, group, width), line),
+                pl.BlockSpec((1, group, width), line),
+                pl.BlockSpec((3, width, ff), lambda g, i, c: (0, 0, 0), pipeline_mode=pl.Buffered(1)),
             ],
-            out_specs=[pl.BlockSpec((1, 1, rows, n), tall) for n in sizes]
-            + [pl.BlockSpec((1, 1, 2, group), line)],
+            out_specs=[pl.BlockSpec((1, rows, n), tall) for n in sizes]
+            + [pl.BlockSpec((1, 2, group), line)],
         ),
-        out_shape=[slots(n) for n in sizes]
-        + [jax.ShapeDtypeStruct((experts, micro, 2, group), F32)],
+        out_shape=[slots(n) for n in sizes] + [jax.ShapeDtypeStruct((micro, 2, group), F32)],
         compiler_params=pltpu.CompilerParams(vmem_limit_bytes=VMEM_LIMIT),
         cost_estimate=pl.CostEstimate(
-            flops=flops, bytes_accessed=100 << 20, transcendentals=experts * micro * capacity * ff
+            flops=flops, bytes_accessed=40 << 20, transcendentals=micro * capacity * ff
         ),
         name="expert_pass",
-    )(counts, place, gate, hn, dy, wg, wu, wd)
-
-
-def grads_body(xe, dgp, dup, hg, dyr, gg_o, gu_o, gd_o):
-    part = xe[0]
-    gg_o[0] = tn(part, dgp[0]).astype(BF16)
-    gu_o[0] = tn(part, dup[0]).astype(BF16)
-    gd_o[0] = tn(hg[0], dyr[0]).astype(BF16)
-
-
-def expert_grads(xe, dgp, dup, hg, dyr):
-    experts, micro, capacity, width = xe.shape
-    ff = dgp.shape[3]
+    )(counts, place, gate, hn, dy, w)
+
+
+def grads_body(xe, dgp, dup, hg, dyr, out):
+    part = xe[...]
+    shared = part.shape[1]
+    out[0] = tn(part, dgp[...]).astype(BF16)
+    out[1] = tn(part, dup[...]).astype(BF16)
+    back = dyr[...]
+    for b in range(hg.shape[1] // shared):
+        low = b * shared
+        out[2, :, low : low + shared] = tn(hg[:, low : low + shared], back).astype(BF16)
+
+
+def expert_grads(xe, dgp, dup, hg, dyr, shared):
+    micro, capacity, width = xe.shape
+    ff = dgp.shape[2]
     rows = micro * capacity
-    xe, dyr = (a.reshape(experts, rows, width) for a in (xe, dyr))
-    dgp, dup, hg = (a.reshape(experts, rows, ff) for a in (dgp, dup, hg))
-    part = min(512, width)
+    xe, dyr = (a.reshape(rows, width) for a in (xe, dyr))
+    dgp, dup, hg = (a.reshape(rows, ff) for a in (dgp, dup, hg))
+    thin = pl.BlockSpec((rows, shared), lambda r: (0, r))
+    whole = pl.BlockSpec((rows, ff), lambda r: (0, 0))
     return pl.pallas_call(
         grads_body,
-        grid=(experts, width // part),
-        in_specs=[
-            pl.BlockSpec((1, rows, part), lambda e, r: (e, 0, r)),
-            pl.BlockSpec((1, rows, ff), lambda e, r: (e, 0, 0)),
-            pl.BlockSpec((1, rows, ff), lambda e, r: (e, 0, 0)),
-            pl.BlockSpec((1, rows, ff), lambda e, r: (e, 0, 0)),
-            pl.BlockSpec((1, rows, part), lambda e, r: (e, 0, r)),
-        ],
-        out_specs=[
-            pl.BlockSpec((1, part, ff), lambda e, r: (e, r, 0)),
-            pl.BlockSpec((1, part, ff), lambda e, r: (e, r, 0)),
-            pl.BlockSpec((1, ff, part), lambda e, r: (e, 0, r)),
-        ],
-        out_shape=[
-            jax.ShapeDtypeStruct((experts, width, ff), BF16),
-            jax.ShapeDtypeStruct((experts, width, ff), BF16),
-            jax.ShapeDtypeStruct((experts, ff, width), BF16),
-        ],
+        grid=(width // shared,),
+        in_specs=[thin, whole, whole, whole, thin],
+        out_specs=pl.BlockSpec((3, shared, ff), lambda r: (0, r, 0)),
+        out_shape=jax.ShapeDtypeStruct((3, width, ff), BF16),
         compiler_params=pltpu.CompilerParams(vmem_limit_bytes=VMEM_LIMIT),
         cost_estimate=pl.CostEstimate(
-            flops=6 * experts * rows * width * ff, bytes_accessed=experts * 26 << 20, transcendentals=0
+            flops=6 * rows * width * ff, bytes_accessed=26 << 20, transcendentals=0
         ),
         name="expert_grads",
     )(xe, dgp, dup, hg, dyr)
 
 
+def pack_body(wg, wu, wd, *rest):
+    outs, sem = rest[:-1], rest[-1]
+    shared, ff = wg.shape[1:]
+    copies = []
+    for e, out in enumerate(outs):
+        moves = [(wg.at[e], out.at[0]), (wu.at[e], out.at[1])]
+        for b in range(ff // shared):
+            low = b * shared
+            moves.append((wd.at[e, pl.ds(low, shared)], out.at[2, :, pl.ds(low, shared)]))
+        for m, (src, dst) in enumerate(moves):
+            copies.append(pltpu.make_async_copy(src, dst, sem.at[e, m]))
+    for c in copies:
+        c.start()
+    for c in copies:
+        c.wait()
+
+
+def pack(wg, wu, wd):
+    experts, shared, ff = wg.shape
+    return pl.pallas_call(
+        pack_body,
+        in_specs=[pl.BlockSpec(memory_space=pl.ANY)] * 3,
+        out_specs=[pl.BlockSpec(memory_space=pl.ANY)] * experts,
+        out_shape=[jax.ShapeDtypeStruct((3, shared, ff), BF16)] * experts,
+        scratch_shapes=[pltpu.SemaphoreType.DMA((experts, 2 + ff // shared))],
+        cost_estimate=pl.CostEstimate(
+            flops=0, bytes_accessed=experts * 6 * shared * ff * 2, transcendentals=0
+        ),
+        name="pack",
+    )(wg, wu, wd)
+
+
 def combine_body(place, *refs):
     out = refs[-1]
-    slots = refs[:-1]
     total = jnp.zeros((out.shape[1], out.shape[2]), F32)
-    at = 0
-    for ref in slots:
-        capacity = ref.shape[2]
-        for e in range(ref.shape[0]):
-            slot = lax.broadcasted_iota(jnp.int32, (out.shape[1], capacity), 1)
-            pick = jnp.where(slot == place[0, :, at : at + 1], 1.0, 0.0).astype(BF16)
-            total = total + nn(pick, ref[e, 0])
-            at += 1
+    for e, ref in enumerate(refs[:-1]):
+        slot = lax.broadcasted_iota(jnp.int32, (out.shape[1], ref.shape[1]), 1)
+        pick = jnp.where(slot == place[0, :, e : e + 1], 1.0, 0.0).astype(BF16)
+        total = total + nn(pick, ref[0])
     out[0] = total.astype(BF16)
 
 
 def combine(place, slots):
     micro, group, local = place.shape
-    capacity, width = slots[0].shape[2:]
+    capacity, width = slots[0].shape[1:]
     tile = min(256, group)
     return pl.pallas_call(
         combine_body,
         grid=(micro, group // tile),
         in_specs=[pl.BlockSpec((1, tile, local), lambda g, i: (g, i, 0))]
-        + [
-            pl.BlockSpec((s.shape[0], 1, capacity, width), lambda g, i: (0, g, 0, 0))
-            for s in slots
-        ],
+        + [pl.BlockSpec((1, capacity, width), lambda g, i: (g, 0, 0)) for s in slots],
         out_specs=pl.BlockSpec((1, tile, width), lambda g, i: (g, i, 0)),
         out_shape=jax.ShapeDtypeStruct((micro, group, width), BF16),
         compiler_params=pltpu.CompilerParams(vmem_limit_bytes=VMEM_LIMIT),
@@ -386,19 +410,14 @@
     return [dma((n,))] + [dma((n, pairs))] * 6
 
 
-def front_body(
-    tokens, gains, cot, wq, wk, wv, wo, wr, wd, x_o, gains_o, dy_o, wh_o, wo_o, wr_o, wd_o, *sems
-):
-    line, (heads_s, heads_r, row_s, row_r, own_s, down_s, down_r) = sems[:7], sems[7:]
+def front_body(tokens, gains, wq, wk, wv, wo, wr, x_o, gains_o, wh_o, wo_o, wr_o, *sems):
+    line, (heads_s, heads_r, row_s, row_r, own_s) = sems[:7], sems[7:]
     row, col, n_row, n_col = places()
     head = wh_o.shape[2]
     part = wq.shape[0]
     per = wq.shape[1] // head
-    shared = wd.shape[2]
     small = [(wo, wo_o), (wr, wr_o)]
-    begin, middle, end = line_gather(
-        (1, 1, 1), [tokens, gains, cot], [x_o, gains_o, dy_o], line
-    )
+    begin, middle, end = line_gather((1, 1), [tokens, gains], [x_o, gains_o], line)
 
     def heads_dst(m, source):
         return wh_o.at[m, pl.ds(pl.multiple_of(source * part, part), part), :]
@@ -451,27 +470,6 @@
 
     def small_own(k):
         return pltpu.make_async_copy(small[k][0], small_dst(k, row), own_s.at[3 + k])
-
-    couples = n_row // 2
-    couple, side = row // 2, row % 2
-
-    def down_to(where_row, slot):
-        return remote(
-            wd, col_slice(wd_o, row, shared), down_s.at[slot], down_r.at[slot], (where_row, col)
-        )
-
-    def down_come(source_row, slot):
-        return remote(
-            wd, col_slice(wd_o, source_row, shared), down_s.at[slot], down_r.at[slot], (row, col)
-        )
-
-    def down_own():
-        return pltpu.make_async_copy(wd, col_slice(wd_o, row, shared), own_s.at[5])
-
-    inner = couple * 2 + 1 - side
-
-    def outer(k):
-        return ((couple + k) % couples) * 2 + side
 
     sources = line_peers() + row_peers()
     targets = [ok for ok, _ in sources]
@@ -499,10 +497,6 @@
                 for m in range(3):
                     heads(m, r, j).start()
 
-    down_to(inner, 0).start()
-    for k in range(1, couples):
-        down_to(outer(k), k).start()
-    down_own().start()
     middle()
     end()
     for k in range(2):
@@ -530,136 +524,77 @@
             for m in range(3):
                 heads_come(m, c).wait_recv()
 
-    down_own().wait()
-    down_to(inner, 0).wait_send()
-    down_come(inner, 0).wait_recv()
-    for k in range(1, couples):
-        down_to(outer(k), k).wait_send()
-        down_come(((couple + couples - k) % couples) * 2 + side, k).wait_recv()
-
 
 ANY = pl.BlockSpec(memory_space=pl.ANY)
 
 
-def front(tokens, gains, cot, wq, wk, wv, wo, wr, wd, head, ident):
+def front(tokens, gains, wq, wk, wv, wo, wr, head, ident):
     n_row, n_col = lax.axis_size("row"), lax.axis_size("col")
     rows, part = tokens.shape
     width = part * n_col
     per = wq.shape[1] // head
-    local_exp, ff, shared = wd.shape
     dma = pltpu.SemaphoreType.DMA
     shapes = [
         ((rows, width), BF16),
         ((gains.shape[0], width), F32),
-        ((rows, width), BF16),
         ((3, width, head), BF16),
         ((wo.shape[0], wo.shape[1] * n_row), BF16),
         ((wr.shape[0] * n_row, part), BF16),
-        ((local_exp, ff, width), BF16),
     ]
     return pl.pallas_call(
         front_body,
-        in_specs=[ANY] * 9,
-        out_specs=[ANY] * 7,
+        in_specs=[ANY] * 7,
+        out_specs=[ANY] * 5,
         out_shape=[jax.ShapeDtypeStruct(s, t) for s, t in shapes],
-        scratch_shapes=line_sems(3, n_col // 2)
+        scratch_shapes=line_sems(2, n_col // 2)
         + [
             dma((3, n_row * per)),
             dma((3, n_col)),
             dma((2, n_row)),
             dma((2, n_row)),
             dma((6,)),
-            dma((n_row,)),
-            dma((n_row,)),
         ],
         compiler_params=pltpu.CompilerParams(collective_id=ident, has_side_effects=True),
         cost_estimate=pl.CostEstimate(
-            flops=0, bytes_accessed=rows * width * 64, transcendentals=0
+            flops=0, bytes_accessed=rows * width * 32, transcendentals=0
         ),
         name="front",
-    )(tokens, gains, cot, wq, wk, wv, wo, wr, wd)
-
-
-def middle_body(o, wo, wr, wd_in, o_o, wo_o, wr_o, wd_o, *sems):
-    line, (near_s, near_r, far_s, far_r) = sems[:7], sems[7:]
-    row, col, n_row, n_col = places()
-    begin, middle, end = line_gather((1, 0, 1), [o, wo, wr], [o_o, wo_o, wr_o], line)
-    couples = n_row // 2
-    couple, side = row // 2, row % 2
-    shared = wd_o.shape[2] // n_row
-    half = wd_o.shape[0] // 2
-    inner = couple * 2 + 1 - side
-
-    def piece(second, source_row):
-        return col_slice(wd_o.at[pl.ds(half if second else 0, half)], source_row, shared)
-
-    def near(k):
-        block = ((couple + k) % couples) * 2 + side
-        return remote(
-            piece(False, block), piece(False, block), near_s.at[k], near_r.at[k], (inner, col)
-        )
-
-    def near_come(k):
-        block = ((couple + k) % couples) * 2 + 1 - side
-        return remote(
-            piece(False, block), piece(False, block), near_s.at[k], near_r.at[k], (inner, col)
-        )
-
-    def far(k):
-        where = ((couple + k) % couples) * 2 + side
-        return remote(
-            piece(True, inner), piece(True, inner), far_s.at[k], far_r.at[k], (where, col)
-        )
-
-    def far_come(k):
-        source = (couple + couples - k) % couples
-        block = source * 2 + 1 - side
-        return remote(
-            piece(True, block), piece(True, block), far_s.at[k], far_r.at[k], (source * 2 + side, col)
-        )
-
-    sources = line_peers() + row_peers()
+    )(tokens, gains, wq, wk, wv, wo, wr)
+
+
+def middle_body(axes, *refs):
+    n = len(axes)
+    begin, middle, end = line_gather(axes, refs[:n], refs[n : 2 * n], refs[2 * n :])
+    sources = line_peers()
     shake(sources, [ok for ok, _ in sources])
     begin()
-    for k in range(1, couples):
-        near(k).start()
-        far(k).start()
     middle()
     end()
-    for k in range(1, couples):
-        near(k).wait_send()
-        near_come(k).wait_recv()
-        far(k).wait_send()
-        far_come(k).wait_recv()
-
-
-def middle_gather(o, wo, wr, wd, ident):
-    n_row, n_col = lax.axis_size("row"), lax.axis_size("col")
-    dma = pltpu.SemaphoreType.DMA
+
+
+def middle_gather(arrays, axes, ident):
+    n_col, n = lax.axis_size("col"), len(arrays)
     shapes = [
-        (o.shape[0], o.shape[1] * n_col),
-        (wo.shape[0] * n_col, wo.shape[1]),
-        (wr.shape[0], wr.shape[1] * n_col),
-        wd.shape,
+        tuple(d * n_col if at == axis else d for at, d in enumerate(a.shape))
+        for a, axis in zip(arrays, axes)
     ]
     return pl.pallas_call(
-        middle_body,
-        in_specs=[ANY] * 4,
-        out_specs=[ANY] * 4,
-        out_shape=[jax.ShapeDtypeStruct(s, BF16) for s in shapes],
-        input_output_aliases={3: 3},
-        scratch_shapes=line_sems(3, n_col // 2) + [dma((n_row,))] * 4,
+        functools.partial(middle_body, axes),
+        in_specs=[ANY] * n,
+        out_specs=[ANY] * n,
+        out_shape=[jax.ShapeDtypeStruct(s, a.dtype) for s, a in zip(shapes, arrays)],
+        scratch_shapes=line_sems(n, n_col // 2),
         compiler_params=pltpu.CompilerParams(collective_id=ident, has_side_effects=True),
         cost_estimate=pl.CostEstimate(
-            flops=0, bytes_accessed=o.shape[0] * o.shape[1] * n_col * 64, transcendentals=0
+            flops=0, bytes_accessed=sum(math.prod(s) for s in shapes) * 32, transcendentals=0
         ),
         name="middle_gather",
-    )(o, wo, wr, wd)
+    )(*arrays)
 
 
 def scatter_body(part, stage, *refs):
-    n_in = (1, 4, 4)[stage]
-    n_out = (1, 4, 4)[stage]
+    n_in = (1, 2, 4)[stage]
+    n_out = (1, 2, 4)[stage]
     x, ins = refs[0], refs[1:n_in]
     out, outs = refs[n_in], refs[n_in + 1 : n_in + n_out]
     rest = refs[n_in + n_out :]
@@ -667,8 +602,6 @@
     right_s, right_r, left_s, left_r = rest[7:11]
     row, col, n_row, n_col = places()
     pairs, pair, core = n_col // 2, col // 2, col % 2
-    couples, couple, inside = n_row // 2, row // 2, row % 2
-    inner = couple * 2 + 1 - inside
     rows = out.shape[0]
     cuts = load.shape[1]
     height = rows // cuts
@@ -717,7 +650,7 @@
 
     copies, arrivals, own = [], [], []
     if stage:
-        small_s, small_r, step_s, step_r, own_s = rest[11:]
+        small_s, small_r, own_s = rest[11:14]
         extra, extra_o = ins[0], outs[0]
         for k in range(1, n_col):
             where, source = (col + k) % n_col, (col + n_col - k) % n_col
@@ -728,53 +661,63 @@
                 remote(extra, extra_o.at[source], small_s.at[k], small_r.at[k], (row, where))
             )
         own.append(pltpu.make_async_copy(extra, extra_o.at[col], own_s))
-    if stage == 1:
-        first, second = ins[1:]
-        near_o, far_o = outs[1:]
-        shared = first.shape[2] // n_row
-        for k in range(couples):
-            dst = near_o.at[k]
-            there = remote(
-                col_slice(first, k * 2 + 1 - inside, shared),
-                dst,
-                step_s.at[k],
-                step_r.at[k],
-                (inner, col),
-            )
-            copies.append(there)
-            arrivals.append(there)
-        for k in range(1, couples):
-            there = remote(
-                col_slice(second, (couple + k) % couples, 2 * shared),
-                far_o.at[k - 1],
-                step_s.at[couples + k],
-                step_r.at[couples + k],
-                (((couple + k) % couples) * 2 + inside, col),
-            )
-            copies.append(there)
-            arrivals.append(there)
+    guarded = []
     if stage == 2:
-        first, second = ins[1:]
-        near_o, far_o = outs[1:]
-        for k in range(1, couples):
-            there = remote(
-                first.at[k - 1],
-                far_o.at[k - 1],
-                step_s.at[k],
-                step_r.at[k],
-                (((couple + k) % couples) * 2 + inside, col),
-            )
-            copies.append(there)
-            arrivals.append(there)
-        there = remote(second, near_o, step_s.at[0], step_r.at[0], (inner, col))
-        copies.append(there)
-        arrivals.append(there)
-
+        give_s, give_r, keep_s = rest[14:]
+        per = n_col // n_row
+        heads, branch = ins[1:]
+        heads_o, branch_o = outs[1:]
+        part_h = heads.shape[1] // n_col
+        rows_b = branch.shape[0] // n_col
+        target = col // per
+        for k in range(n_col):
+            pieces = [
+                (heads.at[:, pl.ds(k * part_h, part_h), :], heads_o.at[row, col % per]),
+                (branch.at[pl.ds(k * rows_b, rows_b), :], branch_o.at[row, col % per]),
+            ]
+            self_here = (row == target) & (col == k)
+            for m, (src, dst) in enumerate(pieces):
+                guarded.append(
+                    (
+                        self_here,
+                        pltpu.make_async_copy(src, dst, keep_s.at[m]),
+                        remote(
+                            src, dst, give_s.at[m, k], give_r.at[m, row * per + col % per], (target, k)
+                        ),
+                    )
+                )
+        takes = []
+        for r in range(n_row):
+            for j in range(per):
+                mine_here = (row == r) & (col == row * per + j)
+                for m, (ref, src) in enumerate(
+                    ((heads_o, heads.at[:, pl.ds(0, part_h), :]), (branch_o, branch.at[pl.ds(0, rows_b), :]))
+                ):
+                    takes.append(
+                        (
+                            jnp.logical_not(mine_here),
+                            remote(
+                                src,
+                                ref.at[r, j],
+                                give_s.at[m, 0],
+                                give_r.at[m, r * per + j],
+                                (r, row * per + j),
+                            ),
+                        )
+                    )
     if stage:
-        peers = [(True, (row, (col + k) % n_col)) for k in range(1, n_col)] + row_peers()
+        peers = [(True, (row, (col + k) % n_col)) for k in range(1, n_col)]
     else:
         peers = line_peers()
-    shake(peers, [ok for ok, _ in peers])
+    targets = [ok for ok, _ in peers]
+    if stage == 2:
+        for r in range(n_row):
+            for j in range(per):
+                here = (row == r) & (col == row * per + j)
+                peers.append((jnp.logical_not(here), (r, row * per + j)))
+        for k in range(n_col):
+            targets.append(jnp.logical_not((row == target) & (col == k)))
+    shake(peers, targets)
     order = []
     for t in range(pairs):
         for d in (pairs - 1 - t, t):
@@ -786,6 +729,15 @@
             fetch(d, q).start()
     for c in copies + own:
         c.start()
+    for here, keep, give in guarded:
+
+        @pl.when(here)
+        def _():
+            keep.start()
+
+        @pl.when(jnp.logical_not(here))
+        def _():
+            give.start()
 
     def add(q, into, *sources):
         def step(i, _):
@@ -879,11 +831,27 @@
         c.wait_recv()
     for c in own:
         c.wait()
+    for here, keep, give in guarded:
+
+        @pl.when(here)
+        def _():
+            keep.wait()
+
+        @pl.when(jnp.logical_not(here))
+        def _():
+            give.wait_send()
+
+    if stage == 2:
+        for away, take in takes:
+
+            @pl.when(away)
+            def _():
+                take.wait_recv()
 
 
 def scatter_col(x, ident, stage=0, others=()):
     n_row, n_col = lax.axis_size("row"), lax.axis_size("col")
-    pairs, couples = n_col // 2, n_row // 2
+    pairs, per = n_col // 2, n_col // n_row
     rows, part = x.shape[0], x.shape[1] // n_col
     cuts = 4 if rows % 1024 == 0 else 1
     dma = pltpu.SemaphoreType.DMA
@@ -893,18 +861,13 @@
     if stage:
         extra = others[0]
         out_shape.append(jax.ShapeDtypeStruct((n_col,) + extra.shape, extra.dtype))
-        scratch += [dma((n_col,)), dma((n_col,)), dma((n_row + 2,)), dma((n_row + 2,)), dma(())]
-    if stage == 1:
-        half, ff, width = others[1].shape
-        shared = width // n_row
+        scratch += [dma((n_col,)), dma((n_col,)), dma(())]
+    if stage == 2:
+        heads, branch = others[1:]
+        scratch += [dma((2, n_col)), dma((2, n_row * per)), dma((2,))]
         out_shape += [
-            jax.ShapeDtypeStruct((couples, half, ff, shared), BF16),
-            jax.ShapeDtypeStruct((couples - 1, half, ff, 2 * shared), BF16),
-        ]
-    if stage == 2:
-        out_shape += [
-            jax.ShapeDtypeStruct(others[2].shape, BF16),
-            jax.ShapeDtypeStruct(others[1].shape, BF16),
+            jax.ShapeDtypeStruct((n_row, per, 3, heads.shape[1] // n_col, heads.shape[2]), BF16),
+            jax.ShapeDtypeStruct((n_row, per, branch.shape[0] // n_col, branch.shape[1]), BF16),
         ]
     return pl.pallas_call(
         functools.partial(scatter_body, part, stage),
@@ -963,20 +926,16 @@
         size = value.shape[axis] // n_col
         return lax.dynamic_slice_in_dim(value, col * size, size, axis)
 
-    step = max(1, local_exp // 2)
-    chunks = [slice(at, at + step) for at in range(0, local_exp, step)]
-    full_g = gather(w_gate, "row", 1)
-    full_u = gather(w_up, "row", 1)
-    inputs_low, gains, upstream_low, w_heads, rows_o, rows_r, half_d = front(
+    shared = w_down.shape[2]
+    big = [gather(w, "row", 1) for w in pack(w_gate, w_up, w_down)]
+    inputs_low, gains, w_heads, rows_o, rows_r = front(
         tokens,
         jnp.stack([gain_attn, gain_ffn]),
-        cotangent,
         w_query,
         w_key,
         w_value,
         w_out,
         w_router.T,
-        w_down,
         head,
         0,
     )
@@ -1026,8 +985,8 @@
     attended = jnp.einsum(
         "ghqk,gkhd->gqhd", probs_low, values_low, preferred_element_type=F32
     ).astype(BF16)
-    attended_full, full_o, full_rt, full_d = middle_gather(
-        attended.reshape(rows, local_heads * head), rows_o, rows_r, half_d, 1
+    attended_full, full_o, full_rt, upstream_low = middle_gather(
+        [attended.reshape(rows, local_heads * head), rows_o, rows_r, cotangent], (1, 0, 1, 1), 1
     )
     full_r = full_rt.T
 
@@ -1043,64 +1002,26 @@
     hn = normed_ffn.reshape(micro, group, width)
 
     outs, weight_grads = [], []
-    for c in chunks:
+    for e in range(local_exp):
         xe, dyr, hg, dgp, dup, ye, dxe, tok = expert_pass(
-            counts[c],
-            place_t[c],
-            gate_t[c],
-            hn,
-            upstream_full,
-            full_g,
-            full_u,
-            full_d,
-            capacity,
-            c.start,
+            counts[e], place_t[e], gate_t[e], hn, upstream_full, big[e], capacity, shared
         )
-        gg, gu, gd = expert_grads(xe, dgp, dup, hg, dyr)
-        hn, upstream_full, ye, dxe, tok, gg, gu, gd = lax.optimization_barrier(
-            (hn, upstream_full, ye, dxe, tok, gg, gu, gd)
+        grad = expert_grads(xe, dgp, dup, hg, dyr, shared)
+        hn, upstream_full, ye, dxe, tok, grad = lax.optimization_barrier(
+            (hn, upstream_full, ye, dxe, tok, grad)
         )
         outs.append((ye, dxe, tok))
-        weight_grads.append(
-            [
-                lax.psum_scatter(gg, "row", scatter_dimension=1, tiled=True),
-                lax.psum_scatter(gu, "row", scatter_dimension=1, tiled=True),
-                gd,
-            ]
-        )
-    def tie(value, c, j):
-        value, done = lax.optimization_barrier((value, weight_grads[c][j]))
-        weight_grads[c][j] = done
+        weight_grads.append(lax.psum_scatter(grad, "row", scatter_dimension=1, tiled=True))
+
+    def tie(value, e):
+        value, weight_grads[e] = lax.optimization_barrier((value, weight_grads[e]))
         return value
 
     row = lax.axis_index("row")
-    couples, couple, inside = n_row // 2, row // 2, row % 2
-    shared = w_down.shape[2]
-    own_tok = jnp.concatenate([o[2] for o in outs], 0)
-    back_sum, tok, near, far = scatter_col(
-        combine(place, [tie(o[1], 0, 0) if n == 0 else o[1] for n, o in enumerate(outs)]),
-        2,
-        1,
-        (own_tok, weight_grads[0][2], weight_grads[1][2]),
-    )
-    back_sum = tie(back_sum, 0, 1)
-
-    def down_block(value, block, size):
-        return lax.dynamic_slice_in_dim(value, block * size, size, 2).astype(F32)
-
-    down_first = [
-        down_block(weight_grads[0][2], ((couple + k) % couples) * 2 + inside, shared)
-        + lax.dynamic_index_in_dim(near, (couple + k) % couples, 0, False).astype(F32)
-        for k in range(couples)
-    ]
-    down_second = down_block(weight_grads[1][2], couple, 2 * shared) + jnp.sum(
-        far.astype(F32), 0
-    )
-    down_first_out = jnp.stack(down_first[1:]).astype(BF16)
-    down_second_out = lax.dynamic_slice_in_dim(
-        down_second, (1 - inside) * shared, shared, 2
-    ).astype(BF16)
-    down_second = lax.dynamic_slice_in_dim(down_second, inside * shared, shared, 2)
+    back_sum, tok = scatter_col(
+        combine(place, [o[1] for o in outs]), 2, 1, (jnp.stack([o[2] for o in outs]),)
+    )
+    back_sum = tie(back_sum, 0)
     tok = tok.reshape((experts,) + tok.shape[2:])
     hidden_part = tokens.astype(F32) + nn(attended_full, mine(full_o, 1))
     gate_dots = tok[:, :, 0].reshape(experts, rows).T
@@ -1125,12 +1046,7 @@
 
     branch_grad = hidden_grad.astype(BF16)
     (attended_grad,) = scatter_col(nt(branch_grad, mine(full_o, 1)).astype(BF16), 3)
-    attended_grad, mixed_slots = lax.optimization_barrier(
-        (attended_grad.astype(BF16).reshape(batch), [o[0] for o in outs])
-    )
-    mixed_sum = lax.psum_scatter(
-        combine(place, mixed_slots), "col", scatter_dimension=1, tiled=True
-    )
+    attended_grad = attended_grad.astype(BF16).reshape(batch)
     grad_out = tn(attended_full, branch_grad)
     scores_again = scores_of()
     probs = jnp.exp(scores_again - log_total)
@@ -1161,11 +1077,16 @@
     dot_part = sum(jnp.sum(g.astype(F32) * p, -1) for g, p in zip(heads_grad, pre))
     sums = jnp.concatenate([dot_part, gain_query_part, gain_key_part])
     sums = jnp.pad(sums, (0, -sums.shape[0] % 1024)).reshape(-1, 128)
-    normed_back, sums, down_near, down_far = scatter_col(
-        back_heads.astype(BF16), 4, 2, (sums, down_first_out, down_second_out)
-    )
-    normed_back, mixed_sum = lax.optimization_barrier((normed_back, mixed_sum))
-    mixed = (hidden_part + mixed_sum.astype(F32)).astype(BF16)
+    heads_weights = jnp.stack([tn(normed, g) for g in heads_grad]).astype(BF16)
+    back_heads, mixed_slots = lax.optimization_barrier(
+        (back_heads.astype(BF16), [o[0] for o in outs])
+    )
+    (mixed_sum,) = scatter_col(combine(place, mixed_slots), 4)
+    mixed = (hidden_part + mixed_sum).astype(BF16)
+    back_heads, mixed = lax.optimization_barrier((back_heads, mixed))
+    normed_back, sums, heads_terms, out_terms = scatter_col(
+        tie(back_heads, 1), 5, 2, (sums, heads_weights, grad_out.astype(BF16))
+    )
     sums = jnp.sum(sums, 0).reshape(-1)
     dot_one = sums[:rows]
     gain_query_sum, gain_key_sum = sums[rows : rows + head], sums[rows + head : rows + 2 * head]
@@ -1178,34 +1099,18 @@
         - inputs_part * scale_one_part**2 * dot_one[:, None] / width
     )
 
-    grad_gate, grad_up = (
-        jnp.concatenate([w[j] for w in weight_grads], 0).astype(F32) for j in range(2)
-    )
+    weight_grads = jnp.stack(weight_grads, 1).astype(F32)
+    grad_gate, grad_up = weight_grads[0], weight_grads[1]
     grad_down = jnp.concatenate(
-        [
-            down_first[0] + jnp.sum(down_far.astype(F32), 0),
-            down_second + down_near.astype(F32),
-        ],
-        0,
-    )
-
-    heads_weights = jnp.stack([tn(normed, g) for g in heads_grad]).astype(BF16)
-    heads_weights = heads_weights.reshape(3, n_col, part, local_heads * head).transpose(1, 0, 2, 3)
-    heads_weights = lax.all_to_all(heads_weights, "col", split_axis=0, concat_axis=0, tiled=True)
-    heads_weights = heads_weights.transpose(1, 2, 0, 3).reshape(3 * part, hd)
-    heads_weights = lax.psum_scatter(heads_weights, "row", scatter_dimension=1, tiled=True)
-    grad_query, grad_key, grad_value = (
-        heads_weights[j * part : (j + 1) * part].astype(F32) for j in range(3)
-    )
-    out_weights = lax.all_to_all(
-        grad_out.astype(BF16).reshape(n_col, local_heads * head, part),
-        "col",
-        split_axis=0,
-        concat_axis=0,
-        tiled=True,
-    )
-    out_weights = out_weights.transpose(1, 0, 2).reshape(local_heads * head, width)
-    grad_out = lax.psum_scatter(out_weights, "row", scatter_dimension=1, tiled=True).astype(F32)
+        [weight_grads[2][..., b * shared : (b + 1) * shared] for b in range(w_down.shape[1] // shared)],
+        1,
+    )
+
+    heads_terms = jnp.sum(heads_terms.astype(F32), 0)
+    heads_sum = jnp.concatenate([heads_terms[j] for j in range(heads_terms.shape[0])], -1)
+    grad_query, grad_key, grad_value = heads_sum[0], heads_sum[1], heads_sum[2]
+    out_terms = jnp.sum(out_terms.astype(F32), 0)
+    grad_out = jnp.concatenate([out_terms[j] for j in range(out_terms.shape[0])], -1)
     smalls = [
         grad_gain_attn,
         grad_gain_ffn,

time: 1400 us -> 1670 us (1.19)
  Pallas kernels: 995 us -> 1360 us
  waiting for transfers between devices: 99.3 us -> 1.99 us
  blocking collectives: 16.8 us -> 36.9 us
  other arithmetic: 96.8 us -> 77.3 us
    pallas_call x6 -> x11, Pallas kernels: 600 us -> 949 us  [the longest x1 382 us: pack(): pl.pallas_call(pack_body, in_specs=[pl.BlockSpec(memory_space=pl.ANY)] *...]
    all_gather x2 -> x4, waiting for transfers between devices: 61.3 us -> 0.01 us  [gather(): return lax.all_gather(value, axis_name, axis=axis, tiled=True)]
    all_to_all x2 -> x0, waiting for transfers between devices: 35.8 us -> none  [the longest x1 35.8 us: shards(): lax.all_to_all(heads_weights, 'col', split_axis=0, concat_axis=0, tiled=T...]
    squeeze x0 -> x8, local copies, waits for them, and re-layouts: none -> 22.6 us  [the longest x1 18 us: shards(): weight_grads[2][..., b * shared:(b + 1) * shared]]
    psum x1, blocking collectives: 16.8 us -> 36.9 us  [shards(): lax.psum(jnp.concatenate(smalls).reshape(-1, 128), 'row').reshape(-1)]
    pallas_call x3 -> x4, Pallas kernels: 343 us -> 363 us  [scatter_col(): pl.pallas_call(functools.partial(scatter_body, part, stage), in_specs=[AN...]
  transfers between devices with their start and end apart: 11 -> 8, of which waited for: 2 -> 0; matrix products, arithmetic and copies ran while one was open for 16% -> 11% of each run, Pallas kernels for 64% -> 59%
where the time goes in v4:
time: 1670 us; the launch traced here: 1660 us
  Pallas kernels  1360 us (81%)
  matrix products  114 us (7%)
  other arithmetic  77.3 us (5%)
  local copies, waits for them, and re-layouts  52.2 us (3%)
  blocking collectives  36.9 us (2%)
    pallas_call x1, Pallas kernels, pack(): pl.pallas_call(pack_body, in_specs=[pl.BlockSpec(memory_space=pl.ANY)] *...  382 us
    pallas_call x4, Pallas kernels, scatter_col(): pl.pallas_call(functools.partial(scatter_body, part, stage), in_specs=[AN...  363 us
    pallas_call x1, Pallas kernels, front(): pl.pallas_call(front_body, in_specs=[ANY] * 7, out_specs=[ANY] * 5, out_s...  179 us
    pallas_call x4, Pallas kernels, expert_pass(): pl.pallas_call(functools.partial(expert_body, shared), grid_spec=pltpu.Pr...  166 us
    pallas_call x1, Pallas kernels, middle_gather(): pl.pallas_call(functools.partial(middle_body, axes), in_specs=[ANY] * n,...  143 us
    pallas_call x4, Pallas kernels, expert_grads(): pl.pallas_call(grads_body, grid=(width // shared,), in_specs=[thin, whole...  78.4 us
    pallas_call x2, Pallas kernels, combine(): pl.pallas_call(combine_body, grid=(micro, group // tile), in_specs=[pl.Bl...  52.8 us
    dot_general x5, matrix products, nt(): lax.dot_general(a, b, (((1,), (1,)), ((), ())), preferred_element_type=F32)  40.8 us
  transfers between devices with their start and end apart: 8, of which 0 were waited for; matrix products, arithmetic and copies ran while one was open for 11% of the time, Pallas kernels for 59%

profile of v4, /device:TPU:0, one launch (start us, length us, event | category | flops | bytes accessed | tf_op | source)
XLA Modules:
  0.0 1663.4 jit_solution(686722222937902501)
XLA Ops:
  7.2 382.4 %pack.1 = (bf16[3,512,1024]{2,1,0:T(8,128)(2,1)}, bf16[3,512,1024]{2,1,0:T(8,128)(2,1)}, bf16[3,512,1024]{2,1,0:T(8,128)(2,1)}, bf16[3,512,1024]{2,1,0:T(8,128)(2,1)}) custom-call(bf16[4,512,1024]{2,1,0:T(8,128)(2,1)} %wg.1, bf16[4,512,1024]{2,1,0:T(8,128)(2,1)} %wu.1, bf16[4,1024,512]{2,1,0:T(8,128)(2,1)} %wd.1), custom_call_target="tpu_custom_call" | custom-call | bytes 25165824 | tf_op jit(solution)/shard_map/pack/pallas_call | solution.py:209
  395.7 2.1 slice_reduce_fusion
  398.9 179.3 %front.1 = (bf16[2048,2048]{1,0:T(8,128)(2,1)}, f32[2,2048]{1,0:T(2,128)}, bf16[3,2048,128]{2,1,0:T(8,128)(2,1)}, bf16[128,2048]{1,0:T(8,128)(2,1)}, bf16[32,256]{1,0:T(8,128)(2,1)}) custom-call(bf16[2048,256]{1,0:T(8,128)(2,1)} %tokens.1, f32[2,256]{1,0:T(2,128)} %pad_maximum_fusion.11.gains, bf16[256,256]{1,0:T(8,128)(2,1)} %wq.1, bf16[256,256]{1,0:T(8,128)(2,1)} %wk.1, ...), custom_call_target="tpu_custom_call" | custom-call | bytes 134217728 | tf_op jit(solution)/shard_map/front/pallas_call | solution.py:544
  578.2 5.1 fusion
  584.0 8.9 fusion.2
  592.8 6.4 multiply_reduce_fusion.6
  599.3 2.9 multiply_reduce_fusion.7
  603.3 3.6 fusion.55
  609.0 1.2 copy.162
  611.2 3.3 fusion.119
  614.6 1.2 exponential_reduce_fusion
  615.7 8.5 fusion.118
  625.0 1.5 fusion.27
  627.5 142.7 %middle_gather.1 = (bf16[2048,1024]{1,0:T(8,128)(2,1)}, bf16[1024,2048]{1,0:T(8,128)(2,1)}, bf16[32,2048]{1,0:T(8,128)(2,1)}, bf16[2048,2048]{1,0:T(8,128)(2,1)}) custom-call(bf16[2048,128]{1,0:T(8,128)(2,1)} %bitcast.296, bf16[128,2048]{1,0:T(8,128)(2,1)} %get-tuple-element.101.refs_1_, bf16[32,256]{1,0:T(8,128)(2,1)} %get-tuple-element.102.refs_2_, ...), custom_call_target="tpu_custom_call" | custom-call | bytes 270532608 | tf_op jit(solution)/shard_map/middle_gather/pallas_call | solution.py:581
  771.1 15.1 multiply_reduce_fusion
  787.0 2.2 multiply_convert_fusion
  789.2 2.9 copy-done.7
  792.1 2.6 select_reduce_fusion
  797.6 7.4 broadcast_multiply_fusion
  805.0 47.7 %expert_pass.4 = (bf16[2,512,2048]{2,1,0:T(8,128)(2,1)}, bf16[2,512,2048]{2,1,0:T(8,128)(2,1)}, bf16[2,512,1024]{2,1,0:T(8,128)(2,1)}, bf16[2,512,1024]{2,1,0:T(...) custom-call(s32[2]{0:T(128)} %get-tuple-element.195.counts, ...), custom_call_target="tpu_custom_call" | custom-call | flops 34359738368 | bytes 41943040 | tf_op jit(solution)/shard_map/expert_pass/pallas_call | solution.py:133
  852.7 20.2 %expert_grads.4 = bf16[3,2048,1024]{2,1,0:T(8,128)(2,1)} custom-call(bf16[1024,2048]{1,0:T(8,128)(2,1)} %bitcast.318, bf16[1024,1024]{1,0:T(8,128)(2,1)} %bitcast.328, bf16[1024,1024]{1,0:T(8,128)(2,1)} %bitcast.329, bf16[1024,1024]{1,0:T(8,128)(2,1)} %bitcast.327, bf16[1024,2048]{1,0:T(8,128)(2,1)} %bitcast.319), custom_call_target="tpu_custom_call" | custom-call | flops 12884901888 | bytes 27262976 | tf_op jit(solution)/shard_map/expert_grads/pallas_call | solution.py:176
  873.6 40.1 %expert_pass.5 = (bf16[2,512,2048]{2,1,0:T(8,128)(2,1)}, bf16[2,512,2048]{2,1,0:T(8,128)(2,1)}, bf16[2,512,1024]{2,1,0:T(8,128)(2,1)}, bf16[2,512,1024]{2,1,0:T(...) custom-call(s32[2]{0:T(128)} %get-tuple-element.194.counts, ...), custom_call_target="tpu_custom_call" | custom-call | flops 34359738368 | bytes 41943040 | tf_op jit(solution)/shard_map/expert_pass/pallas_call | solution.py:133
  913.6 19.1 %expert_grads.5 = bf16[3,2048,1024]{2,1,0:T(8,128)(2,1)} custom-call(bf16[1024,2048]{1,0:T(8,128)(2,1)} %bitcast.320, bf16[1024,1024]{1,0:T(8,128)(2,1)} %bitcast.331, bf16[1024,1024]{1,0:T(8,128)(2,1)} %bitcast.332, bf16[1024,1024]{1,0:T(8,128)(2,1)} %bitcast.330, bf16[1024,2048]{1,0:T(8,128)(2,1)} %bitcast.321), custom_call_target="tpu_custom_call" | custom-call | flops 12884901888 | bytes 27262976 | tf_op jit(solution)/shard_map/expert_grads/pallas_call | solution.py:176
  934.0 39.0 %expert_pass.6 = (bf16[2,512,2048]{2,1,0:T(8,128)(2,1)}, bf16[2,512,2048]{2,1,0:T(8,128)(2,1)}, bf16[2,512,1024]{2,1,0:T(8,128)(2,1)}, bf16[2,512,1024]{2,1,0:T(...) custom-call(s32[2]{0:T(128)} %get-tuple-element.193.counts, ...), custom_call_target="tpu_custom_call" | custom-call | flops 34359738368 | bytes 41943040 | tf_op jit(solution)/shard_map/expert_pass/pallas_call | solution.py:133
  972.9 20.1 %expert_grads.6 = bf16[3,2048,1024]{2,1,0:T(8,128)(2,1)} custom-call(bf16[1024,2048]{1,0:T(8,128)(2,1)} %bitcast.322, bf16[1024,1024]{1,0:T(8,128)(2,1)} %bitcast.334, bf16[1024,1024]{1,0:T(8,128)(2,1)} %bitcast.335, bf16[1024,1024]{1,0:T(8,128)(2,1)} %bitcast.333, bf16[1024,2048]{1,0:T(8,128)(2,1)} %bitcast.323), custom_call_target="tpu_custom_call" | custom-call | flops 12884901888 | bytes 27262976 | tf_op jit(solution)/shard_map/expert_grads/pallas_call | solution.py:176
  994.3 39.6 %expert_pass.7 = (bf16[2,512,2048]{2,1,0:T(8,128)(2,1)}, bf16[2,512,2048]{2,1,0:T(8,128)(2,1)}, bf16[2,512,1024]{2,1,0:T(8,128)(2,1)}, bf16[2,512,1024]{2,1,0:T(...) custom-call(s32[2]{0:T(128)} %get-tuple-element.192.counts, ...), custom_call_target="tpu_custom_call" | custom-call | flops 34359738368 | bytes 41943040 | tf_op jit(solution)/shard_map/expert_pass/pallas_call | solution.py:133
  1034.0 19.0 %expert_grads.7 = bf16[3,2048,1024]{2,1,0:T(8,128)(2,1)} custom-call(bf16[1024,2048]{1,0:T(8,128)(2,1)} %bitcast.316, bf16[1024,1024]{1,0:T(8,128)(2,1)} %bitcast.325, bf16[1024,1024]{1,0:T(8,128)(2,1)} %bitcast.326, bf16[1024,1024]{1,0:T(8,128)(2,1)} %bitcast.324, bf16[1024,2048]{1,0:T(8,128)(2,1)} %bitcast.317), custom_call_target="tpu_custom_call" | custom-call | flops 12884901888 | bytes 27262976 | tf_op jit(solution)/shard_map/expert_grads/pallas_call | solution.py:176
  1054.5 26.4 %combine.2 = bf16[2,1024,2048]{2,1,0:T(8,128)(2,1)} custom-call(s32[2,1024,4]{2,1,0:T(8,128)} %copy-done.8, bf16[2,512,2048]{2,1,0:T(8,128)(2,1)} %get-tuple-element.116.refs_0_, bf16[2,512,2048]{2,1,0:T(8,128)(2,1)} %get-tuple-element.128.refs_1_, bf16[2,512,2048]{2,1,0:T(8,128)(2,1)} %get-tuple-element.140.refs_2_, ...), custom_call_target="tpu_custom_call" | custom-call | flops 17179869184 | bytes 25165824 | tf_op jit(solution)/shard_map/combine/pallas_call | solution.py:236
  1080.9 106.7 %scatter_col.4 = (f32[2048,256]{1,0:T(8,128)}, f32[8,4,2,2,1024]{4,3,2,1,0:T(2,128)}) custom-call(bf16[2048,2048]{1,0:T(8,128)(2,1)} %bitcast.272, f32[4,2,2,1024]{3,2,1,0:T(2,128)} %pad_maximum_fusion.10.refs_1_), custom_call_target="tpu_custom_call" | custom-call | bytes 167772160 | tf_op jit(solution)/shard_map/scatter_col/pallas_call | solution.py:872
  1187.6 2.3 slice_reduce_fusion.4
  1190.1 1.5 convolution_bitcast_fusion
  1191.8 3.0 multiply_reduce_fusion.2
  1194.8 4.5 convolution_convert_fusion.refs_0_
  1199.3 56.7 %scatter_col.5 = f32[2048,128]{1,0:T(8,128)} custom-call(bf16[2048,1024]{1,0:T(8,128)(2,1)} %convolution_convert_fusion.refs_0_), custom_call_target="tpu_custom_call" | custom-call | bytes 83886080 | tf_op jit(solution)/shard_map/scatter_col/pallas_call | solution.py:872
  1256.0 1.3 convert_element_type.198
  1258.1 6.2 fusion.28
  1264.3 1.3 copy.148
  1265.6 5.8 multiply_reduce_fusion.1
  1271.4 5.1 multiply_convert_fusion.1
  1276.5 1.1 fusion.26
  1277.8 1.5 fusion.25
  1279.5 2.4 fusion.64
  1283.7 8.1 fusion.75
  1291.8 9.0 fusion.71
  1300.7 16.3 add_convert_fusion.refs_0_
  1317.0 26.4 %combine.3 = bf16[2,1024,2048]{2,1,0:T(8,128)(2,1)} custom-call(s32[2,1024,4]{2,1,0:T(8,128)} %copy-done.8, bf16[2,512,2048]{2,1,0:T(8,128)(2,1)} %get-tuple-element.166.refs_0_, bf16[2,512,2048]{2,1,0:T(8,128)(2,1)} %get-tuple-element.167.refs_1_, bf16[2,512,2048]{2,1,0:T(8,128)(2,1)} %get-tuple-element.168.refs_2_, ...), custom_call_target="tpu_custom_call" | custom-call | flops 17179869184 | bytes 25165824 | tf_op jit(solution)/shard_map/combine/pallas_call | solution.py:236
  1343.4 76.0 %scatter_col.6 = f32[2048,256]{1,0:T(8,128)} custom-call(bf16[2048,2048]{1,0:T(8,128)(2,1)} %bitcast.271), custom_call_target="tpu_custom_call" | custom-call | bytes 167772160 | tf_op jit(solution)/shard_map/scatter_col/pallas_call | solution.py:872
  1419.4 3.5 add_convert_fusion.1
  1422.9 1.4 multiply_reduce_fusion.3
  1425.0 6.0 fusion.9
  1431.0 5.9 fusion.7
  1437.0 2.5 fusion.8
  1439.4 1.3 pad_maximum_fusion.1.refs_2_
  1440.7 2.2 convolution_convert_fusion.6.refs_3_
  1442.9 123.4 %scatter_col.7 = (f32[2048,256]{1,0:T(8,128)}, f32[8,24,128]{2,1,0:T(8,128)}, bf16[4,2,3,256,128]{4,3,2,1,0:T(8,128)(2,1)}, bf16[4,2,128,256]{3,2,1,0:T(8,128)(2,1)}) custom-call(bf16[2048,2048]{1,0:T(8,128)(2,1)} %add_convert_fusion.refs_0_, f32[24,128]{1,0:T(8,128)} %fusion.100.refs_1_, bf16[3,2048,128]{2,1,0:T(8,128)(2,1)} %pad_maximum_fusion.1.refs_2_, ...), custom_call_target="tpu_custom_call" | custom-call | bytes 167772160 | tf_op jit(solution)/shard_map/scatter_col/pallas_call | solution.py:872
  1567.3 3.2 fusion.14
  1570.6 36.9 %psum.7 = f32[70,128]{1,0:T(8,128)S(1)} all-reduce(f32[70,128]{1,0:T(8,128)S(1)} %bitcast.303), channel_id=1, replica_groups=mesh['row'=4,'col'=8] {'row'}, use_global_device_ids=true, to_apply=%region_29.30 | all-reduce | flops 8960 | bytes 71680 | tf_op jit(solution)/shard_map/psum | solution.py:1121
  1608.1 1.1 convert_reduce_fusion.1
  1609.2 1.7 convert_reduce_fusion
  1613.6 12.2 maximum_convert_fusion
  1625.8 18.0 %slice_bitcast_fusion = (f32[4,512,1024]{2,1,0:T(8,128)}, f32[4,512,1024]{2,1,0:T(8,128)}, f32[4,512,1024]{2,1,0:T(8,128)}) fusion(f32[3,4,512,1024]{3,2,0,1:T(8,128)} %maximum_convert_fusion), kind=kLoop, calls=%fused_computation.10 | loop fusion | bytes 50331648 | tf_op jit(solution)/shard_map/squeeze | solution.py:1105
  1643.8 5.2 fusion.116
  1649.1 1.3 dynamic-slice_bitcast_fusion
  1652.0 4.4 pad_maximum_fusion
  (249 shorter events, 32.2 us)
Async XLA Ops:
  7.2 797.8 %all-gather.5.cloned.1.call-start = ((), (), s32[]{:S(2)}) async-start(), calls=%async_computation.4 | async-start | bytes 15728640 | tf_op jit(solution)/shard_map/all_gather | solution.py:923
  389.7 483.9 %all-gather.7.cloned.1.call-start = ((), (), s32[]{:S(2)}) async-start(), calls=%async_computation.5 | async-start | bytes 15728640 | tf_op jit(solution)/shard_map/all_gather | solution.py:923
  389.7 3.0 copy-start.52
  390.4 543.5 %all-gather.9.cloned.1.call-start = ((), (), s32[]{:S(2)}) async-start(), calls=%async_computation.6 | async-start | bytes 15728640 | tf_op jit(solution)/shard_map/all_gather | solution.py:923
  391.2 603.2 %all-gather.11.cloned.1.call-start = ((), (), s32[]{:S(2)}) async-start(), calls=%async_computation.7 | async-start | bytes 15728640 | tf_op jit(solution)/shard_map/all_gather | solution.py:923
  391.7 800.0 %reduce-scatter.5.cloned.1.call-start = ((), (), s32[]{:S(2)}) async-start(), calls=%async_computation.8 | async-start | bytes 15728640 | tf_op jit(solution)/shard_map/reduce_scatter | solution.py:1014
  391.8 211.5 %copy-start.71 = (f32[64]{0:T(128)}, f32[64]{0:T(128)S(1)}, u32[]{:S(2)}) copy-start(f32[64]{0:T(128)S(1)} %multiply_exponential_fusion) | copy-start | bytes 772
  392.7 210.6 %copy-start.44 = (f32[1,8,2,128]{3,1,2,0:T(8,128)}, f32[1,8,2,128]{3,1,2,0:T(8,128)S(1)}, u32[]{:S(2)}) copy-start(f32[1,8,2,128]{3,1,2,0:T(8,128)S(1)} %copy.176) | copy-start | bytes 24580
  393.9 4.4 copy-start.68
  393.9 4.4 copy-start.73
  578.2 5.7 copy-start.58
  583.9 8.9 copy-start.42
  583.9 8.9 copy-start.9
  592.8 6.5 copy-start
  599.3 3.0 copy-start.46
  599.3 3.0 copy-start.3
  599.3 3.0 copy-start.38
  599.3 3.0 copy-start.64
  599.3 3.0 copy-start.66
  610.2 4.3 copy-start.26
  614.5 9.7 copy-start.1
  615.7 8.5 copy-start.35
  786.3 5.8 copy-start.7
  787.0 5.1 copy-start.54
  787.0 5.1 copy-start.37
  792.1 3.4 copy-start.2
  872.9 550.0 %reduce-scatter.7.cloned.1.call-start = ((), (), s32[]{:S(2)}) async-start(), calls=%async_computation.9 | async-start | bytes 15728640 | tf_op jit(solution)/shard_map/reduce_scatter | solution.py:1014
  932.7 680.9 %reduce-scatter.9.cloned.1.call-start = ((), (), s32[]{:S(2)}) async-start(), calls=%async_computation.10 | async-start | bytes 15728640 | tf_op jit(solution)/shard_map/reduce_scatter | solution.py:1014
  993.1 620.5 %reduce-scatter.11.cloned.1.call-start = ((), (), s32[]{:S(2)}) async-start(), calls=%async_computation.11 | async-start | bytes 15728640 | tf_op jit(solution)/shard_map/reduce_scatter | solution.py:1014
  1080.9 109.1 %copy-start.21 = (f32[2048,32]{0,1:T(8,128)S(1)}, f32[2048,32]{0,1:T(8,128)}, u32[]{:S(2)}) copy-start(f32[2048,32]{0,1:T(8,128)} %copy-done.20) | copy-start | bytes 786436
  1080.9 109.2 %copy-start.15 = (f32[2048,32]{0,1:T(8,128)S(1)}, f32[2048,32]{0,1:T(8,128)}, u32[]{:S(2)}) copy-start(f32[2048,32]{0,1:T(8,128)} %copy-done.14) | copy-start | bytes 786436
  1080.9 110.9 %copy-start.32 = (bf16[2048,256]{1,0:T(8,128)(2,1)S(1)}, bf16[2048,256]{1,0:T(8,128)(2,1)}, u32[]{:S(2)}) copy-start(bf16[2048,256]{1,0:T(8,128)(2,1)} %refs_3_.1) | copy-start | bytes 3145732
  1080.9 110.9 %copy-start.55 = (f32[2048]{0:T(1024)S(1)}, f32[2048]{0:T(1024)}, u32[]{:S(2)}) copy-start(f32[2048]{0:T(1024)} %copy-done.54) | copy-start | bytes 24580
  1080.9 110.9 %copy-start.63 = (f32[2048]{0:T(1024)S(1)}, f32[2048]{0:T(1024)}, u32[]{:S(2)}) copy-start(f32[2048]{0:T(1024)} %get-tuple-element.242) | copy-start | bytes 24580
  1080.9 110.9 %copy-start.74 = (f32[256]{0:T(256)S(1)}, f32[256]{0:T(256)}, u32[]{:S(2)}) copy-start(f32[256]{0:T(256)} %param.18) | copy-start | bytes 3076
  1199.3 58.8 %copy-start.36 = (f32[2,1024]{1,0:T(2,128)S(1)}, f32[2,1024]{1,0:T(2,128)}, u32[]{:S(2)}) copy-start(f32[2,1024]{1,0:T(2,128)} %copy-done.35) | copy-start | bytes 24580
  1258.1 7.5 copy-start.12
  1265.6 35.1 %copy-start.16 = (bf16[2,1024,1,128]{3,1,0,2:T(8,128)(2,1)}, bf16[2,1024,1,128]{3,1,0,2:T(8,128)(2,1)S(1)}, u32[]{:S(2)}) copy-start(bf16[2,1024,1,128]{3,1,0,2:T(8,128)(2,1)S(1)} %copy.148) | copy-start | bytes 1572868
  1271.4 5.1 copy-start.28
  1271.4 5.1 copy-start.29
  1279.3 2.6 copy-start.6
  1279.3 2.6 copy-start.41
  1279.3 2.6 copy-start.65
  1279.3 2.9 copy-start.4
  1279.4 2.9 copy-start.39
  1279.4 2.9 copy-start.67
  1279.5 3.2 copy-start.49
  1279.5 3.2 copy-start.47
  1283.0 8.7 copy-start.22
  1283.4 8.4 copy-start.24
  1419.4 3.5 copy-start.13
  1425.0 6.0 copy-start.25
  1425.0 11.9 slice-start
  1431.0 6.0 slice-start.1
  1431.0 6.0 copy-start.23
  1437.0 3.8 copy-start.75
  1442.9 124.4 %copy-start.18 = (bf16[2048,256]{1,0:T(8,128)(2,1)S(1)}, bf16[2048,256]{1,0:T(8,128)(2,1)}, u32[]{:S(2)}) copy-start(bf16[2048,256]{1,0:T(8,128)(2,1)} %tokens.1) | copy-start | bytes 3145732
  1442.9 124.4 %copy-start.43 = (f32[2048]{0:T(1024)S(1)}, f32[2048]{0:T(1024)}, u32[]{:S(2)}) copy-start(f32[2048]{0:T(1024)} %copy-done.42) | copy-start | bytes 24580
  1442.9 124.4 %copy-start.53 = (f32[2048]{0:T(1024)S(1)}, f32[2048]{0:T(1024)}, u32[]{:S(2)}) copy-start(f32[2048]{0:T(1024)} %get-tuple-element.240) | copy-start | bytes 24580
  1442.9 124.4 %copy-start.69 = (f32[256]{0:T(256)S(1)}, f32[256]{0:T(256)}, u32[]{:S(2)}) copy-start(f32[256]{0:T(256)} %param.17) | copy-start | bytes 3076
  1570.5 43.1 %copy-start.19 = (bf16[3,512,1024]{2,1,0:T(8,128)(2,1)S(1)}, bf16[3,512,1024]{2,1,0:T(8,128)(2,1)}, u32[]{:S(2)}) copy-start(bf16[3,512,1024]{2,1,0:T(8,128)(2,1)} %reduce-scatter.5.cloned.1.call-done) | copy-start | bytes 9437188
  1643.8 6.5 copy-start.33
  1643.8 6.5 copy-start.34
  1643.8 7.3 copy-start.31
  (22 other events, 22.1 us)
Sparse Core Ops, SparseCore 0:
  389.8 202.4 all-gather.4
  594.1 122.0 all-gather.6
  718.1 122.5 all-gather.8
  842.3 122.5 all-gather.10
  967.8 120.7 reduce-scatter.4
  1091.6 120.7 reduce-scatter.6
  1215.4 120.7 reduce-scatter.8
  1339.3 140.6 reduce-scatter.10

commit v5 on v4

--- a/solution.py
+++ b/solution.py
@@ -15,6 +15,7 @@
 BF16 = jnp.bfloat16
 VMEM_LIMIT = 60 * 1024 * 1024
 MESH = pl.DeviceIdType.MESH
+ANY = pl.BlockSpec(memory_space=pl.ANY)
 
 
 def inverse_rms(values):
@@ -187,36 +188,62 @@
     )(xe, dgp, dup, hg, dyr)
 
 
-def pack_body(wg, wu, wd, *rest):
-    outs, sem = rest[:-1], rest[-1]
-    shared, ff = wg.shape[1:]
-    copies = []
-    for e, out in enumerate(outs):
-        moves = [(wg.at[e], out.at[0]), (wu.at[e], out.at[1])]
-        for b in range(ff // shared):
-            low = b * shared
-            moves.append((wd.at[e, pl.ds(low, shared)], out.at[2, :, pl.ds(low, shared)]))
-        for m, (src, dst) in enumerate(moves):
-            copies.append(pltpu.make_async_copy(src, dst, sem.at[e, m]))
-    for c in copies:
-        c.start()
-    for c in copies:
-        c.wait()
-
-
-def pack(wg, wu, wd):
-    experts, shared, ff = wg.shape
+def pack_body(wg, wu, wd, out):
+    shared = out.shape[1]
+    out[0] = wg[0]
+    out[1] = wu[0]
+    for b in range(out.shape[2] // shared):
+        low = b * shared
+        out[2, :, low : low + shared] = wd[0, low : low + shared, :]
+
+
+def pack(wg, wu, wd, e):
+    _, shared, ff = wg.shape
+    block = pl.BlockSpec((1, shared, ff), lambda i: (e, 0, 0))
     return pl.pallas_call(
         pack_body,
-        in_specs=[pl.BlockSpec(memory_space=pl.ANY)] * 3,
-        out_specs=[pl.BlockSpec(memory_space=pl.ANY)] * experts,
-        out_shape=[jax.ShapeDtypeStruct((3, shared, ff), BF16)] * experts,
-        scratch_shapes=[pltpu.SemaphoreType.DMA((experts, 2 + ff // shared))],
+        grid=(1,),
+        in_specs=[block, block, pl.BlockSpec((1, ff, shared), lambda i: (e, 0, 0))],
+        out_specs=pl.BlockSpec((3, shared, ff), lambda i: (0, 0, 0)),
+        out_shape=jax.ShapeDtypeStruct((3, shared, ff), BF16),
         cost_estimate=pl.CostEstimate(
-            flops=0, bytes_accessed=experts * 6 * shared * ff * 2, transcendentals=0
+            flops=0, bytes_accessed=12 * shared * ff, transcendentals=0
         ),
         name="pack",
     )(wg, wu, wd)
+
+
+def unpack_body(x, *refs):
+    gg, gu, gd = refs[-3:]
+    shared = x.shape[1]
+    gg[0] = x[0].astype(F32)
+    gu[0] = x[1].astype(F32)
+    for b in range(x.shape[2] // shared):
+        low = b * shared
+        gd[0, low : low + shared, :] = x[2, :, low : low + shared].astype(F32)
+
+
+def unpack(x, held, e, experts):
+    _, shared, ff = x.shape
+    block = pl.BlockSpec((1, shared, ff), lambda i: (e, 0, 0))
+    held = list(held)
+    return pl.pallas_call(
+        unpack_body,
+        grid=(1,),
+        in_specs=[pl.BlockSpec((3, shared, ff), lambda i: (0, 0, 0))] + [ANY] * len(held),
+        out_specs=[block, block, pl.BlockSpec((1, ff, shared), lambda i: (e, 0, 0))],
+        out_shape=[
+            jax.ShapeDtypeStruct((experts, shared, ff), F32),
+            jax.ShapeDtypeStruct((experts, shared, ff), F32),
+            jax.ShapeDtypeStruct((experts, ff, shared), F32),
+        ],
+        input_output_aliases={1 + j: j for j in range(len(held))},
+        compiler_params=pltpu.CompilerParams(vmem_limit_bytes=VMEM_LIMIT),
+        cost_estimate=pl.CostEstimate(
+            flops=0, bytes_accessed=18 * shared * ff, transcendentals=0
+        ),
+        name="unpack",
+    )(x, *held)
 
 
 def combine_body(place, *refs):
@@ -410,48 +437,21 @@
     return [dma((n,))] + [dma((n, pairs))] * 6
 
 
-def front_body(tokens, gains, wq, wk, wv, wo, wr, x_o, gains_o, wh_o, wo_o, wr_o, *sems):
-    line, (heads_s, heads_r, row_s, row_r, own_s) = sems[:7], sems[7:]
+def front_body(tokens, gains, wq, wk, wv, wo, wr, *refs):
+    x_o, gains_o, wh_o, wo_o, wr_o = refs[:5]
+    wide = refs[5:8]
+    line, (heads_s, heads_r, row_s, row_r, own_s) = refs[8:15], refs[15:]
     row, col, n_row, n_col = places()
     head = wh_o.shape[2]
     part = wq.shape[0]
-    per = wq.shape[1] // head
-    small = [(wo, wo_o), (wr, wr_o)]
     begin, middle, end = line_gather((1, 1), [tokens, gains], [x_o, gains_o], line)
-
-    def heads_dst(m, source):
-        return wh_o.at[m, pl.ds(pl.multiple_of(source * part, part), part), :]
-
-    def heads(m, r, j):
-        src = (wq, wk, wv)[m].at[:, pl.ds(j * head, head)]
-        return remote(
-            src,
-            heads_dst(m, col),
-            heads_s.at[m, r * per + j],
-            heads_r.at[m, col],
-            (r, row * per + j),
-        )
-
-    def heads_own(m, j):
-        src = (wq, wk, wv)[m].at[:, pl.ds(j * head, head)]
-        return pltpu.make_async_copy(src, heads_dst(m, col), own_s.at[m])
-
-    def to_self(r, j):
-        return (row == r) & (col == row * per + j)
-
-    def heads_come(m, c):
-        return remote(
-            heads_dst(m, c), heads_dst(m, c), heads_r.at[m, c], heads_r.at[m, c], (row, col)
-        )
-
-    def from_self(c):
-        return (row == col // per) & (col == c)
+    small = [(wq, wide[0]), (wk, wide[1]), (wv, wide[2]), (wo, wo_o), (wr, wr_o)]
 
     def small_dst(k, source):
-        if k == 0:
-            return col_slice(wo_o, source, wo.shape[1])
-        size = wr.shape[0]
-        return wr_o.at[pl.ds(pl.multiple_of(source * size, size), size), :]
+        src, dst = small[k]
+        if k < 4:
+            return col_slice(dst, source, src.shape[1])
+        return dst.at[pl.ds(pl.multiple_of(source * src.shape[0], src.shape[0]), src.shape[0]), :]
 
     def small_copy(k, step):
         return remote(
@@ -469,70 +469,71 @@
         )
 
     def small_own(k):
-        return pltpu.make_async_copy(small[k][0], small_dst(k, row), own_s.at[3 + k])
-
-    sources = line_peers() + row_peers()
-    targets = [ok for ok, _ in sources]
-    for c in range(n_col):
-        sources.append((jnp.logical_not(from_self(c)), (col // per, c)))
-    for r in range(n_row):
-        for j in range(per):
-            targets.append(jnp.logical_not(to_self(r, j)))
-    shake(sources, targets)
-    begin()
-    for k in range(2):
-        small_own(k).start()
+        return pltpu.make_async_copy(small[k][0], small_dst(k, row), own_s.at[k])
+
+    def heads_dst(m, source):
+        return wh_o.at[m, pl.ds(pl.multiple_of(source * part, part), part), :]
+
+    def heads(m, step):
+        where = (col + step) % n_col
+        return remote(
+            col_slice(wide[m], where, head),
+            heads_dst(m, col),
+            heads_s.at[m, step],
+            heads_r.at[m, step],
+            (row, where),
+        )
+
+    def heads_come(m, step):
+        source = (col + n_col - step) % n_col
+        return remote(
+            heads_dst(m, source),
+            heads_dst(m, source),
+            heads_s.at[m, step],
+            heads_r.at[m, step],
+            (row, source),
+        )
+
+    def heads_own(m):
+        return pltpu.make_async_copy(
+            col_slice(wide[m], col, head), heads_dst(m, col), own_s.at[5 + m]
+        )
+
+    peers = [(True, (row, (col + k) % n_col)) for k in range(1, n_col)] + row_peers()
+    shake(peers, [ok for ok, _ in peers])
+    for k in range(5):
         for step in range(1, n_row):
             small_copy(k, step).start()
-    for r in range(n_row):
-        for j in range(per):
-
-            @pl.when(to_self(r, j))
-            def _():
-                for m in range(3):
-                    heads_own(m, j).start()
-
-            @pl.when(jnp.logical_not(to_self(r, j)))
-            def _():
-                for m in range(3):
-                    heads(m, r, j).start()
-
+        small_own(k).start()
+    begin()
+    for k in range(3):
+        small_own(k).wait()
+        for step in range(1, n_row):
+            small_come(k, step).wait_recv()
+    for m in range(3):
+        heads_own(m).start()
+        for step in range(1, n_col):
+            heads(m, step).start()
     middle()
     end()
-    for k in range(2):
-        small_own(k).wait()
+    for k in range(5):
+        if k >= 3:
+            small_own(k).wait()
         for step in range(1, n_row):
             small_copy(k, step).wait_send()
-            small_come(k, step).wait_recv()
-    for r in range(n_row):
-        for j in range(per):
-
-            @pl.when(to_self(r, j))
-            def _():
-                for m in range(3):
-                    heads_own(m, j).wait()
-
-            @pl.when(jnp.logical_not(to_self(r, j)))
-            def _():
-                for m in range(3):
-                    heads(m, r, j).wait_send()
-
-    for c in range(n_col):
-
-        @pl.when(jnp.logical_not(from_self(c)))
-        def _():
-            for m in range(3):
-                heads_come(m, c).wait_recv()
-
-
-ANY = pl.BlockSpec(memory_space=pl.ANY)
+            if k >= 3:
+                small_come(k, step).wait_recv()
+    for m in range(3):
+        heads_own(m).wait()
+        for step in range(1, n_col):
+            heads(m, step).wait_send()
+            heads_come(m, step).wait_recv()
 
 
 def front(tokens, gains, wq, wk, wv, wo, wr, head, ident):
     n_row, n_col = lax.axis_size("row"), lax.axis_size("col")
     rows, part = tokens.shape
     width = part * n_col
-    per = wq.shape[1] // head
     dma = pltpu.SemaphoreType.DMA
     shapes = [
         ((rows, width), BF16),
@@ -540,26 +541,26 @@
         ((3, width, head), BF16),
         ((wo.shape[0], wo.shape[1] * n_row), BF16),
         ((wr.shape[0] * n_row, part), BF16),
-    ]
+    ] + [((part, wq.shape[1] * n_row), BF16)] * 3
     return pl.pallas_call(
         front_body,
         in_specs=[ANY] * 7,
-        out_specs=[ANY] * 5,
+        out_specs=[ANY] * 8,
         out_shape=[jax.ShapeDtypeStruct(s, t) for s, t in shapes],
         scratch_shapes=line_sems(2, n_col // 2)
         + [
-            dma((3, n_row * per)),
             dma((3, n_col)),
-            dma((2, n_row)),
-            dma((2, n_row)),
-            dma((6,)),
+            dma((3, n_col)),
+            dma((5, n_row)),
+            dma((5, n_row)),
+            dma((8,)),
         ],
         compiler_params=pltpu.CompilerParams(collective_id=ident, has_side_effects=True),
         cost_estimate=pl.CostEstimate(
             flops=0, bytes_accessed=rows * width * 32, transcendentals=0
         ),
         name="front",
-    )(tokens, gains, wq, wk, wv, wo, wr)
+    )(tokens, gains, wq, wk, wv, wo, wr)[:5]
 
 
 def middle_body(axes, *refs):
@@ -593,8 +594,8 @@
 
 
 def scatter_body(part, stage, *refs):
-    n_in = (1, 2, 4)[stage]
-    n_out = (1, 2, 4)[stage]
+    n_in = (1, 2, 4, 3)[stage]
+    n_out = (1, 2, 4, 3)[stage]
     x, ins = refs[0], refs[1:n_in]
     out, outs = refs[n_in], refs[n_in + 1 : n_in + n_out]
     rest = refs[n_in + n_out :]
@@ -649,7 +650,7 @@
         )
 
     copies, arrivals, own = [], [], []
-    if stage:
+    if stage in (1, 2):
         small_s, small_r, own_s = rest[11:14]
         extra, extra_o = ins[0], outs[0]
         for k in range(1, n_col):
@@ -661,63 +662,44 @@
                 remote(extra, extra_o.at[source], small_s.at[k], small_r.at[k], (row, where))
             )
         own.append(pltpu.make_async_copy(extra, extra_o.at[col], own_s))
-    guarded = []
     if stage == 2:
         give_s, give_r, keep_s = rest[14:]
         per = n_col // n_row
-        heads, branch = ins[1:]
-        heads_o, branch_o = outs[1:]
-        part_h = heads.shape[1] // n_col
-        rows_b = branch.shape[0] // n_col
-        target = col // per
-        for k in range(n_col):
-            pieces = [
-                (heads.at[:, pl.ds(k * part_h, part_h), :], heads_o.at[row, col % per]),
-                (branch.at[pl.ds(k * rows_b, rows_b), :], branch_o.at[row, col % per]),
-            ]
-            self_here = (row == target) & (col == k)
-            for m, (src, dst) in enumerate(pieces):
-                guarded.append(
-                    (
-                        self_here,
-                        pltpu.make_async_copy(src, dst, keep_s.at[m]),
-                        remote(
-                            src, dst, give_s.at[m, k], give_r.at[m, row * per + col % per], (target, k)
-                        ),
-                    )
-                )
-        takes = []
-        for r in range(n_row):
-            for j in range(per):
-                mine_here = (row == r) & (col == row * per + j)
-                for m, (ref, src) in enumerate(
-                    ((heads_o, heads.at[:, pl.ds(0, part_h), :]), (branch_o, branch.at[pl.ds(0, rows_b), :]))
-                ):
-                    takes.append(
-                        (
-                            jnp.logical_not(mine_here),
-                            remote(
-                                src,
-                                ref.at[r, j],
-                                give_s.at[m, 0],
-                                give_r.at[m, r * per + j],
-                                (r, row * per + j),
-                            ),
-                        )
-                    )
+        for m in range(2):
+            src, dst = ins[1 + m], outs[1 + m]
+
+            def block_of(r):
+                return src.at[pl.ds(r * per, per)]
+
+            for step in range(1, n_row):
+                where, source = (row + step) % n_row, (row + n_row - step) % n_row
+                sems = (give_s.at[m, step], give_r.at[m, step])
+                copies.append(remote(block_of(where), dst.at[row], *sems, (where, col)))
+                arrivals.append(remote(block_of(where), dst.at[source], *sems, (where, col)))
+            own.append(pltpu.make_async_copy(block_of(row), dst.at[row], keep_s.at[m]))
+    if stage == 3:
+        give_s, give_r, keep_s = rest[11:]
+        for m in range(2):
+            src, dst = ins[m], outs[m]
+            size = src.shape[1 - m] // n_col
+
+            def block_for(c):
+                at_c = pl.ds(pl.multiple_of(c * size, size), size)
+                return src.at[:, at_c, :] if m == 0 else src.at[at_c, :]
+
+            for step in range(1, n_col):
+                where, source = (col + step) % n_col, (col + n_col - step) % n_col
+                sems = (give_s.at[m, step], give_r.at[m, step])
+                copies.append(remote(block_for(where), dst.at[col], *sems, (row, where)))
+                arrivals.append(remote(block_for(where), dst.at[source], *sems, (row, where)))
+            own.append(pltpu.make_async_copy(block_for(col), dst.at[col], keep_s.at[m]))
     if stage:
         peers = [(True, (row, (col + k) % n_col)) for k in range(1, n_col)]
     else:
         peers = line_peers()
-    targets = [ok for ok, _ in peers]
     if stage == 2:
-        for r in range(n_row):
-            for j in range(per):
-                here = (row == r) & (col == row * per + j)
-                peers.append((jnp.logical_not(here), (r, row * per + j)))
-        for k in range(n_col):
-            targets.append(jnp.logical_not((row == target) & (col == k)))
-    shake(peers, targets)
+        peers += row_peers()
+    shake(peers, [ok for ok, _ in peers])
     order = []
     for t in range(pairs):
         for d in (pairs - 1 - t, t):
@@ -729,15 +711,6 @@
             fetch(d, q).start()
     for c in copies + own:
         c.start()
-    for here, keep, give in guarded:
-
-        @pl.when(here)
-        def _():
-            keep.start()
-
-        @pl.when(jnp.logical_not(here))
-        def _():
-            give.start()
 
     def add(q, into, *sources):
         def step(i, _):
@@ -831,22 +804,6 @@
         c.wait_recv()
     for c in own:
         c.wait()
-    for here, keep, give in guarded:
-
-        @pl.when(here)
-        def _():
-            keep.wait()
-
-        @pl.when(jnp.logical_not(here))
-        def _():
-            give.wait_send()
-
-    if stage == 2:
-        for away, take in takes:
-
-            @pl.when(away)
-            def _():
-                take.wait_recv()
 
 
 def scatter_col(x, ident, stage=0, others=()):
@@ -858,16 +815,20 @@
     buffer = pltpu.VMEM((pairs, rows, part), BF16)
     scratch = [buffer] * 4 + [dma((pairs, cuts))] * 7
     out_shape = [jax.ShapeDtypeStruct((rows, part), F32)]
-    if stage:
+    if stage in (1, 2):
         extra = others[0]
         out_shape.append(jax.ShapeDtypeStruct((n_col,) + extra.shape, extra.dtype))
         scratch += [dma((n_col,)), dma((n_col,)), dma(())]
     if stage == 2:
-        heads, branch = others[1:]
-        scratch += [dma((2, n_col)), dma((2, n_row * per)), dma((2,))]
+        scratch += [dma((2, n_row)), dma((2, n_row)), dma((2,))]
+        for value in others[1:]:
+            out_shape.append(jax.ShapeDtypeStruct((n_row, per) + value.shape[1:], BF16))
+    if stage == 3:
+        heads, branch = others
+        scratch += [dma((2, n_col)), dma((2, n_col)), dma((2,))]
         out_shape += [
-            jax.ShapeDtypeStruct((n_row, per, 3, heads.shape[1] // n_col, heads.shape[2]), BF16),
-            jax.ShapeDtypeStruct((n_row, per, branch.shape[0] // n_col, branch.shape[1]), BF16),
+            jax.ShapeDtypeStruct((n_col, 3, heads.shape[1] // n_col, heads.shape[2]), BF16),
+            jax.ShapeDtypeStruct((n_col, branch.shape[0] // n_col, branch.shape[1]), BF16),
         ]
     return pl.pallas_call(
         functools.partial(scatter_body, part, stage),
@@ -927,7 +888,7 @@
         return lax.dynamic_slice_in_dim(value, col * size, size, axis)
 
     shared = w_down.shape[2]
-    big = [gather(w, "row", 1) for w in pack(w_gate, w_up, w_down)]
+    big = [gather(pack(w_gate, w_up, w_down, e), "row", 1) for e in range(local_exp)]
     inputs_low, gains, w_heads, rows_o, rows_r = front(
         tokens,
         jnp.stack([gain_attn, gain_ffn]),
@@ -1081,11 +1042,13 @@
     back_heads, mixed_slots = lax.optimization_barrier(
         (back_heads.astype(BF16), [o[0] for o in outs])
     )
-    (mixed_sum,) = scatter_col(combine(place, mixed_slots), 4)
+    mixed_sum, heads_terms, out_terms = scatter_col(
+        combine(place, mixed_slots), 4, 3, (heads_weights, grad_out.astype(BF16))
+    )
     mixed = (hidden_part + mixed_sum).astype(BF16)
     back_heads, mixed = lax.optimization_barrier((back_heads, mixed))
     normed_back, sums, heads_terms, out_terms = scatter_col(
-        tie(back_heads, 1), 5, 2, (sums, heads_weights, grad_out.astype(BF16))
+        tie(back_heads, 1), 5, 2, (sums, heads_terms, out_terms)
     )
     sums = jnp.sum(sums, 0).reshape(-1)
     dot_one = sums[:rows]
@@ -1099,12 +1062,10 @@
         - inputs_part * scale_one_part**2 * dot_one[:, None] / width
     )
 
-    weight_grads = jnp.stack(weight_grads, 1).astype(F32)
-    grad_gate, grad_up = weight_grads[0], weight_grads[1]
-    grad_down = jnp.concatenate(
-        [weight_grads[2][..., b * shared : (b + 1) * shared] for b in range(w_down.shape[1] // shared)],
-        1,
-    )
+    held = ()
+    for e, grad in enumerate(weight_grads):
+        held = unpack(grad, held, e, local_exp)
+    grad_gate, grad_up, grad_down = held
 
     heads_terms = jnp.sum(heads_terms.astype(F32), 0)
     heads_sum = jnp.concatenate([heads_terms[j] for j in range(heads_terms.shape[0])], -1)

time: 1670 us -> 1210 us (0.72)
  Pallas kernels: 1360 us -> 961 us
  local copies, waits for them, and re-layouts: 52.2 us -> 26.1 us
  blocking collectives: 36.9 us -> 17.5 us
  other arithmetic: 77.3 us -> 58.6 us
    pallas_call x2 -> x9, Pallas kernels: 562 us -> 162 us  [the longest x1 128 us: front(): pl.pallas_call(front_body, in_specs=[ANY] * 7, out_specs=[ANY] * 8, out_s...]
    pallas_call x4, Pallas kernels: 363 us -> 340 us  [scatter_col(): pl.pallas_call(functools.partial(scatter_body, part, stage), in_specs=[AN...]
    pallas_call x4, Pallas kernels: 166 us -> 186 us  [expert_pass(): pl.pallas_call(functools.partial(expert_body, shared), grid_spec=pltpu.Pr...]
    psum x1, blocking collectives: 36.9 us -> 17.5 us  [shards(): lax.psum(jnp.concatenate(smalls).reshape(-1, 128), 'row').reshape(-1)]
    squeeze x1 -> x0, local copies, waits for them, and re-layouts: 18 us -> none  [shards(): weight_grads[2][..., b * shared:(b + 1) * shared]]
  transfers between devices with their start and end apart: 8 -> 8, of which waited for: 0 -> 0; matrix products, arithmetic and copies ran while one was open for 11% -> 16% of each run, Pallas kernels for 59% -> 80%
where the time goes in v5:
time: 1210 us; the launch traced here: 1190 us
  Pallas kernels  961 us (79%)
  matrix products  114 us (9%)
  other arithmetic  58.6 us (5%)
  local copies, waits for them, and re-layouts  26.1 us (2%)
  blocking collectives  17.5 us (1%)
  between operations  15.5 us (1%)
    pallas_call x4, Pallas kernels, scatter_col(): pl.pallas_call(functools.partial(scatter_body, part, stage), in_specs=[AN...  340 us
    pallas_call x4, Pallas kernels, expert_pass(): pl.pallas_call(functools.partial(expert_body, shared), grid_spec=pltpu.Pr...  186 us
    pallas_call x1, Pallas kernels, middle_gather(): pl.pallas_call(functools.partial(middle_body, axes), in_specs=[ANY] * n,...  143 us
    pallas_call x1, Pallas kernels, front(): pl.pallas_call(front_body, in_specs=[ANY] * 7, out_specs=[ANY] * 8, out_s...  128 us
    pallas_call x4, Pallas kernels, expert_grads(): pl.pallas_call(grads_body, grid=(width // shared,), in_specs=[thin, whole...  76.3 us
    pallas_call x2, Pallas kernels, combine(): pl.pallas_call(combine_body, grid=(micro, group // tile), in_specs=[pl.Bl...  53.7 us
    dot_general x5, matrix products, nt(): lax.dot_general(a, b, (((1,), (1,)), ((), ())), preferred_element_type=F32)  41.7 us
    dot_general x5, matrix products, nn(): lax.dot_general(a, b, (((1,), (0,)), ((), ())), preferred_element_type=F32)  34.5 us
  transfers between devices with their start and end apart: 8, of which 0 were waited for; matrix products, arithmetic and copies ran while one was open for 16% of the time, Pallas kernels for 80%

profile of v5, /device:TPU:0, one launch (start us, length us, event | category | flops | bytes accessed | tf_op | source)
XLA Modules:
  0.0 1193.4 jit_solution(10367772808299787310)
XLA Ops:
  7.2 3.7 pack.4
  11.0 3.7 pack.5
  14.8 3.7 pack.6
  18.6 4.2 pack.7
  26.7 2.1 slice_reduce_fusion
  29.9 128.0 %front.1 = (bf16[2048,2048]{1,0:T(8,128)(2,1)}, f32[2,2048]{1,0:T(2,128)}, bf16[3,2048,128]{2,1,0:T(8,128)(2,1)}, bf16[128,2048]{1,0:T(8,128)(2,1)}, bf16[32,256...) custom-call(bf16[2048,256]{1,0:T(8,128)(2,1)} %tokens.1, ...), custom_call_target="tpu_custom_call" | custom-call | bytes 134217728 | tf_op jit(solution)/shard_map/front/pallas_call | solution.py:545
  158.0 5.1 fusion
  163.7 9.7 fusion.2
  173.4 6.8 multiply_reduce_fusion.6
  180.3 2.9 multiply_reduce_fusion.7
  184.3 3.6 fusion.55
  189.9 1.2 copy.171
  192.1 3.3 fusion.118
  195.5 1.2 exponential_reduce_fusion
  196.7 8.5 fusion.117
  205.9 1.5 fusion.27
  208.4 142.7 %middle_gather.1 = (bf16[2048,1024]{1,0:T(8,128)(2,1)}, bf16[1024,2048]{1,0:T(8,128)(2,1)}, bf16[32,2048]{1,0:T(8,128)(2,1)}, bf16[2048,2048]{1,0:T(8,128)(2,1)}) custom-call(bf16[2048,128]{1,0:T(8,128)(2,1)} %bitcast.282, bf16[128,2048]{1,0:T(8,128)(2,1)} %get-tuple-element.112.refs_1_, bf16[32,256]{1,0:T(8,128)(2,1)} %get-tuple-element.113.refs_2_, ...), custom_call_target="tpu_custom_call" | custom-call | bytes 270532608 | tf_op jit(solution)/shard_map/middle_gather/pallas_call | solution.py:582
  352.1 13.7 %multiply_reduce_fusion = (f32[2048]{0:T(1024)S(1)}, f32[2048,2048]{1,0:T(8,128)S(1)}) fusion(bf16[2048,1024]{1,0:T(8,128)(2,1)} %get-tuple-element.114, bf16[1024,2048]{1,0:T(8,128)(2,1)} %get-tuple-element.115, bf16[2048,2048]{1,0:T(8,128)(2,1)} %get-tuple-element.109), kind=kOutput, calls=%fused_computation.8 | convolution fusion | flops 8606709760 | bytes 33562624 | tf_op jit(solution)/shard_map/dot_general | solution.py:51
  366.4 2.2 multiply_convert_fusion
  368.6 2.8 copy-done.7
  371.5 2.6 select_reduce_fusion
  377.0 7.4 broadcast_multiply_fusion
  384.4 47.1 %expert_pass.4 = (bf16[2,512,2048]{2,1,0:T(8,128)(2,1)}, bf16[2,512,2048]{2,1,0:T(8,128)(2,1)}, bf16[2,512,1024]{2,1,0:T(8,128)(2,1)}, bf16[2,512,1024]{2,1,0:T(...) custom-call(s32[2]{0:T(128)} %get-tuple-element.217.counts, ...), custom_call_target="tpu_custom_call" | custom-call | flops 34359738368 | bytes 41943040 | tf_op jit(solution)/shard_map/expert_pass/pallas_call | solution.py:134
  431.5 19.0 %expert_grads.4 = bf16[3,2048,1024]{2,1,0:T(8,128)(2,1)} custom-call(bf16[1024,2048]{1,0:T(8,128)(2,1)} %bitcast.304, bf16[1024,1024]{1,0:T(8,128)(2,1)} %bitcast.314, bf16[1024,1024]{1,0:T(8,128)(2,1)} %bitcast.315, bf16[1024,1024]{1,0:T(8,128)(2,1)} %bitcast.313, bf16[1024,2048]{1,0:T(8,128)(2,1)} %bitcast.305), custom_call_target="tpu_custom_call" | custom-call | flops 12884901888 | bytes 27262976 | tf_op jit(solution)/shard_map/expert_grads/pallas_call | solution.py:177
  451.2 49.7 %expert_pass.5 = (bf16[2,512,2048]{2,1,0:T(8,128)(2,1)}, bf16[2,512,2048]{2,1,0:T(8,128)(2,1)}, bf16[2,512,1024]{2,1,0:T(8,128)(2,1)}, bf16[2,512,1024]{2,1,0:T(...) custom-call(s32[2]{0:T(128)} %get-tuple-element.216.counts, ...), custom_call_target="tpu_custom_call" | custom-call | flops 34359738368 | bytes 41943040 | tf_op jit(solution)/shard_map/expert_pass/pallas_call | solution.py:134
  500.9 19.1 %expert_grads.5 = bf16[3,2048,1024]{2,1,0:T(8,128)(2,1)} custom-call(bf16[1024,2048]{1,0:T(8,128)(2,1)} %bitcast.306, bf16[1024,1024]{1,0:T(8,128)(2,1)} %bitcast.317, bf16[1024,1024]{1,0:T(8,128)(2,1)} %bitcast.318, bf16[1024,1024]{1,0:T(8,128)(2,1)} %bitcast.316, bf16[1024,2048]{1,0:T(8,128)(2,1)} %bitcast.307), custom_call_target="tpu_custom_call" | custom-call | flops 12884901888 | bytes 27262976 | tf_op jit(solution)/shard_map/expert_grads/pallas_call | solution.py:177
  521.2 49.4 %expert_pass.6 = (bf16[2,512,2048]{2,1,0:T(8,128)(2,1)}, bf16[2,512,2048]{2,1,0:T(8,128)(2,1)}, bf16[2,512,1024]{2,1,0:T(8,128)(2,1)}, bf16[2,512,1024]{2,1,0:T(...) custom-call(s32[2]{0:T(128)} %get-tuple-element.215.counts, ...), custom_call_target="tpu_custom_call" | custom-call | flops 34359738368 | bytes 41943040 | tf_op jit(solution)/shard_map/expert_pass/pallas_call | solution.py:134
  570.7 19.1 %expert_grads.6 = bf16[3,2048,1024]{2,1,0:T(8,128)(2,1)} custom-call(bf16[1024,2048]{1,0:T(8,128)(2,1)} %bitcast.308, bf16[1024,1024]{1,0:T(8,128)(2,1)} %bitcast.320, bf16[1024,1024]{1,0:T(8,128)(2,1)} %bitcast.321, bf16[1024,1024]{1,0:T(8,128)(2,1)} %bitcast.319, bf16[1024,2048]{1,0:T(8,128)(2,1)} %bitcast.309), custom_call_target="tpu_custom_call" | custom-call | flops 12884901888 | bytes 27262976 | tf_op jit(solution)/shard_map/expert_grads/pallas_call | solution.py:177
  591.1 39.5 %expert_pass.7 = (bf16[2,512,2048]{2,1,0:T(8,128)(2,1)}, bf16[2,512,2048]{2,1,0:T(8,128)(2,1)}, bf16[2,512,1024]{2,1,0:T(8,128)(2,1)}, bf16[2,512,1024]{2,1,0:T(...) custom-call(s32[2]{0:T(128)} %get-tuple-element.214.counts, ...), custom_call_target="tpu_custom_call" | custom-call | flops 34359738368 | bytes 41943040 | tf_op jit(solution)/shard_map/expert_pass/pallas_call | solution.py:134
  630.6 19.1 %expert_grads.7 = bf16[3,2048,1024]{2,1,0:T(8,128)(2,1)} custom-call(bf16[1024,2048]{1,0:T(8,128)(2,1)} %bitcast.302, bf16[1024,1024]{1,0:T(8,128)(2,1)} %bitcast.311, bf16[1024,1024]{1,0:T(8,128)(2,1)} %bitcast.312, bf16[1024,1024]{1,0:T(8,128)(2,1)} %bitcast.310, bf16[1024,2048]{1,0:T(8,128)(2,1)} %bitcast.303), custom_call_target="tpu_custom_call" | custom-call | flops 12884901888 | bytes 27262976 | tf_op jit(solution)/shard_map/expert_grads/pallas_call | solution.py:177
  651.2 26.8 %combine.2 = bf16[2,1024,2048]{2,1,0:T(8,128)(2,1)} custom-call(s32[2,1024,4]{2,1,0:T(8,128)} %copy-done.8, bf16[2,512,2048]{2,1,0:T(8,128)(2,1)} %get-tuple-element.126.refs_0_, bf16[2,512,2048]{2,1,0:T(8,128)(2,1)} %get-tuple-element.137.refs_1_, bf16[2,512,2048]{2,1,0:T(8,128)(2,1)} %get-tuple-element.148.refs_2_, ...), custom_call_target="tpu_custom_call" | custom-call | flops 17179869184 | bytes 25165824 | tf_op jit(solution)/shard_map/combine/pallas_call | solution.py:263
  678.0 84.9 %scatter_col.4 = (f32[2048,256]{1,0:T(8,128)}, f32[8,4,2,2,1024]{4,3,2,1,0:T(2,128)}) custom-call(bf16[2048,2048]{1,0:T(8,128)(2,1)} %bitcast.262, f32[4,2,2,1024]{3,2,1,0:T(2,128)} %pad_maximum_fusion.9.refs_1_), custom_call_target="tpu_custom_call" | custom-call | bytes 167772160 | tf_op jit(solution)/shard_map/scatter_col/pallas_call | solution.py:833
  763.0 2.3 slice_reduce_fusion.4
  765.5 1.5 convolution_bitcast_fusion
  767.2 3.0 multiply_reduce_fusion.2
  770.2 4.4 convolution_convert_fusion.refs_0_
  774.6 56.8 %scatter_col.5 = f32[2048,128]{1,0:T(8,128)} custom-call(bf16[2048,1024]{1,0:T(8,128)(2,1)} %convolution_convert_fusion.refs_0_), custom_call_target="tpu_custom_call" | custom-call | bytes 83886080 | tf_op jit(solution)/shard_map/scatter_col/pallas_call | solution.py:833
  831.3 1.3 convert_element_type.195
  833.4 6.2 fusion.28
  839.6 1.3 copy.157
  841.0 5.8 multiply_reduce_fusion.1
  846.8 4.8 multiply_convert_fusion.1
  851.7 1.1 fusion.26
  852.9 1.5 fusion.25
  854.6 2.4 fusion.64
  858.8 9.0 fusion.75
  867.8 8.3 fusion.71
  876.1 17.0 %add_convert_fusion.refs_0_ = bf16[2048,2048]{1,0:T(8,128)(2,1)} fusion(f32[2048,2048]{1,0:T(8,128)} %fusion.71, f32[2048,2048]{1,0:T(8,128)} %fusion.75, bf16[2048,128]{1,0:T(8,128)(2,1)S(1)} %bitcast.265, bf16[3,2048,128]{2,1,0:T(8,128)(2,1)} %get-tuple-element.111), kind=kOutput, calls=%fused_computation.6 | convolution fusion | flops 1086324736 | bytes 42991616 | tf_op jit(solution)/shard_map/dot_general | solution.py:55
  893.2 6.1 fusion.9
  899.3 5.9 fusion.7
  905.3 2.5 fusion.8
  907.7 1.3 pad_maximum_fusion.refs_1_
  909.0 2.2 convolution_convert_fusion.6.refs_2_
  911.2 26.9 %combine.3 = bf16[2,1024,2048]{2,1,0:T(8,128)(2,1)} custom-call(s32[2,1024,4]{2,1,0:T(8,128)} %copy-done.8, bf16[2,512,2048]{2,1,0:T(8,128)(2,1)} %get-tuple-element.173.refs_0_, bf16[2,512,2048]{2,1,0:T(8,128)(2,1)} %get-tuple-element.174.refs_1_, bf16[2,512,2048]{2,1,0:T(8,128)(2,1)} %get-tuple-element.175.refs_2_, ...), custom_call_target="tpu_custom_call" | custom-call | flops 17179869184 | bytes 25165824 | tf_op jit(solution)/shard_map/combine/pallas_call | solution.py:263
  938.1 111.6 %scatter_col.6 = (f32[2048,256]{1,0:T(8,128)}, bf16[8,3,256,128]{3,2,1,0:T(8,128)(2,1)}, bf16[8,128,256]{2,1,0:T(8,128)(2,1)}) custom-call(bf16[2048,2048]{1,0:T(8,128)(2,1)} %bitcast.261, bf16[3,2048,128]{2,1,0:T(8,128)(2,1)} %pad_maximum_fusion.refs_1_, bf16[1024,256]{1,0:T(8,128)(2,1)} %convolution_convert_fusion.6.refs_2_), custom_call_target="tpu_custom_call" | custom-call | bytes 167772160 | tf_op jit(solution)/shard_map/scatter_col/pallas_call | solution.py:833
  1049.8 3.5 add_convert_fusion.1
  1053.3 1.4 multiply_reduce_fusion.3
  1055.3 86.5 %scatter_col.7 = (f32[2048,256]{1,0:T(8,128)}, f32[8,24,128]{2,1,0:T(8,128)}, bf16[4,2,3,256,128]{4,3,2,1,0:T(8,128)(2,1)}, bf16[4,2,128,256]{3,2,1,0:T(8,128)(2,1)}) custom-call(bf16[2048,2048]{1,0:T(8,128)(2,1)} %add_convert_fusion.refs_0_, f32[24,128]{1,0:T(8,128)} %fusion.100.refs_1_, bf16[8,3,256,128]{3,2,1,0:T(8,128)(2,1)} %get-tuple-element.182.refs_2_, ...), custom_call_target="tpu_custom_call" | custom-call | bytes 167772160 | tf_op jit(solution)/shard_map/scatter_col/pallas_call | solution.py:833
  1142.8 3.2 fusion.14
  1146.1 17.5 %psum.7 = f32[70,128]{1,0:T(8,128)S(1)} all-reduce(f32[70,128]{1,0:T(8,128)S(1)} %bitcast.289), channel_id=1, replica_groups=mesh['row'=4,'col'=8] {'row'}, use_global_device_ids=true, to_apply=%region_29.30 | all-reduce | flops 8960 | bytes 71680 | tf_op jit(solution)/shard_map/psum | solution.py:1082
  1163.6 4.7 unpack.4
  1168.3 4.7 unpack.5
  1173.1 4.9 unpack.6
  1181.6 4.7 unpack.7
  (248 shorter events, 29.2 us)
Async XLA Ops:
  7.2 377.2 %all-gather.5.cloned.1.call-start = ((), (), s32[]{:S(2)}) async-start(), calls=%async_computation.4 | async-start | bytes 15728640 | tf_op jit(solution)/shard_map/all_gather | solution.py:884
  10.9 440.2 %all-gather.7.cloned.1.call-start = ((), (), s32[]{:S(2)}) async-start(), calls=%async_computation.5 | async-start | bytes 15728640 | tf_op jit(solution)/shard_map/all_gather | solution.py:884
  14.7 506.5 %all-gather.9.cloned.1.call-start = ((), (), s32[]{:S(2)}) async-start(), calls=%async_computation.6 | async-start | bytes 15728640 | tf_op jit(solution)/shard_map/all_gather | solution.py:884
  18.5 4.3 copy-start.68
  18.5 5.2 copy-start.50
  18.5 572.6 %all-gather.11.cloned.1.call-start = ((), (), s32[]{:S(2)}) async-start(), calls=%async_computation.7 | async-start | bytes 15728640 | tf_op jit(solution)/shard_map/all_gather | solution.py:884
  22.8 744.3 %reduce-scatter.5.cloned.1.call-start = ((), (), s32[]{:S(2)}) async-start(), calls=%async_computation.8 | async-start | bytes 15728640 | tf_op jit(solution)/shard_map/reduce_scatter | solution.py:975
  22.8 161.4 %copy-start.69 = (f32[64]{0:T(128)}, f32[64]{0:T(128)S(1)}, u32[]{:S(2)}) copy-start(f32[64]{0:T(128)S(1)} %multiply_exponential_fusion) | copy-start | bytes 772
  23.8 160.5 %copy-start.42 = (f32[1,8,2,128]{3,1,2,0:T(8,128)}, f32[1,8,2,128]{3,1,2,0:T(8,128)S(1)}, u32[]{:S(2)}) copy-start(f32[1,8,2,128]{3,1,2,0:T(8,128)S(1)} %copy.185) | copy-start | bytes 24580
  25.0 4.4 copy-start.66
  25.0 4.4 copy-start.71
  158.0 5.7 copy-start.56
  163.7 9.7 copy-start.40
  163.7 9.7 copy-start.9
  173.4 6.9 copy-start
  180.3 3.0 copy-start.44
  180.3 3.0 copy-start.3
  180.3 3.0 copy-start.36
  180.3 3.0 copy-start.62
  180.3 3.0 copy-start.64
  191.1 4.3 copy-start.25
  195.5 9.7 copy-start.1
  196.7 8.5 copy-start.33
  365.7 5.7 copy-start.7
  366.4 5.1 copy-start.52
  366.4 5.1 copy-start.35
  371.5 3.4 copy-start.2
  450.5 602.8 %reduce-scatter.7.cloned.1.call-start = ((), (), s32[]{:S(2)}) async-start(), calls=%async_computation.9 | async-start | bytes 15728640 | tf_op jit(solution)/shard_map/reduce_scatter | solution.py:975
  520.0 653.1 %reduce-scatter.11.cloned.1.call-start = ((), (), s32[]{:S(2)}) async-start(), calls=%async_computation.11 | async-start | bytes 15728640 | tf_op jit(solution)/shard_map/reduce_scatter | solution.py:975
  589.8 591.8 %reduce-scatter.9.cloned.1.call-start = ((), (), s32[]{:S(2)}) async-start(), calls=%async_computation.10 | async-start | bytes 15728640 | tf_op jit(solution)/shard_map/reduce_scatter | solution.py:975
  678.0 87.4 %copy-start.20 = (f32[2048,32]{0,1:T(8,128)S(1)}, f32[2048,32]{0,1:T(8,128)}, u32[]{:S(2)}) copy-start(f32[2048,32]{0,1:T(8,128)} %copy-done.19) | copy-start | bytes 786436
  678.0 87.5 %copy-start.15 = (f32[2048,32]{0,1:T(8,128)S(1)}, f32[2048,32]{0,1:T(8,128)}, u32[]{:S(2)}) copy-start(f32[2048,32]{0,1:T(8,128)} %copy-done.14) | copy-start | bytes 786436
  678.0 89.1 %copy-start.31 = (bf16[2048,256]{1,0:T(8,128)(2,1)S(1)}, bf16[2048,256]{1,0:T(8,128)(2,1)}, u32[]{:S(2)}) copy-start(bf16[2048,256]{1,0:T(8,128)(2,1)} %refs_3_.1) | copy-start | bytes 3145732
  678.0 89.1 %copy-start.53 = (f32[2048]{0:T(1024)S(1)}, f32[2048]{0:T(1024)}, u32[]{:S(2)}) copy-start(f32[2048]{0:T(1024)} %copy-done.52) | copy-start | bytes 24580
  678.0 89.1 %copy-start.61 = (f32[2048]{0:T(1024)S(1)}, f32[2048]{0:T(1024)}, u32[]{:S(2)}) copy-start(f32[2048]{0:T(1024)} %get-tuple-element.259) | copy-start | bytes 24580
  678.0 89.1 %copy-start.72 = (f32[256]{0:T(256)S(1)}, f32[256]{0:T(256)}, u32[]{:S(2)}) copy-start(f32[256]{0:T(256)} %param.18) | copy-start | bytes 3076
  774.6 58.9 %copy-start.34 = (f32[2,1024]{1,0:T(2,128)S(1)}, f32[2,1024]{1,0:T(2,128)}, u32[]{:S(2)}) copy-start(f32[2,1024]{1,0:T(2,128)} %copy-done.33) | copy-start | bytes 24580
  833.4 7.5 copy-start.12
  841.0 52.2 %copy-start.16 = (bf16[2,1024,1,128]{3,1,0,2:T(8,128)(2,1)}, bf16[2,1024,1,128]{3,1,0,2:T(8,128)(2,1)S(1)}, u32[]{:S(2)}) copy-start(bf16[2,1024,1,128]{3,1,0,2:T(8,128)(2,1)S(1)} %copy.157) | copy-start | bytes 1572868
  846.8 4.9 copy-start.27
  846.8 4.9 copy-start.28
  852.9 1.7 copy-start.70
  854.4 2.6 copy-start.6
  854.5 2.6 copy-start.39
  854.5 2.6 copy-start.63
  854.5 2.9 copy-start.4
  854.5 2.9 copy-start.37
  854.5 2.9 copy-start.65
  854.6 3.2 copy-start.47
  854.6 3.2 copy-start.45
  858.2 9.6 copy-start.21
  858.5 9.2 copy-start.23
  893.2 6.1 copy-start.24
  893.2 12.0 %slice-start = ((s8[8388608]{0:T(1024)(128)(4,1)}), s8[4194304]{0:T(1024)(128)(4,1)S(1)}, s32[]{:S(2)}) async-start(s8[8388608]{0:T(1024)(128)(4,1)} %bitcast.250), calls=%async_computation.12 | async-start | bytes 8388608
  899.2 6.0 slice-start.1
  899.3 6.0 copy-start.22
  905.2 3.8 copy-start.73
  1049.8 3.5 copy-start.13
  1055.3 87.5 %copy-start.18 = (bf16[2048,256]{1,0:T(8,128)(2,1)S(1)}, bf16[2048,256]{1,0:T(8,128)(2,1)}, u32[]{:S(2)}) copy-start(bf16[2048,256]{1,0:T(8,128)(2,1)} %tokens.1) | copy-start | bytes 3145732
  1055.3 87.5 %copy-start.41 = (f32[2048]{0:T(1024)S(1)}, f32[2048]{0:T(1024)}, u32[]{:S(2)}) copy-start(f32[2048]{0:T(1024)} %copy-done.40) | copy-start | bytes 24580
  1055.3 87.5 %copy-start.51 = (f32[2048]{0:T(1024)S(1)}, f32[2048]{0:T(1024)}, u32[]{:S(2)}) copy-start(f32[2048]{0:T(1024)} %get-tuple-element.257) | copy-start | bytes 24580
  1055.3 87.5 %copy-start.67 = (f32[256]{0:T(256)S(1)}, f32[256]{0:T(256)}, u32[]{:S(2)}) copy-start(f32[256]{0:T(256)} %param.17) | copy-start | bytes 3076
  1173.1 5.5 copy-start.32
  1173.1 6.3 copy-start.30
  (20 other events, 18.1 us)
Sparse Core Ops, SparseCore 0:
  11.1 147.8 all-gather.4
  160.8 122.5 all-gather.6
  285.2 122.5 all-gather.8
  409.5 122.5 all-gather.10
  535.0 120.7 reduce-scatter.4
  658.7 120.7 reduce-scatter.6
  782.5 120.7 reduce-scatter.10
  906.4 120.7 reduce-scatter.8

commit v6 on v5

--- a/solution.py
+++ b/solution.py
@@ -246,37 +246,6 @@
     )(x, *held)
 
 
-def combine_body(place, *refs):
-    out = refs[-1]
-    total = jnp.zeros((out.shape[1], out.shape[2]), F32)
-    for e, ref in enumerate(refs[:-1]):
-        slot = lax.broadcasted_iota(jnp.int32, (out.shape[1], ref.shape[1]), 1)
-        pick = jnp.where(slot == place[0, :, e : e + 1], 1.0, 0.0).astype(BF16)
-        total = total + nn(pick, ref[0])
-    out[0] = total.astype(BF16)
-
-
-def combine(place, slots):
-    micro, group, local = place.shape
-    capacity, width = slots[0].shape[1:]
-    tile = min(256, group)
-    return pl.pallas_call(
-        combine_body,
-        grid=(micro, group // tile),
-        in_specs=[pl.BlockSpec((1, tile, local), lambda g, i: (g, i, 0))]
-        + [pl.BlockSpec((1, capacity, width), lambda g, i: (g, 0, 0)) for s in slots],
-        out_specs=pl.BlockSpec((1, tile, width), lambda g, i: (g, i, 0)),
-        out_shape=jax.ShapeDtypeStruct((micro, group, width), BF16),
-        compiler_params=pltpu.CompilerParams(vmem_limit_bytes=VMEM_LIMIT),
-        cost_estimate=pl.CostEstimate(
-            flops=2 * micro * group * local * capacity * width,
-            bytes_accessed=micro * (local * capacity + group) * width * 2,
-            transcendentals=0,
-        ),
-        name="combine",
-    )(place, *slots).reshape(micro * group, width)
-
-
 def places():
     row, col = lax.axis_index("row"), lax.axis_index("col")
     n_row, n_col = lax.axis_size("row"), lax.axis_size("col")
@@ -593,14 +562,19 @@
     )(*arrays)
 
 
-def scatter_body(part, stage, *refs):
+def scatter_body(part, stage, local, *refs):
     n_in = (1, 2, 4, 3)[stage]
     n_out = (1, 2, 4, 3)[stage]
+    if local:
+        place, slots, refs = refs[0], refs[1 : 1 + local], refs[local:]
     x, ins = refs[0], refs[1:n_in]
     out, outs = refs[n_in], refs[n_in + 1 : n_in + n_out]
     rest = refs[n_in + n_out :]
     acc, side, from_left, from_right, load, side_s, side_r = rest[:7]
     right_s, right_r, left_s, left_r = rest[7:11]
+    if local:
+        give, chosen, held, held_s = rest[11:15]
+        rest = rest[4:]
     row, col, n_row, n_col = places()
     pairs, pair, core = n_col // 2, col // 2, col % 2
     rows = out.shape[0]
@@ -624,7 +598,7 @@
 
     def across(d, q):
         return remote(
-            block(d * 2 + 1 - core, q),
+            cut(give, d, q) if local else block(d * 2 + 1 - core, q),
             cut(side, d, q),
             side_s.at[d, q],
             side_r.at[d, q],
@@ -705,10 +679,72 @@
         for d in (pairs - 1 - t, t):
             if d not in order:
                 order.append(d)
-    for d in order:
-        for q in range(cuts):
-            across(d, q).start()
-            fetch(d, q).start()
+    if local:
+        micro, capacity = held.shape[2], held.shape[3]
+        group = chosen.shape[1]
+        owners = []
+        for d in order:
+            owners += [d * 2 + 1 - core, d * 2 + core]
+
+        def bring(n):
+            return [
+                pltpu.make_async_copy(
+                    slots[e].at[:, :, pl.ds(pl.multiple_of(owners[n] * part, part), part)],
+                    held.at[n % 2, e],
+                    held_s.at[n % 2, e],
+                )
+                for e in range(local)
+            ]
+
+        def make(n, into):
+            for c in bring(n):
+                c.wait()
+            if n + 1 < len(owners):
+                for c in bring(n + 1):
+                    c.start()
+            steps = group // tile
+
+            def step(i, _):
+                g, at_row = i // steps, pl.multiple_of((i % steps) * tile, tile)
+                total = None
+                for e in range(local):
+                    term = nn(
+                        chosen[g, pl.ds(at_row, tile), e * capacity : (e + 1) * capacity],
+                        held[n % 2, e, g],
+                    )
+                    total = term if total is None else total + term
+                into[pl.ds(pl.multiple_of(i * tile, tile), tile), :] = total.astype(BF16)
+                return 0
+
+            lax.fori_loop(0, micro * steps, step, 0)
+
+        def make_pair(m):
+            d = order[m]
+            make(2 * m, give.at[d])
+            for q in range(cuts):
+                across(d, q).start()
+            make(2 * m + 1, acc.at[d])
+
+        for c in bring(0):
+            c.start()
+
+        def choose(i, _):
+            steps = group // tile
+            g, at_row = i // steps, pl.multiple_of((i % steps) * tile, tile)
+            for e in range(local):
+                slot = lax.broadcasted_iota(jnp.int32, (tile, capacity), 1)
+                hit = slot == place[g, pl.ds(at_row, tile), e : e + 1]
+                chosen[g, pl.ds(at_row, tile), e * capacity : (e + 1) * capacity] = jnp.where(
+                    hit, 1.0, 0.0
+                ).astype(BF16)
+            return 0
+
+        lax.fori_loop(0, micro * (group // tile), choose, 0)
+    else:
+        for d in order:
+            for q in range(cuts):
+                across(d, q).start()
+                fetch(d, q).start()
     for c in copies + own:
         c.start()
 
@@ -724,7 +760,8 @@
         lax.fori_loop(0, height // tile, step, 0)
 
     def ready(d, q):
-        fetch(d, q).wait()
+        if not local:
+            fetch(d, q).wait()
         across(d, q).wait_recv()
 
     def go_right(d, q):
@@ -755,15 +792,33 @@
 
         left(d, q).start()
 
+    if local:
+        for m in range(2):
+            make_pair(m)
+        for q in range(cuts):
+
+            @pl.when(pair == 0)
+            def _():
+                go_right(pairs - 1, q)
+
+            @pl.when(pair == pairs - 1)
+            def _():
+                go_left(0, q)
+
+        for m in range(2, pairs):
+            make_pair(m)
     for t in range(pairs - 1):
         far, near = pairs - 1 - t, t
+        go_far, go_near = far > pair, near < pair
+        if local and t == 0:
+            go_far, go_near = go_far & (pair > 0), go_near & (pair < pairs - 1)
         for q in range(cuts):
 
-            @pl.when(far > pair)
+            @pl.when(go_far)
             def _():
                 go_right(far, q)
 
-            @pl.when(near < pair)
+            @pl.when(go_near)
             def _():
                 go_left(near, q)
 
@@ -806,14 +861,27 @@
         c.wait()
 
 
-def scatter_col(x, ident, stage=0, others=()):
+def scatter_col(x, ident, stage=0, others=(), place=None):
     n_row, n_col = lax.axis_size("row"), lax.axis_size("col")
     pairs, per = n_col // 2, n_col // n_row
-    rows, part = x.shape[0], x.shape[1] // n_col
+    local = 0 if place is None else len(x)
+    if local:
+        micro, group, _ = place.shape
+        capacity = x[0].shape[1]
+        rows, part = micro * group, x[0].shape[2] // n_col
+    else:
+        rows, part = x.shape[0], x.shape[1] // n_col
     cuts = 4 if rows % 1024 == 0 else 1
     dma = pltpu.SemaphoreType.DMA
     buffer = pltpu.VMEM((pairs, rows, part), BF16)
     scratch = [buffer] * 4 + [dma((pairs, cuts))] * 7
+    if local:
+        scratch += [
+            buffer,
+            pltpu.VMEM((micro, group, local * capacity), BF16),
+            pltpu.VMEM((2, local, micro, capacity, part), BF16),
+            dma((2, local)),
+        ]
     out_shape = [jax.ShapeDtypeStruct((rows, part), F32)]
     if stage in (1, 2):
         extra = others[0]
@@ -830,9 +898,11 @@
             jax.ShapeDtypeStruct((n_col, 3, heads.shape[1] // n_col, heads.shape[2]), BF16),
             jax.ShapeDtypeStruct((n_col, branch.shape[0] // n_col, branch.shape[1]), BF16),
         ]
+    first = [pl.BlockSpec(memory_space=pltpu.VMEM)] + [ANY] * local if local else [ANY]
+    values = (place, *x) if local else (x,)
     return pl.pallas_call(
-        functools.partial(scatter_body, part, stage),
-        in_specs=[ANY] * (1 + len(others)),
+        functools.partial(scatter_body, part, stage, local),
+        in_specs=first + [ANY] * len(others),
         out_specs=[pl.BlockSpec(memory_space=pltpu.VMEM)] + [ANY] * (len(out_shape) - 1),
         out_shape=out_shape,
         scratch_shapes=scratch,
@@ -843,7 +913,7 @@
             flops=0, bytes_accessed=rows * part * n_col * 40, transcendentals=0
         ),
         name="scatter_col",
-    )(x, *others)
+    )(*values, *others)
 
 
 def shards(
@@ -888,7 +958,8 @@
         return lax.dynamic_slice_in_dim(value, col * size, size, axis)
 
     shared = w_down.shape[2]
-    big = [gather(pack(w_gate, w_up, w_down, e), "row", 1) for e in range(local_exp)]
+    packed = [pack(w_gate, w_up, w_down, e) for e in range(local_exp)]
+    big = [gather(p, "row", 1) for p in packed]
     inputs_low, gains, w_heads, rows_o, rows_r = front(
         tokens,
         jnp.stack([gain_attn, gain_ffn]),
@@ -904,6 +975,7 @@
     segment, position, live = jax.vmap(lambda l: layout(l, group))(lengths)
     position = position.reshape(rows)
     live = live.reshape(rows)
+    upstream_part = cotangent.astype(F32) * live[:, None]
     member = jnp.any(
         routes[:, None, :] == jnp.arange(experts, dtype=jnp.int32)[None, :, None], -1
     )
@@ -920,7 +992,8 @@
     inputs = inputs_low.astype(F32)
     scale_one = inverse_rms(inputs)
     normed = (inputs * scale_one * gains[0]).astype(BF16)
-    query_pre, key_pre, value_pre = (nn(normed, w_heads[j]) for j in range(3))
+    all_heads = jnp.concatenate([w_heads[j] for j in range(3)], 1)
+    query_pre, key_pre, value_pre = jnp.split(nn(normed, all_heads), 3, 1)
     shape = (rows, local_heads, head)
     cosine, sine = rope_tables(position, head)
 
@@ -947,7 +1020,9 @@
         "ghqk,gkhd->gqhd", probs_low, values_low, preferred_element_type=F32
     ).astype(BF16)
     attended_full, full_o, full_rt, upstream_low = middle_gather(
-        [attended.reshape(rows, local_heads * head), rows_o, rows_r, cotangent], (1, 0, 1, 1), 1
+        [attended.reshape(rows, local_heads * head), rows_o, rows_r, upstream_part.astype(BF16)],
+        (1, 0, 1, 1),
+        1,
     )
     full_r = full_rt.T
 
@@ -959,7 +1034,7 @@
     raised = jnp.where(member, jnp.exp(jnp.where(member, logits - peak, 0.0)), 0.0)
     gates = raised / jnp.sum(raised, -1, keepdims=True)
     gate_t = mine(gates, 1).reshape(micro, group, local_exp).transpose(2, 0, 1)[:, :, None, :]
-    upstream_full = (upstream_low * live[:, None].astype(BF16)).reshape(micro, group, width)
+    upstream_full = upstream_low.reshape(micro, group, width)
     hn = normed_ffn.reshape(micro, group, width)
 
     outs, weight_grads = [], []
@@ -980,7 +1055,7 @@
 
     row = lax.axis_index("row")
     back_sum, tok = scatter_col(
-        combine(place, [o[1] for o in outs]), 2, 1, (jnp.stack([o[2] for o in outs]),)
+        [o[1] for o in outs], 2, 1, (jnp.stack([o[2] for o in outs]),), place
     )
     back_sum = tie(back_sum, 0)
     tok = tok.reshape((experts,) + tok.shape[2:])
@@ -998,7 +1073,6 @@
     dot_two = jnp.sum(tok[:, :, 1].reshape(experts, rows), 0) + jnp.sum(
         logit_grad.astype(F32) * logits, 1
     )
-    upstream_part = cotangent.astype(F32) * live[:, None]
     hidden_grad = (
         upstream_part
         + scale_two * (normed_grad * gain_ffn)
@@ -1033,17 +1107,19 @@
     heads_grad = [
         v.reshape(flat).astype(BF16) for v in (query_grad, key_grad, values_grad)
     ]
-    back_heads = sum(nt(g, w_heads[j]) for j, g in enumerate(heads_grad))
+    all_grads = jnp.concatenate(heads_grad, 1)
+    back_heads = nt(all_grads, all_heads)
     pre = (query_pre, key_pre, value_pre)
     dot_part = sum(jnp.sum(g.astype(F32) * p, -1) for g, p in zip(heads_grad, pre))
     sums = jnp.concatenate([dot_part, gain_query_part, gain_key_part])
     sums = jnp.pad(sums, (0, -sums.shape[0] % 1024)).reshape(-1, 128)
-    heads_weights = jnp.stack([tn(normed, g) for g in heads_grad]).astype(BF16)
+    heads_weights = tn(normed, all_grads).astype(BF16)
+    heads_weights = jnp.stack(jnp.split(heads_weights, 3, 1))
     back_heads, mixed_slots = lax.optimization_barrier(
         (back_heads.astype(BF16), [o[0] for o in outs])
     )
     mixed_sum, heads_terms, out_terms = scatter_col(
-        combine(place, mixed_slots), 4, 3, (heads_weights, grad_out.astype(BF16))
+        mixed_slots, 4, 3, (heads_weights, grad_out.astype(BF16)), place
     )
     mixed = (hidden_part + mixed_sum).astype(BF16)
     back_heads, mixed = lax.optimization_barrier((back_heads, mixed))

time: 1210 us -> 1110 us (0.917)
  matrix products: 114 us -> 61.5 us
  Pallas kernels: 961 us -> 935 us
  other arithmetic: 58.6 us -> 38.7 us
    dot_general x5 -> x3, matrix products: 41.7 us -> 14.3 us  [nt(): lax.dot_general(a, b, (((1,), (1,)), ((), ())), preferred_element_type=F32)]
    pallas_call x6 -> x4, Pallas kernels: 394 us -> 374 us  [scatter_col(): pl.pallas_call(functools.partial(scatter_body, part, stage, local), in_sp...]
    dot_general x5 -> x3, matrix products: 34.5 us -> 20.5 us  [nn(): lax.dot_general(a, b, (((1,), (0,)), ((), ())), preferred_element_type=F32)]
  transfers between devices with their start and end apart: 8 -> 8, of which waited for: 0 -> 0; matrix products, arithmetic and copies ran while one was open for 16% -> 11% of each run, Pallas kernels for 80% -> 85%
where the time goes in v6:
time: 1110 us; the launch traced here: 1100 us
  Pallas kernels  935 us (84%)
  matrix products  61.5 us (6%)
  other arithmetic  38.7 us (3%)
  local copies, waits for them, and re-layouts  29.6 us (3%)
  between operations  15.7 us (1%)
  blocking collectives  14.4 us (1%)
    pallas_call x4, Pallas kernels, scatter_col(): pl.pallas_call(functools.partial(scatter_body, part, stage, local), in_sp...  374 us
    pallas_call x4, Pallas kernels, expert_pass(): pl.pallas_call(functools.partial(expert_body, shared), grid_spec=pltpu.Pr...  179 us
    pallas_call x1, Pallas kernels, middle_gather(): pl.pallas_call(functools.partial(middle_body, axes), in_specs=[ANY] * n,...  143 us
    pallas_call x1, Pallas kernels, front(): pl.pallas_call(front_body, in_specs=[ANY] * 7, out_specs=[ANY] * 8, out_s...  128 us
    pallas_call x4, Pallas kernels, expert_grads(): pl.pallas_call(grads_body, grid=(width // shared,), in_specs=[thin, whole...  77.2 us
  transfers between devices with their start and end apart: 8, of which 0 were waited for; matrix products, arithmetic and copies ran while one was open for 11% of the time, Pallas kernels for 85%

profile of v6, /device:TPU:0, one launch (start us, length us, event | category | flops | bytes accessed | tf_op | source)
XLA Modules:
  0.0 1095.1 jit_solution(5002902929245411866)
XLA Ops:
  7.2 3.7 pack.4
  11.0 3.7 pack.5
  14.8 3.7 pack.6
  18.6 4.1 pack.7
  23.3 0.8 fusion.16
  25.3 1.0 copy-done.2
  26.2 2.1 slice_reduce_fusion
  29.5 128.0 %front.1 = (bf16[2048,2048]{1,0:T(8,128)(2,1)}, f32[2,2048]{1,0:T(2,128)}, bf16[3,2048,128]{2,1,0:T(8,128)(2,1)}, bf16[128,2048]{1,0:T(8,128)(2,1)}, bf16[32,256...) custom-call(bf16[2048,256]{1,0:T(8,128)(2,1)} %tokens.1, ...), custom_call_target="tpu_custom_call" | custom-call | bytes 134217728 | tf_op jit(solution)/shard_map/front/pallas_call | solution.py:514
  157.5 5.2 fusion
  163.4 1.5 slice_bitcast_fusion.5
  164.9 4.0 fusion.8
  169.0 0.9 split.79
  169.8 2.5 copy.176
  173.5 2.7 fusion.56
  177.3 1.9 fusion.103
  179.3 1.2 exponential_reduce_fusion
  180.5 2.2 copy-done
  182.7 1.5 fusion.28
  184.2 1.0 copy.145
  185.2 1.3 fusion.15.refs_3_
  186.6 142.7 %middle_gather.1 = (bf16[2048,1024]{1,0:T(8,128)(2,1)}, bf16[1024,2048]{1,0:T(8,128)(2,1)}, bf16[32,2048]{1,0:T(8,128)(2,1)}, bf16[2048,2048]{1,0:T(8,128)(2,1)}) custom-call(bf16[2048,128]{1,0:T(8,128)(2,1)} %bitcast.251, bf16[128,2048]{1,0:T(8,128)(2,1)} %get-tuple-element.112.refs_1_, bf16[32,256]{1,0:T(8,128)(2,1)} %get-tuple-element.113.refs_2_, ...), custom_call_target="tpu_custom_call" | custom-call | bytes 270532608 | tf_op jit(solution)/shard_map/middle_gather/pallas_call | solution.py:551
  330.2 14.0 %multiply_reduce_fusion = (f32[2048]{0:T(1024)S(1)}, f32[2048,2048]{1,0:T(8,128)S(1)}) fusion(bf16[2048,1024]{1,0:T(8,128)(2,1)} %get-tuple-element.114, bf16[1024,2048]{1,0:T(8,128)(2,1)} %get-tuple-element.115, bf16[2048,2048]{1,0:T(8,128)(2,1)} %get-tuple-element.109), kind=kOutput, calls=%fused_computation.7 | convolution fusion | flops 8606709760 | bytes 33562624 | tf_op jit(solution)/shard_map/dot_general | solution.py:51
  344.8 2.3 multiply_convert_fusion
  347.1 2.8 copy-done.5
  349.9 2.6 select_reduce_fusion
  352.5 0.8 copy-done.1
  355.4 49.5 %expert_pass.4 = (bf16[2,512,2048]{2,1,0:T(8,128)(2,1)}, bf16[2,512,2048]{2,1,0:T(8,128)(2,1)}, bf16[2,512,1024]{2,1,0:T(8,128)(2,1)}, bf16[2,512,1024]{2,1,0:T(...) custom-call(s32[2]{0:T(128)} %get-tuple-element.224.counts, ...), custom_call_target="tpu_custom_call" | custom-call | flops 34359738368 | bytes 41943040 | tf_op jit(solution)/shard_map/expert_pass/pallas_call | solution.py:134
  405.0 19.1 %expert_grads.4 = bf16[3,2048,1024]{2,1,0:T(8,128)(2,1)} custom-call(bf16[1024,2048]{1,0:T(8,128)(2,1)} %bitcast.278, bf16[1024,1024]{1,0:T(8,128)(2,1)} %bitcast.288, bf16[1024,1024]{1,0:T(8,128)(2,1)} %bitcast.289, bf16[1024,1024]{1,0:T(8,128)(2,1)} %bitcast.287, bf16[1024,2048]{1,0:T(8,128)(2,1)} %bitcast.279), custom_call_target="tpu_custom_call" | custom-call | flops 12884901888 | bytes 27262976 | tf_op jit(solution)/shard_map/expert_grads/pallas_call | solution.py:177
  424.7 40.0 %expert_pass.5 = (bf16[2,512,2048]{2,1,0:T(8,128)(2,1)}, bf16[2,512,2048]{2,1,0:T(8,128)(2,1)}, bf16[2,512,1024]{2,1,0:T(8,128)(2,1)}, bf16[2,512,1024]{2,1,0:T(...) custom-call(s32[2]{0:T(128)} %get-tuple-element.223.counts, ...), custom_call_target="tpu_custom_call" | custom-call | flops 34359738368 | bytes 41943040 | tf_op jit(solution)/shard_map/expert_pass/pallas_call | solution.py:134
  464.7 19.6 %expert_grads.5 = bf16[3,2048,1024]{2,1,0:T(8,128)(2,1)} custom-call(bf16[1024,2048]{1,0:T(8,128)(2,1)} %bitcast.280, bf16[1024,1024]{1,0:T(8,128)(2,1)} %bitcast.291, bf16[1024,1024]{1,0:T(8,128)(2,1)} %bitcast.292, bf16[1024,1024]{1,0:T(8,128)(2,1)} %bitcast.290, bf16[1024,2048]{1,0:T(8,128)(2,1)} %bitcast.281), custom_call_target="tpu_custom_call" | custom-call | flops 12884901888 | bytes 27262976 | tf_op jit(solution)/shard_map/expert_grads/pallas_call | solution.py:177
  485.5 39.2 %expert_pass.6 = (bf16[2,512,2048]{2,1,0:T(8,128)(2,1)}, bf16[2,512,2048]{2,1,0:T(8,128)(2,1)}, bf16[2,512,1024]{2,1,0:T(8,128)(2,1)}, bf16[2,512,1024]{2,1,0:T(...) custom-call(s32[2]{0:T(128)} %get-tuple-element.222.counts, ...), custom_call_target="tpu_custom_call" | custom-call | flops 34359738368 | bytes 41943040 | tf_op jit(solution)/shard_map/expert_pass/pallas_call | solution.py:134
  524.8 19.1 %expert_grads.6 = bf16[3,2048,1024]{2,1,0:T(8,128)(2,1)} custom-call(bf16[1024,2048]{1,0:T(8,128)(2,1)} %bitcast.282, bf16[1024,1024]{1,0:T(8,128)(2,1)} %bitcast.294, bf16[1024,1024]{1,0:T(8,128)(2,1)} %bitcast.295, bf16[1024,1024]{1,0:T(8,128)(2,1)} %bitcast.293, bf16[1024,2048]{1,0:T(8,128)(2,1)} %bitcast.283), custom_call_target="tpu_custom_call" | custom-call | flops 12884901888 | bytes 27262976 | tf_op jit(solution)/shard_map/expert_grads/pallas_call | solution.py:177
  545.2 49.9 %expert_pass.7 = (bf16[2,512,2048]{2,1,0:T(8,128)(2,1)}, bf16[2,512,2048]{2,1,0:T(8,128)(2,1)}, bf16[2,512,1024]{2,1,0:T(8,128)(2,1)}, bf16[2,512,1024]{2,1,0:T(...) custom-call(s32[2]{0:T(128)} %get-tuple-element.221.counts, ...), custom_call_target="tpu_custom_call" | custom-call | flops 34359738368 | bytes 41943040 | tf_op jit(solution)/shard_map/expert_pass/pallas_call | solution.py:134
  595.1 19.5 %expert_grads.7 = bf16[3,2048,1024]{2,1,0:T(8,128)(2,1)} custom-call(bf16[1024,2048]{1,0:T(8,128)(2,1)} %bitcast.276, bf16[1024,1024]{1,0:T(8,128)(2,1)} %bitcast.285, bf16[1024,1024]{1,0:T(8,128)(2,1)} %bitcast.286, bf16[1024,1024]{1,0:T(8,128)(2,1)} %bitcast.284, bf16[1024,2048]{1,0:T(8,128)(2,1)} %bitcast.277), custom_call_target="tpu_custom_call" | custom-call | flops 12884901888 | bytes 27262976 | tf_op jit(solution)/shard_map/expert_grads/pallas_call | solution.py:177
  616.1 108.8 %scatter_col.4 = (f32[2048,256]{1,0:T(8,128)}, f32[8,4,2,2,1024]{4,3,2,1,0:T(2,128)}) custom-call(s32[2,1024,4]{2,1,0:T(8,128)} %copy-done.2, bf16[2,512,2048]{2,1,0:T(8,128)(2,1)} %get-tuple-element.126.refs_1_, bf16[2,512,2048]{2,1,0:T(8,128)(2,1)} %get-tuple-element.137.refs_2_, bf16[2,512,2048]{2,1,0:T(8,128)(2,1)} %get-tuple-element.148.refs_3_, ...), custom_call_target="tpu_custom_call" | custom-call | bytes 167772160 | tf_op jit(solution)/shard_map/scatter_col/pallas_call | solution.py:903
  724.9 2.4 slice_reduce_fusion.4
  727.5 1.6 convolution_bitcast_fusion
  729.2 3.0 multiply_reduce_fusion.2
  732.2 4.4 convolution_convert_fusion.1.refs_0_
  736.6 63.0 %scatter_col.5 = f32[2048,128]{1,0:T(8,128)} custom-call(bf16[2048,1024]{1,0:T(8,128)(2,1)} %convolution_convert_fusion.1.refs_0_), custom_call_target="tpu_custom_call" | custom-call | bytes 83886080 | tf_op jit(solution)/shard_map/scatter_col/pallas_call | solution.py:903
  799.6 1.3 convert_element_type.183
  800.9 5.3 fusion.29
  806.9 5.4 multiply_reduce_fusion.1
  813.0 2.5 multiply_convert_fusion.1
  815.6 1.1 fusion.27
  816.8 1.5 fusion.26
  818.5 2.4 fusion.65
  821.6 0.9 multiply_reduce_fusion.4
  823.1 7.0 convolution_convert_fusion.refs_0_
  830.2 5.5 convolution_convert_fusion.2
  836.0 1.3 pad_maximum_fusion.2.refs_5_
  837.3 1.2 copy-done.76
  838.4 2.1 convolution_convert_fusion.5.refs_6_
  840.6 115.6 %scatter_col.6 = (f32[2048,256]{1,0:T(8,128)}, bf16[8,3,256,128]{3,2,1,0:T(8,128)(2,1)}, bf16[8,128,256]{2,1,0:T(8,128)(2,1)}) custom-call(s32[2,1024,4]{2,1,0:T(8,128)} %copy-done.2, bf16[2,512,2048]{2,1,0:T(8,128)(2,1)} %get-tuple-element.173.refs_1_, bf16[2,512,2048]{2,1,0:T(8,128)(2,1)} %get-tuple-element.174.refs_2_, ...), custom_call_target="tpu_custom_call" | custom-call | bytes 167772160 | tf_op jit(solution)/shard_map/scatter_col/pallas_call | solution.py:903
  956.2 3.4 add_convert_fusion
  960.2 86.4 %scatter_col.7 = (f32[2048,256]{1,0:T(8,128)}, f32[8,24,128]{2,1,0:T(8,128)}, bf16[4,2,3,256,128]{4,3,2,1,0:T(8,128)(2,1)}, bf16[4,2,128,256]{3,2,1,0:T(8,128)(2,1)}) custom-call(bf16[2048,2048]{1,0:T(8,128)(2,1)} %convolution_convert_fusion.refs_0_, f32[24,128]{1,0:T(8,128)} %fusion.84.refs_1_, bf16[8,3,256,128]{3,2,1,0:T(8,128)(2,1)} %get-tuple-element.182.refs_2_, ...), custom_call_target="tpu_custom_call" | custom-call | bytes 167772160 | tf_op jit(solution)/shard_map/scatter_col/pallas_call | solution.py:903
  1046.6 0.9 reduce_sum.264
  1047.5 3.3 fusion.14
  1050.9 14.4 %psum.7 = f32[70,128]{1,0:T(8,128)S(1)} all-reduce(f32[70,128]{1,0:T(8,128)S(1)} %bitcast.258), channel_id=1, replica_groups=mesh['row'=4,'col'=8] {'row'}, use_global_device_ids=true, to_apply=%region_29.30 | all-reduce | flops 8960 | bytes 71680 | tf_op jit(solution)/shard_map/psum | solution.py:1158
  1065.3 4.7 unpack.4
  1070.0 4.7 unpack.5
  1074.7 4.9 unpack.6
  1081.3 0.9 fusion.77
  1083.3 4.7 unpack.7
  (251 shorter events, 21.0 us)
Async XLA Ops:
  7.2 348.2 %all-gather.5.cloned.1.call-start = ((), (), s32[]{:S(2)}) async-start(), calls=%async_computation.4 | async-start | bytes 15728640 | tf_op jit(solution)/shard_map/all_gather | solution.py:954
  11.0 413.7 %all-gather.7.cloned.1.call-start = ((), (), s32[]{:S(2)}) async-start(), calls=%async_computation.5 | async-start | bytes 15728640 | tf_op jit(solution)/shard_map/all_gather | solution.py:954
  14.7 470.8 %all-gather.9.cloned.1.call-start = ((), (), s32[]{:S(2)}) async-start(), calls=%async_computation.6 | async-start | bytes 15728640 | tf_op jit(solution)/shard_map/all_gather | solution.py:954
  18.5 4.3 copy-start.71
  18.5 4.8 copy-start.47
  18.6 526.6 %all-gather.11.cloned.1.call-start = ((), (), s32[]{:S(2)}) async-start(), calls=%async_computation.7 | async-start | bytes 15728640 | tf_op jit(solution)/shard_map/all_gather | solution.py:954
  22.8 706.4 %reduce-scatter.5.cloned.1.call-start = ((), (), s32[]{:S(2)}) async-start(), calls=%async_computation.8 | async-start | bytes 15728640 | tf_op jit(solution)/shard_map/reduce_scatter | solution.py:1050
  23.3 150.2 %copy-start.41 = (f32[1,8,2,128]{3,1,2,0:T(8,128)}, f32[1,8,2,128]{3,1,2,0:T(8,128)S(1)}, u32[]{:S(2)}) copy-start(f32[1,8,2,128]{3,1,2,0:T(8,128)S(1)} %copy.189) | copy-start | bytes 24580
  23.3 162.0 %copy-start.53 = (f32[1,8,2,128]{3,1,2,0:T(8,128)}, f32[1,8,2,128]{3,1,2,0:T(8,128)S(1)}, u32[]{:S(2)}) copy-start(f32[1,8,2,128]{3,1,2,0:T(8,128)S(1)} %copy.188) | copy-start | bytes 24580
  24.5 133.0 %copy-start.12 = (f32[2048,4]{1,0:T(8,128)}, f32[2048,4]{1,0:T(8,128)S(1)}, u32[]{:S(2)}) copy-start(f32[2048,4]{1,0:T(8,128)S(1)} %copy.146) | copy-start | bytes 98308
  24.5 4.4 copy-start.69
  24.5 4.4 copy-start.74
  157.5 5.9 copy-start.57
  157.5 7.4 copy-start.6
  163.4 5.5 copy-start.49
  163.4 5.5 copy-start.63
  164.9 4.0 copy-start.28
  164.9 4.0 copy-start.30
  164.9 4.0 copy-start.32
  168.9 4.5 copy-start.3
  168.9 4.2 copy-start.65
  169.0 4.2 copy-start.67
  172.4 3.8 copy-start.72
  172.6 3.6 copy-start.37
  173.2 3.0 copy-start.39
  176.5 2.8 copy-start.18
  179.3 3.4 copy-start
  179.3 3.4 copy-start.9
  180.5 3.7 copy-start.34
  184.2 145.1 %copy-start.13 = (f32[2048,4]{1,0:T(8,128)S(1)}, f32[2048,4]{1,0:T(8,128)}, u32[]{:S(2)}) copy-start(f32[2048,4]{1,0:T(8,128)} %copy-done.12) | copy-start | bytes 98308
  344.2 5.7 copy-start.5
  344.8 5.1 copy-start.51
  344.8 5.1 copy-start.36
  349.9 3.4 copy-start.1
  424.0 535.6 %reduce-scatter.7.cloned.1.call-start = ((), (), s32[]{:S(2)}) async-start(), calls=%async_computation.9 | async-start | bytes 15728640 | tf_op jit(solution)/shard_map/reduce_scatter | solution.py:1050
  484.3 590.5 %reduce-scatter.11.cloned.1.call-start = ((), (), s32[]{:S(2)}) async-start(), calls=%async_computation.11 | async-start | bytes 15728640 | tf_op jit(solution)/shard_map/reduce_scatter | solution.py:1050
  543.9 539.4 %reduce-scatter.9.cloned.1.call-start = ((), (), s32[]{:S(2)}) async-start(), calls=%async_computation.10 | async-start | bytes 15728640 | tf_op jit(solution)/shard_map/reduce_scatter | solution.py:1050
  616.0 111.3 %copy-start.15 = (f32[2048,32]{0,1:T(8,128)S(1)}, f32[2048,32]{0,1:T(8,128)}, u32[]{:S(2)}) copy-start(f32[2048,32]{0,1:T(8,128)} %copy-done.14) | copy-start | bytes 786436
  616.0 111.4 %copy-start.8 = (f32[2048,32]{0,1:T(8,128)S(1)}, f32[2048,32]{0,1:T(8,128)}, u32[]{:S(2)}) copy-start(f32[2048,32]{0,1:T(8,128)} %copy-done.7) | copy-start | bytes 786436
  616.0 113.1 %copy-start.26 = (bf16[2048,256]{1,0:T(8,128)(2,1)S(1)}, bf16[2048,256]{1,0:T(8,128)(2,1)}, u32[]{:S(2)}) copy-start(bf16[2048,256]{1,0:T(8,128)(2,1)} %param.31) | copy-start | bytes 3145732
  616.0 113.1 %copy-start.52 = (f32[2048]{0:T(1024)S(1)}, f32[2048]{0:T(1024)}, u32[]{:S(2)}) copy-start(f32[2048]{0:T(1024)} %copy-done.51) | copy-start | bytes 24580
  616.0 113.1 %copy-start.54 = (f32[1,8,2,128]{3,1,2,0:T(8,128)S(1)}, f32[1,8,2,128]{3,1,2,0:T(8,128)}, u32[]{:S(2)}) copy-start(f32[1,8,2,128]{3,1,2,0:T(8,128)} %copy-done.53) | copy-start | bytes 24580
  616.1 113.1 %copy-start.62 = (f32[2048]{0:T(1024)S(1)}, f32[2048]{0:T(1024)}, u32[]{:S(2)}) copy-start(f32[2048]{0:T(1024)} %get-tuple-element.272) | copy-start | bytes 24580
  616.1 113.1 %copy-start.75 = (f32[256]{0:T(256)S(1)}, f32[256]{0:T(256)}, u32[]{:S(2)}) copy-start(f32[256]{0:T(256)} %param.18) | copy-start | bytes 3076
  736.6 64.3 %copy-start.35 = (f32[2,1024]{1,0:T(2,128)S(1)}, f32[2,1024]{1,0:T(2,128)}, u32[]{:S(2)}) copy-start(f32[2,1024]{1,0:T(2,128)} %copy-done.34) | copy-start | bytes 24580
  800.9 6.0 copy-start.10
  806.7 5.6 slice-start
  806.9 6.2 slice-start.1
  818.3 2.6 copy-start.4
  818.3 2.6 copy-start.38
  818.3 2.6 copy-start.40
  818.3 2.6 copy-start.66
  818.4 3.2 copy-start.44
  818.4 3.2 copy-start.46
  821.6 8.5 slice-start.2
  823.1 7.0 slice-start.3
  823.1 7.0 copy-start.50
  823.1 7.0 copy-start.64
  835.7 2.8 copy-start.76
  960.2 87.3 %copy-start.11 = (bf16[2048,256]{1,0:T(8,128)(2,1)S(1)}, bf16[2048,256]{1,0:T(8,128)(2,1)}, u32[]{:S(2)}) copy-start(bf16[2048,256]{1,0:T(8,128)(2,1)} %tokens.1) | copy-start | bytes 3145732
  960.2 87.3 %copy-start.48 = (f32[2048]{0:T(1024)S(1)}, f32[2048]{0:T(1024)}, u32[]{:S(2)}) copy-start(f32[2048]{0:T(1024)} %get-tuple-element.270) | copy-start | bytes 24580
  960.2 87.3 %copy-start.70 = (f32[256]{0:T(256)S(1)}, f32[256]{0:T(256)}, u32[]{:S(2)}) copy-start(f32[256]{0:T(256)} %param.17) | copy-start | bytes 3076
  1074.7 5.5 copy-start.27
  1074.7 6.3 copy-start.24
  (25 other events, 34.5 us)
Sparse Core Ops, SparseCore 0:
  11.1 147.8 all-gather.4
  160.9 122.5 all-gather.6
  285.3 122.5 all-gather.8
  409.5 122.5 all-gather.10
  535.0 120.7 reduce-scatter.4
  658.7 120.7 reduce-scatter.6
  782.6 120.7 reduce-scatter.10
  906.5 142.1 reduce-scatter.8

commit v7 on v6

--- a/solution.py
+++ b/solution.py
@@ -60,52 +60,46 @@
 
 
 def expert_body(shared, counts, place, gate, hn, dy, w, xe_o, dyr_o, hg_o, dgp_o, dup_o, ye_o, dxe_o, tok_o):
-    g, i = pl.program_id(0), pl.program_id(1)
-    rows = xe_o.shape[1]
-    width, ff = w.shape[1:]
-    base = i * rows
-
-    @pl.when(i == 0)
-    def _():
-        tok_o[...] = jnp.zeros_like(tok_o)
-
-    @pl.when(counts[g] <= base)
-    def _():
+    g = pl.program_id(0)
+    full = xe_o.shape[1]
+    half = full // 2
+    width, ff = w.shape[2:]
+
+    def clear(low):
         for ref in (xe_o, dyr_o, hg_o, dgp_o, dup_o, ye_o, dxe_o):
-            ref[...] = jnp.zeros_like(ref)
-
-    @pl.when(counts[g] > base)
-    def _():
-        slot = lax.broadcasted_iota(jnp.int32, (rows, place.shape[2]), 0) + base
+            ref[0, low:] = jnp.zeros((full - low, ref.shape[2]), BF16)
+
+    def run(rows):
+        slot = lax.broadcasted_iota(jnp.int32, (rows, place.shape[2]), 0)
         hit = slot == place[0]
         pick = jnp.where(hit, 1.0, 0.0).astype(BF16)
         weight = jnp.sum(jnp.where(hit, gate[0], 0.0), 1, keepdims=True)
         xe = nn(pick, hn[0]).astype(BF16)
-        xe_o[0] = xe
-        gp = nn(xe, w[0])
-        up = nn(xe, w[1])
+        xe_o[0, :rows] = xe
+        gp = nn(xe, w[0, 0])
+        up = nn(xe, w[0, 1])
         sig = jax.nn.sigmoid(gp)
         silu = gp * sig
         hid = silu * up
         hg = (hid * weight).astype(BF16)
-        hg_o[0] = hg
+        hg_o[0, :rows] = hg
         dyr = nn(pick, dy[0]).astype(BF16)
-        dyr_o[0] = dyr
+        dyr_o[0, :rows] = dyr
         parts = []
         for r in range(width // shared):
             at = r * shared
             total = None
             for b in range(ff // shared):
                 low = b * shared
-                term = nn(hg[:, low : low + shared], w[2, at : at + shared, low : low + shared])
+                term = nn(hg[:, low : low + shared], w[0, 2, at : at + shared, low : low + shared])
                 total = term if total is None else total + term
-            ye_o[0, :, at : at + shared] = total.astype(BF16)
+            ye_o[0, :rows, at : at + shared] = total.astype(BF16)
         for b in range(ff // shared):
             low = b * shared
             total = None
             for r in range(width // shared):
                 at = r * shared
-                term = nt(dyr[:, at : at + shared], w[2, at : at + shared, low : low + shared])
+                term = nt(dyr[:, at : at + shared], w[0, 2, at : at + shared, low : low + shared])
                 total = term if total is None else total + term
             parts.append(total)
         back = jnp.concatenate(parts, 1)
@@ -113,37 +107,49 @@
         dhid = back * weight
         dgp = (dhid * up * sig * (1.0 + gp * (1.0 - sig))).astype(BF16)
         dup = (dhid * silu).astype(BF16)
-        dgp_o[0] = dgp
-        dup_o[0] = dup
+        dgp_o[0, :rows] = dgp
+        dup_o[0, :rows] = dup
         dots = jnp.sum(dgp.astype(F32) * gp + dup.astype(F32) * up, 1, keepdims=True)
-        dxe_o[0] = (nt(dgp, w[0]) + nt(dup, w[1])).astype(BF16)
-        tok_o[0, 0:1, :] += jnp.sum(jnp.where(hit, dgate, 0.0), 0, keepdims=True)
-        tok_o[0, 1:2, :] += jnp.sum(jnp.where(hit, dots, 0.0), 0, keepdims=True)
-
-
-def expert_pass(counts, place, gate, hn, dy, w, capacity, shared):
-    _, width, ff = w.shape
+        dxe_o[0, :rows] = (nt(dgp, w[0, 0]) + nt(dup, w[0, 1])).astype(BF16)
+        tok_o[0, 0:1, :] = jnp.sum(jnp.where(hit, dgate, 0.0), 0, keepdims=True)
+        tok_o[0, 1:2, :] = jnp.sum(jnp.where(hit, dots, 0.0), 0, keepdims=True)
+
+    @pl.when(counts[g] == 0)
+    def _():
+        clear(0)
+        tok_o[...] = jnp.zeros_like(tok_o)
+
+    @pl.when((counts[g] > 0) & (counts[g] <= half))
+    def _():
+        run(half)
+        clear(half)
+
+    @pl.when(counts[g] > half)
+    def _():
+        run(full)
+
+
+def expert_pass(counts, place, gate, hn, dy, w, at, capacity, shared):
+    width, ff = w.shape[2:]
     micro, group, _ = hn.shape
-    rows = min(256, capacity)
-    blocks = capacity // rows
-    tall = lambda g, i, c: (g, i, 0)
-    line = lambda g, i, c: (g, 0, 0)
+    line = lambda g, c: (g, 0, 0)
     slots = lambda n: jax.ShapeDtypeStruct((micro, capacity, n), BF16)
     sizes = (width, width, ff, ff, ff, width, width)
     flops = 2 * micro * capacity * width * (6 * ff + 2 * group)
+    once = pl.Buffered(1)
     return pl.pallas_call(
         functools.partial(expert_body, shared),
         grid_spec=pltpu.PrefetchScalarGridSpec(
             num_scalar_prefetch=1,
-            grid=(micro, blocks),
+            grid=(micro,),
             in_specs=[
                 pl.BlockSpec((1, 1, group), line),
                 pl.BlockSpec((1, 1, group), line),
-                pl.BlockSpec((1, group, width), line),
-                pl.BlockSpec((1, group, width), line),
-                pl.BlockSpec((3, width, ff), lambda g, i, c: (0, 0, 0), pipeline_mode=pl.Buffered(1)),
+                pl.BlockSpec((1, group, width), line, pipeline_mode=once),
+                pl.BlockSpec((1, group, width), line, pipeline_mode=once),
+                pl.BlockSpec((1, 3, width, ff), lambda g, c: (at, 0, 0, 0), pipeline_mode=once),
             ],
-            out_specs=[pl.BlockSpec((1, rows, n), tall) for n in sizes]
+            out_specs=[pl.BlockSpec((1, capacity, n), line, pipeline_mode=once) for n in sizes]
             + [pl.BlockSpec((1, 2, group), line)],
         ),
         out_shape=[slots(n) for n in sizes] + [jax.ShapeDtypeStruct((micro, 2, group), F32)],
@@ -155,18 +161,19 @@
     )(counts, place, gate, hn, dy, w)
 
 
-def grads_body(xe, dgp, dup, hg, dyr, out):
+def grads_body(xe, dgp, dup, hg, dyr, *rest):
+    out = rest[-1]
     part = xe[...]
     shared = part.shape[1]
-    out[0] = tn(part, dgp[...]).astype(BF16)
-    out[1] = tn(part, dup[...]).astype(BF16)
+    out[0, 0] = tn(part, dgp[...]).astype(BF16)
+    out[0, 1] = tn(part, dup[...]).astype(BF16)
     back = dyr[...]
     for b in range(hg.shape[1] // shared):
         low = b * shared
-        out[2, :, low : low + shared] = tn(hg[:, low : low + shared], back).astype(BF16)
-
-
-def expert_grads(xe, dgp, dup, hg, dyr, shared):
+        out[0, 2, :, low : low + shared] = tn(hg[:, low : low + shared], back).astype(BF16)
+
+
+def expert_grads(xe, dgp, dup, hg, dyr, shared, at, pair, held):
     micro, capacity, width = xe.shape
     ff = dgp.shape[2]
     rows = micro * capacity
@@ -177,37 +184,38 @@
     return pl.pallas_call(
         grads_body,
         grid=(width // shared,),
-        in_specs=[thin, whole, whole, whole, thin],
-        out_specs=pl.BlockSpec((3, shared, ff), lambda r: (0, r, 0)),
-        out_shape=jax.ShapeDtypeStruct((3, width, ff), BF16),
+        in_specs=[thin, whole, whole, whole, thin] + [ANY] * len(held),
+        out_specs=pl.BlockSpec((1, 3, shared, ff), lambda r: (at, 0, r, 0)),
+        out_shape=jax.ShapeDtypeStruct((pair, 3, width, ff), BF16),
+        input_output_aliases={5: 0} if held else {},
         compiler_params=pltpu.CompilerParams(vmem_limit_bytes=VMEM_LIMIT),
         cost_estimate=pl.CostEstimate(
             flops=6 * rows * width * ff, bytes_accessed=26 << 20, transcendentals=0
         ),
         name="expert_grads",
-    )(xe, dgp, dup, hg, dyr)
+    )(xe, dgp, dup, hg, dyr, *held)
 
 
 def pack_body(wg, wu, wd, out):
-    shared = out.shape[1]
-    out[0] = wg[0]
-    out[1] = wu[0]
-    for b in range(out.shape[2] // shared):
+    shared = out.shape[2]
+    out[0, 0] = wg[0]
+    out[0, 1] = wu[0]
+    for b in range(out.shape[3] // shared):
         low = b * shared
-        out[2, :, low : low + shared] = wd[0, low : low + shared, :]
-
-
-def pack(wg, wu, wd, e):
+        out[0, 2, :, low : low + shared] = wd[0, low : low + shared, :]
+
+
+def pack(wg, wu, wd, first, pair):
     _, shared, ff = wg.shape
-    block = pl.BlockSpec((1, shared, ff), lambda i: (e, 0, 0))
+    block = pl.BlockSpec((1, shared, ff), lambda i: (first + i, 0, 0))
     return pl.pallas_call(
         pack_body,
-        grid=(1,),
-        in_specs=[block, block, pl.BlockSpec((1, ff, shared), lambda i: (e, 0, 0))],
-        out_specs=pl.BlockSpec((3, shared, ff), lambda i: (0, 0, 0)),
-        out_shape=jax.ShapeDtypeStruct((3, shared, ff), BF16),
+        grid=(pair,),
+        in_specs=[block, block, pl.BlockSpec((1, ff, shared), lambda i: (first + i, 0, 0))],
+        out_specs=pl.BlockSpec((1, 3, shared, ff), lambda i: (i, 0, 0, 0)),
+        out_shape=jax.ShapeDtypeStruct((pair, 3, shared, ff), BF16),
         cost_estimate=pl.CostEstimate(
-            flops=0, bytes_accessed=12 * shared * ff, transcendentals=0
+            flops=0, bytes_accessed=pair * 12 * shared * ff, transcendentals=0
         ),
         name="pack",
     )(wg, wu, wd)
@@ -215,23 +223,22 @@
 
 def unpack_body(x, *refs):
     gg, gu, gd = refs[-3:]
-    shared = x.shape[1]
-    gg[0] = x[0].astype(F32)
-    gu[0] = x[1].astype(F32)
-    for b in range(x.shape[2] // shared):
+    shared = x.shape[2]
+    gg[0] = x[0, 0].astype(F32)
+    gu[0] = x[0, 1].astype(F32)
+    for b in range(x.shape[3] // shared):
         low = b * shared
-        gd[0, low : low + shared, :] = x[2, :, low : low + shared].astype(F32)
-
-
-def unpack(x, held, e, experts):
-    _, shared, ff = x.shape
-    block = pl.BlockSpec((1, shared, ff), lambda i: (e, 0, 0))
-    held = list(held)
+        gd[0, low : low + shared, :] = x[0, 2, :, low : low + shared].astype(F32)
+
+
+def unpack(x, held, first, experts):
+    pair, _, shared, ff = x.shape
+    block = pl.BlockSpec((1, shared, ff), lambda i: (first + i, 0, 0))
     return pl.pallas_call(
         unpack_body,
-        grid=(1,),
-        in_specs=[pl.BlockSpec((3, shared, ff), lambda i: (0, 0, 0))] + [ANY] * len(held),
-        out_specs=[block, block, pl.BlockSpec((1, ff, shared), lambda i: (e, 0, 0))],
+        grid=(pair,),
+        in_specs=[pl.BlockSpec((1, 3, shared, ff), lambda i: (i, 0, 0, 0))] + [ANY] * len(held),
+        out_specs=[block, block, pl.BlockSpec((1, ff, shared), lambda i: (first + i, 0, 0))],
         out_shape=[
             jax.ShapeDtypeStruct((experts, shared, ff), F32),
             jax.ShapeDtypeStruct((experts, shared, ff), F32),
@@ -240,7 +247,7 @@
         input_output_aliases={1 + j: j for j in range(len(held))},
         compiler_params=pltpu.CompilerParams(vmem_limit_bytes=VMEM_LIMIT),
         cost_estimate=pl.CostEstimate(
-            flops=0, bytes_accessed=18 * shared * ff, transcendentals=0
+            flops=0, bytes_accessed=pair * 18 * shared * ff, transcendentals=0
         ),
         name="unpack",
     )(x, *held)
@@ -529,7 +536,7 @@
             flops=0, bytes_accessed=rows * width * 32, transcendentals=0
         ),
         name="front",
-    )(tokens, gains, wq, wk, wv, wo, wr)[:5]
+    )(tokens, gains, wq, wk, wv, wo, wr)
 
 
 def middle_body(axes, *refs):
@@ -563,8 +570,8 @@
 
 
 def scatter_body(part, stage, local, *refs):
-    n_in = (1, 2, 4, 3)[stage]
-    n_out = (1, 2, 4, 3)[stage]
+    n_in = (1, 2, 4, 4)[stage]
+    n_out = (1, 2, 4, 4)[stage]
     if local:
         place, slots, refs = refs[0], refs[1 : 1 + local], refs[local:]
     x, ins = refs[0], refs[1:n_in]
@@ -624,18 +631,16 @@
         )
 
     copies, arrivals, own = [], [], []
-    if stage in (1, 2):
+    if stage:
         small_s, small_r, own_s = rest[11:14]
         extra, extra_o = ins[0], outs[0]
-        for k in range(1, n_col):
-            where, source = (col + k) % n_col, (col + n_col - k) % n_col
-            copies.append(
-                remote(extra, extra_o.at[col], small_s.at[k], small_r.at[k], (row, where))
-            )
-            arrivals.append(
-                remote(extra, extra_o.at[source], small_s.at[k], small_r.at[k], (row, where))
-            )
-        own.append(pltpu.make_async_copy(extra, extra_o.at[col], own_s))
+        here, ring = (row, n_row) if stage == 2 else (col, n_col)
+        for k in range(1, ring):
+            where, source = (here + k) % ring, (here + ring - k) % ring
+            to = (where, col) if stage == 2 else (row, where)
+            copies.append(remote(extra, extra_o.at[here], small_s.at[k], small_r.at[k], to))
+            arrivals.append(remote(extra, extra_o.at[source], small_s.at[k], small_r.at[k], to))
+        own.append(pltpu.make_async_copy(extra, extra_o.at[here], own_s))
     if stage == 2:
         give_s, give_r, keep_s = rest[14:]
         per = n_col // n_row
@@ -652,9 +657,9 @@
                 arrivals.append(remote(block_of(where), dst.at[source], *sems, (where, col)))
             own.append(pltpu.make_async_copy(block_of(row), dst.at[row], keep_s.at[m]))
     if stage == 3:
-        give_s, give_r, keep_s = rest[11:]
+        give_s, give_r, keep_s = rest[14:]
         for m in range(2):
-            src, dst = ins[m], outs[m]
+            src, dst = ins[1 + m], outs[1 + m]
             size = src.shape[1 - m] // n_col
 
             def block_for(c):
@@ -883,16 +888,16 @@
             dma((2, local)),
         ]
     out_shape = [jax.ShapeDtypeStruct((rows, part), F32)]
-    if stage in (1, 2):
-        extra = others[0]
-        out_shape.append(jax.ShapeDtypeStruct((n_col,) + extra.shape, extra.dtype))
-        scratch += [dma((n_col,)), dma((n_col,)), dma(())]
+    if stage:
+        extra, ring = others[0], n_row if stage == 2 else n_col
+        out_shape.append(jax.ShapeDtypeStruct((ring,) + extra.shape, extra.dtype))
+        scratch += [dma((ring,)), dma((ring,)), dma(())]
     if stage == 2:
         scratch += [dma((2, n_row)), dma((2, n_row)), dma((2,))]
         for value in others[1:]:
             out_shape.append(jax.ShapeDtypeStruct((n_row, per) + value.shape[1:], BF16))
     if stage == 3:
-        heads, branch = others
+        heads, branch = others[1:]
         scratch += [dma((2, n_col)), dma((2, n_col)), dma((2,))]
         out_shape += [
             jax.ShapeDtypeStruct((n_col, 3, heads.shape[1] // n_col, heads.shape[2]), BF16),
@@ -958,9 +963,11 @@
         return lax.dynamic_slice_in_dim(value, col * size, size, axis)
 
     shared = w_down.shape[2]
-    packed = [pack(w_gate, w_up, w_down, e) for e in range(local_exp)]
-    big = [gather(p, "row", 1) for p in packed]
-    inputs_low, gains, w_heads, rows_o, rows_r = front(
+    pair = 2 if local_exp % 2 == 0 else 1
+    big = [
+        gather(pack(w_gate, w_up, w_down, at, pair), "row", 2) for at in range(0, local_exp, pair)
+    ]
+    inputs_low, gains, w_heads, rows_o, rows_r, *wide = front(
         tokens,
         jnp.stack([gain_attn, gain_ffn]),
         w_query,
@@ -1037,17 +1044,27 @@
     upstream_full = upstream_low.reshape(micro, group, width)
     hn = normed_ffn.reshape(micro, group, width)
 
-    outs, weight_grads = [], []
+    outs, weight_grads, grad = [], [], None
     for e in range(local_exp):
         xe, dyr, hg, dgp, dup, ye, dxe, tok = expert_pass(
-            counts[e], place_t[e], gate_t[e], hn, upstream_full, big[e], capacity, shared
+            counts[e],
+            place_t[e],
+            gate_t[e],
+            hn,
+            upstream_full,
+            big[e // pair],
+            e % pair,
+            capacity,
+            shared,
         )
-        grad = expert_grads(xe, dgp, dup, hg, dyr, shared)
+        held = () if e % pair == 0 else (grad,)
+        grad = expert_grads(xe, dgp, dup, hg, dyr, shared, e % pair, pair, held)
         hn, upstream_full, ye, dxe, tok, grad = lax.optimization_barrier(
             (hn, upstream_full, ye, dxe, tok, grad)
         )
         outs.append((ye, dxe, tok))
-        weight_grads.append(lax.psum_scatter(grad, "row", scatter_dimension=1, tiled=True))
+        if e % pair == pair - 1:
+            weight_grads.append(lax.psum_scatter(grad, "row", scatter_dimension=2, tiled=True))
 
     def tie(value, e):
         value, weight_grads[e] = lax.optimization_barrier((value, weight_grads[e]))
@@ -1057,7 +1074,6 @@
     back_sum, tok = scatter_col(
         [o[1] for o in outs], 2, 1, (jnp.stack([o[2] for o in outs]),), place
     )
-    back_sum = tie(back_sum, 0)
     tok = tok.reshape((experts,) + tok.shape[2:])
     hidden_part = tokens.astype(F32) + nn(attended_full, mine(full_o, 1))
     gate_dots = tok[:, :, 0].reshape(experts, rows).T
@@ -1118,20 +1134,33 @@
     back_heads, mixed_slots = lax.optimization_barrier(
         (back_heads.astype(BF16), [o[0] for o in outs])
     )
-    mixed_sum, heads_terms, out_terms = scatter_col(
-        mixed_slots, 4, 3, (heads_weights, grad_out.astype(BF16)), place
+    mixed_sum, sums, heads_terms, out_terms = scatter_col(
+        mixed_slots, 4, 3, (sums, heads_weights, grad_out.astype(BF16)), place
     )
     mixed = (hidden_part + mixed_sum).astype(BF16)
-    back_heads, mixed = lax.optimization_barrier((back_heads, mixed))
-    normed_back, sums, heads_terms, out_terms = scatter_col(
-        tie(back_heads, 1), 5, 2, (sums, heads_terms, out_terms)
-    )
     sums = jnp.sum(sums, 0).reshape(-1)
     dot_one = sums[:rows]
-    gain_query_sum, gain_key_sum = sums[rows : rows + head], sums[rows + head : rows + 2 * head]
+    gain_attn_part = 0.0
+    for m in range(3):
+        for c in range(n_col):
+            columns = wide[m][:, c * local_heads * head : (c + 1) * local_heads * head]
+            gain_attn_part = gain_attn_part + jnp.sum(
+                columns.astype(F32) * heads_terms[c, m].astype(F32), -1
+            )
+    smalls = jnp.concatenate(
+        [
+            gain_attn_part,
+            grad_gain_ffn,
+            sums[rows : rows + 2 * head],
+            grad_router.T.reshape(-1),
+        ]
+    ).reshape(-1, 128)
+    back_heads, mixed = lax.optimization_barrier((back_heads, mixed))
+    normed_back, smalls, heads_terms, out_terms = scatter_col(
+        tie(back_heads, 0), 5, 2, (smalls, heads_terms, out_terms)
+    )
     scale_one_part = scale_one
     inputs_part = tokens.astype(F32)
-    grad_gain_attn = jnp.sum(normed_back * inputs_part * scale_one_part, 0)
     input_grad = (
         hidden_grad
         + scale_one_part * (normed_back * gain_attn)
@@ -1140,7 +1169,7 @@
 
     held = ()
     for e, grad in enumerate(weight_grads):
-        held = unpack(grad, held, e, local_exp)
+        held = unpack(grad, held, e * pair, local_exp)
     grad_gate, grad_up, grad_down = held
 
     heads_terms = jnp.sum(heads_terms.astype(F32), 0)
@@ -1148,15 +1177,9 @@
     grad_query, grad_key, grad_value = heads_sum[0], heads_sum[1], heads_sum[2]
     out_terms = jnp.sum(out_terms.astype(F32), 0)
     grad_out = jnp.concatenate([out_terms[j] for j in range(out_terms.shape[0])], -1)
-    smalls = [
-        grad_gain_attn,
-        grad_gain_ffn,
-        gain_query_sum,
-        gain_key_sum,
-        grad_router.T.reshape(-1),
-    ]
-    total = lax.psum(jnp.concatenate(smalls).reshape(-1, 128), "row").reshape(-1)
-    grad_gain_attn, grad_gain_ffn = total[:part], total[part : 2 * part]
+    row = lax.axis_index("row")
+    total = jnp.sum(smalls, 0).reshape(-1)
+    grad_gain_attn, grad_gain_ffn = total[:part] / gain_attn, total[part : 2 * part]
     grad_gain_query = total[2 * part : 2 * part + head]
     grad_gain_key = total[2 * part + head : 2 * part + 2 * head]
     grad_router = lax.dynamic_slice_in_dim(

time: 1110 us -> 1160 us (1.045); the launches traced: 1100 us -> 1160 us
  Pallas kernels: 935 us -> 1000 us
  blocking collectives: 14.4 us -> 0 us
    pallas_call x4, Pallas kernels: 374 us -> 422 us  [scatter_col(): pl.pallas_call(functools.partial(scatter_body, part, stage, local), in_sp...]
    pallas_call x4, Pallas kernels: 179 us -> 217 us  [expert_pass(): pl.pallas_call(functools.partial(expert_body, shared), grid_spec=pltpu.Pr...]
    psum x1 -> x0, blocking collectives: 14.4 us -> none  [shards(): lax.psum(jnp.concatenate(smalls).reshape(-1, 128), 'row').reshape(-1)]
    pallas_call x8 -> x4, Pallas kernels: 34.3 us -> 23 us  [the longest x2 13.5 us: unpack(): pl.pallas_call(unpack_body, grid=(pair,), in_specs=[pl.BlockSpec((1, 3, s...]
  transfers between devices with their start and end apart: 8 -> 4, of which waited for: 0 -> 0; matrix products, arithmetic and copies ran while one was open for 11% -> 11% of each run, Pallas kernels for 85% -> 86%
where the time goes in v7:
time: 1160 us
  Pallas kernels  1000 us (86%)
  matrix products  61.9 us (5%)
  other arithmetic  45.2 us (4%)
  local copies, waits for them, and re-layouts  29.4 us (3%)
  between operations  15.3 us (1%)
    pallas_call x4, Pallas kernels, scatter_col(): pl.pallas_call(functools.partial(scatter_body, part, stage, local), in_sp...  422 us
    pallas_call x4, Pallas kernels, expert_pass(): pl.pallas_call(functools.partial(expert_body, shared), grid_spec=pltpu.Pr...  217 us
    pallas_call x1, Pallas kernels, middle_gather(): pl.pallas_call(functools.partial(middle_body, axes), in_specs=[ANY] * n,...  143 us
    pallas_call x1, Pallas kernels, front(): pl.pallas_call(front_body, in_specs=[ANY] * 7, out_specs=[ANY] * 8, out_s...  123 us
    pallas_call x4, Pallas kernels, expert_grads(): pl.pallas_call(grads_body, grid=(width // shared,), in_specs=[thin, whole...  77 us
  transfers between devices with their start and end apart: 4, of which 0 were waited for; matrix products, arithmetic and copies ran while one was open for 11% of the time, Pallas kernels for 86%

profile of v7, /device:TPU:0, one launch (start us, length us, event | category | flops | bytes accessed | tf_op | source)
XLA Modules:
  0.0 1157.0 jit_solution(15522194891733918848)
XLA Ops:
  7.2 4.8 pack.2
  12.1 4.7 pack.3
  17.9 0.8 fusion.11
  19.9 1.0 copy-done.2
  20.9 2.1 slice_reduce_fusion
  24.7 123.3 %front.1 = (bf16[2048,2048]{1,0:T(8,128)(2,1)}, f32[2,2048]{1,0:T(2,128)}, bf16[3,2048,128]{2,1,0:T(8,128)(2,1)}, bf16[128,2048]{1,0:T(8,128)(2,1)}, bf16[32,256...) custom-call(bf16[2048,256]{1,0:T(8,128)(2,1)} %tokens.1, ...), custom_call_target="tpu_custom_call" | custom-call | bytes 134217728 | tf_op jit(solution)/shard_map/front/pallas_call | solution.py:521
  148.1 5.2 fusion
  154.0 1.5 slice_bitcast_fusion.5
  155.5 4.0 fusion.8
  159.5 0.9 split.79
  160.4 2.5 copy.172
  164.0 2.9 fusion.51
  168.1 1.9 fusion.123
  170.1 1.2 exponential_reduce_fusion
  171.2 2.2 copy-done
  173.4 1.5 fusion.23
  175.0 1.0 copy.141
  176.0 1.3 fusion.10.refs_3_
  177.3 142.7 %middle_gather.1 = (bf16[2048,1024]{1,0:T(8,128)(2,1)}, bf16[1024,2048]{1,0:T(8,128)(2,1)}, bf16[32,2048]{1,0:T(8,128)(2,1)}, bf16[2048,2048]{1,0:T(8,128)(2,1)}) custom-call(bf16[2048,128]{1,0:T(8,128)(2,1)} %bitcast.330, bf16[128,2048]{1,0:T(8,128)(2,1)} %get-tuple-element.108.refs_1_, bf16[32,256]{1,0:T(8,128)(2,1)} %get-tuple-element.109.refs_2_, ...), custom_call_target="tpu_custom_call" | custom-call | bytes 270532608 | tf_op jit(solution)/shard_map/middle_gather/pallas_call | solution.py:558
  320.2 0.7 slice_reduce_fusion.6
  320.9 13.5 %multiply_reduce_fusion = (f32[2048]{0:T(1024)S(1)}, f32[2048,2048]{1,0:T(8,128)S(1)}) fusion(bf16[2048,1024]{1,0:T(8,128)(2,1)} %get-tuple-element.110, bf16[1024,2048]{1,0:T(8,128)(2,1)} %get-tuple-element.111, bf16[2048,2048]{1,0:T(8,128)(2,1)} %get-tuple-element.105), kind=kOutput, calls=%fused_computation.7 | convolution fusion | flops 8606709760 | bytes 33562624 | tf_op jit(solution)/shard_map/dot_general | solution.py:51
  335.1 2.2 multiply_convert_fusion
  337.3 2.8 copy-done.5
  340.1 2.6 select_reduce_fusion
  342.7 0.8 copy-done.1
  345.7 56.7 %expert_pass.4 = (bf16[2,512,2048]{2,1,0:T(8,128)(2,1)}, bf16[2,512,2048]{2,1,0:T(8,128)(2,1)}, bf16[2,512,1024]{2,1,0:T(8,128)(2,1)}, bf16[2,512,1024]{2,1,0:T(...) custom-call(s32[2]{0:T(128)} %get-tuple-element.240.counts, ...), custom_call_target="tpu_custom_call" | custom-call | flops 34359738368 | bytes 41943040 | tf_op jit(solution)/shard_map/expert_pass/pallas_call | solution.py:140
  402.4 19.1 %expert_grads.4.rest_0_ = bf16[2,3,2048,1024]{3,2,1,0:T(8,128)(2,1)} custom-call(bf16[1024,2048]{1,0:T(8,128)(2,1)} %bitcast.354, bf16[1024,1024]{1,0:T(8,128)(2,1)} %bitcast.359, bf16[1024,1024]{1,0:T(8,128)(2,1)} %bitcast.360, bf16[1024,1024]{1,0:T(8,128)(2,1)} %bitcast.358, bf16[1024,2048]{1,0:T(8,128)(2,1)} %bitcast.355), custom_call_target="tpu_custom_call" | custom-call | flops 12884901888 | bytes 27262976 | tf_op jit(solution)/shard_map/expert_grads/pallas_call | solution.py:184
  421.5 64.3 %expert_pass.5 = (bf16[2,512,2048]{2,1,0:T(8,128)(2,1)}, bf16[2,512,2048]{2,1,0:T(8,128)(2,1)}, bf16[2,512,1024]{2,1,0:T(8,128)(2,1)}, bf16[2,512,1024]{2,1,0:T(...) custom-call(s32[2]{0:T(128)} %get-tuple-element.239.counts, ...), custom_call_target="tpu_custom_call" | custom-call | flops 34359738368 | bytes 41943040 | tf_op jit(solution)/shard_map/expert_pass/pallas_call | solution.py:140
  485.8 19.0 %expert_grads.5 = bf16[2,3,2048,1024]{3,2,1,0:T(8,128)(2,1)} custom-call(bf16[1024,2048]{1,0:T(8,128)(2,1)} %bitcast.305, bf16[1024,1024]{1,0:T(8,128)(2,1)} %bitcast.316, bf16[1024,1024]{1,0:T(8,128)(2,1)} %bitcast.317, bf16[1024,1024]{1,0:T(8,128)(2,1)} %bitcast.315, bf16[1024,2048]{1,0:T(8,128)(2,1)} %bitcast.306, ...), custom_call_target="tpu_custom_call", output_to_operand_aliasing={{}: (5, {})} | custom-call | flops 12884901888 | bytes 27262976 | tf_op jit(solution)/shard_map/expert_grads/pallas_call | solution.py:184
  506.8 39.9 %expert_pass.6 = (bf16[2,512,2048]{2,1,0:T(8,128)(2,1)}, bf16[2,512,2048]{2,1,0:T(8,128)(2,1)}, bf16[2,512,1024]{2,1,0:T(8,128)(2,1)}, bf16[2,512,1024]{2,1,0:T(...) custom-call(s32[2]{0:T(128)} %get-tuple-element.238.counts, ...), custom_call_target="tpu_custom_call" | custom-call | flops 34359738368 | bytes 41943040 | tf_op jit(solution)/shard_map/expert_pass/pallas_call | solution.py:140
  546.7 19.5 %expert_grads.6.rest_0_ = bf16[2,3,2048,1024]{3,2,1,0:T(8,128)(2,1)} custom-call(bf16[1024,2048]{1,0:T(8,128)(2,1)} %bitcast.356, bf16[1024,1024]{1,0:T(8,128)(2,1)} %bitcast.362, bf16[1024,1024]{1,0:T(8,128)(2,1)} %bitcast.363, bf16[1024,1024]{1,0:T(8,128)(2,1)} %bitcast.361, bf16[1024,2048]{1,0:T(8,128)(2,1)} %bitcast.357), custom_call_target="tpu_custom_call" | custom-call | flops 12884901888 | bytes 27262976 | tf_op jit(solution)/shard_map/expert_grads/pallas_call | solution.py:184
  566.2 56.1 %expert_pass.7 = (bf16[2,512,2048]{2,1,0:T(8,128)(2,1)}, bf16[2,512,2048]{2,1,0:T(8,128)(2,1)}, bf16[2,512,1024]{2,1,0:T(8,128)(2,1)}, bf16[2,512,1024]{2,1,0:T(...) custom-call(s32[2]{0:T(128)} %get-tuple-element.237.counts, ...), custom_call_target="tpu_custom_call" | custom-call | flops 34359738368 | bytes 41943040 | tf_op jit(solution)/shard_map/expert_pass/pallas_call | solution.py:140
  622.3 19.4 %expert_grads.7 = bf16[2,3,2048,1024]{3,2,1,0:T(8,128)(2,1)} custom-call(bf16[1024,2048]{1,0:T(8,128)(2,1)} %bitcast.303, bf16[1024,1024]{1,0:T(8,128)(2,1)} %bitcast.313, bf16[1024,1024]{1,0:T(8,128)(2,1)} %bitcast.314, bf16[1024,1024]{1,0:T(8,128)(2,1)} %bitcast.312, bf16[1024,2048]{1,0:T(8,128)(2,1)} %bitcast.304, ...), custom_call_target="tpu_custom_call", output_to_operand_aliasing={{}: (5, {})} | custom-call | flops 12884901888 | bytes 27262976 | tf_op jit(solution)/shard_map/expert_grads/pallas_call | solution.py:184
  643.2 157.4 %scatter_col.4 = (f32[2048,256]{1,0:T(8,128)}, f32[8,4,2,2,1024]{4,3,2,1,0:T(2,128)}) custom-call(s32[2,1024,4]{2,1,0:T(8,128)} %copy-done.2, bf16[2,512,2048]{2,1,0:T(8,128)(2,1)} %get-tuple-element.122.refs_1_, bf16[2,512,2048]{2,1,0:T(8,128)(2,1)} %get-tuple-element.134.refs_2_, bf16[2,512,2048]{2,1,0:T(8,128)(2,1)} %get-tuple-element.145.refs_3_, ...), custom_call_target="tpu_custom_call" | custom-call | bytes 167772160 | tf_op jit(solution)/shard_map/scatter_col/pallas_call | solution.py:908
  800.6 2.3 slice_reduce_fusion.4
  803.2 3.2 multiply_reduce_fusion.2
  806.4 4.4 convolution_convert_fusion.1.refs_0_
  810.9 62.1 %scatter_col.5 = f32[2048,128]{1,0:T(8,128)} custom-call(bf16[2048,1024]{1,0:T(8,128)(2,1)} %convolution_convert_fusion.1.refs_0_), custom_call_target="tpu_custom_call" | custom-call | bytes 83886080 | tf_op jit(solution)/shard_map/scatter_col/pallas_call | solution.py:908
  872.9 1.3 convert_element_type.399
  874.3 1.5 convolution_bitcast_fusion
  875.9 5.4 fusion.24
  881.9 5.5 multiply_reduce_fusion.1
  888.1 2.7 multiply_convert_fusion.1
  890.8 1.1 fusion.22
  892.0 1.5 fusion.21
  893.7 2.4 fusion.60
  896.9 0.8 multiply_reduce_fusion.4
  898.2 7.4 convolution_convert_fusion.refs_0_
  906.3 5.5 convolution_convert_fusion.2
  912.1 1.3 pad_maximum_fusion.2.refs_6_
  913.4 1.4 copy-done.79
  914.8 2.1 convolution_convert_fusion.5.refs_7_
  916.9 116.7 %scatter_col.6 = (f32[2048,256]{1,0:T(8,128)}, f32[8,24,128]{2,1,0:T(8,128)}, bf16[8,3,256,128]{3,2,1,0:T(8,128)(2,1)}, bf16[8,128,256]{2,1,0:T(8,128)(2,1)}) custom-call(s32[2,1024,4]{2,1,0:T(8,128)} %copy-done.2, bf16[2,512,2048]{2,1,0:T(8,128)(2,1)} %get-tuple-element.169.refs_1_, bf16[2,512,2048]{2,1,0:T(8,128)(2,1)} %get-tuple-element.170.refs_2_, ...), custom_call_target="tpu_custom_call" | custom-call | bytes 167772160 | tf_op jit(solution)/shard_map/scatter_col/pallas_call | solution.py:908
  1033.6 3.5 add_convert_fusion
  1037.1 1.6 fusion.85
  1038.8 1.4 fusion.100
  1040.2 1.4 fusion.93
  1042.3 85.6 %scatter_col.7 = (f32[2048,256]{1,0:T(8,128)}, f32[4,70,128]{2,1,0:T(8,128)}, bf16[4,2,3,256,128]{4,3,2,1,0:T(8,128)(2,1)}, bf16[4,2,128,256]{3,2,1,0:T(8,128)(2,1)}) custom-call(bf16[2048,2048]{1,0:T(8,128)(2,1)} %convolution_convert_fusion.refs_0_, f32[70,128]{1,0:T(8,128)} %maximum_bitcast_fusion.refs_1_, ...), custom_call_target="tpu_custom_call" | custom-call | bytes 167772160 | tf_op jit(solution)/shard_map/scatter_col/pallas_call | solution.py:908
  1127.9 1.0 reduce_sum.506
  1128.9 6.8 unpack.2
  1137.2 1.7 convert_reduce_fusion
  1139.0 0.9 fusion.72
  1141.5 2.0 multiply_subtract_fusion
  1143.5 6.8 unpack.3
  (242 shorter events, 20.8 us)
Async XLA Ops:
  7.2 338.5 %all-gather.3.cloned.1.call-start = ((), (), s32[]{:S(2)}) async-start(), calls=%async_computation.2 | async-start | bytes 31457280 | tf_op jit(solution)/shard_map/all_gather | solution.py:959
  12.0 494.7 %all-gather.5.cloned.1.call-start = ((), (), s32[]{:S(2)}) async-start(), calls=%async_computation.3 | async-start | bytes 31457280 | tf_op jit(solution)/shard_map/all_gather | solution.py:959
  16.8 1025.4 %reduce-scatter.3.cloned.1.call-start = ((), (), s32[]{:S(2)}) async-start(), calls=%async_computation.4 | async-start | bytes 31457280 | tf_op jit(solution)/shard_map/reduce_scatter | solution.py:1067
  17.9 146.1 %copy-start.44 = (f32[1,8,2,128]{3,1,2,0:T(8,128)}, f32[1,8,2,128]{3,1,2,0:T(8,128)S(1)}, u32[]{:S(2)}) copy-start(f32[1,8,2,128]{3,1,2,0:T(8,128)S(1)} %copy.185) | copy-start | bytes 24580
  17.9 158.1 %copy-start.56 = (f32[1,8,2,128]{3,1,2,0:T(8,128)}, f32[1,8,2,128]{3,1,2,0:T(8,128)S(1)}, u32[]{:S(2)}) copy-start(f32[1,8,2,128]{3,1,2,0:T(8,128)S(1)} %copy.184) | copy-start | bytes 24580
  19.2 128.9 %copy-start.12 = (f32[2048,4]{1,0:T(8,128)}, f32[2048,4]{1,0:T(8,128)S(1)}, u32[]{:S(2)}) copy-start(f32[2048,4]{1,0:T(8,128)S(1)} %copy.142) | copy-start | bytes 98308
  19.2 5.0 copy-start.65
  19.2 5.0 copy-start.77
  148.1 5.9 copy-start.60
  148.1 7.4 copy-start.6
  153.9 5.5 copy-start.52
  154.0 5.5 copy-start.68
  155.4 4.0 copy-start.30
  155.4 4.0 copy-start.32
  155.4 4.0 copy-start.34
  159.5 4.4 copy-start.3
  159.5 4.2 copy-start.70
  159.5 4.1 copy-start.72
  162.9 4.0 copy-start.75
  163.1 3.8 copy-start.39
  163.7 3.2 copy-start.41
  167.2 2.8 copy-start.19
  170.0 3.4 copy-start
  170.0 3.4 copy-start.9
  171.2 3.7 copy-start.36
  175.0 145.1 %copy-start.13 = (f32[2048,4]{1,0:T(8,128)S(1)}, f32[2048,4]{1,0:T(8,128)}, u32[]{:S(2)}) copy-start(f32[2048,4]{1,0:T(8,128)} %copy-done.12) | copy-start | bytes 98308
  334.4 5.7 copy-start.5
  335.1 5.0 copy-start.54
  335.1 5.0 copy-start.38
  340.1 3.4 copy-start.1
  504.9 638.6 %reduce-scatter.5.cloned.1.call-start = ((), (), s32[]{:S(2)}) async-start(), calls=%async_computation.5 | async-start | bytes 31457280 | tf_op jit(solution)/shard_map/reduce_scatter | solution.py:1067
  643.2 159.9 %copy-start.15 = (f32[2048,32]{0,1:T(8,128)S(1)}, f32[2048,32]{0,1:T(8,128)}, u32[]{:S(2)}) copy-start(f32[2048,32]{0,1:T(8,128)} %copy-done.14) | copy-start | bytes 786436
  643.2 159.9 %copy-start.8 = (f32[2048,32]{0,1:T(8,128)S(1)}, f32[2048,32]{0,1:T(8,128)}, u32[]{:S(2)}) copy-start(f32[2048,32]{0,1:T(8,128)} %copy-done.7) | copy-start | bytes 786436
  643.2 160.0 %copy-start.26 = (bf16[2048,256]{1,0:T(8,128)(2,1)S(1)}, bf16[2048,256]{1,0:T(8,128)(2,1)}, u32[]{:S(2)}) copy-start(bf16[2048,256]{1,0:T(8,128)(2,1)} %param.31) | copy-start | bytes 3145732
  643.2 160.0 %copy-start.55 = (f32[2048]{0:T(1024)S(1)}, f32[2048]{0:T(1024)}, u32[]{:S(2)}) copy-start(f32[2048]{0:T(1024)} %copy-done.54) | copy-start | bytes 24580
  643.2 160.0 %copy-start.57 = (f32[1,8,2,128]{3,1,2,0:T(8,128)S(1)}, f32[1,8,2,128]{3,1,2,0:T(8,128)}, u32[]{:S(2)}) copy-start(f32[1,8,2,128]{3,1,2,0:T(8,128)} %copy-done.56) | copy-start | bytes 24580
  643.2 160.0 %copy-start.67 = (f32[2048]{0:T(1024)S(1)}, f32[2048]{0:T(1024)}, u32[]{:S(2)}) copy-start(f32[2048]{0:T(1024)} %get-tuple-element.284) | copy-start | bytes 24580
  643.2 160.0 %copy-start.78 = (f32[256]{0:T(256)S(1)}, f32[256]{0:T(256)}, u32[]{:S(2)}) copy-start(f32[256]{0:T(256)} %param.18) | copy-start | bytes 3076
  810.8 65.0 %copy-start.37 = (f32[2,1024]{1,0:T(2,128)S(1)}, f32[2,1024]{1,0:T(2,128)}, u32[]{:S(2)}) copy-start(f32[2,1024]{1,0:T(2,128)} %copy-done.36) | copy-start | bytes 24580
  875.8 6.1 copy-start.10
  881.8 5.6 slice-start
  881.9 6.2 slice-start.1
  888.1 2.7 copy-start.20
  888.1 2.7 copy-start.22
  893.5 2.6 copy-start.4
  893.6 2.6 copy-start.40
  893.6 2.6 copy-start.42
  893.6 2.6 copy-start.71
  893.6 2.6 copy-start.73
  893.7 3.2 copy-start.47
  893.7 3.2 copy-start.49
  896.9 9.3 slice-start.2
  898.2 8.0 slice-start.3
  898.2 8.0 copy-start.53
  898.2 8.0 copy-start.69
  911.8 3.0 copy-start.79
  1033.6 3.5 copy-start.43
  1033.6 5.2 copy-start.29
  1033.6 6.6 copy-start.28
  1127.9 8.4 copy-start.27
  1135.7 5.2 copy-start.66
  1135.7 5.8 copy-start.11
  1135.7 5.8 copy-start.16
  1135.7 5.8 copy-start.51
  (24 other events, 28.9 us)
Sparse Core Ops, SparseCore 0:
  12.2 250.7 all-gather.2
  264.8 227.6 all-gather.4
  505.0 245.6 reduce-scatter.2
  754.0 221.8 reduce-scatter.4

commit v8 on v7

--- a/solution.py
+++ b/solution.py
@@ -60,31 +60,37 @@
 
 
 def expert_body(shared, counts, place, gate, hn, dy, w, xe_o, dyr_o, hg_o, dgp_o, dup_o, ye_o, dxe_o, tok_o):
-    g = pl.program_id(0)
-    full = xe_o.shape[1]
-    half = full // 2
+    g, i = pl.program_id(0), pl.program_id(1)
+    rows = xe_o.shape[1]
     width, ff = w.shape[2:]
-
-    def clear(low):
+    base = i * rows
+
+    @pl.when(i == 0)
+    def _():
+        tok_o[...] = jnp.zeros_like(tok_o)
+
+    @pl.when(counts[g] <= base)
+    def _():
         for ref in (xe_o, dyr_o, hg_o, dgp_o, dup_o, ye_o, dxe_o):
-            ref[0, low:] = jnp.zeros((full - low, ref.shape[2]), BF16)
-
-    def run(rows):
-        slot = lax.broadcasted_iota(jnp.int32, (rows, place.shape[2]), 0)
+            ref[...] = jnp.zeros_like(ref)
+
+    @pl.when(counts[g] > base)
+    def _():
+        slot = lax.broadcasted_iota(jnp.int32, (rows, place.shape[2]), 0) + base
         hit = slot == place[0]
         pick = jnp.where(hit, 1.0, 0.0).astype(BF16)
         weight = jnp.sum(jnp.where(hit, gate[0], 0.0), 1, keepdims=True)
         xe = nn(pick, hn[0]).astype(BF16)
-        xe_o[0, :rows] = xe
+        xe_o[0] = xe
         gp = nn(xe, w[0, 0])
         up = nn(xe, w[0, 1])
         sig = jax.nn.sigmoid(gp)
         silu = gp * sig
         hid = silu * up
         hg = (hid * weight).astype(BF16)
-        hg_o[0, :rows] = hg
+        hg_o[0] = hg
         dyr = nn(pick, dy[0]).astype(BF16)
-        dyr_o[0, :rows] = dyr
+        dyr_o[0] = dyr
         parts = []
         for r in range(width // shared):
             at = r * shared
@@ -93,7 +99,7 @@
                 low = b * shared
                 term = nn(hg[:, low : low + shared], w[0, 2, at : at + shared, low : low + shared])
                 total = term if total is None else total + term
-            ye_o[0, :rows, at : at + shared] = total.astype(BF16)
+            ye_o[0, :, at : at + shared] = total.astype(BF16)
         for b in range(ff // shared):
             low = b * shared
             total = None
@@ -107,49 +113,39 @@
         dhid = back * weight
         dgp = (dhid * up * sig * (1.0 + gp * (1.0 - sig))).astype(BF16)
         dup = (dhid * silu).astype(BF16)
-        dgp_o[0, :rows] = dgp
-        dup_o[0, :rows] = dup
+        dgp_o[0] = dgp
+        dup_o[0] = dup
         dots = jnp.sum(dgp.astype(F32) * gp + dup.astype(F32) * up, 1, keepdims=True)
-        dxe_o[0, :rows] = (nt(dgp, w[0, 0]) + nt(dup, w[0, 1])).astype(BF16)
-        tok_o[0, 0:1, :] = jnp.sum(jnp.where(hit, dgate, 0.0), 0, keepdims=True)
-        tok_o[0, 1:2, :] = jnp.sum(jnp.where(hit, dots, 0.0), 0, keepdims=True)
-
-    @pl.when(counts[g] == 0)
-    def _():
-        clear(0)
-        tok_o[...] = jnp.zeros_like(tok_o)
-
-    @pl.when((counts[g] > 0) & (counts[g] <= half))
-    def _():
-        run(half)
-        clear(half)
-
-    @pl.when(counts[g] > half)
-    def _():
-        run(full)
+        dxe_o[0] = (nt(dgp, w[0, 0]) + nt(dup, w[0, 1])).astype(BF16)
+        tok_o[0, 0:1, :] += jnp.sum(jnp.where(hit, dgate, 0.0), 0, keepdims=True)
+        tok_o[0, 1:2, :] += jnp.sum(jnp.where(hit, dots, 0.0), 0, keepdims=True)
 
 
 def expert_pass(counts, place, gate, hn, dy, w, at, capacity, shared):
     width, ff = w.shape[2:]
     micro, group, _ = hn.shape
-    line = lambda g, c: (g, 0, 0)
+    rows = min(256, capacity)
+    blocks = capacity // rows
+    tall = lambda g, i, c: (g, i, 0)
+    line = lambda g, i, c: (g, 0, 0)
     slots = lambda n: jax.ShapeDtypeStruct((micro, capacity, n), BF16)
     sizes = (width, width, ff, ff, ff, width, width)
     flops = 2 * micro * capacity * width * (6 * ff + 2 * group)
-    once = pl.Buffered(1)
     return pl.pallas_call(
         functools.partial(expert_body, shared),
         grid_spec=pltpu.PrefetchScalarGridSpec(
             num_scalar_prefetch=1,
-            grid=(micro,),
+            grid=(micro, blocks),
             in_specs=[
                 pl.BlockSpec((1, 1, group), line),
                 pl.BlockSpec((1, 1, group), line),
-                pl.BlockSpec((1, group, width), line, pipeline_mode=once),
-                pl.BlockSpec((1, group, width), line, pipeline_mode=once),
-                pl.BlockSpec((1, 3, width, ff), lambda g, c: (at, 0, 0, 0), pipeline_mode=once),
+                pl.BlockSpec((1, group, width), line),
+                pl.BlockSpec((1, group, width), line),
+                pl.BlockSpec(
+                    (1, 3, width, ff), lambda g, i, c: (at, 0, 0, 0), pipeline_mode=pl.Buffered(1)
+                ),
             ],
-            out_specs=[pl.BlockSpec((1, capacity, n), line, pipeline_mode=once) for n in sizes]
+            out_specs=[pl.BlockSpec((1, rows, n), tall) for n in sizes]
             + [pl.BlockSpec((1, 2, group), line)],
         ),
         out_shape=[slots(n) for n in sizes] + [jax.ShapeDtypeStruct((micro, 2, group), F32)],

time: 1160 us -> 1100 us (0.948); the launches traced: 1160 us -> 1080 us
  Pallas kernels: 1000 us -> 899 us
  waiting for transfers between devices: 0.07 us -> 26.2 us
    pallas_call x4, Pallas kernels: 422 us -> 362 us  [scatter_col(): pl.pallas_call(functools.partial(scatter_body, part, stage, local), in_sp...]
    pallas_call x4, Pallas kernels: 217 us -> 171 us  [expert_pass(): pl.pallas_call(functools.partial(expert_body, shared), grid_spec=pltpu.Pr...]
    all_gather x2, waiting for transfers between devices: 0.01 us -> 26.1 us  [gather(): return lax.all_gather(value, axis_name, axis=axis, tiled=True)]
  transfers between devices with their start and end apart: 4 -> 4, of which waited for: 0 -> 1; matrix products, arithmetic and copies ran while one was open for 11% -> 11% of each run, Pallas kernels for 86% -> 82%
where the time goes in v8:
time: 1100 us; the launch traced here: 1080 us
  Pallas kernels  899 us (82%)
  matrix products  61.7 us (6%)
  other arithmetic  44.7 us (4%)
  local copies, waits for them, and re-layouts  29.5 us (3%)
  waiting for transfers between devices  26.2 us (2%)
  between operations  15.3 us (1%)
    pallas_call x4, Pallas kernels, scatter_col(): pl.pallas_call(functools.partial(scatter_body, part, stage, local), in_sp...  362 us
    pallas_call x4, Pallas kernels, expert_pass(): pl.pallas_call(functools.partial(expert_body, shared), grid_spec=pltpu.Pr...  171 us
    pallas_call x1, Pallas kernels, middle_gather(): pl.pallas_call(functools.partial(middle_body, axes), in_specs=[ANY] * n,...  143 us
    pallas_call x1, Pallas kernels, front(): pl.pallas_call(front_body, in_specs=[ANY] * 7, out_specs=[ANY] * 8, out_s...  123 us
    pallas_call x4, Pallas kernels, expert_grads(): pl.pallas_call(grads_body, grid=(width // shared,), in_specs=[thin, whole...  77 us
    all_gather x2, waiting for transfers between devices, gather(): return lax.all_gather(value, axis_name, axis=axis, tiled=True)  26.1 us
  transfers between devices with their start and end apart: 4, of which 1 were waited for; matrix products, arithmetic and copies ran while one was open for 11% of the time, Pallas kernels for 82%

profile of v8, /device:TPU:0, one launch (start us, length us, event | category | flops | bytes accessed | tf_op | source)
XLA Modules:
  0.0 1076.6 jit_solution(18027704866707001641)
XLA Ops:
  7.2 4.8 pack.2
  12.1 4.7 pack.3
  17.9 0.8 fusion.11
  19.9 1.0 copy-done.2
  20.9 2.1 slice_reduce_fusion
  24.7 123.3 %front.1 = (bf16[2048,2048]{1,0:T(8,128)(2,1)}, f32[2,2048]{1,0:T(2,128)}, bf16[3,2048,128]{2,1,0:T(8,128)(2,1)}, bf16[128,2048]{1,0:T(8,128)(2,1)}, bf16[32,256...) custom-call(bf16[2048,256]{1,0:T(8,128)(2,1)} %tokens.1, ...), custom_call_target="tpu_custom_call" | custom-call | bytes 134217728 | tf_op jit(solution)/shard_map/front/pallas_call | solution.py:517
  148.0 5.2 fusion
  153.9 1.5 slice_bitcast_fusion.5
  155.4 4.0 fusion.8
  159.5 0.9 split.79
  160.3 2.5 copy.172
  163.9 2.7 fusion.51
  167.8 1.9 fusion.123
  169.8 1.2 exponential_reduce_fusion
  171.0 2.2 copy-done
  173.2 1.5 fusion.23
  174.7 1.0 copy.141
  175.7 1.3 fusion.10.refs_3_
  177.0 142.7 %middle_gather.1 = (bf16[2048,1024]{1,0:T(8,128)(2,1)}, bf16[1024,2048]{1,0:T(8,128)(2,1)}, bf16[32,2048]{1,0:T(8,128)(2,1)}, bf16[2048,2048]{1,0:T(8,128)(2,1)}) custom-call(bf16[2048,128]{1,0:T(8,128)(2,1)} %bitcast.330, bf16[128,2048]{1,0:T(8,128)(2,1)} %get-tuple-element.108.refs_1_, bf16[32,256]{1,0:T(8,128)(2,1)} %get-tuple-element.109.refs_2_, ...), custom_call_target="tpu_custom_call" | custom-call | bytes 270532608 | tf_op jit(solution)/shard_map/middle_gather/pallas_call | solution.py:554
  320.6 13.8 %multiply_reduce_fusion = (f32[2048]{0:T(1024)S(1)}, f32[2048,2048]{1,0:T(8,128)S(1)}) fusion(bf16[2048,1024]{1,0:T(8,128)(2,1)} %get-tuple-element.110, bf16[1024,2048]{1,0:T(8,128)(2,1)} %get-tuple-element.111, bf16[2048,2048]{1,0:T(8,128)(2,1)} %get-tuple-element.105), kind=kOutput, calls=%fused_computation.7 | convolution fusion | flops 8606709760 | bytes 33562624 | tf_op jit(solution)/shard_map/dot_general | solution.py:51
  335.1 2.2 multiply_convert_fusion
  337.3 2.8 copy-done.5
  340.1 2.6 select_reduce_fusion
  342.7 0.8 copy-done.1
  345.7 41.8 %expert_pass.4 = (bf16[2,512,2048]{2,1,0:T(8,128)(2,1)}, bf16[2,512,2048]{2,1,0:T(8,128)(2,1)}, bf16[2,512,1024]{2,1,0:T(8,128)(2,1)}, bf16[2,512,1024]{2,1,0:T(...) custom-call(s32[2]{0:T(128)} %get-tuple-element.240.counts, ...), custom_call_target="tpu_custom_call" | custom-call | flops 34359738368 | bytes 41943040 | tf_op jit(solution)/shard_map/expert_pass/pallas_call | solution.py:134
  387.5 19.1 %expert_grads.4.rest_0_ = bf16[2,3,2048,1024]{3,2,1,0:T(8,128)(2,1)} custom-call(bf16[1024,2048]{1,0:T(8,128)(2,1)} %bitcast.354, bf16[1024,1024]{1,0:T(8,128)(2,1)} %bitcast.359, bf16[1024,1024]{1,0:T(8,128)(2,1)} %bitcast.360, bf16[1024,1024]{1,0:T(8,128)(2,1)} %bitcast.358, bf16[1024,2048]{1,0:T(8,128)(2,1)} %bitcast.355), custom_call_target="tpu_custom_call" | custom-call | flops 12884901888 | bytes 27262976 | tf_op jit(solution)/shard_map/expert_grads/pallas_call | solution.py:180
  406.5 39.0 %expert_pass.5 = (bf16[2,512,2048]{2,1,0:T(8,128)(2,1)}, bf16[2,512,2048]{2,1,0:T(8,128)(2,1)}, bf16[2,512,1024]{2,1,0:T(8,128)(2,1)}, bf16[2,512,1024]{2,1,0:T(...) custom-call(s32[2]{0:T(128)} %get-tuple-element.239.counts, ...), custom_call_target="tpu_custom_call" | custom-call | flops 34359738368 | bytes 41943040 | tf_op jit(solution)/shard_map/expert_pass/pallas_call | solution.py:134
  445.5 19.0 %expert_grads.5 = bf16[2,3,2048,1024]{3,2,1,0:T(8,128)(2,1)} custom-call(bf16[1024,2048]{1,0:T(8,128)(2,1)} %bitcast.305, bf16[1024,1024]{1,0:T(8,128)(2,1)} %bitcast.316, bf16[1024,1024]{1,0:T(8,128)(2,1)} %bitcast.317, bf16[1024,1024]{1,0:T(8,128)(2,1)} %bitcast.315, bf16[1024,2048]{1,0:T(8,128)(2,1)} %bitcast.306, ...), custom_call_target="tpu_custom_call", output_to_operand_aliasing={{}: (5, {})} | custom-call | flops 12884901888 | bytes 27262976 | tf_op jit(solution)/shard_map/expert_grads/pallas_call | solution.py:180
  466.5 26.1 %all-gather.5.cloned.1.call-done.w = bf16[2,3,2048,1024]{3,2,1,0:T(8,128)(2,1)} async-done(((bf16[2,3,512,1024]{3,2,1,0:T(8,128)(2,1)}), bf16[2,3,2048,1024]{3,2,1,0:T(8,128)(2,1)}) %all-gather.5.cloned.1.call-update) | async-done | bytes 25165840 | tf_op jit(solution)/shard_map/all_gather | solution.py:955
  492.6 49.5 %expert_pass.6 = (bf16[2,512,2048]{2,1,0:T(8,128)(2,1)}, bf16[2,512,2048]{2,1,0:T(8,128)(2,1)}, bf16[2,512,1024]{2,1,0:T(8,128)(2,1)}, bf16[2,512,1024]{2,1,0:T(...) custom-call(s32[2]{0:T(128)} %get-tuple-element.238.counts, ...), custom_call_target="tpu_custom_call" | custom-call | flops 34359738368 | bytes 41943040 | tf_op jit(solution)/shard_map/expert_pass/pallas_call | solution.py:134
  542.1 19.6 %expert_grads.6.rest_0_ = bf16[2,3,2048,1024]{3,2,1,0:T(8,128)(2,1)} custom-call(bf16[1024,2048]{1,0:T(8,128)(2,1)} %bitcast.356, bf16[1024,1024]{1,0:T(8,128)(2,1)} %bitcast.362, bf16[1024,1024]{1,0:T(8,128)(2,1)} %bitcast.363, bf16[1024,1024]{1,0:T(8,128)(2,1)} %bitcast.361, bf16[1024,2048]{1,0:T(8,128)(2,1)} %bitcast.357), custom_call_target="tpu_custom_call" | custom-call | flops 12884901888 | bytes 27262976 | tf_op jit(solution)/shard_map/expert_grads/pallas_call | solution.py:180
  561.7 40.3 %expert_pass.7 = (bf16[2,512,2048]{2,1,0:T(8,128)(2,1)}, bf16[2,512,2048]{2,1,0:T(8,128)(2,1)}, bf16[2,512,1024]{2,1,0:T(8,128)(2,1)}, bf16[2,512,1024]{2,1,0:T(...) custom-call(s32[2]{0:T(128)} %get-tuple-element.237.counts, ...), custom_call_target="tpu_custom_call" | custom-call | flops 34359738368 | bytes 41943040 | tf_op jit(solution)/shard_map/expert_pass/pallas_call | solution.py:134
  602.0 19.4 %expert_grads.7 = bf16[2,3,2048,1024]{3,2,1,0:T(8,128)(2,1)} custom-call(bf16[1024,2048]{1,0:T(8,128)(2,1)} %bitcast.303, bf16[1024,1024]{1,0:T(8,128)(2,1)} %bitcast.313, bf16[1024,1024]{1,0:T(8,128)(2,1)} %bitcast.314, bf16[1024,1024]{1,0:T(8,128)(2,1)} %bitcast.312, bf16[1024,2048]{1,0:T(8,128)(2,1)} %bitcast.304, ...), custom_call_target="tpu_custom_call", output_to_operand_aliasing={{}: (5, {})} | custom-call | flops 12884901888 | bytes 27262976 | tf_op jit(solution)/shard_map/expert_grads/pallas_call | solution.py:180
  622.9 95.6 %scatter_col.4 = (f32[2048,256]{1,0:T(8,128)}, f32[8,4,2,2,1024]{4,3,2,1,0:T(2,128)}) custom-call(s32[2,1024,4]{2,1,0:T(8,128)} %copy-done.2, bf16[2,512,2048]{2,1,0:T(8,128)(2,1)} %get-tuple-element.122.refs_1_, bf16[2,512,2048]{2,1,0:T(8,128)(2,1)} %get-tuple-element.134.refs_2_, bf16[2,512,2048]{2,1,0:T(8,128)(2,1)} %get-tuple-element.145.refs_3_, ...), custom_call_target="tpu_custom_call" | custom-call | bytes 167772160 | tf_op jit(solution)/shard_map/scatter_col/pallas_call | solution.py:904
  718.5 2.3 slice_reduce_fusion.4
  721.1 3.0 multiply_reduce_fusion.2
  724.1 4.7 convolution_convert_fusion.1.refs_0_
  728.9 62.1 %scatter_col.5 = f32[2048,128]{1,0:T(8,128)} custom-call(bf16[2048,1024]{1,0:T(8,128)(2,1)} %convolution_convert_fusion.1.refs_0_), custom_call_target="tpu_custom_call" | custom-call | bytes 83886080 | tf_op jit(solution)/shard_map/scatter_col/pallas_call | solution.py:904
  790.9 1.3 convert_element_type.399
  792.2 1.5 convolution_bitcast_fusion
  793.8 5.3 fusion.24
  799.8 5.4 multiply_reduce_fusion.1
  806.0 2.5 multiply_convert_fusion.1
  808.5 1.1 fusion.22
  809.7 1.5 fusion.21
  811.4 2.4 fusion.60
  814.6 0.8 multiply_reduce_fusion.4
  816.0 7.0 convolution_convert_fusion.refs_0_
  823.6 5.5 convolution_convert_fusion.2
  829.4 1.3 pad_maximum_fusion.2.refs_6_
  830.7 1.2 copy-done.79
  831.9 2.1 convolution_convert_fusion.5.refs_7_
  834.0 118.5 %scatter_col.6 = (f32[2048,256]{1,0:T(8,128)}, f32[8,24,128]{2,1,0:T(8,128)}, bf16[8,3,256,128]{3,2,1,0:T(8,128)(2,1)}, bf16[8,128,256]{2,1,0:T(8,128)(2,1)}) custom-call(s32[2,1024,4]{2,1,0:T(8,128)} %copy-done.2, bf16[2,512,2048]{2,1,0:T(8,128)(2,1)} %get-tuple-element.169.refs_1_, bf16[2,512,2048]{2,1,0:T(8,128)(2,1)} %get-tuple-element.170.refs_2_, ...), custom_call_target="tpu_custom_call" | custom-call | bytes 167772160 | tf_op jit(solution)/shard_map/scatter_col/pallas_call | solution.py:904
  952.5 3.5 add_convert_fusion
  956.1 1.6 fusion.85
  957.7 1.4 fusion.100
  959.1 1.4 fusion.93
  961.2 86.3 %scatter_col.7 = (f32[2048,256]{1,0:T(8,128)}, f32[4,70,128]{2,1,0:T(8,128)}, bf16[4,2,3,256,128]{4,3,2,1,0:T(8,128)(2,1)}, bf16[4,2,128,256]{3,2,1,0:T(8,128)(2,1)}) custom-call(bf16[2048,2048]{1,0:T(8,128)(2,1)} %convolution_convert_fusion.refs_0_, f32[70,128]{1,0:T(8,128)} %maximum_bitcast_fusion.refs_1_, ...), custom_call_target="tpu_custom_call" | custom-call | bytes 167772160 | tf_op jit(solution)/shard_map/scatter_col/pallas_call | solution.py:904
  1047.5 1.0 reduce_sum.506
  1048.6 6.8 unpack.2
  1056.8 1.7 convert_reduce_fusion
  1058.6 0.9 fusion.72
  1061.1 2.0 multiply_subtract_fusion
  1063.1 6.8 unpack.3
  (242 shorter events, 21.8 us)
Async XLA Ops:
  7.2 338.5 %all-gather.3.cloned.1.call-start = ((), (), s32[]{:S(2)}) async-start(), calls=%async_computation.2 | async-start | bytes 31457280 | tf_op jit(solution)/shard_map/all_gather | solution.py:955
  12.0 480.6 %all-gather.5.cloned.1.call-start = ((), (), s32[]{:S(2)}) async-start(), calls=%async_computation.3 | async-start | bytes 31457280 | tf_op jit(solution)/shard_map/all_gather | solution.py:955
  16.8 944.4 %reduce-scatter.3.cloned.1.call-start = ((), (), s32[]{:S(2)}) async-start(), calls=%async_computation.4 | async-start | bytes 31457280 | tf_op jit(solution)/shard_map/reduce_scatter | solution.py:1063
  17.9 146.0 %copy-start.44 = (f32[1,8,2,128]{3,1,2,0:T(8,128)}, f32[1,8,2,128]{3,1,2,0:T(8,128)S(1)}, u32[]{:S(2)}) copy-start(f32[1,8,2,128]{3,1,2,0:T(8,128)S(1)} %copy.185) | copy-start | bytes 24580
  17.9 157.8 %copy-start.56 = (f32[1,8,2,128]{3,1,2,0:T(8,128)}, f32[1,8,2,128]{3,1,2,0:T(8,128)S(1)}, u32[]{:S(2)}) copy-start(f32[1,8,2,128]{3,1,2,0:T(8,128)S(1)} %copy.184) | copy-start | bytes 24580
  19.2 128.9 %copy-start.12 = (f32[2048,4]{1,0:T(8,128)}, f32[2048,4]{1,0:T(8,128)S(1)}, u32[]{:S(2)}) copy-start(f32[2048,4]{1,0:T(8,128)S(1)} %copy.142) | copy-start | bytes 98308
  19.2 5.0 copy-start.65
  19.2 5.0 copy-start.77
  148.0 5.9 copy-start.60
  148.0 7.4 copy-start.6
  153.9 5.5 copy-start.52
  153.9 5.5 copy-start.68
  155.4 4.0 copy-start.30
  155.4 4.0 copy-start.32
  155.4 4.0 copy-start.34
  159.5 4.4 copy-start.3
  159.5 4.2 copy-start.70
  159.5 4.1 copy-start.72
  162.8 3.8 copy-start.75
  163.0 3.6 copy-start.39
  163.6 3.0 copy-start.41
  166.9 2.8 copy-start.19
  167.2 2.5 copy-start.21
  169.8 3.4 copy-start
  169.8 3.4 copy-start.9
  171.0 3.7 copy-start.36
  173.2 2.5 copy-start.25
  174.7 145.1 %copy-start.13 = (f32[2048,4]{1,0:T(8,128)S(1)}, f32[2048,4]{1,0:T(8,128)}, u32[]{:S(2)}) copy-start(f32[2048,4]{1,0:T(8,128)} %copy-done.12) | copy-start | bytes 98308
  334.4 5.7 copy-start.5
  335.1 5.0 copy-start.54
  335.1 5.0 copy-start.38
  340.1 3.4 copy-start.1
  464.6 598.5 %reduce-scatter.5.cloned.1.call-start = ((), (), s32[]{:S(2)}) async-start(), calls=%async_computation.5 | async-start | bytes 31457280 | tf_op jit(solution)/shard_map/reduce_scatter | solution.py:1063
  622.8 98.0 %copy-start.15 = (f32[2048,32]{0,1:T(8,128)S(1)}, f32[2048,32]{0,1:T(8,128)}, u32[]{:S(2)}) copy-start(f32[2048,32]{0,1:T(8,128)} %copy-done.14) | copy-start | bytes 786436
  622.8 98.1 %copy-start.8 = (f32[2048,32]{0,1:T(8,128)S(1)}, f32[2048,32]{0,1:T(8,128)}, u32[]{:S(2)}) copy-start(f32[2048,32]{0,1:T(8,128)} %copy-done.7) | copy-start | bytes 786436
  622.9 98.2 %copy-start.26 = (bf16[2048,256]{1,0:T(8,128)(2,1)S(1)}, bf16[2048,256]{1,0:T(8,128)(2,1)}, u32[]{:S(2)}) copy-start(bf16[2048,256]{1,0:T(8,128)(2,1)} %param.31) | copy-start | bytes 3145732
  622.9 98.2 %copy-start.55 = (f32[2048]{0:T(1024)S(1)}, f32[2048]{0:T(1024)}, u32[]{:S(2)}) copy-start(f32[2048]{0:T(1024)} %copy-done.54) | copy-start | bytes 24580
  622.9 98.2 %copy-start.57 = (f32[1,8,2,128]{3,1,2,0:T(8,128)S(1)}, f32[1,8,2,128]{3,1,2,0:T(8,128)}, u32[]{:S(2)}) copy-start(f32[1,8,2,128]{3,1,2,0:T(8,128)} %copy-done.56) | copy-start | bytes 24580
  622.9 98.2 %copy-start.67 = (f32[2048]{0:T(1024)S(1)}, f32[2048]{0:T(1024)}, u32[]{:S(2)}) copy-start(f32[2048]{0:T(1024)} %get-tuple-element.284) | copy-start | bytes 24580
  622.9 98.2 %copy-start.78 = (f32[256]{0:T(256)S(1)}, f32[256]{0:T(256)}, u32[]{:S(2)}) copy-start(f32[256]{0:T(256)} %param.18) | copy-start | bytes 3076
  728.9 64.9 %copy-start.37 = (f32[2,1024]{1,0:T(2,128)S(1)}, f32[2,1024]{1,0:T(2,128)}, u32[]{:S(2)}) copy-start(f32[2,1024]{1,0:T(2,128)} %copy-done.36) | copy-start | bytes 24580
  793.8 6.0 copy-start.10
  799.7 5.5 slice-start
  799.8 6.2 slice-start.1
  811.2 2.6 copy-start.4
  811.2 2.6 copy-start.40
  811.2 2.6 copy-start.42
  811.3 2.6 copy-start.71
  811.3 2.6 copy-start.73
  811.4 3.2 copy-start.47
  811.4 3.2 copy-start.49
  814.6 9.0 slice-start.2
  816.0 7.6 slice-start.3
  816.0 7.6 copy-start.53
  816.0 7.6 copy-start.69
  829.1 2.8 copy-start.79
  952.5 3.5 copy-start.43
  952.5 5.2 copy-start.29
  952.5 6.6 copy-start.28
  1047.5 8.4 copy-start.27
  1055.3 5.2 copy-start.66
  1055.3 5.8 copy-start.11
  1055.3 5.8 copy-start.16
  1055.3 5.8 copy-start.51
  (24 other events, 29.1 us)
Sparse Core Ops, SparseCore 0:
  12.2 250.7 all-gather.2
  264.8 227.7 all-gather.4
  495.7 221.8 reduce-scatter.2
  720.9 221.8 reduce-scatter.4

commit v9 on v8

--- a/solution.py
+++ b/solution.py
@@ -247,6 +247,37 @@
         ),
         name="unpack",
     )(x, *held)
+
+
+def combine_body(place, *refs):
+    out = refs[-1]
+    total = jnp.zeros((out.shape[1], out.shape[2]), F32)
+    for e, ref in enumerate(refs[:-1]):
+        slot = lax.broadcasted_iota(jnp.int32, (out.shape[1], ref.shape[1]), 1)
+        pick = jnp.where(slot == place[0, :, e : e + 1], 1.0, 0.0).astype(BF16)
+        total = total + nn(pick, ref[0])
+    out[0] = total.astype(BF16)
+
+
+def combine(place, slots):
+    micro, group, local = place.shape
+    capacity, width = slots[0].shape[1:]
+    tile = min(256, group)
+    return pl.pallas_call(
+        combine_body,
+        grid=(micro, group // tile),
+        in_specs=[pl.BlockSpec((1, tile, local), lambda g, i: (g, i, 0))]
+        + [pl.BlockSpec((1, capacity, width), lambda g, i: (g, 0, 0)) for s in slots],
+        out_specs=pl.BlockSpec((1, tile, width), lambda g, i: (g, i, 0)),
+        out_shape=jax.ShapeDtypeStruct((micro, group, width), BF16),
+        compiler_params=pltpu.CompilerParams(vmem_limit_bytes=VMEM_LIMIT),
+        cost_estimate=pl.CostEstimate(
+            flops=2 * micro * group * local * capacity * width,
+            bytes_accessed=micro * (local * capacity + group) * width * 2,
+            transcendentals=0,
+        ),
+        name="combine",
+    )(place, *slots).reshape(micro * group, width)
 
 
 def places():
@@ -917,6 +948,58 @@
     )(*values, *others)
 
 
+def exchange_body(extra, heads, branch, extra_o, heads_o, branch_o, sends, recvs, keep):
+    row, col, n_row, n_col = places()
+    part, rows = heads.shape[1] // n_col, branch.shape[0] // n_col
+
+    def pieces(c):
+        at_part = pl.ds(pl.multiple_of(c * part, part), part)
+        at_rows = pl.ds(pl.multiple_of(c * rows, rows), rows)
+        return heads.at[:, at_part, :], branch.at[at_rows, :], extra
+
+    peers = [(True, (row, (col + k) % n_col)) for k in range(1, n_col)]
+    shake(peers, [ok for ok, _ in peers])
+    outs = (heads_o, branch_o, extra_o)
+    copies, arrivals = [], []
+    for k in range(1, n_col):
+        where, source = (col + k) % n_col, (col + n_col - k) % n_col
+        for m, src in enumerate(pieces(where)):
+            sems = (sends.at[m, k], recvs.at[m, k])
+            copies.append(remote(src, outs[m].at[col], *sems, (row, where)))
+            arrivals.append(remote(src, outs[m].at[source], *sems, (row, where)))
+    own = [
+        pltpu.make_async_copy(src, outs[m].at[col], keep.at[m])
+        for m, src in enumerate(pieces(col))
+    ]
+    for c in copies + own:
+        c.start()
+    for c in copies:
+        c.wait_send()
+    for c in arrivals:
+        c.wait_recv()
+    for c in own:
+        c.wait()
+
+
+def exchange_col(extra, heads, branch, ident):
+    n_col = lax.axis_size("col")
+    dma = pltpu.SemaphoreType.DMA
+    return pl.pallas_call(
+        exchange_body,
+        in_specs=[ANY] * 3,
+        out_specs=[ANY] * 3,
+        out_shape=[
+            jax.ShapeDtypeStruct((n_col,) + extra.shape, F32),
+            jax.ShapeDtypeStruct((n_col, 3, heads.shape[1] // n_col, heads.shape[2]), BF16),
+            jax.ShapeDtypeStruct((n_col, branch.shape[0] // n_col, branch.shape[1]), BF16),
+        ],
+        scratch_shapes=[dma((3, n_col)), dma((3, n_col)), dma((3,))],
+        compiler_params=pltpu.CompilerParams(collective_id=ident, has_side_effects=True),
+        cost_estimate=pl.CostEstimate(flops=0, bytes_accessed=64 << 20, transcendentals=0),
+        name="exchange_col",
+    )(extra, heads, branch)
+
+
 def shards(
     tokens,
     gain_attn,
@@ -1093,7 +1176,7 @@
 
     branch_grad = hidden_grad.astype(BF16)
     (attended_grad,) = scatter_col(nt(branch_grad, mine(full_o, 1)).astype(BF16), 3)
-    attended_grad = attended_grad.astype(BF16).reshape(batch)
+    attended_grad = tie(attended_grad.astype(BF16).reshape(batch), 0)
     grad_out = tn(attended_full, branch_grad)
     scores_again = scores_of()
     probs = jnp.exp(scores_again - log_total)
@@ -1127,13 +1210,11 @@
     sums = jnp.pad(sums, (0, -sums.shape[0] % 1024)).reshape(-1, 128)
     heads_weights = tn(normed, all_grads).astype(BF16)
     heads_weights = jnp.stack(jnp.split(heads_weights, 3, 1))
-    back_heads, mixed_slots = lax.optimization_barrier(
-        (back_heads.astype(BF16), [o[0] for o in outs])
-    )
-    mixed_sum, sums, heads_terms, out_terms = scatter_col(
-        mixed_slots, 4, 3, (sums, heads_weights, grad_out.astype(BF16)), place
-    )
-    mixed = (hidden_part + mixed_sum).astype(BF16)
+    sums, heads_terms, out_terms = exchange_col(sums, heads_weights, grad_out.astype(BF16), 4)
+    sums, mixed_slots = lax.optimization_barrier((sums, [o[0] for o in outs]))
+    mixed_sum = lax.psum_scatter(
+        combine(place, mixed_slots), "col", scatter_dimension=1, tiled=True
+    )
     sums = jnp.sum(sums, 0).reshape(-1)
     dot_one = sums[:rows]
     gain_attn_part = 0.0
@@ -1151,10 +1232,11 @@
             grad_router.T.reshape(-1),
         ]
     ).reshape(-1, 128)
-    back_heads, mixed = lax.optimization_barrier((back_heads, mixed))
     normed_back, smalls, heads_terms, out_terms = scatter_col(
-        tie(back_heads, 0), 5, 2, (smalls, heads_terms, out_terms)
-    )
+        back_heads.astype(BF16), 5, 2, (smalls, heads_terms, out_terms)
+    )
+    normed_back, mixed_sum = lax.optimization_barrier((normed_back, mixed_sum))
+    mixed = (hidden_part + mixed_sum.astype(F32)).astype(BF16)
     scale_one_part = scale_one
     inputs_part = tokens.astype(F32)
     input_grad = (

time: 1100 us -> 1110 us (level); the launches traced: 1080 us -> 1100 us
  waiting for transfers between devices: 26.2 us -> 42 us
    pallas_call x4 -> x3, Pallas kernels: 362 us -> 292 us  [scatter_col(): pl.pallas_call(functools.partial(scatter_body, part, stage, local), in_sp...]
    pallas_call x0 -> x2, Pallas kernels: none -> 69 us  [the longest x1 42.8 us: exchange_col(): pl.pallas_call(exchange_body, in_specs=[ANY] * 3, out_specs=[ANY] * 3, ou...]
    reduce_scatter x0 -> x1, waiting for transfers between devices: none -> 13.5 us  [shards(): lax.psum_scatter(combine(place, mixed_slots), 'col', scatter_dimension=1,...]
  transfers between devices with their start and end apart: 4 -> 5, of which waited for: 1 -> 2; matrix products, arithmetic and copies ran while one was open for 11% -> 11% of each run, Pallas kernels for 82% -> 82%
where the time goes in v9:
time: 1110 us; the launch traced here: 1100 us
  Pallas kernels  905 us (82%)
  matrix products  66 us (6%)
  other arithmetic  45.8 us (4%)
  waiting for transfers between devices  42 us (4%)
  local copies, waits for them, and re-layouts  27.6 us (2%)
  between operations  15.3 us (1%)
    pallas_call x3, Pallas kernels, scatter_col(): pl.pallas_call(functools.partial(scatter_body, part, stage, local), in_sp...  292 us
    pallas_call x4, Pallas kernels, expert_pass(): pl.pallas_call(functools.partial(expert_body, shared), grid_spec=pltpu.Pr...  178 us
    pallas_call x1, Pallas kernels, middle_gather(): pl.pallas_call(functools.partial(middle_body, axes), in_specs=[ANY] * n,...  143 us
    pallas_call x1, Pallas kernels, front(): pl.pallas_call(front_body, in_specs=[ANY] * 7, out_specs=[ANY] * 8, out_s...  123 us
    pallas_call x4, Pallas kernels, expert_grads(): pl.pallas_call(grads_body, grid=(width // shared,), in_specs=[thin, whole...  76.6 us
    pallas_call x1, Pallas kernels, exchange_col(): pl.pallas_call(exchange_body, in_specs=[ANY] * 3, out_specs=[ANY] * 3, ou...  42.8 us
    all_gather x2, waiting for transfers between devices, gather(): return lax.all_gather(value, axis_name, axis=axis, tiled=True)  28.4 us
    pallas_call x1, Pallas kernels, combine(): pl.pallas_call(combine_body, grid=(micro, group // tile), in_specs=[pl.Bl...  26.2 us
  transfers between devices with their start and end apart: 5, of which 2 were waited for; matrix products, arithmetic and copies ran while one was open for 11% of the time, Pallas kernels for 82%

profile of v9, /device:TPU:0, one launch (start us, length us, event | category | flops | bytes accessed | tf_op | source)
XLA Modules:
  0.0 1101.9 jit_solution(7603038204614333153)
XLA Ops:
  7.2 4.8 pack.2
  12.1 4.7 pack.3
  19.9 1.0 copy-done.4
  20.9 2.1 slice_reduce_fusion
  24.7 123.3 %front.1 = (bf16[2048,2048]{1,0:T(8,128)(2,1)}, f32[2,2048]{1,0:T(2,128)}, bf16[3,2048,128]{2,1,0:T(8,128)(2,1)}, bf16[128,2048]{1,0:T(8,128)(2,1)}, bf16[32,256...) custom-call(bf16[2048,256]{1,0:T(8,128)(2,1)} %tokens.1, ...), custom_call_target="tpu_custom_call" | custom-call | bytes 134217728 | tf_op jit(solution)/shard_map/front/pallas_call | solution.py:548
  148.0 5.2 fusion
  153.9 1.5 slice_bitcast_fusion.5
  155.4 4.0 fusion.8
  159.5 0.9 split.79
  160.3 2.5 copy.179
  163.9 3.0 fusion.51
  168.1 1.9 fusion.126
  170.1 1.2 exponential_reduce_fusion
  171.3 2.2 copy-done
  173.5 1.5 fusion.23
  175.0 1.0 copy.145
  176.0 1.3 fusion.10.refs_3_
  177.3 142.7 %middle_gather.1 = (bf16[2048,1024]{1,0:T(8,128)(2,1)}, bf16[1024,2048]{1,0:T(8,128)(2,1)}, bf16[32,2048]{1,0:T(8,128)(2,1)}, bf16[2048,2048]{1,0:T(8,128)(2,1)}) custom-call(bf16[2048,128]{1,0:T(8,128)(2,1)} %bitcast.339, bf16[128,2048]{1,0:T(8,128)(2,1)} %get-tuple-element.107.refs_1_, bf16[32,256]{1,0:T(8,128)(2,1)} %get-tuple-element.108.refs_2_, ...), custom_call_target="tpu_custom_call" | custom-call | bytes 270532608 | tf_op jit(solution)/shard_map/middle_gather/pallas_call | solution.py:585
  321.0 13.7 %multiply_reduce_fusion = (f32[2048]{0:T(1024)S(1)}, f32[2048,2048]{1,0:T(8,128)S(1)}) fusion(bf16[2048,1024]{1,0:T(8,128)(2,1)} %get-tuple-element.109, bf16[1024,2048]{1,0:T(8,128)(2,1)} %get-tuple-element.110, bf16[2048,2048]{1,0:T(8,128)(2,1)} %get-tuple-element.104), kind=kOutput, calls=%fused_computation.7 | convolution fusion | flops 8606709760 | bytes 33562624 | tf_op jit(solution)/shard_map/dot_general | solution.py:51
  335.3 2.2 multiply_convert_fusion
  337.5 2.8 copy-done.5
  340.4 2.6 select_reduce_fusion
  342.9 0.8 copy-done.1
  345.9 39.0 %expert_pass.4 = (bf16[2,512,2048]{2,1,0:T(8,128)(2,1)}, bf16[2,512,2048]{2,1,0:T(8,128)(2,1)}, bf16[2,512,1024]{2,1,0:T(8,128)(2,1)}, bf16[2,512,1024]{2,1,0:T(...) custom-call(s32[2]{0:T(128)} %get-tuple-element.238.counts, ...), custom_call_target="tpu_custom_call" | custom-call | flops 34359738368 | bytes 41943040 | tf_op jit(solution)/shard_map/expert_pass/pallas_call | solution.py:134
  384.9 19.1 %expert_grads.4.rest_0_ = bf16[2,3,2048,1024]{3,2,1,0:T(8,128)(2,1)} custom-call(bf16[1024,2048]{1,0:T(8,128)(2,1)} %bitcast.363, bf16[1024,1024]{1,0:T(8,128)(2,1)} %bitcast.368, bf16[1024,1024]{1,0:T(8,128)(2,1)} %bitcast.369, bf16[1024,1024]{1,0:T(8,128)(2,1)} %bitcast.367, bf16[1024,2048]{1,0:T(8,128)(2,1)} %bitcast.364), custom_call_target="tpu_custom_call" | custom-call | flops 12884901888 | bytes 27262976 | tf_op jit(solution)/shard_map/expert_grads/pallas_call | solution.py:180
  404.0 39.2 %expert_pass.5 = (bf16[2,512,2048]{2,1,0:T(8,128)(2,1)}, bf16[2,512,2048]{2,1,0:T(8,128)(2,1)}, bf16[2,512,1024]{2,1,0:T(8,128)(2,1)}, bf16[2,512,1024]{2,1,0:T(...) custom-call(s32[2]{0:T(128)} %get-tuple-element.237.counts, ...), custom_call_target="tpu_custom_call" | custom-call | flops 34359738368 | bytes 41943040 | tf_op jit(solution)/shard_map/expert_pass/pallas_call | solution.py:134
  443.2 19.0 %expert_grads.5 = bf16[2,3,2048,1024]{3,2,1,0:T(8,128)(2,1)} custom-call(bf16[1024,2048]{1,0:T(8,128)(2,1)} %bitcast.314, bf16[1024,1024]{1,0:T(8,128)(2,1)} %bitcast.325, bf16[1024,1024]{1,0:T(8,128)(2,1)} %bitcast.326, bf16[1024,1024]{1,0:T(8,128)(2,1)} %bitcast.324, bf16[1024,2048]{1,0:T(8,128)(2,1)} %bitcast.315, ...), custom_call_target="tpu_custom_call", output_to_operand_aliasing={{}: (5, {})} | custom-call | flops 12884901888 | bytes 27262976 | tf_op jit(solution)/shard_map/expert_grads/pallas_call | solution.py:180
  464.2 28.4 %all-gather.5.cloned.1.call-done.w = bf16[2,3,2048,1024]{3,2,1,0:T(8,128)(2,1)} async-done(((bf16[2,3,512,1024]{3,2,1,0:T(8,128)(2,1)}), bf16[2,3,2048,1024]{3,2,1,0:T(8,128)(2,1)}) %all-gather.5.cloned.1.call-update) | async-done | bytes 25165840 | tf_op jit(solution)/shard_map/all_gather | solution.py:1038
  492.6 49.5 %expert_pass.6 = (bf16[2,512,2048]{2,1,0:T(8,128)(2,1)}, bf16[2,512,2048]{2,1,0:T(8,128)(2,1)}, bf16[2,512,1024]{2,1,0:T(8,128)(2,1)}, bf16[2,512,1024]{2,1,0:T(...) custom-call(s32[2]{0:T(128)} %get-tuple-element.236.counts, ...), custom_call_target="tpu_custom_call" | custom-call | flops 34359738368 | bytes 41943040 | tf_op jit(solution)/shard_map/expert_pass/pallas_call | solution.py:134
  542.1 19.6 %expert_grads.6.rest_0_ = bf16[2,3,2048,1024]{3,2,1,0:T(8,128)(2,1)} custom-call(bf16[1024,2048]{1,0:T(8,128)(2,1)} %bitcast.365, bf16[1024,1024]{1,0:T(8,128)(2,1)} %bitcast.371, bf16[1024,1024]{1,0:T(8,128)(2,1)} %bitcast.372, bf16[1024,1024]{1,0:T(8,128)(2,1)} %bitcast.370, bf16[1024,2048]{1,0:T(8,128)(2,1)} %bitcast.366), custom_call_target="tpu_custom_call" | custom-call | flops 12884901888 | bytes 27262976 | tf_op jit(solution)/shard_map/expert_grads/pallas_call | solution.py:180
  561.6 50.4 %expert_pass.7 = (bf16[2,512,2048]{2,1,0:T(8,128)(2,1)}, bf16[2,512,2048]{2,1,0:T(8,128)(2,1)}, bf16[2,512,1024]{2,1,0:T(8,128)(2,1)}, bf16[2,512,1024]{2,1,0:T(...) custom-call(s32[2]{0:T(128)} %get-tuple-element.235.counts, ...), custom_call_target="tpu_custom_call" | custom-call | flops 34359738368 | bytes 41943040 | tf_op jit(solution)/shard_map/expert_pass/pallas_call | solution.py:134
  612.1 19.0 %expert_grads.7 = bf16[2,3,2048,1024]{3,2,1,0:T(8,128)(2,1)} custom-call(bf16[1024,2048]{1,0:T(8,128)(2,1)} %bitcast.312, bf16[1024,1024]{1,0:T(8,128)(2,1)} %bitcast.322, bf16[1024,1024]{1,0:T(8,128)(2,1)} %bitcast.323, bf16[1024,1024]{1,0:T(8,128)(2,1)} %bitcast.321, bf16[1024,2048]{1,0:T(8,128)(2,1)} %bitcast.313, ...), custom_call_target="tpu_custom_call", output_to_operand_aliasing={{}: (5, {})} | custom-call | flops 12884901888 | bytes 27262976 | tf_op jit(solution)/shard_map/expert_grads/pallas_call | solution.py:180
  632.6 96.9 %scatter_col.3 = (f32[2048,256]{1,0:T(8,128)}, f32[8,4,2,2,1024]{4,3,2,1,0:T(2,128)}) custom-call(s32[2,1024,4]{2,1,0:T(8,128)} %copy-done.4, bf16[2,512,2048]{2,1,0:T(8,128)(2,1)} %get-tuple-element.121.refs_1_, bf16[2,512,2048]{2,1,0:T(8,128)(2,1)} %get-tuple-element.133.refs_2_, bf16[2,512,2048]{2,1,0:T(8,128)(2,1)} %get-tuple-element.144.refs_3_, ...), custom_call_target="tpu_custom_call" | custom-call | bytes 167772160 | tf_op jit(solution)/shard_map/scatter_col/pallas_call | solution.py:935
  729.4 2.3 slice_reduce_fusion.4
  732.1 3.0 multiply_reduce_fusion.2
  735.1 4.5 convolution_convert_fusion.1.refs_0_
  739.6 61.9 %scatter_col.4 = f32[2048,128]{1,0:T(8,128)} custom-call(bf16[2048,1024]{1,0:T(8,128)(2,1)} %convolution_convert_fusion.1.refs_0_), custom_call_target="tpu_custom_call" | custom-call | bytes 83886080 | tf_op jit(solution)/shard_map/scatter_col/pallas_call | solution.py:935
  801.5 1.3 convert_element_type.402
  802.8 4.5 convolution_convert_fusion.5.branch
  807.2 5.0 fusion.24
  812.9 5.6 multiply_reduce_fusion.1
  819.1 2.9 multiply_convert_fusion.1
  822.0 1.1 fusion.22
  823.2 1.5 fusion.21
  825.0 2.4 fusion.60
  828.2 0.8 multiply_reduce_fusion.4
  829.8 5.2 convolution_convert_fusion.2
  835.3 1.3 pad_maximum_fusion.2.heads
  836.6 42.8 %exchange_col.1 = (f32[8,24,128]{2,1,0:T(8,128)}, bf16[8,3,256,128]{3,2,1,0:T(8,128)(2,1)}, bf16[8,128,256]{2,1,0:T(8,128)(2,1)}) custom-call(f32[24,128]{1,0:T(8,128)} %fusion.106.extra, bf16[3,2048,128]{2,1,0:T(8,128)(2,1)} %pad_maximum_fusion.2.heads, bf16[1024,256]{1,0:T(8,128)(2,1)} %convolution_convert_fusion.5.branch), custom_call_target="tpu_custom_call" | custom-call | bytes 67108864 | tf_op jit(solution)/shard_map/exchange_col/pallas_call | solution.py:987
  879.4 26.2 %combine.1 = bf16[2,1024,2048]{2,1,0:T(8,128)(2,1)} custom-call(s32[2,1024,4]{2,1,0:T(8,128)} %copy-done.4, bf16[2,512,2048]{2,1,0:T(8,128)(2,1)} %get-tuple-element.177.refs_0_, bf16[2,512,2048]{2,1,0:T(8,128)(2,1)} %get-tuple-element.178.refs_1_, bf16[2,512,2048]{2,1,0:T(8,128)(2,1)} %get-tuple-element.179.refs_2_, ...), custom_call_target="tpu_custom_call" | custom-call | flops 17179869184 | bytes 25165824 | tf_op jit(solution)/shard_map/combine/pallas_call | solution.py:266
  905.7 1.6 convolution_bitcast_fusion
  907.3 1.6 fusion.88
  908.9 1.7 fusion.103
  910.6 1.6 fusion.96
  912.9 9.7 convolution_convert_fusion.refs_0_
  922.6 133.0 %scatter_col.5 = (f32[2048,256]{1,0:T(8,128)}, f32[4,70,128]{2,1,0:T(8,128)}, bf16[4,2,3,256,128]{4,3,2,1,0:T(8,128)(2,1)}, bf16[4,2,128,256]{3,2,1,0:T(8,128)(2,1)}) custom-call(bf16[2048,2048]{1,0:T(8,128)(2,1)} %convolution_convert_fusion.refs_0_, f32[70,128]{1,0:T(8,128)} %maximum_bitcast_fusion.refs_1_, ...), custom_call_target="tpu_custom_call" | custom-call | bytes 167772160 | tf_op jit(solution)/shard_map/scatter_col/pallas_call | solution.py:935
  1055.7 0.9 reduce_sum.506
  1056.6 7.0 unpack.2
  1063.6 6.9 unpack.3
  1072.0 1.8 convert_reduce_fusion
  1073.8 0.9 fusion.75
  1076.4 13.5 %reduce-scatter.6.cloned.1.call-done = bf16[2048,256]{1,0:T(8,128)(2,1)} async-done(((bf16[2048,2048]{1,0:T(8,128)(2,1)}), bf16[2048,256]{1,0:T(8,128)(2,1)}) %reduce-scatter.6.cloned.1.call-update) | async-done | bytes 1048592 | tf_op jit(solution)/shard_map/reduce_scatter | solution.py:1215
  1089.8 3.3 add_convert_fusion
  1093.1 2.0 multiply_subtract_fusion
  (240 shorter events, 22.0 us)
Async XLA Ops:
  7.2 338.7 %all-gather.3.cloned.1.call-start = ((), (), s32[]{:S(2)}) async-start(), calls=%async_computation.3 | async-start | bytes 31457280 | tf_op jit(solution)/shard_map/all_gather | solution.py:1038
  12.0 480.6 %all-gather.5.cloned.1.call-start = ((), (), s32[]{:S(2)}) async-start(), calls=%async_computation.4 | async-start | bytes 31457280 | tf_op jit(solution)/shard_map/all_gather | solution.py:1038
  16.8 790.4 %reduce-scatter.4.cloned.1.call-start = ((), (), s32[]{:S(2)}) async-start(), calls=%async_computation.5 | async-start | bytes 31457280 | tf_op jit(solution)/shard_map/reduce_scatter | solution.py:1146
  17.9 146.0 %copy-start.42 = (f32[1,8,2,128]{3,1,2,0:T(8,128)}, f32[1,8,2,128]{3,1,2,0:T(8,128)S(1)}, u32[]{:S(2)}) copy-start(f32[1,8,2,128]{3,1,2,0:T(8,128)S(1)} %copy.192) | copy-start | bytes 24580
  17.9 158.1 %copy-start.54 = (f32[1,8,2,128]{3,1,2,0:T(8,128)}, f32[1,8,2,128]{3,1,2,0:T(8,128)S(1)}, u32[]{:S(2)}) copy-start(f32[1,8,2,128]{3,1,2,0:T(8,128)S(1)} %copy.191) | copy-start | bytes 24580
  19.2 128.9 %copy-start.12 = (f32[2048,4]{1,0:T(8,128)}, f32[2048,4]{1,0:T(8,128)S(1)}, u32[]{:S(2)}) copy-start(f32[2048,4]{1,0:T(8,128)S(1)} %copy.146) | copy-start | bytes 98308
  19.2 5.0 copy-start.63
  19.2 5.0 copy-start.75
  148.0 5.9 copy-start.58
  148.0 7.4 copy-start.6
  153.9 5.5 copy-start.50
  153.9 5.5 copy-start.66
  155.4 4.0 copy-start.31
  155.4 4.0 copy-start.32
  155.4 4.0 copy-start.33
  159.5 4.4 copy-start.2
  159.5 4.2 copy-start.68
  159.5 4.2 copy-start.70
  162.8 4.1 copy-start.73
  163.0 3.9 copy-start.37
  163.6 3.3 copy-start.39
  167.2 2.8 copy-start.17
  167.5 2.5 copy-start.19
  167.8 2.3 copy-start.21
  170.1 3.4 copy-start
  170.1 3.4 copy-start.9
  171.3 3.7 copy-start.34
  173.5 2.5 copy-start.25
  175.0 145.1 %copy-start.13 = (f32[2048,4]{1,0:T(8,128)S(1)}, f32[2048,4]{1,0:T(8,128)}, u32[]{:S(2)}) copy-start(f32[2048,4]{1,0:T(8,128)} %copy-done.12) | copy-start | bytes 98308
  334.7 5.7 copy-start.5
  335.3 5.0 copy-start.52
  335.3 5.0 copy-start.36
  340.4 3.4 copy-start.1
  462.3 601.3 %reduce-scatter.8.cloned.1.call-start = ((), (), s32[]{:S(2)}) async-start(), calls=%async_computation.7 | async-start | bytes 31457280 | tf_op jit(solution)/shard_map/reduce_scatter | solution.py:1146
  631.1 458.7 %reduce-scatter.6.cloned.1.call-start = ((), (), s32[]{:S(2)}) async-start(), calls=%async_computation.6 | async-start | bytes 9437184 | tf_op jit(solution)/shard_map/reduce_scatter | solution.py:1215
  632.5 99.4 %copy-start.15 = (f32[2048,32]{0,1:T(8,128)S(1)}, f32[2048,32]{0,1:T(8,128)}, u32[]{:S(2)}) copy-start(f32[2048,32]{0,1:T(8,128)} %copy-done.14) | copy-start | bytes 786436
  632.5 99.4 %copy-start.8 = (f32[2048,32]{0,1:T(8,128)S(1)}, f32[2048,32]{0,1:T(8,128)}, u32[]{:S(2)}) copy-start(f32[2048,32]{0,1:T(8,128)} %copy-done.7) | copy-start | bytes 786436
  632.5 99.5 %copy-start.26 = (bf16[2048,256]{1,0:T(8,128)(2,1)S(1)}, bf16[2048,256]{1,0:T(8,128)(2,1)}, u32[]{:S(2)}) copy-start(bf16[2048,256]{1,0:T(8,128)(2,1)} %param.31) | copy-start | bytes 3145732
  632.5 99.5 %copy-start.53 = (f32[2048]{0:T(1024)S(1)}, f32[2048]{0:T(1024)}, u32[]{:S(2)}) copy-start(f32[2048]{0:T(1024)} %copy-done.52) | copy-start | bytes 24580
  632.5 99.5 %copy-start.55 = (f32[1,8,2,128]{3,1,2,0:T(8,128)S(1)}, f32[1,8,2,128]{3,1,2,0:T(8,128)}, u32[]{:S(2)}) copy-start(f32[1,8,2,128]{3,1,2,0:T(8,128)} %copy-done.54) | copy-start | bytes 24580
  632.5 99.5 %copy-start.65 = (f32[2048]{0:T(1024)S(1)}, f32[2048]{0:T(1024)}, u32[]{:S(2)}) copy-start(f32[2048]{0:T(1024)} %get-tuple-element.282) | copy-start | bytes 24580
  632.5 99.5 %copy-start.76 = (f32[256]{0:T(256)S(1)}, f32[256]{0:T(256)}, u32[]{:S(2)}) copy-start(f32[256]{0:T(256)} %param.18) | copy-start | bytes 3076
  802.7 4.5 copy-start.35
  807.2 5.7 copy-start.10
  812.8 5.8 slice-start
  812.9 6.2 slice-start.1
  819.1 2.9 copy-start.22
  819.1 2.9 copy-start.24
  823.2 6.6 slice-start.2
  824.8 2.7 copy-start.3
  824.8 2.7 copy-start.38
  824.8 2.7 copy-start.40
  824.8 2.7 copy-start.69
  824.8 2.6 copy-start.71
  825.0 3.2 copy-start.45
  825.0 3.2 copy-start.47
  825.0 4.8 slice-start.3
  829.0 6.0 copy-start.29
  905.7 7.3 copy-start.28
  1063.6 7.5 copy-start.30
  1070.5 5.3 copy-start.64
  1073.7 19.4 %copy-start.11 = (bf16[2048,256]{1,0:T(8,128)(2,1)S(1)}, bf16[2048,256]{1,0:T(8,128)(2,1)}, u32[]{:S(2)}) copy-start(bf16[2048,256]{1,0:T(8,128)(2,1)} %tokens.1) | copy-start | bytes 3145732
  1073.8 19.4 %copy-start.49 = (f32[2048]{0:T(1024)S(1)}, f32[2048]{0:T(1024)}, u32[]{:S(2)}) copy-start(f32[2048]{0:T(1024)} %get-tuple-element.280) | copy-start | bytes 24580
  1089.8 3.3 copy-start.16
  (22 other events, 23.9 us)
Sparse Core Ops, SparseCore 0:
  12.2 250.7 all-gather.2
  264.8 227.7 all-gather.4
  495.7 221.8 reduce-scatter.3
  720.9 223.0 reduce-scatter.7
  946.2 143.6 reduce-scatter.5

commit v10 on v8

--- a/solution.py
+++ b/solution.py
@@ -960,9 +960,12 @@
 
     shared = w_down.shape[2]
     pair = 2 if local_exp % 2 == 0 else 1
-    big = [
-        gather(pack(w_gate, w_up, w_down, at, pair), "row", 2) for at in range(0, local_exp, pair)
-    ]
+    spans = [(0, pair)] + [(at, 1) for at in range(pair, local_exp)]
+    big = {}
+    for first, count in spans:
+        whole = gather(pack(w_gate, w_up, w_down, first, count), "row", 2)
+        for e in range(count):
+            big[first + e] = (whole, e)
     inputs_low, gains, w_heads, rows_o, rows_r, *wide = front(
         tokens,
         jnp.stack([gain_attn, gain_ffn]),
@@ -1048,8 +1051,7 @@
             gate_t[e],
             hn,
             upstream_full,
-            big[e // pair],
-            e % pair,
+            *big[e],
             capacity,
             shared,
         )

time: 1100 us -> 1080 us (0.982); the launches traced: 1080 us -> 1070 us
  waiting for transfers between devices: 26.2 us -> 0.09 us
  Pallas kernels: 899 us -> 917 us
    pallas_call x4, Pallas kernels: 362 us -> 395 us  [scatter_col(): pl.pallas_call(functools.partial(scatter_body, part, stage, local), in_sp...]
    all_gather x2 -> x3, waiting for transfers between devices: 26.1 us -> 0.01 us  [gather(): return lax.all_gather(value, axis_name, axis=axis, tiled=True)]
    pallas_call x4, Pallas kernels: 171 us -> 158 us  [expert_pass(): pl.pallas_call(functools.partial(expert_body, shared), grid_spec=pltpu.Pr...]
  transfers between devices with their start and end apart: 4 -> 5, of which waited for: 1 -> 0; matrix products, arithmetic and copies ran while one was open for 11% -> 12% of each run, Pallas kernels for 82% -> 85%
where the time goes in v10:
time: 1080 us; the launch traced here: 1070 us
  Pallas kernels  917 us (85%)
  matrix products  62.8 us (6%)
  other arithmetic  44.9 us (4%)
  local copies, waits for them, and re-layouts  30.1 us (3%)
  between operations  15.4 us (1%)
    pallas_call x4, Pallas kernels, scatter_col(): pl.pallas_call(functools.partial(scatter_body, part, stage, local), in_sp...  395 us
    pallas_call x4, Pallas kernels, expert_pass(): pl.pallas_call(functools.partial(expert_body, shared), grid_spec=pltpu.Pr...  158 us
    pallas_call x1, Pallas kernels, middle_gather(): pl.pallas_call(functools.partial(middle_body, axes), in_specs=[ANY] * n,...  143 us
    pallas_call x1, Pallas kernels, front(): pl.pallas_call(front_body, in_specs=[ANY] * 7, out_specs=[ANY] * 8, out_s...  119 us
    pallas_call x4, Pallas kernels, expert_grads(): pl.pallas_call(grads_body, grid=(width // shared,), in_specs=[thin, whole...  76.2 us
  transfers between devices with their start and end apart: 5, of which 0 were waited for; matrix products, arithmetic and copies ran while one was open for 12% of the time, Pallas kernels for 85%

profile of v10, /device:TPU:0, one launch (start us, length us, event | category | flops | bytes accessed | tf_op | source)
XLA Modules:
  0.0 1070.2 jit_solution(17439839340748696453)
XLA Ops:
  7.2 4.8 pack.3
  12.1 3.7 pack.4
  15.9 3.7 pack.5
  20.7 119.1 %front.1 = (bf16[2048,2048]{1,0:T(8,128)(2,1)}, f32[2,2048]{1,0:T(2,128)}, bf16[3,2048,128]{2,1,0:T(8,128)(2,1)}, bf16[128,2048]{1,0:T(8,128)(2,1)}, bf16[32,256...) custom-call(bf16[2048,256]{1,0:T(8,128)(2,1)} %tokens.1, ...), custom_call_target="tpu_custom_call" | custom-call | bytes 134217728 | tf_op jit(solution)/shard_map/front/pallas_call | solution.py:517
  140.6 5.2 fusion
  146.5 1.5 slice_bitcast_fusion.5
  148.0 4.0 fusion.8
  152.2 1.1 split.79
  154.3 1.3 copy.142
  155.7 2.3 fusion.18.refs_0_
  158.0 1.0 copy-done.2
  159.0 2.1 slice_reduce_fusion
  162.3 2.0 copy.172
  164.7 2.6 fusion.51
  168.5 1.9 fusion.123
  170.5 1.2 exponential_reduce_fusion
  171.7 2.2 copy-done
  173.9 1.5 fusion.23
  175.4 1.0 copy.141
  176.4 1.3 fusion.10.refs_3_
  177.7 142.7 %middle_gather.1 = (bf16[2048,1024]{1,0:T(8,128)(2,1)}, bf16[1024,2048]{1,0:T(8,128)(2,1)}, bf16[32,2048]{1,0:T(8,128)(2,1)}, bf16[2048,2048]{1,0:T(8,128)(2,1)}) custom-call(bf16[2048,128]{1,0:T(8,128)(2,1)} %bitcast.330, bf16[128,2048]{1,0:T(8,128)(2,1)} %get-tuple-element.108.refs_1_, bf16[32,256]{1,0:T(8,128)(2,1)} %get-tuple-element.109.refs_2_, ...), custom_call_target="tpu_custom_call" | custom-call | bytes 270532608 | tf_op jit(solution)/shard_map/middle_gather/pallas_call | solution.py:554
  321.4 13.5 %multiply_reduce_fusion = (f32[2048]{0:T(1024)S(1)}, f32[2048,2048]{1,0:T(8,128)S(1)}) fusion(bf16[2048,1024]{1,0:T(8,128)(2,1)} %get-tuple-element.110, bf16[1024,2048]{1,0:T(8,128)(2,1)} %get-tuple-element.111, bf16[2048,2048]{1,0:T(8,128)(2,1)} %get-tuple-element.105), kind=kOutput, calls=%fused_computation.7 | convolution fusion | flops 8606709760 | bytes 33562624 | tf_op jit(solution)/shard_map/dot_general | solution.py:51
  335.6 2.2 multiply_convert_fusion
  337.8 2.9 copy-done.5
  340.7 2.6 select_reduce_fusion
  346.3 39.2 %expert_pass.4 = (bf16[2,512,2048]{2,1,0:T(8,128)(2,1)}, bf16[2,512,2048]{2,1,0:T(8,128)(2,1)}, bf16[2,512,1024]{2,1,0:T(8,128)(2,1)}, bf16[2,512,1024]{2,1,0:T(...) custom-call(s32[2]{0:T(128)} %get-tuple-element.240.counts, ...), custom_call_target="tpu_custom_call" | custom-call | flops 34359738368 | bytes 41943040 | tf_op jit(solution)/shard_map/expert_pass/pallas_call | solution.py:134
  385.5 19.1 %expert_grads.4.rest_0_ = bf16[2,3,2048,1024]{3,2,1,0:T(8,128)(2,1)} custom-call(bf16[1024,2048]{1,0:T(8,128)(2,1)} %bitcast.356, bf16[1024,1024]{1,0:T(8,128)(2,1)} %bitcast.362, bf16[1024,1024]{1,0:T(8,128)(2,1)} %bitcast.363, bf16[1024,1024]{1,0:T(8,128)(2,1)} %bitcast.361, bf16[1024,2048]{1,0:T(8,128)(2,1)} %bitcast.357), custom_call_target="tpu_custom_call" | custom-call | flops 12884901888 | bytes 27262976 | tf_op jit(solution)/shard_map/expert_grads/pallas_call | solution.py:180
  404.6 39.4 %expert_pass.5 = (bf16[2,512,2048]{2,1,0:T(8,128)(2,1)}, bf16[2,512,2048]{2,1,0:T(8,128)(2,1)}, bf16[2,512,1024]{2,1,0:T(8,128)(2,1)}, bf16[2,512,1024]{2,1,0:T(...) custom-call(s32[2]{0:T(128)} %get-tuple-element.239.counts, ...), custom_call_target="tpu_custom_call" | custom-call | flops 34359738368 | bytes 41943040 | tf_op jit(solution)/shard_map/expert_pass/pallas_call | solution.py:134
  443.9 19.0 %expert_grads.5 = bf16[2,3,2048,1024]{3,2,1,0:T(8,128)(2,1)} custom-call(bf16[1024,2048]{1,0:T(8,128)(2,1)} %bitcast.305, bf16[1024,1024]{1,0:T(8,128)(2,1)} %bitcast.316, bf16[1024,1024]{1,0:T(8,128)(2,1)} %bitcast.317, bf16[1024,1024]{1,0:T(8,128)(2,1)} %bitcast.315, bf16[1024,2048]{1,0:T(8,128)(2,1)} %bitcast.306, ...), custom_call_target="tpu_custom_call", output_to_operand_aliasing={{}: (5, {})} | custom-call | flops 12884901888 | bytes 27262976 | tf_op jit(solution)/shard_map/expert_grads/pallas_call | solution.py:180
  464.9 39.0 %expert_pass.6 = (bf16[2,512,2048]{2,1,0:T(8,128)(2,1)}, bf16[2,512,2048]{2,1,0:T(8,128)(2,1)}, bf16[2,512,1024]{2,1,0:T(8,128)(2,1)}, bf16[2,512,1024]{2,1,0:T(...) custom-call(s32[2]{0:T(128)} %get-tuple-element.238.counts, ...), custom_call_target="tpu_custom_call" | custom-call | flops 34359738368 | bytes 41943040 | tf_op jit(solution)/shard_map/expert_pass/pallas_call | solution.py:134
  503.9 19.0 %expert_grads.6.rest_0_ = bf16[2,3,2048,1024]{3,2,1,0:T(8,128)(2,1)} custom-call(bf16[1024,2048]{1,0:T(8,128)(2,1)} %bitcast.354, bf16[1024,1024]{1,0:T(8,128)(2,1)} %bitcast.359, bf16[1024,1024]{1,0:T(8,128)(2,1)} %bitcast.360, bf16[1024,1024]{1,0:T(8,128)(2,1)} %bitcast.358, bf16[1024,2048]{1,0:T(8,128)(2,1)} %bitcast.355), custom_call_target="tpu_custom_call" | custom-call | flops 12884901888 | bytes 27262976 | tf_op jit(solution)/shard_map/expert_grads/pallas_call | solution.py:180
  522.9 40.2 %expert_pass.7 = (bf16[2,512,2048]{2,1,0:T(8,128)(2,1)}, bf16[2,512,2048]{2,1,0:T(8,128)(2,1)}, bf16[2,512,1024]{2,1,0:T(8,128)(2,1)}, bf16[2,512,1024]{2,1,0:T(...) custom-call(s32[2]{0:T(128)} %get-tuple-element.237.counts, ...), custom_call_target="tpu_custom_call" | custom-call | flops 34359738368 | bytes 41943040 | tf_op jit(solution)/shard_map/expert_pass/pallas_call | solution.py:134
  563.2 19.1 %expert_grads.7 = bf16[2,3,2048,1024]{3,2,1,0:T(8,128)(2,1)} custom-call(bf16[1024,2048]{1,0:T(8,128)(2,1)} %bitcast.303, bf16[1024,1024]{1,0:T(8,128)(2,1)} %bitcast.313, bf16[1024,1024]{1,0:T(8,128)(2,1)} %bitcast.314, bf16[1024,1024]{1,0:T(8,128)(2,1)} %bitcast.312, bf16[1024,2048]{1,0:T(8,128)(2,1)} %bitcast.304, ...), custom_call_target="tpu_custom_call", output_to_operand_aliasing={{}: (5, {})} | custom-call | flops 12884901888 | bytes 27262976 | tf_op jit(solution)/shard_map/expert_grads/pallas_call | solution.py:180
  583.7 128.4 %scatter_col.4 = (f32[2048,256]{1,0:T(8,128)}, f32[8,4,2,2,1024]{4,3,2,1,0:T(2,128)}) custom-call(s32[2,1024,4]{2,1,0:T(8,128)} %copy-done.2, bf16[2,512,2048]{2,1,0:T(8,128)(2,1)} %get-tuple-element.122.refs_1_, bf16[2,512,2048]{2,1,0:T(8,128)(2,1)} %get-tuple-element.134.refs_2_, bf16[2,512,2048]{2,1,0:T(8,128)(2,1)} %get-tuple-element.145.refs_3_, ...), custom_call_target="tpu_custom_call" | custom-call | bytes 167772160 | tf_op jit(solution)/shard_map/scatter_col/pallas_call | solution.py:904
  712.1 2.4 slice_reduce_fusion.4
  714.8 3.4 multiply_reduce_fusion.2
  718.2 4.4 convolution_convert_fusion.1.refs_0_
  722.6 61.7 %scatter_col.5 = f32[2048,128]{1,0:T(8,128)} custom-call(bf16[2048,1024]{1,0:T(8,128)(2,1)} %convolution_convert_fusion.1.refs_0_), custom_call_target="tpu_custom_call" | custom-call | bytes 83886080 | tf_op jit(solution)/shard_map/scatter_col/pallas_call | solution.py:904
  784.3 1.3 convert_element_type.399
  785.6 1.5 convolution_bitcast_fusion
  787.2 5.4 fusion.24
  793.3 5.2 multiply_reduce_fusion.1
  798.5 0.9 slice-done.1
  799.4 2.5 multiply_convert_fusion.1
  802.0 1.1 fusion.22
  803.1 1.5 fusion.21
  804.9 2.4 fusion.60
  809.3 7.0 convolution_convert_fusion.refs_0_
  816.9 5.5 convolution_convert_fusion.2
  822.7 1.3 pad_maximum_fusion.2.refs_6_
  824.1 1.2 copy-done.77
  825.2 2.1 convolution_convert_fusion.5.refs_7_
  827.4 118.7 %scatter_col.6 = (f32[2048,256]{1,0:T(8,128)}, f32[8,24,128]{2,1,0:T(8,128)}, bf16[8,3,256,128]{3,2,1,0:T(8,128)(2,1)}, bf16[8,128,256]{2,1,0:T(8,128)(2,1)}) custom-call(s32[2,1024,4]{2,1,0:T(8,128)} %copy-done.2, bf16[2,512,2048]{2,1,0:T(8,128)(2,1)} %get-tuple-element.169.refs_1_, bf16[2,512,2048]{2,1,0:T(8,128)(2,1)} %get-tuple-element.170.refs_2_, ...), custom_call_target="tpu_custom_call" | custom-call | bytes 167772160 | tf_op jit(solution)/shard_map/scatter_col/pallas_call | solution.py:904
  946.1 3.5 add_convert_fusion
  949.7 1.6 fusion.85
  951.3 1.4 fusion.100
  952.7 1.5 fusion.93
  954.9 86.2 %scatter_col.7 = (f32[2048,256]{1,0:T(8,128)}, f32[4,70,128]{2,1,0:T(8,128)}, bf16[4,2,3,256,128]{4,3,2,1,0:T(8,128)(2,1)}, bf16[4,2,128,256]{3,2,1,0:T(8,128)(2,1)}) custom-call(bf16[2048,2048]{1,0:T(8,128)(2,1)} %convolution_convert_fusion.refs_0_, f32[70,128]{1,0:T(8,128)} %maximum_bitcast_fusion.refs_1_, ...), custom_call_target="tpu_custom_call" | custom-call | bytes 167772160 | tf_op jit(solution)/shard_map/scatter_col/pallas_call | solution.py:904
  1041.1 1.0 reduce_sum.506
  1042.1 6.8 unpack.2
  1050.3 1.7 convert_reduce_fusion
  1052.1 0.9 fusion.72
  1054.7 2.0 multiply_subtract_fusion
  1056.6 6.8 unpack.3
  (242 shorter events, 21.9 us)
Async XLA Ops:
  7.2 339.1 %all-gather.4.cloned.1.call-start = ((), (), s32[]{:S(2)}) async-start(), calls=%async_computation.2 | async-start | bytes 31457280 | tf_op jit(solution)/shard_map/all_gather | solution.py:955
  12.0 452.8 %all-gather.6.cloned.1.call-start = ((), (), s32[]{:S(2)}) async-start(), calls=%async_computation.3 | async-start | bytes 15728640 | tf_op jit(solution)/shard_map/all_gather | solution.py:955
  15.8 3.9 copy-start.72
  15.9 4.2 copy-start.63
  15.9 4.2 copy-start.75
  15.9 507.0 %all-gather.8.cloned.1.call-start = ((), (), s32[]{:S(2)}) async-start(), calls=%async_computation.4 | async-start | bytes 15728640 | tf_op jit(solution)/shard_map/all_gather | solution.py:955
  19.7 935.1 %reduce-scatter.3.cloned.1.call-start = ((), (), s32[]{:S(2)}) async-start(), calls=%async_computation.5 | async-start | bytes 31457280 | tf_op jit(solution)/shard_map/reduce_scatter | solution.py:1065
  140.6 7.4 copy-start.66
  140.6 7.4 copy-start.6
  146.5 5.5 copy-start.51
  147.9 4.0 copy-start.29
  148.0 4.0 copy-start.31
  148.0 4.0 copy-start.33
  148.0 5.5 copy-start.49
  152.0 12.4 %copy-start.3 = (f32[2048,384]{0,1:T(8,128)}, f32[2048,384]{0,1:T(8,128)S(1)}, u32[]{:S(2)}) copy-start(f32[2048,384]{0,1:T(8,128)S(1)} %fusion.8) | copy-start | bytes 9437188
  152.2 12.1 %copy-start.45 = (f32[2048]{0:T(1024)}, f32[2048]{0:T(1024)S(1)}, u32[]{:S(2)}) copy-start(f32[2048]{0:T(1024)S(1)} %get-tuple-element.205) | copy-start | bytes 24580
  152.2 12.1 %copy-start.47 = (f32[2048]{0:T(1024)}, f32[2048]{0:T(1024)S(1)}, u32[]{:S(2)}) copy-start(f32[2048]{0:T(1024)S(1)} %get-tuple-element.206) | copy-start | bytes 24580
  153.5 11.2 %copy-start.43 = (f32[1,8,2,128]{3,1,2,0:T(8,128)}, f32[1,8,2,128]{3,1,2,0:T(8,128)S(1)}, u32[]{:S(2)}) copy-start(f32[1,8,2,128]{3,1,2,0:T(8,128)S(1)} %copy.185) | copy-start | bytes 24580
  153.5 22.9 %copy-start.55 = (f32[1,8,2,128]{3,1,2,0:T(8,128)}, f32[1,8,2,128]{3,1,2,0:T(8,128)S(1)}, u32[]{:S(2)}) copy-start(f32[1,8,2,128]{3,1,2,0:T(8,128)S(1)} %copy.184) | copy-start | bytes 24580
  155.7 8.7 copy-start.68
  155.7 8.7 copy-start.70
  164.3 3.6 copy-start.73
  164.4 3.0 copy-start.38
  164.4 2.9 copy-start.40
  167.6 2.8 copy-start.18
  170.5 3.4 copy-start
  170.5 3.4 copy-start.9
  171.7 3.7 copy-start.35
  175.4 145.1 %copy-start.12 = (f32[2048,4]{1,0:T(8,128)S(1)}, f32[2048,4]{1,0:T(8,128)}, u32[]{:S(2)}) copy-start(f32[2048,4]{1,0:T(8,128)} %copy.142) | copy-start | bytes 98308
  334.9 5.8 copy-start.5
  335.6 5.2 copy-start.53
  335.6 5.2 copy-start.37
  340.7 3.4 copy-start.1
  463.0 593.6 %reduce-scatter.5.cloned.1.call-start = ((), (), s32[]{:S(2)}) async-start(), calls=%async_computation.6 | async-start | bytes 31457280 | tf_op jit(solution)/shard_map/reduce_scatter | solution.py:1065
  583.7 130.9 %copy-start.14 = (f32[2048,32]{0,1:T(8,128)S(1)}, f32[2048,32]{0,1:T(8,128)}, u32[]{:S(2)}) copy-start(f32[2048,32]{0,1:T(8,128)} %copy-done.13) | copy-start | bytes 786436
  583.7 131.0 %copy-start.8 = (f32[2048,32]{0,1:T(8,128)S(1)}, f32[2048,32]{0,1:T(8,128)}, u32[]{:S(2)}) copy-start(f32[2048,32]{0,1:T(8,128)} %copy-done.7) | copy-start | bytes 786436
  583.7 131.1 %copy-start.25 = (bf16[2048,256]{1,0:T(8,128)(2,1)S(1)}, bf16[2048,256]{1,0:T(8,128)(2,1)}, u32[]{:S(2)}) copy-start(bf16[2048,256]{1,0:T(8,128)(2,1)} %param.31) | copy-start | bytes 3145732
  583.7 131.1 %copy-start.54 = (f32[2048]{0:T(1024)S(1)}, f32[2048]{0:T(1024)}, u32[]{:S(2)}) copy-start(f32[2048]{0:T(1024)} %copy-done.53) | copy-start | bytes 24580
  583.7 131.1 %copy-start.56 = (f32[1,8,2,128]{3,1,2,0:T(8,128)S(1)}, f32[1,8,2,128]{3,1,2,0:T(8,128)}, u32[]{:S(2)}) copy-start(f32[1,8,2,128]{3,1,2,0:T(8,128)} %copy-done.55) | copy-start | bytes 24580
  583.7 131.1 %copy-start.65 = (f32[2048]{0:T(1024)S(1)}, f32[2048]{0:T(1024)}, u32[]{:S(2)}) copy-start(f32[2048]{0:T(1024)} %get-tuple-element.284) | copy-start | bytes 24580
  583.7 131.1 %copy-start.76 = (f32[256]{0:T(256)S(1)}, f32[256]{0:T(256)}, u32[]{:S(2)}) copy-start(f32[256]{0:T(256)} %param.18) | copy-start | bytes 3076
  722.6 64.6 %copy-start.36 = (f32[2,1024]{1,0:T(2,128)S(1)}, f32[2,1024]{1,0:T(2,128)}, u32[]{:S(2)}) copy-start(f32[2,1024]{1,0:T(2,128)} %copy-done.35) | copy-start | bytes 24580
  787.2 6.1 copy-start.10
  793.1 5.4 slice-start
  793.3 6.2 slice-start.1
  804.7 2.6 copy-start.4
  804.7 2.6 copy-start.39
  804.7 2.6 copy-start.41
  804.7 2.6 copy-start.69
  804.8 3.2 copy-start.46
  804.8 3.2 copy-start.48
  808.0 8.9 slice-start.2
  809.3 7.6 slice-start.3
  809.3 7.6 copy-start.52
  809.3 7.6 copy-start.67
  822.5 2.8 copy-start.77
  946.1 3.5 copy-start.42
  946.1 5.2 copy-start.28
  946.1 6.6 copy-start.27
  1041.1 8.4 copy-start.26
  1048.9 5.2 copy-start.64
  1048.9 5.8 copy-start.11
  1048.9 5.8 copy-start.15
  1048.9 5.8 copy-start.50
  (23 other events, 33.5 us)
Sparse Core Ops, SparseCore 0:
  12.2 246.6 all-gather.3
  260.7 122.5 all-gather.5
  385.1 122.5 all-gather.7
  510.7 221.8 reduce-scatter.2
  735.8 221.8 reduce-scatter.4

commit v11 on v10

--- a/solution.py
+++ b/solution.py
@@ -683,8 +683,10 @@
     if local:
         micro, capacity = held.shape[2], held.shape[3]
         group = chosen.shape[1]
+        upper = pair // (pairs // 2)
+        turns = [(pairs - 1 - m) * (1 - upper) + m * upper for m in range(pairs)]
         owners = []
-        for d in order:
+        for d in turns:
             owners += [d * 2 + 1 - core, d * 2 + core]
 
         def bring(n):
@@ -720,7 +722,7 @@
             lax.fori_loop(0, micro * steps, step, 0)
 
         def make_pair(m):
-            d = order[m]
+            d = turns[m]
             make(2 * m, give.at[d])
             for q in range(cuts):
                 across(d, q).start()
@@ -794,25 +796,37 @@
         left(d, q).start()
 
     if local:
-        for m in range(2):
+        half = pairs // 2
+        for m in range(pairs):
             make_pair(m)
-        for q in range(cuts):
-
-            @pl.when(pair == 0)
-            def _():
-                go_right(pairs - 1, q)
-
-            @pl.when(pair == pairs - 1)
-            def _():
-                go_left(0, q)
-
-        for m in range(2, pairs):
-            make_pair(m)
+            for q in range(cuts):
+                if m < pairs - 1:
+
+                    @pl.when(pair == 0)
+                    def _():
+                        go_right(pairs - 1 - m, q)
+
+                    @pl.when(pair == pairs - 1)
+                    def _():
+                        go_left(m, q)
+
+                if m == 1:
+
+                    @pl.when((pair > 0) & (pair < half))
+                    def _():
+                        go_right(pairs - 1, q)
+
+                    @pl.when((pair >= half) & (pair < pairs - 1))
+                    def _():
+                        go_left(0, q)
+
     for t in range(pairs - 1):
         far, near = pairs - 1 - t, t
         go_far, go_near = far > pair, near < pair
+        if local:
+            go_far, go_near = go_far & (pair > 0), go_near & (pair < pairs - 1)
         if local and t == 0:
-            go_far, go_near = go_far & (pair > 0), go_near & (pair < pairs - 1)
+            go_far, go_near = go_far & (pair >= half), go_near & (pair < half)
         for q in range(cuts):
 
             @pl.when(go_far)

time: 1080 us -> 1060 us (0.981); the launches traced: 1070 us -> 1040 us
  Pallas kernels: 917 us -> 882 us
    pallas_call x4, Pallas kernels: 395 us -> 338 us  [scatter_col(): pl.pallas_call(functools.partial(scatter_body, part, stage, local), in_sp...]
    pallas_call x4, Pallas kernels: 158 us -> 179 us  [expert_pass(): pl.pallas_call(functools.partial(expert_body, shared), grid_spec=pltpu.Pr...]
  transfers between devices with their start and end apart: 5 -> 5, of which waited for: 0 -> 0; matrix products, arithmetic and copies ran while one was open for 12% -> 12% of each run, Pallas kernels for 85% -> 84%
where the time goes in v11:
time: 1060 us; the launch traced here: 1040 us
  Pallas kernels  882 us (83%)
  matrix products  62.7 us (6%)
  other arithmetic  45.2 us (4%)
  local copies, waits for them, and re-layouts  30 us (3%)
  between operations  15.6 us (1%)
    pallas_call x4, Pallas kernels, scatter_col(): pl.pallas_call(functools.partial(scatter_body, part, stage, local), in_sp...  338 us
    pallas_call x4, Pallas kernels, expert_pass(): pl.pallas_call(functools.partial(expert_body, shared), grid_spec=pltpu.Pr...  179 us
    pallas_call x1, Pallas kernels, middle_gather(): pl.pallas_call(functools.partial(middle_body, axes), in_specs=[ANY] * n,...  143 us
    pallas_call x1, Pallas kernels, front(): pl.pallas_call(front_body, in_specs=[ANY] * 7, out_specs=[ANY] * 8, out_s...  119 us
    pallas_call x4, Pallas kernels, expert_grads(): pl.pallas_call(grads_body, grid=(width // shared,), in_specs=[thin, whole...  77.8 us
  transfers between devices with their start and end apart: 5, of which 0 were waited for; matrix products, arithmetic and copies ran while one was open for 12% of the time, Pallas kernels for 84%

profile of v11, /device:TPU:0, one launch (start us, length us, event | category | flops | bytes accessed | tf_op | source)
XLA Modules:
  0.0 1036.1 jit_solution(8525973787926449583)
XLA Ops:
  7.2 4.8 pack.3
  12.1 3.7 pack.4
  15.9 3.7 pack.5
  20.7 119.1 %front.1 = (bf16[2048,2048]{1,0:T(8,128)(2,1)}, f32[2,2048]{1,0:T(2,128)}, bf16[3,2048,128]{2,1,0:T(8,128)(2,1)}, bf16[128,2048]{1,0:T(8,128)(2,1)}, bf16[32,256...) custom-call(bf16[2048,256]{1,0:T(8,128)(2,1)} %tokens.1, ...), custom_call_target="tpu_custom_call" | custom-call | bytes 134217728 | tf_op jit(solution)/shard_map/front/pallas_call | solution.py:517
  140.6 5.2 fusion
  146.5 1.5 slice_bitcast_fusion.5
  148.0 4.0 fusion.8
  152.2 1.1 split.79
  154.3 1.3 copy.142
  155.7 2.3 fusion.18.refs_0_
  158.0 1.0 copy-done.2
  159.0 2.1 slice_reduce_fusion
  162.3 2.0 copy.172
  164.7 2.6 fusion.51
  168.5 1.9 fusion.123
  170.5 1.2 exponential_reduce_fusion
  171.7 2.2 copy-done
  173.9 1.5 fusion.23
  175.4 1.0 copy.141
  176.4 1.3 fusion.10.refs_3_
  177.7 142.7 %middle_gather.1 = (bf16[2048,1024]{1,0:T(8,128)(2,1)}, bf16[1024,2048]{1,0:T(8,128)(2,1)}, bf16[32,2048]{1,0:T(8,128)(2,1)}, bf16[2048,2048]{1,0:T(8,128)(2,1)}) custom-call(bf16[2048,128]{1,0:T(8,128)(2,1)} %bitcast.330, bf16[128,2048]{1,0:T(8,128)(2,1)} %get-tuple-element.108.refs_1_, bf16[32,256]{1,0:T(8,128)(2,1)} %get-tuple-element.109.refs_2_, ...), custom_call_target="tpu_custom_call" | custom-call | bytes 270532608 | tf_op jit(solution)/shard_map/middle_gather/pallas_call | solution.py:554
  321.3 13.5 %multiply_reduce_fusion = (f32[2048]{0:T(1024)S(1)}, f32[2048,2048]{1,0:T(8,128)S(1)}) fusion(bf16[2048,1024]{1,0:T(8,128)(2,1)} %get-tuple-element.110, bf16[1024,2048]{1,0:T(8,128)(2,1)} %get-tuple-element.111, bf16[2048,2048]{1,0:T(8,128)(2,1)} %get-tuple-element.105), kind=kOutput, calls=%fused_computation.7 | convolution fusion | flops 8606709760 | bytes 33562624 | tf_op jit(solution)/shard_map/dot_general | solution.py:51
  335.5 2.2 multiply_convert_fusion
  337.8 2.9 copy-done.5
  340.7 2.6 select_reduce_fusion
  346.2 50.0 %expert_pass.4 = (bf16[2,512,2048]{2,1,0:T(8,128)(2,1)}, bf16[2,512,2048]{2,1,0:T(8,128)(2,1)}, bf16[2,512,1024]{2,1,0:T(8,128)(2,1)}, bf16[2,512,1024]{2,1,0:T(...) custom-call(s32[2]{0:T(128)} %get-tuple-element.240.counts, ...), custom_call_target="tpu_custom_call" | custom-call | flops 34359738368 | bytes 41943040 | tf_op jit(solution)/shard_map/expert_pass/pallas_call | solution.py:134
  396.3 20.1 %expert_grads.4.rest_0_ = bf16[2,3,2048,1024]{3,2,1,0:T(8,128)(2,1)} custom-call(bf16[1024,2048]{1,0:T(8,128)(2,1)} %bitcast.356, bf16[1024,1024]{1,0:T(8,128)(2,1)} %bitcast.362, bf16[1024,1024]{1,0:T(8,128)(2,1)} %bitcast.363, bf16[1024,1024]{1,0:T(8,128)(2,1)} %bitcast.361, bf16[1024,2048]{1,0:T(8,128)(2,1)} %bitcast.357), custom_call_target="tpu_custom_call" | custom-call | flops 12884901888 | bytes 27262976 | tf_op jit(solution)/shard_map/expert_grads/pallas_call | solution.py:180
  416.3 40.0 %expert_pass.5 = (bf16[2,512,2048]{2,1,0:T(8,128)(2,1)}, bf16[2,512,2048]{2,1,0:T(8,128)(2,1)}, bf16[2,512,1024]{2,1,0:T(8,128)(2,1)}, bf16[2,512,1024]{2,1,0:T(...) custom-call(s32[2]{0:T(128)} %get-tuple-element.239.counts, ...), custom_call_target="tpu_custom_call" | custom-call | flops 34359738368 | bytes 41943040 | tf_op jit(solution)/shard_map/expert_pass/pallas_call | solution.py:134
  456.3 19.0 %expert_grads.5 = bf16[2,3,2048,1024]{3,2,1,0:T(8,128)(2,1)} custom-call(bf16[1024,2048]{1,0:T(8,128)(2,1)} %bitcast.305, bf16[1024,1024]{1,0:T(8,128)(2,1)} %bitcast.316, bf16[1024,1024]{1,0:T(8,128)(2,1)} %bitcast.317, bf16[1024,1024]{1,0:T(8,128)(2,1)} %bitcast.315, bf16[1024,2048]{1,0:T(8,128)(2,1)} %bitcast.306, ...), custom_call_target="tpu_custom_call", output_to_operand_aliasing={{}: (5, {})} | custom-call | flops 12884901888 | bytes 27262976 | tf_op jit(solution)/shard_map/expert_grads/pallas_call | solution.py:180
  477.2 49.5 %expert_pass.6 = (bf16[2,512,2048]{2,1,0:T(8,128)(2,1)}, bf16[2,512,2048]{2,1,0:T(8,128)(2,1)}, bf16[2,512,1024]{2,1,0:T(8,128)(2,1)}, bf16[2,512,1024]{2,1,0:T(...) custom-call(s32[2]{0:T(128)} %get-tuple-element.238.counts, ...), custom_call_target="tpu_custom_call" | custom-call | flops 34359738368 | bytes 41943040 | tf_op jit(solution)/shard_map/expert_pass/pallas_call | solution.py:134
  526.8 19.3 %expert_grads.6.rest_0_ = bf16[2,3,2048,1024]{3,2,1,0:T(8,128)(2,1)} custom-call(bf16[1024,2048]{1,0:T(8,128)(2,1)} %bitcast.354, bf16[1024,1024]{1,0:T(8,128)(2,1)} %bitcast.359, bf16[1024,1024]{1,0:T(8,128)(2,1)} %bitcast.360, bf16[1024,1024]{1,0:T(8,128)(2,1)} %bitcast.358, bf16[1024,2048]{1,0:T(8,128)(2,1)} %bitcast.355), custom_call_target="tpu_custom_call" | custom-call | flops 12884901888 | bytes 27262976 | tf_op jit(solution)/shard_map/expert_grads/pallas_call | solution.py:180
  546.1 39.8 %expert_pass.7 = (bf16[2,512,2048]{2,1,0:T(8,128)(2,1)}, bf16[2,512,2048]{2,1,0:T(8,128)(2,1)}, bf16[2,512,1024]{2,1,0:T(8,128)(2,1)}, bf16[2,512,1024]{2,1,0:T(...) custom-call(s32[2]{0:T(128)} %get-tuple-element.237.counts, ...), custom_call_target="tpu_custom_call" | custom-call | flops 34359738368 | bytes 41943040 | tf_op jit(solution)/shard_map/expert_pass/pallas_call | solution.py:134
  585.9 19.4 %expert_grads.7 = bf16[2,3,2048,1024]{3,2,1,0:T(8,128)(2,1)} custom-call(bf16[1024,2048]{1,0:T(8,128)(2,1)} %bitcast.303, bf16[1024,1024]{1,0:T(8,128)(2,1)} %bitcast.313, bf16[1024,1024]{1,0:T(8,128)(2,1)} %bitcast.314, bf16[1024,1024]{1,0:T(8,128)(2,1)} %bitcast.312, bf16[1024,2048]{1,0:T(8,128)(2,1)} %bitcast.304, ...), custom_call_target="tpu_custom_call", output_to_operand_aliasing={{}: (5, {})} | custom-call | flops 12884901888 | bytes 27262976 | tf_op jit(solution)/shard_map/expert_grads/pallas_call | solution.py:180
  606.8 89.2 %scatter_col.4 = (f32[2048,256]{1,0:T(8,128)}, f32[8,4,2,2,1024]{4,3,2,1,0:T(2,128)}) custom-call(s32[2,1024,4]{2,1,0:T(8,128)} %copy-done.2, bf16[2,512,2048]{2,1,0:T(8,128)(2,1)} %get-tuple-element.122.refs_1_, bf16[2,512,2048]{2,1,0:T(8,128)(2,1)} %get-tuple-element.134.refs_2_, bf16[2,512,2048]{2,1,0:T(8,128)(2,1)} %get-tuple-element.145.refs_3_, ...), custom_call_target="tpu_custom_call" | custom-call | bytes 167772160 | tf_op jit(solution)/shard_map/scatter_col/pallas_call | solution.py:918
  696.0 2.4 slice_reduce_fusion.4
  698.7 3.1 multiply_reduce_fusion.2
  701.8 4.4 convolution_convert_fusion.1.refs_0_
  706.2 50.5 %scatter_col.5 = f32[2048,128]{1,0:T(8,128)} custom-call(bf16[2048,1024]{1,0:T(8,128)(2,1)} %convolution_convert_fusion.1.refs_0_), custom_call_target="tpu_custom_call" | custom-call | bytes 83886080 | tf_op jit(solution)/shard_map/scatter_col/pallas_call | solution.py:918
  756.7 1.3 convert_element_type.399
  758.0 1.7 convolution_bitcast_fusion
  759.7 5.0 fusion.24
  765.4 5.6 multiply_reduce_fusion.1
  771.5 2.5 multiply_convert_fusion.1
  774.1 1.1 fusion.22
  775.2 1.5 fusion.21
  777.0 2.4 fusion.60
  780.1 0.8 multiply_reduce_fusion.4
  781.5 7.0 convolution_convert_fusion.refs_0_
  789.1 5.5 convolution_convert_fusion.2
  794.9 1.3 pad_maximum_fusion.2.refs_6_
  796.2 1.4 copy-done.77
  797.6 2.1 convolution_convert_fusion.5.refs_7_
  799.8 115.4 %scatter_col.6 = (f32[2048,256]{1,0:T(8,128)}, f32[8,24,128]{2,1,0:T(8,128)}, bf16[8,3,256,128]{3,2,1,0:T(8,128)(2,1)}, bf16[8,128,256]{2,1,0:T(8,128)(2,1)}) custom-call(s32[2,1024,4]{2,1,0:T(8,128)} %copy-done.2, bf16[2,512,2048]{2,1,0:T(8,128)(2,1)} %get-tuple-element.169.refs_1_, bf16[2,512,2048]{2,1,0:T(8,128)(2,1)} %get-tuple-element.170.refs_2_, ...), custom_call_target="tpu_custom_call" | custom-call | bytes 167772160 | tf_op jit(solution)/shard_map/scatter_col/pallas_call | solution.py:918
  915.2 3.7 add_convert_fusion
  918.9 1.9 fusion.85
  920.8 1.4 fusion.100
  922.2 1.4 fusion.93
  924.3 82.4 %scatter_col.7 = (f32[2048,256]{1,0:T(8,128)}, f32[4,70,128]{2,1,0:T(8,128)}, bf16[4,2,3,256,128]{4,3,2,1,0:T(8,128)(2,1)}, bf16[4,2,128,256]{3,2,1,0:T(8,128)(2,1)}) custom-call(bf16[2048,2048]{1,0:T(8,128)(2,1)} %convolution_convert_fusion.refs_0_, f32[70,128]{1,0:T(8,128)} %maximum_bitcast_fusion.refs_1_, ...), custom_call_target="tpu_custom_call" | custom-call | bytes 167772160 | tf_op jit(solution)/shard_map/scatter_col/pallas_call | solution.py:918
  1006.8 1.0 reduce_sum.506
  1007.8 6.8 unpack.2
  1016.0 1.7 convert_reduce_fusion
  1017.8 0.9 fusion.72
  1020.4 2.0 multiply_subtract_fusion
  1022.3 6.8 unpack.3
  (242 shorter events, 21.7 us)
Async XLA Ops:
  7.2 339.1 %all-gather.4.cloned.1.call-start = ((), (), s32[]{:S(2)}) async-start(), calls=%async_computation.2 | async-start | bytes 31457280 | tf_op jit(solution)/shard_map/all_gather | solution.py:969
  12.0 465.2 %all-gather.6.cloned.1.call-start = ((), (), s32[]{:S(2)}) async-start(), calls=%async_computation.3 | async-start | bytes 15728640 | tf_op jit(solution)/shard_map/all_gather | solution.py:969
  15.8 3.9 copy-start.72
  15.9 4.2 copy-start.63
  15.9 4.2 copy-start.75
  15.9 530.2 %all-gather.8.cloned.1.call-start = ((), (), s32[]{:S(2)}) async-start(), calls=%async_computation.4 | async-start | bytes 15728640 | tf_op jit(solution)/shard_map/all_gather | solution.py:969
  19.7 904.6 %reduce-scatter.3.cloned.1.call-start = ((), (), s32[]{:S(2)}) async-start(), calls=%async_computation.5 | async-start | bytes 31457280 | tf_op jit(solution)/shard_map/reduce_scatter | solution.py:1079
  140.6 7.4 copy-start.66
  140.6 7.4 copy-start.6
  146.5 5.5 copy-start.51
  147.9 4.0 copy-start.29
  148.0 4.0 copy-start.31
  148.0 4.0 copy-start.33
  148.0 5.5 copy-start.49
  152.0 12.3 %copy-start.3 = (f32[2048,384]{0,1:T(8,128)}, f32[2048,384]{0,1:T(8,128)S(1)}, u32[]{:S(2)}) copy-start(f32[2048,384]{0,1:T(8,128)S(1)} %fusion.8) | copy-start | bytes 9437188
  152.2 12.1 %copy-start.45 = (f32[2048]{0:T(1024)}, f32[2048]{0:T(1024)S(1)}, u32[]{:S(2)}) copy-start(f32[2048]{0:T(1024)S(1)} %get-tuple-element.205) | copy-start | bytes 24580
  152.2 12.1 %copy-start.47 = (f32[2048]{0:T(1024)}, f32[2048]{0:T(1024)S(1)}, u32[]{:S(2)}) copy-start(f32[2048]{0:T(1024)S(1)} %get-tuple-element.206) | copy-start | bytes 24580
  153.5 11.2 %copy-start.43 = (f32[1,8,2,128]{3,1,2,0:T(8,128)}, f32[1,8,2,128]{3,1,2,0:T(8,128)S(1)}, u32[]{:S(2)}) copy-start(f32[1,8,2,128]{3,1,2,0:T(8,128)S(1)} %copy.185) | copy-start | bytes 24580
  153.5 22.9 %copy-start.55 = (f32[1,8,2,128]{3,1,2,0:T(8,128)}, f32[1,8,2,128]{3,1,2,0:T(8,128)S(1)}, u32[]{:S(2)}) copy-start(f32[1,8,2,128]{3,1,2,0:T(8,128)S(1)} %copy.184) | copy-start | bytes 24580
  155.7 8.7 copy-start.68
  155.7 8.7 copy-start.70
  164.3 3.6 copy-start.73
  164.3 3.0 copy-start.38
  164.4 2.9 copy-start.40
  167.6 2.8 copy-start.18
  170.5 3.4 copy-start
  170.5 3.4 copy-start.9
  171.7 3.7 copy-start.35
  175.4 145.1 %copy-start.12 = (f32[2048,4]{1,0:T(8,128)S(1)}, f32[2048,4]{1,0:T(8,128)}, u32[]{:S(2)}) copy-start(f32[2048,4]{1,0:T(8,128)} %copy.142) | copy-start | bytes 98308
  334.9 5.8 copy-start.5
  335.5 5.2 copy-start.53
  335.5 5.2 copy-start.37
  340.7 3.4 copy-start.1
  475.4 547.0 %reduce-scatter.5.cloned.1.call-start = ((), (), s32[]{:S(2)}) async-start(), calls=%async_computation.6 | async-start | bytes 31457280 | tf_op jit(solution)/shard_map/reduce_scatter | solution.py:1079
  606.7 91.8 %copy-start.14 = (f32[2048,32]{0,1:T(8,128)S(1)}, f32[2048,32]{0,1:T(8,128)}, u32[]{:S(2)}) copy-start(f32[2048,32]{0,1:T(8,128)} %copy-done.13) | copy-start | bytes 786436
  606.7 91.8 %copy-start.8 = (f32[2048,32]{0,1:T(8,128)S(1)}, f32[2048,32]{0,1:T(8,128)}, u32[]{:S(2)}) copy-start(f32[2048,32]{0,1:T(8,128)} %copy-done.7) | copy-start | bytes 786436
  606.7 91.9 %copy-start.25 = (bf16[2048,256]{1,0:T(8,128)(2,1)S(1)}, bf16[2048,256]{1,0:T(8,128)(2,1)}, u32[]{:S(2)}) copy-start(bf16[2048,256]{1,0:T(8,128)(2,1)} %param.31) | copy-start | bytes 3145732
  606.7 91.9 %copy-start.54 = (f32[2048]{0:T(1024)S(1)}, f32[2048]{0:T(1024)}, u32[]{:S(2)}) copy-start(f32[2048]{0:T(1024)} %copy-done.53) | copy-start | bytes 24580
  606.7 91.9 %copy-start.56 = (f32[1,8,2,128]{3,1,2,0:T(8,128)S(1)}, f32[1,8,2,128]{3,1,2,0:T(8,128)}, u32[]{:S(2)}) copy-start(f32[1,8,2,128]{3,1,2,0:T(8,128)} %copy-done.55) | copy-start | bytes 24580
  606.8 91.9 %copy-start.65 = (f32[2048]{0:T(1024)S(1)}, f32[2048]{0:T(1024)}, u32[]{:S(2)}) copy-start(f32[2048]{0:T(1024)} %get-tuple-element.284) | copy-start | bytes 24580
  606.8 91.9 %copy-start.76 = (f32[256]{0:T(256)S(1)}, f32[256]{0:T(256)}, u32[]{:S(2)}) copy-start(f32[256]{0:T(256)} %param.18) | copy-start | bytes 3076
  706.2 53.5 %copy-start.36 = (f32[2,1024]{1,0:T(2,128)S(1)}, f32[2,1024]{1,0:T(2,128)}, u32[]{:S(2)}) copy-start(f32[2,1024]{1,0:T(2,128)} %copy-done.35) | copy-start | bytes 24580
  759.7 5.7 copy-start.10
  765.2 5.8 slice-start
  765.4 6.2 slice-start.1
  776.8 2.6 copy-start.4
  776.8 2.6 copy-start.39
  776.8 2.6 copy-start.41
  776.8 2.6 copy-start.69
  776.9 3.2 copy-start.46
  776.9 3.2 copy-start.48
  780.1 8.9 slice-start.2
  781.5 7.6 slice-start.3
  781.5 7.6 copy-start.52
  781.5 7.6 copy-start.67
  794.6 3.0 copy-start.77
  915.2 3.7 copy-start.42
  915.2 5.6 copy-start.28
  915.2 7.0 copy-start.27
  1006.8 8.4 copy-start.26
  1014.6 5.2 copy-start.64
  1014.6 5.8 copy-start.11
  1014.6 5.8 copy-start.15
  1014.6 5.8 copy-start.50
  (23 other events, 33.8 us)
Sparse Core Ops, SparseCore 0:
  12.2 246.6 all-gather.3
  260.7 122.5 all-gather.5
  385.1 122.5 all-gather.7
  510.6 221.8 reduce-scatter.2
  735.8 245.6 reduce-scatter.4
